TPU v7x, 256 devices: a whole 4x4x8 slice. The times are simulated.
256 devices in a mesh: row: 8 (over x, core), col: 32 (over z, y).
Axes of the slice: x: 4, y: 4, z: 8, core: 2. Of those that a mesh axis runs over, the one named last changes fastest.
Arguments:
- picture_embedding_matrix: bfloat16 [16384, 1152], P(('row', 'col')), may hold values from -0.19921875 to 0.19921875
- caption_embedding_matrix: bfloat16 [16384, 1152], P(('row', 'col')), may hold values from -0.19921875 to 0.19921875
- sharpness_scale: float32 [1], replicated, may hold values from 4 to 12
- additive_shift: float32 [1], replicated, may hold values from -4 to -2
Outputs:
- grad_images: float32 [16384, 1152], P(('row', 'col'))
- grad_texts: float32 [16384, 1152], P(('row', 'col'))
- image_loss: float32 [16384], P(('row', 'col'))
All inputs are finite; a program needn't handle non-finite values.
Results may differ from a plain program's by a relative error of at most 0.0053.
Values may be sent and summed in bfloat16 or wider, within the bound.
No kernel may reach another device: no remote copies, remote signals or barrier semaphores. Data moves between devices by JAX's collectives and lax.ppermute only.
A program may use at most 128 MiB of HBM per device.

v0:
```python
import jax
import jax.numpy as jnp
from jax import lax
from jax.sharding import Mesh
from jax.sharding import PartitionSpec as P

COL = ("col_0", "col_1")
ROW_COL = ("row", "col_0", "col_1")


EPS = 1e-06


def laid_out(blocks, dim):
    dims = list(blocks.shape[1:])
    dims[dim] *= blocks.shape[0]
    return jnp.moveaxis(blocks, 0, dim).reshape(dims)


def copy_for_each(shard, axis):
    copies = jnp.broadcast_to(shard, (lax.axis_size(axis), *shard.shape))
    return lax.all_to_all(copies, axis, split_axis=0, concat_axis=0, tiled=True)


def gather_directly(shard, axis, dim):
    return laid_out(copy_for_each(shard, axis), dim)


def gathered_by_axis(shard, axes, dim):
    if not axes:
        return shard
    nearer = lax.all_gather(shard, axes[-1], axis=dim, tiled=True)
    return gathered_by_axis(nearer, axes[:-1], dim)


def summed_rows(shard, axes, dim):
    if not axes:
        return shard
    nearer = lax.psum_scatter(shard, axes[0], scatter_dimension=dim, tiled=True)
    return summed_rows(nearer, axes[1:], dim)


def cut_along(shard, dim, count):
    before, after = (shard.shape[:dim], shard.shape[dim + 1 :])
    return jnp.moveaxis(shard.reshape(*before, count, -1, *after), dim, 0)


def sent_and_summed(shard, axis, dim):
    blocks = cut_along(shard, dim, lax.axis_size(axis))
    arrived = lax.all_to_all(blocks, axis, split_axis=0, concat_axis=0, tiled=True)
    return arrived.sum(axis=0)


def normalize(feats):
    values = feats.astype(jnp.float32)
    inverse = lax.rsqrt(jnp.sum(values * values, axis=-1, keepdims=True) + EPS)
    return (values * inverse, inverse)


def back_norm(grad, unit, inverse):
    return inverse * (grad - unit * jnp.sum(unit * grad, axis=-1, keepdims=True))


def similarity_entry(
    picture_group,
    caption_group,
    picture_position,
    caption_position,
    sharpness_scale,
    additive_shift,
):
    similarity_matrix = (
        jnp.dot(picture_group, caption_group.T, preferred_element_type=jnp.float32)
        * sharpness_scale[0]
        + additive_shift[0]
    )
    match_sign = picture_position[:, None] == caption_position[None, :]
    label = jnp.where(match_sign, jnp.float32(1.0), jnp.float32(-1.0))
    sigmoid_loss = jnp.sum(jnp.log1p(jnp.exp(-label * similarity_matrix)), axis=1)
    logistic_weight = (
        sharpness_scale[0] * (jax.nn.sigmoid(similarity_matrix) - match_sign.astype(jnp.float32))
    ).astype(jnp.bfloat16)
    return (logistic_weight, sigmoid_loss)


def transpose_product(logistic_weight, picture_group):
    return lax.dot_general(
        logistic_weight, picture_group, (((0,), (0,)), ((), ())), preferred_element_type=jnp.float32
    )


def on_device(picture_embedding_matrix, caption_embedding_matrix, sharpness_scale, additive_shift):
    img_f, img_inv = normalize(picture_embedding_matrix)
    txt_f, txt_inv = normalize(caption_embedding_matrix)
    img_b = img_f.astype(jnp.bfloat16)
    caption_segment = txt_f.astype(jnp.bfloat16)
    sample_total = img_b.shape[0]
    n_row = lax.axis_size("row")
    n_col = lax.axis_size(COL)
    row_at = lax.axis_index("row")
    col_at = lax.axis_index(COL)
    caption_group = gather_directly(caption_segment, "row", 0)
    picture_group = gathered_by_axis(img_b, COL, 0)
    picture_position = row_at * (n_col * sample_total) + jnp.arange(
        n_col * sample_total, dtype=jnp.int32
    )
    text_local = jnp.arange(n_row * sample_total, dtype=jnp.int32)
    caption_position = (
        text_local // sample_total * (n_col * sample_total)
        + col_at * sample_total
        + text_local % sample_total
    )
    logistic_weight, sigmoid_loss = similarity_entry(
        picture_group,
        caption_group,
        picture_position,
        caption_position,
        sharpness_scale,
        additive_shift,
    )
    partial_value = jnp.dot(logistic_weight, caption_group, preferred_element_type=jnp.float32)
    g_img, loss_own = (summed_rows(partial_value, COL, 0), summed_rows(sigmoid_loss, COL, 0))
    g_txt = sent_and_summed(transpose_product(logistic_weight, picture_group), "row", 0)
    return (back_norm(g_img, img_f, img_inv), back_norm(g_txt, txt_f, txt_inv), loss_own)


def solution(mesh):
    torus = Mesh(mesh.devices.reshape(mesh.shape["row"], 8, 4), ("row", "col_0", "col_1"))
    return jax.shard_map(
        on_device,
        mesh=torus,
        in_specs=(P(ROW_COL, None), P(ROW_COL, None), P(), P()),
        out_specs=(P(ROW_COL, None), P(ROW_COL, None), P(ROW_COL)),
        check_vma=False,
    )
```

profile of v0, /device:TPU:1, one launch (start us, length us, event | category | flops | bytes accessed | tf_op | source)
XLA Modules:
  0.0 240.8 jit_solution(1095393702636922605)
XLA Ops:
  7.2 0.0 all-gather.2.cloned.1.call-start
  7.2 1.0 fusion.17
  8.3 1.0 fusion.13
  9.3 13.3 %all_gather.6 = bf16[256,1152]{1,0:T(8,128)(2,1)} all-gather(bf16[64,1152]{1,0:T(8,128)(2,1)S(1)} %fusion.13), channel_id=1, replica_groups=mesh['row'=8,'col_0'=8,'col_1'=4] {'col_1'}, dimensions={0}, use_global_device_ids=true | all-gather | bytes 737280 | tf_op jit(solution)/shard_map/all_gather | solution.py:32
  22.5 0.0 all-gather.2.cloned.1.call-update
  22.6 1.0 fusion.21
  23.6 1.0 fusion.10
  24.6 1.2 broadcast_in_dim.6
  25.8 7.5 %all-to-all-start = ((bf16[8,64,1152]{2,1,0:T(8,128)(2,1)}), bf16[8,64,1152]{2,1,0:T(8,128)(2,1)S(1)}, u32[]{:S(2)}, u32[]{:S(2)}) async-start(bf16[8,64,1152]{2,1,0:T(8,128)(2,1)} %broadcast_in_dim.6), calls=%async_computation | async-start | bytes 2359296 | tf_op jit(solution)/shard_map/all_to_all | solution.py:22
  34.6 15.2 %all-to-all-done = bf16[8,64,1152]{2,1,0:T(8,128)(2,1)S(1)} async-done(((bf16[8,64,1152]{2,1,0:T(8,128)(2,1)}), bf16[8,64,1152]{2,1,0:T(8,128)(2,1)S(1)}, u32[]{:S(2)}, u32[]{:S(2)}) %all-to-all-start) | async-done | bytes 1179680 | tf_op jit(solution)/shard_map/all_to_all | solution.py:22
  49.8 37.4 %all-gather.2.cloned.1.call-done = bf16[2048,1152]{1,0:T(8,128)(2,1)} async-done(((bf16[256,1152]{1,0:T(8,128)(2,1)}), bf16[2048,1152]{1,0:T(8,128)(2,1)}) %all-gather.2.cloned.1.call-update) | async-done | bytes 4718608 | tf_op jit(solution)/shard_map/all_gather | solution.py:32
  87.2 8.2 %fusion.7 = (f32[2048]{0:T(1024)S(1)}, bf16[2048,512]{0,1:T(8,128)(2,1)S(1)}) fusion(s32[2048]{0:T(1024)S(1)} %iota_add_fusion, f32[]{:T(128)} %bitcast.13, f32[]{:T(128)} %bitcast.12, s32[512]{0:T(512)S(1)} %fusion.28, bf16[2048,1152]{1,0:T(8,128)(2,1)} %all-gather.2.cloned.1.call-done, bf16[512,1152]{1,0:T(8,128)(2,1)S(1)} %bitcast.15), kind=kOutput, calls=%fused_computation.9 | convolution fusion | flops 2430597120 | bytes 8013832 | tf_op jit(solution)/shard_map/dot_general | solution.py:73
  95.5 5.4 %fusion.32 = f32[2048,1152]{1,0:T(8,128)} fusion(bf16[2048,512]{0,1:T(8,128)(2,1)S(1)} %get-tuple-element.4, bf16[512,1152]{1,0:T(8,128)(2,1)S(1)} %bitcast.16), kind=kOutput, calls=%fused_computation.46 | convolution fusion | flops 2415919104 | bytes 12713984 | tf_op jit(solution)/shard_map/dot_general | solution.py:121
  100.8 0.0 reduce-scatter.3.cloned.1.call-update
  100.9 6.6 %fusion.33 = f32[512,1152]{1,0:T(8,128)} fusion(bf16[2048,512]{0,1:T(8,128)(2,1)S(1)} %get-tuple-element.4, bf16[2048,1152]{1,0:T(8,128)(2,1)} %all-gather.2.cloned.1.call-done), kind=kOutput, calls=%fused_computation.47 | convolution fusion | flops 2415919104 | bytes 9175040 | tf_op jit(solution)/shard_map/dot_general | solution.py:87
  107.5 5.1 %all-to-all-start.1 = ((f32[8,64,1152]{2,1,0:T(8,128)}), f32[8,64,1152]{2,1,0:T(8,128)S(1)}, u32[]{:S(2)}, u32[]{:S(2)}) async-start(f32[8,64,1152]{2,1,0:T(8,128)} %bitcast.14), calls=%async_computation.3 | async-start | bytes 4718592 | tf_op jit(solution)/shard_map/all_to_all | solution.py:50
  112.6 0.0 reduce-scatter.5.cloned.1.call-start
  112.6 91.9 %reduce-scatter.3.cloned.1.call-done = f32[256,1152]{1,0:T(8,128)} async-done(((f32[2048,1152]{1,0:T(8,128)}), f32[256,1152]{1,0:T(8,128)}) %reduce-scatter.3.cloned.1.call-update) | async-done | bytes 1179664 | tf_op jit(solution)/shard_map/reduce_scatter | solution.py:39
  204.5 0.0 reduce-scatter.5.cloned.1.call-update
  204.5 0.6 dynamic-slice.2
  205.1 0.6 dynamic-slice
  207.0 12.1 %all-reduce = f32[2048]{0:T(1024)S(1)} all-reduce(f32[2048]{0:T(1024)S(1)} %get-tuple-element.3), channel_id=4, replica_groups=mesh['row'=8,'col_0'=8,'col_1'=4] {'col_0'}, use_global_device_ids=true, to_apply=%region_8.9.clone | all-reduce | flops 2048 | bytes 16384
  219.1 0.1 dynamic-slice.1
  219.2 9.6 %all-reduce.1 = f32[256]{0:T(256)S(1)} all-reduce(f32[256]{0:T(256)S(1)} %dynamic-slice.1), channel_id=5, replica_groups=mesh['row'=8,'col_0'=8,'col_1'=4] {'col_1'}, use_global_device_ids=true, to_apply=%region_9.10.clone | all-reduce | flops 256 | bytes 2048
  228.8 0.6 dynamic-slice.3
  229.4 0.0 all-to-all-done.1
  229.4 0.1 reduce_sum.57
  229.6 0.2 fusion.18
  229.8 0.8 fusion.20
  230.6 0.6 reduce-scatter.5.cloned.1.call-done
  231.3 1.2 fusion.14
  232.4 1.8 fusion.16
  (13 shorter events, 0.0 us)
Async XLA Ops:
  7.2 80.1 %all-gather.2.cloned.1.call-start = ((), (), s32[]{:S(2)}) async-start(), calls=%async_computation.4 | async-start | bytes 5308416 | tf_op jit(solution)/shard_map/all_gather | solution.py:32
  25.8 24.0 %all-to-all-start = ((bf16[8,64,1152]{2,1,0:T(8,128)(2,1)}), bf16[8,64,1152]{2,1,0:T(8,128)(2,1)S(1)}, u32[]{:S(2)}, u32[]{:S(2)}) async-start(bf16[8,64,1152]{2,1,0:T(8,128)(2,1)} %broadcast_in_dim.6), calls=%async_computation | async-start | bytes 2359296 | tf_op jit(solution)/shard_map/all_to_all | solution.py:22
  33.3 171.2 %reduce-scatter.3.cloned.1.call-start = ((), (), s32[]{:S(2)}) async-start(), calls=%async_computation.5 | async-start | bytes 10616832 | tf_op jit(solution)/shard_map/reduce_scatter | solution.py:39
  107.5 97.0 %copy-start.3 = (u32[256]{0:T(256)S(1)}, u32[256]{0:T(256)}, u32[]{:S(2)}) copy-start(u32[256]{0:T(256)} %constant.66) | copy-start | bytes 3076
  107.5 97.6 %copy-start.2 = (u32[256]{0:T(256)S(1)}, u32[256]{0:T(256)}, u32[]{:S(2)}) copy-start(u32[256]{0:T(256)} %constant.62) | copy-start | bytes 3076
  107.5 122.1 %copy-start = (bf16[64,1152]{1,0:T(8,128)(2,1)S(1)}, bf16[64,1152]{1,0:T(8,128)(2,1)}, u32[]{:S(2)}) copy-start(bf16[64,1152]{1,0:T(8,128)(2,1)} %param.5) | copy-start | bytes 442372
  107.5 123.8 %copy-start.1 = (bf16[64,1152]{1,0:T(8,128)(2,1)S(1)}, bf16[64,1152]{1,0:T(8,128)(2,1)}, u32[]{:S(2)}) copy-start(bf16[64,1152]{1,0:T(8,128)(2,1)} %param.4) | copy-start | bytes 442372
  107.5 121.9 %all-to-all-start.1 = ((f32[8,64,1152]{2,1,0:T(8,128)}), f32[8,64,1152]{2,1,0:T(8,128)S(1)}, u32[]{:S(2)}, u32[]{:S(2)}) async-start(f32[8,64,1152]{2,1,0:T(8,128)} %bitcast.14), calls=%async_computation.3 | async-start | bytes 4718592 | tf_op jit(solution)/shard_map/all_to_all | solution.py:50
  112.6 118.7 %reduce-scatter.5.cloned.1.call-start = ((), (), s32[]{:S(2)}) async-start(), calls=%async_computation.6 | async-start | bytes 1474560 | tf_op jit(solution)/shard_map/reduce_scatter | solution.py:39
Sparse Core Ops, SparseCore 0:
  22.7 64.5 all-gather.1
  101.0 103.4 reduce-scatter.2
  207.1 24.1 reduce-scatter.4
where the time goes:
time: 244 us; the launch traced here: 241 us
  waiting for transfers between devices  145 us (59%)
  blocking collectives  35 us (14%)
  matrix products  20.2 us (8%)
  between operations  16.4 us (7%)
  starting transfers between devices  12.6 us (5%)
  other arithmetic  8.27 us (3%)
  local copies, waits for them, and re-layouts  3 us (1%)
    reduce_scatter x2, waiting for transfers between devices, summed_rows(): nearer = lax.psum_scatter(shard, axes[0], scatter_dimension=dim, tiled=True)  92.6 us
    all_gather x1, waiting for transfers between devices, gathered_by_axis(): nearer = lax.all_gather(shard, axes[-1], axis=dim, tiled=True)  37.4 us
    unnamed x2, blocking collectives  21.8 us
    all_to_all x1, waiting for transfers between devices, copy_for_each(): return lax.all_to_all(copies, axis, split_axis=0, concat_axis=0, tiled=True)  15.2 us
    all_gather x1, blocking collectives, gathered_by_axis(): nearer = lax.all_gather(shard, axes[-1], axis=dim, tiled=True)  13.3 us
    dot_general x1, matrix products, similarity_entry(): jnp.dot(picture_group, caption_group.T, preferred_element_type=jnp.float32)  8.23 us
    all_to_all x1, starting transfers between devices, copy_for_each(): return lax.all_to_all(copies, axis, split_axis=0, concat_axis=0, tiled=True)  7.51 us
    dot_general x1, matrix products, transpose_product(): lax.dot_general(logistic_weight, picture_group, (((0,), (0,)), ((), ())),...  6.62 us
  transfers between devices with their start and end apart: 5, of which 4 were waited for; matrix products, arithmetic and copies ran while one was open for 5% of the time, Pallas kernels for 0%

commit v1 on v0

v1 whole, which is shorter than its diff:
```python
import functools

import jax
import jax.numpy as jnp
from jax import lax
from jax.experimental import pallas as pl
from jax.experimental.pallas import tpu as pltpu
from jax.sharding import Mesh
from jax.sharding import PartitionSpec as P

AXES = ("x", "core", "z", "y")
NX, NC, NZ, NY = 4, 2, 8, 4
EPS = 1e-06
F32 = jnp.float32
BF16 = jnp.bfloat16
MIB = 1 << 20
VMEM = pl.BlockSpec(memory_space=pltpu.VMEM)
SMEM = pl.BlockSpec(memory_space=pltpu.SMEM)


def device(x, core, z, y):
    return ((x % NX * NC + core) * NZ + z % NZ) * NY + y % NY


def permutation(move):
    return [
        (device(x, c, z, y), device(*move(x, c, z, y)))
        for x in range(NX)
        for c in range(NC)
        for z in range(NZ)
        for y in range(NY)
    ]


def first(a, s):
    return lax.ppermute(
        a, AXES, permutation(lambda x, c, z, y: (x, c, z, y + s) if c else (x + s, c, z, y))
    )


def second(a, s):
    return lax.ppermute(
        a, AXES, permutation(lambda x, c, z, y: (x + s, c, z, y) if c else (x, c, z, y + s))
    )


def along_z(a, s):
    return lax.ppermute(a, AXES, permutation(lambda x, c, z, y: (x, c, z + s, y)))


def swap_core(a):
    return lax.ppermute(a, AXES, permutation(lambda x, c, z, y: (x, 1 - c, z, y)))


def call(body, outs, n_in, flops, moved, name, scalars=0):
    return pl.pallas_call(
        body,
        out_shape=outs,
        in_specs=[SMEM] * scalars + [VMEM] * (n_in - scalars),
        out_specs=[VMEM] * len(outs),
        name=name,
        cost_estimate=pl.CostEstimate(flops=flops, bytes_accessed=moved, transcendentals=0),
        compiler_params=pltpu.CompilerParams(vmem_limit_bytes=20 * MIB),
    )


def shape(*dims, dtype=BF16):
    return jax.ShapeDtypeStruct(dims, dtype)


def normalize_body(img_ref, txt_ref, img_unit, txt_unit, img_inv, txt_inv):
    for raw, unit, inv in ((img_ref, img_unit, img_inv), (txt_ref, txt_unit, txt_inv)):
        v = raw[...].astype(F32)
        r = lax.rsqrt(jnp.sum(v * v, axis=-1, keepdims=True) + EPS)
        unit[...] = (v * r).astype(BF16)
        inv[...] = r


def split3(v):
    hi = v.astype(BF16).astype(F32)
    mid = (v - hi).astype(BF16).astype(F32)
    return hi, mid, v - hi - mid


def loss_rows(total):
    hi, mid, low = split3(total)
    at = lax.broadcasted_iota(jnp.int32, total.shape, 0)
    return jnp.where(at == 0, hi, jnp.where(at == 1, mid, jnp.where(at == 2, low, 0.0))).astype(BF16)


def loss_sum(rows):
    return jnp.sum(rows.astype(F32), axis=0, keepdims=True)


def entry_body(own, scale_ref, bias_ref, img_ref, txt_ref, coeff_ref, grad_ref, loss_ref=None):
    scale, bias = scale_ref[0], bias_ref[0]
    rows, cols = img_ref.shape[0], txt_ref.shape[0]
    step = 256
    total = jnp.zeros((rows, step), F32)
    for n in range(cols // step):
        at = slice(n * step, (n + 1) * step)
        dots = lax.dot_general(
            img_ref[...], txt_ref[at, :], (((1,), (1,)), ((), ())), preferred_element_type=F32
        )
        logits = dots * scale + bias
        if own and n == 0:
            r = lax.broadcasted_iota(jnp.int32, logits.shape, 0)
            c = lax.broadcasted_iota(jnp.int32, logits.shape, 1)
            match = (r == c) & (r < 64)
            e = jnp.exp(jnp.where(match, -logits, logits))
        else:
            e = jnp.exp(logits)
        u = 1.0 + e
        inv = 1.0 / u
        total = total + (jnp.log(u) + (e - (u - 1.0)) * inv)
        if own and n == 0:
            weight = jnp.where(match, -scale, scale) * (e * inv)
        else:
            weight = scale * (e * inv)
        coeff_ref[:, at] = weight.astype(BF16)
    grad = jnp.dot(coeff_ref[...], txt_ref[...], preferred_element_type=F32)
    loss = jnp.sum(total, axis=1, keepdims=True)
    across = jnp.transpose(jnp.broadcast_to(loss, (rows, 128)))[:8, :]
    if loss_ref is not None:
        grad_ref[...] = grad
        loss_ref[...] = across
    else:
        grad_ref[:rows, :] = grad.astype(BF16)
        grad_ref[rows:, :] = jnp.zeros((8, grad.shape[1]), BF16)
        grad_ref[rows:, :rows] = loss_rows(across)


def texts_body(c0, c1, c2, c3, s0, s1, s2, s3, out_ref, *, half):
    n = out_ref.shape[0]
    at = slice(half * n, (half + 1) * n)
    total = None
    for c, s in ((c0, s0), (c1, s1), (c2, s2), (c3, s3)):
        part = lax.dot_general(
            c[:, at], s[...], (((0,), (0,)), ((), ())), preferred_element_type=F32
        )
        total = part if total is None else total + part
    out_ref[...] = total.astype(out_ref.dtype)


def merge_img_body(g_ref, l_ref, r1, r2, r3, own_ref, own_loss, m1, m2, m3):
    rows = g_ref.shape[0]
    loss = l_ref[...] + (
        loss_sum(r1[rows:, :rows]) + loss_sum(r2[rows:, :rows]) + loss_sum(r3[rows:, :rows])
    )
    own_loss[...] = loss
    marks = loss_rows(loss)
    for j, out in enumerate((own_ref, m1, m2, m3)):
        at = slice(64 * j, 64 * j + 64)
        total = g_ref[at, :] + (
            r1[at, :].astype(F32) + r2[at, :].astype(F32) + r3[at, :].astype(F32)
        )
        out[:64, :] = total.astype(out.dtype)
        if j:
            out[64:, :] = jnp.zeros((8, total.shape[1]), BF16)
            out[64:, :rows] = marks


def merge_txt_body(g_ref, o_ref, a_ref, b_ref, far_a, far_b, near_ref):
    del a_ref, b_ref
    far_a[...] = (g_ref[256:384, :] + o_ref[256:384, :].astype(F32)).astype(BF16)
    far_b[...] = (g_ref[384:512, :] + o_ref[384:512, :].astype(F32)).astype(BF16)
    near_ref[...] = g_ref[:256, :] + o_ref[:256, :].astype(F32)


def merge_near_body(near_ref, a_ref, b_ref, own, back, ahead, across):
    own[...] = near_ref[:64, :]
    back[...] = (near_ref[64:128, :] + a_ref[:64, :].astype(F32)).astype(BF16)
    ahead[...] = (near_ref[128:192, :] + b_ref[:64, :].astype(F32)).astype(BF16)
    across[...] = (
        near_ref[192:256, :] + (a_ref[64:, :].astype(F32) + b_ref[64:, :].astype(F32))
    ).astype(BF16)


def back_norm(g, raw, inv):
    unit = raw[...].astype(F32) * inv[...]
    return inv[...] * (g - unit * jnp.sum(unit * g, axis=-1, keepdims=True))


def finish_img_body(g_ref, l_ref, r1, r2, r3, raw, inv, out_ref, loss_ref):
    g = g_ref[...] + (
        r1[:64, :].astype(F32) + r2[:64, :].astype(F32) + r3[:64, :].astype(F32)
    )
    out_ref[...] = back_norm(g, raw, inv)
    loss = l_ref[:1, :64]
    for j, r in enumerate((r1, r2, r3)):
        loss = loss + loss_sum(r[64:, 64 * (j + 1) : 64 * (j + 2)])
    loss_ref[...] = loss


def finish_txt_body(g_ref, r1, r2, r3, raw, inv, out_ref):
    g = g_ref[...] + (r1[...].astype(F32) + r2[...].astype(F32) + r3[...].astype(F32))
    out_ref[...] = back_norm(g, raw, inv)


def on_device(picture, caption, scale, bias):
    rows, d = picture.shape
    img, txt, img_inv, txt_inv = call(
        normalize_body,
        [shape(rows, d), shape(rows, d), shape(rows, 1, dtype=F32), shape(rows, 1, dtype=F32)],
        2, 0, 4 * rows * d * 2, "normalize",
    )(picture, caption)

    f1, f3, f2 = first(img, 1), first(img, 3), first(img, 2)
    t_back, t_ahead = along_z(txt, 1), along_z(txt, -1)
    t_across = along_z(txt, 4)
    group = jnp.concatenate([img, f1, f2, f3], axis=0)
    g1, g3, g2 = second(group, 1), second(group, 3), second(group, 2)
    groups = (group, g1, g2, g3)
    m_back = along_z(jnp.concatenate([t_back, t_across], axis=0), 1)
    m_ahead = along_z(jnp.concatenate([t_ahead, t_across], axis=0), -1)
    near = jnp.concatenate([txt, t_back, t_ahead, t_across], axis=0)
    far = jnp.concatenate([m_back, m_ahead], axis=0)
    texts = jnp.concatenate([near, far, swap_core(near), swap_core(far)], axis=0)

    n = texts.shape[0]
    m = group.shape[0]
    coeffs, grads = [], []
    cost = (4 * m * n * d, (2 * m * d + n * d + m * n) * 2)
    for k in (0, 1, 3, 2):
        outs = [shape(m, n)]
        if k == 0:
            outs += [shape(m, d, dtype=F32), shape(8, m, dtype=F32)]
        else:
            outs += [shape(m + 8, d)]
        res = call(functools.partial(entry_body, k == 0), outs, 4, *cost, f"entry{k}", scalars=2)(
            scale, bias, groups[k], texts
        )
        coeffs.append(res[0])
        grads.append(res[1:])
    order = (0, 1, 3, 2)
    by = [groups[k] for k in order]
    halves = [
        call(
            functools.partial(texts_body, half=h),
            [shape(n // 2, d, dtype=F32 if h == 0 else BF16)],
            8, m * 4 * n * d, (4 * m * d + 2 * m * n + n * d) * 2, f"texts{h}",
        )(*coeffs, *by)[0]
        for h in (1, 0)
    ]
    other, mine = halves

    r1, r3, r2 = second(grads[1][0], -1), second(grads[2][0], -3), second(grads[3][0], -2)
    own_img, own_loss, p1, p2, p3 = call(
        merge_img_body,
        [shape(rows, d, dtype=F32), shape(8, m, dtype=F32)] + [shape(rows + 8, d)] * 3,
        5, 0, 10 * m * d, "merge_img",
    )(*grads[0], r1, r2, r3)
    q1, q3, q2 = first(p1, -1), first(p3, -3), first(p2, -2)

    got = swap_core(other)
    far_a, far_b, near_f = call(
        lambda g, o, a, b, c: merge_txt_body(g, o, None, None, a, b, c),
        [shape(2 * rows, d), shape(2 * rows, d), shape(4 * rows, d, dtype=F32)],
        2, 0, 8 * rows * d * 8, "merge_txt",
    )(mine, got)
    a, b = along_z(far_a, -1), along_z(far_b, 1)
    own_txt, back, ahead, across = call(
        merge_near_body,
        [shape(rows, d, dtype=F32)] + [shape(rows, d)] * 3,
        3, 0, 4 * rows * d * 8, "merge_near",
    )(near_f, a, b)
    u1, u2, u3 = along_z(back, -1), along_z(ahead, 1), along_z(across, 4)

    grad_img, loss = call(
        finish_img_body,
        [shape(rows, d, dtype=F32), shape(1, rows, dtype=F32)],
        7, 0, rows * d * 16, "finish_img",
    )(own_img, own_loss, q1, q2, q3, picture, img_inv)
    grad_txt = call(
        finish_txt_body, [shape(rows, d, dtype=F32)], 6, 0, rows * d * 16, "finish_txt"
    )(own_txt, u1, u2, u3, caption, txt_inv)[0]
    return grad_img, grad_txt, loss.reshape(rows)


def solution(mesh):
    torus = Mesh(mesh.devices.reshape(NX, NC, NZ, NY), AXES)
    return jax.shard_map(
        on_device,
        mesh=torus,
        in_specs=(P(AXES, None), P(AXES, None), P(), P()),
        out_specs=(P(AXES, None), P(AXES, None), P(AXES)),
        check_vma=False,
    )
```

time: 244 us -> 87.2 us (0.36); the launches traced: 241 us -> 86.8 us
  waiting for transfers between devices: 145 us -> 31.6 us
  blocking collectives: 35 us -> 0 us
  starting transfers between devices: 12.6 us -> 37.6 us
  matrix products: 20.2 us -> 0 us
  between operations: 16.4 us -> 2.14 us
  Pallas kernels: 0 us -> 13.3 us
  other arithmetic: 8.27 us -> 0.14 us
    reduce_scatter x2 -> x0, waiting for transfers between devices: 92.6 us -> none  [summed_rows(): nearer = lax.psum_scatter(shard, axes[0], scatter_dimension=dim, tiled=True)]
    ppermute x0 -> x25, starting transfers between devices: none -> 37.6 us  [the longest x10 16.2 us: along_z(): lax.ppermute(a, AXES, permutation(lambda x, c, z, y: (x, c, z + s, y)))]
    all_gather x1 -> x0, waiting for transfers between devices: 37.4 us -> none  [gathered_by_axis(): nearer = lax.all_gather(shard, axes[-1], axis=dim, tiled=True)]
    ppermute x0 -> x25, waiting for transfers between devices: none -> 31.6 us  [the longest x10 17.4 us: along_z(): lax.ppermute(a, AXES, permutation(lambda x, c, z, y: (x, c, z + s, y)))]
    unnamed x2 -> x0, blocking collectives: 21.8 us -> none
    dot_general x3 -> x0, matrix products: 20.2 us -> none  [the longest x1 8.23 us: similarity_entry(): jnp.dot(picture_group, caption_group.T, preferred_element_type=jnp.float32)]
    all_to_all x2 -> x0, waiting for transfers between devices: 15.2 us -> none  [the longest x1 15.2 us: copy_for_each(): return lax.all_to_all(copies, axis, split_axis=0, concat_axis=0, tiled=True)]
    pallas_call x0 -> x12, Pallas kernels: none -> 13.3 us  [the longest x4 7.58 us: on_device(): call(functools.partial(entry_body, k == 0), outs, 4, *cost, f'entry{k}',...]
  transfers between devices with their start and end apart: 5 -> 25, of which waited for: 4 -> 10; matrix products, arithmetic and copies ran while one was open for 5% -> 1% of each run, Pallas kernels for 0% -> 10%
where the time goes in v1:
time: 87.2 us; the launch traced here: 86.8 us
  starting transfers between devices  37.6 us (43%)
  waiting for transfers between devices  31.6 us (36%)
  Pallas kernels  13.3 us (15%)
  local copies, waits for them, and re-layouts  2.16 us (2%)
  between operations  2.14 us (2%)
    ppermute x10, waiting for transfers between devices, along_z(): lax.ppermute(a, AXES, permutation(lambda x, c, z, y: (x, c, z + s, y)))  17.4 us
    ppermute x10, starting transfers between devices, along_z(): lax.ppermute(a, AXES, permutation(lambda x, c, z, y: (x, c, z + s, y)))  16.2 us
    ppermute x6, waiting for transfers between devices, second(): lax.ppermute(a, AXES, permutation(lambda x, c, z, y: (x + s, c, z, y) if...  9.49 us
    ppermute x6, starting transfers between devices, second(): lax.ppermute(a, AXES, permutation(lambda x, c, z, y: (x + s, c, z, y) if...  8.6 us
    ppermute x6, starting transfers between devices, first(): lax.ppermute(a, AXES, permutation(lambda x, c, z, y: (x, c, z, y + s) if...  7.91 us
    pallas_call x4, Pallas kernels, on_device(): call(functools.partial(entry_body, k == 0), outs, 4, *cost, f'entry{k}',...  7.58 us
    ppermute x3, starting transfers between devices, swap_core(): lax.ppermute(a, AXES, permutation(lambda x, c, z, y: (x, 1 - c, z, y)))  4.87 us
    ppermute x6, waiting for transfers between devices, first(): lax.ppermute(a, AXES, permutation(lambda x, c, z, y: (x, c, z, y + s) if...  3.15 us
  transfers between devices with their start and end apart: 25, of which 10 were waited for; matrix products, arithmetic and copies ran while one was open for 1% of the time, Pallas kernels for 10%

profile of v1, /device:TPU:1, one launch (start us, length us, event | category | flops | bytes accessed | tf_op | source)
XLA Modules:
  0.0 86.8 jit_solution(5753782357687052709)
XLA Ops:
  1.5 0.9 %copy-done.2 = bf16[64,1152]{1,0:T(8,128)(2,1)S(1)} copy-done((bf16[64,1152]{1,0:T(8,128)(2,1)S(1)}, bf16[64,1152]{1,0:T(8,128)(2,1)}, u32[]{:S(2)}) %copy-start.2) | copy-done | bytes 147480
  2.6 3.6 %collective-permute-start.2 = (bf16[64,1152]{1,0:T(8,128)(2,1)S(1)}, bf16[64,1152]{1,0:T(8,128)(2,1)S(1)}, u32[]{:S(2)}, u32[]{:S(2)}) collective-permute-start(bf16[64,1152]{1,0:T(8,128)(2,1)S(1)} %get-tuple-element.30), channel_id=1, source_target_pairs={{0,192},{1,193},{2,194},{3,195},{4,196},{5,197},{6,198},{7,199},{8... | collective-permute-start | bytes 442376 | tf_op jit(solution)/shard_map/ppermute | solution.py:36
  7.3 6.9 %collective-permute-start.5 = (bf16[64,1152]{1,0:T(8,128)(2,1)S(1)}, bf16[64,1152]{1,0:T(8,128)(2,1)S(1)}, u32[]{:S(2)}, u32[]{:S(2)}) collective-permute-start(bf16[64,1152]{1,0:T(8,128)(2,1)S(1)} %get-tuple-element.31), channel_id=1, source_target_pairs={{0,16},{1,17},{2,18},{3,19},{4,20},{5,21},{6,22},{7,23},{8,24},{9,... | collective-permute-start | bytes 442376 | tf_op jit(solution)/shard_map/ppermute | solution.py:48
  15.5 1.5 %collective-permute-start.3 = (bf16[64,1152]{1,0:T(8,128)(2,1)S(1)}, bf16[64,1152]{1,0:T(8,128)(2,1)S(1)}, u32[]{:S(2)}, u32[]{:S(2)}) collective-permute-start(bf16[64,1152]{1,0:T(8,128)(2,1)S(1)} %get-tuple-element.31), channel_id=1, source_target_pairs={{0,4},{1,5},{2,6},{3,7},{4,8},{5,9},{6,10},{7,11},{8,12},{9,13},{1... | collective-permute-start | bytes 442376 | tf_op jit(solution)/shard_map/ppermute | solution.py:48
  17.2 2.6 %collective-permute-start.14 = (bf16[256,1152]{1,0:T(8,128)(2,1)S(1)}, bf16[256,1152]{1,0:T(8,128)(2,1)S(1)}, u32[]{:S(2)}, u32[]{:S(2)}) collective-permute-start(bf16[256,1152]{1,0:T(8,128)(2,1)S(1)} %constant_dynamic-update-slice_fusion.img_ref.s0), channel_id=1, source_target_pairs={{0,3},{1,0},{2,1},{3,2},{4,7},{5,4},{6,5},{7,6},{8,11},{9,8},{10,9... | collective-permute-start | bytes 1769480 | tf_op jit(solution)/shard_map/ppermute | solution.py:42
  20.9 3.2 %collective-permute-done.4 = bf16[64,1152]{1,0:T(8,128)(2,1)S(1)} collective-permute-done((bf16[64,1152]{1,0:T(8,128)(2,1)S(1)}, bf16[64,1152]{1,0:T(8,128)(2,1)S(1)}, u32[]{:S(2)}, u32[]{:S(2)}) %collective-permute-start.4) | collective-permute-done | bytes 147488 | tf_op jit(solution)/shard_map/ppermute | solution.py:48
  24.2 2.9 %collective-permute-start.7 = (bf16[128,1152]{1,0:T(8,128)(2,1)S(1)}, bf16[128,1152]{1,0:T(8,128)(2,1)S(1)}, u32[]{:S(2)}, u32[]{:S(2)}) collective-permute-start(bf16[128,1152]{1,0:T(8,128)(2,1)S(1)} %get-tuple-element.57), channel_id=1, source_target_pairs={{0,28},{1,29},{2,30},{3,31},{4,0},{5,1},{6,2},{7,3},{8,4},{9,5},{1... | collective-permute-start | bytes 884744 | tf_op jit(solution)/shard_map/ppermute | solution.py:48
  27.2 5.2 %collective-permute-done.7 = bf16[128,1152]{1,0:T(8,128)(2,1)S(1)} collective-permute-done((bf16[128,1152]{1,0:T(8,128)(2,1)S(1)}, bf16[128,1152]{1,0:T(8,128)(2,1)S(1)}, u32[]{:S(2)}, u32[]{:S(2)}) %collective-permute-start.7) | collective-permute-done | bytes 294944 | tf_op jit(solution)/shard_map/ppermute | solution.py:48
  32.4 1.9 %collective-permute-start.8 = (bf16[256,1152]{1,0:T(8,128)(2,1)S(1)}, bf16[256,1152]{1,0:T(8,128)(2,1)S(1)}, u32[]{:S(2)}, u32[]{:S(2)}) collective-permute-start(bf16[256,1152]{1,0:T(8,128)(2,1)S(1)} %pad_maximum_fusion), channel_id=1, source_target_pairs={{0,32},{1,33},{2,34},{3,35},{4,36},{5,37},{6,38},{7,39},{8,40},{9,... | collective-permute-start | bytes 1769480 | tf_op jit(solution)/shard_map/ppermute | solution.py:52
  34.3 1.2 %collective-permute-done.6 = bf16[128,1152]{1,0:T(8,128)(2,1)S(1)} collective-permute-done((bf16[128,1152]{1,0:T(8,128)(2,1)S(1)}, bf16[128,1152]{1,0:T(8,128)(2,1)S(1)}, u32[]{:S(2)}, u32[]{:S(2)}) %collective-permute-start.6) | collective-permute-done | bytes 294944 | tf_op jit(solution)/shard_map/ppermute | solution.py:48
  35.6 2.5 %collective-permute-start.9 = (bf16[256,1152]{1,0:T(8,128)(2,1)S(1)}, bf16[256,1152]{1,0:T(8,128)(2,1)S(1)}, u32[]{:S(2)}, u32[]{:S(2)}) collective-permute-start(bf16[256,1152]{1,0:T(8,128)(2,1)S(1)} %pad_maximum_fusion.1), channel_id=1, source_target_pairs={{0,32},{1,33},{2,34},{3,35},{4,36},{5,37},{6,38},{7,39},{8,40},{9,... | collective-permute-start | bytes 1769480 | tf_op jit(solution)/shard_map/ppermute | solution.py:52
  38.2 1.5 %collective-permute-done.9 = bf16[256,1152]{1,0:T(8,128)(2,1)S(1)} collective-permute-done((bf16[256,1152]{1,0:T(8,128)(2,1)S(1)}, bf16[256,1152]{1,0:T(8,128)(2,1)S(1)}, u32[]{:S(2)}, u32[]{:S(2)}) %collective-permute-start.9) | collective-permute-done | bytes 589856 | tf_op jit(solution)/shard_map/ppermute | solution.py:52
  39.8 1.9 %entry0.1 = (bf16[256,1024]{1,0:T(8,128)(2,1)S(1)}, f32[256,1152]{1,0:T(8,128)S(1)}, f32[8,256]{1,0:T(8,128)S(1)}) custom-call(f32[1]{0:T(128)S(6)} %copy.17.scale_ref, f32[1]{0:T(128)S(6)} %copy.18.bias_ref, bf16[256,1152]{1,0:T(8,128)(2,1)S(1)} %constant_dynamic-update-slice_fusion.img_ref.s0, ...), custom_call_target="tpu_custom_call" | custom-call | flops 1207959552 | bytes 4063232 | tf_op jit(solution)/shard_map/entry0/pallas_call | solution.py:230
  41.7 1.9 %entry3.1 = (bf16[256,1024]{1,0:T(8,128)(2,1)S(1)}, bf16[264,1152]{1,0:T(8,128)(2,1)S(1)}) custom-call(f32[1]{0:T(128)S(6)} %copy.17.scale_ref, f32[1]{0:T(128)S(6)} %copy.18.bias_ref, bf16[256,1152]{1,0:T(8,128)(2,1)S(1)} %collective-permute-done.14.img_ref.s2, bf16[1024,1152]{1,0:T(8,128)(2,1)S(1)} %constant_dynamic-update-slice_fusion.4.txt_ref), custom_call_target="tpu_custom_call" | custom-call | flops 1207959552 | bytes 4063232 | tf_op jit(solution)/shard_map/entry3/pallas_call | solution.py:230
  43.6 1.9 %entry2.1 = (bf16[256,1024]{1,0:T(8,128)(2,1)S(1)}, bf16[264,1152]{1,0:T(8,128)(2,1)S(1)}) custom-call(f32[1]{0:T(128)S(6)} %copy.17.scale_ref, f32[1]{0:T(128)S(6)} %copy.18.bias_ref, bf16[256,1152]{1,0:T(8,128)(2,1)S(1)} %collective-permute-done.12.img_ref.s3, bf16[1024,1152]{1,0:T(8,128)(2,1)S(1)} %constant_dynamic-update-slice_fusion.4.txt_ref), custom_call_target="tpu_custom_call" | custom-call | flops 1207959552 | bytes 4063232 | tf_op jit(solution)/shard_map/entry2/pallas_call | solution.py:230
  45.5 1.9 %entry1.1 = (bf16[256,1024]{1,0:T(8,128)(2,1)S(1)}, bf16[264,1152]{1,0:T(8,128)(2,1)S(1)}) custom-call(f32[1]{0:T(128)S(6)} %copy.17.scale_ref, f32[1]{0:T(128)S(6)} %copy.18.bias_ref, bf16[256,1152]{1,0:T(8,128)(2,1)S(1)} %collective-permute-done.10.img_ref.s1, bf16[1024,1152]{1,0:T(8,128)(2,1)S(1)} %constant_dynamic-update-slice_fusion.4.txt_ref), custom_call_target="tpu_custom_call" | custom-call | flops 1207959552 | bytes 4063232 | tf_op jit(solution)/shard_map/entry1/pallas_call | solution.py:230
  47.4 1.6 %texts1.1 = bf16[512,1152]{1,0:T(8,128)(2,1)S(1)} custom-call(bf16[256,1024]{1,0:T(8,128)(2,1)S(1)} %get-tuple-element.44.c0, bf16[256,1024]{1,0:T(8,128)(2,1)S(1)} %get-tuple-element.45.c1, bf16[256,1024]{1,0:T(8,128)(2,1)S(1)} %get-tuple-element.46.c2, bf16[256,1024]{1,0:T(8,128)(2,1)S(1)} %get-tuple-element.47.c3, ...), custom_call_target="tpu_custom_call" | custom-call | flops 1207959552 | bytes 5767168 | tf_op jit(solution)/shard_map/texts1/pallas_call | solution.py:238
  49.4 1.2 %collective-permute-start.15 = (bf16[264,1152]{1,0:T(8,128)(2,1)S(1)}, bf16[264,1152]{1,0:T(8,128)(2,1)S(1)}, u32[]{:S(2)}, u32[]{:S(2)}) collective-permute-start(bf16[264,1152]{1,0:T(8,128)(2,1)S(1)} %get-tuple-element.36), channel_id=1, source_target_pairs={{0,1},{1,2},{2,3},{3,0},{4,5},{5,6},{6,7},{7,4},{8,9},{9,10},{10,1... | collective-permute-start | bytes 1824776 | tf_op jit(solution)/shard_map/ppermute | solution.py:42
  50.6 2.5 %collective-permute-start.13 = (bf16[264,1152]{1,0:T(8,128)(2,1)S(1)}, bf16[264,1152]{1,0:T(8,128)(2,1)S(1)}, u32[]{:S(2)}, u32[]{:S(2)}) collective-permute-start(bf16[264,1152]{1,0:T(8,128)(2,1)S(1)} %get-tuple-element.35), channel_id=1, source_target_pairs={{0,2},{1,3},{2,0},{3,1},{4,6},{5,7},{6,4},{7,5},{8,10},{9,11},{10,... | collective-permute-start | bytes 1824776 | tf_op jit(solution)/shard_map/ppermute | solution.py:42
  53.1 1.3 %collective-permute-start.11 = (bf16[264,1152]{1,0:T(8,128)(2,1)S(1)}, bf16[264,1152]{1,0:T(8,128)(2,1)S(1)}, u32[]{:S(2)}, u32[]{:S(2)}) collective-permute-start(bf16[264,1152]{1,0:T(8,128)(2,1)S(1)} %get-tuple-element.34), channel_id=1, source_target_pairs={{0,3},{1,0},{2,1},{3,2},{4,7},{5,4},{6,5},{7,6},{8,11},{9,8},{10,9... | collective-permute-start | bytes 1824776 | tf_op jit(solution)/shard_map/ppermute | solution.py:42
  54.3 1.6 %texts0.1.g = f32[512,1152]{1,0:T(8,128)S(1)} custom-call(bf16[256,1024]{1,0:T(8,128)(2,1)S(1)} %get-tuple-element.44.c0, bf16[256,1024]{1,0:T(8,128)(2,1)S(1)} %get-tuple-element.45.c1, bf16[256,1024]{1,0:T(8,128)(2,1)S(1)} %get-tuple-element.46.c2, bf16[256,1024]{1,0:T(8,128)(2,1)S(1)} %get-tuple-element.47.c3, ...), custom_call_target="tpu_custom_call" | custom-call | flops 1207959552 | bytes 5767168 | tf_op jit(solution)/shard_map/texts0/pallas_call | solution.py:238
  56.9 0.9 %collective-permute-start.21 = (bf16[128,1152]{1,0:T(8,128)(2,1)S(1)}, bf16[128,1152]{1,0:T(8,128)(2,1)S(1)}, u32[]{:S(2)}, u32[]{:S(2)}) collective-permute-start(bf16[128,1152]{1,0:T(8,128)(2,1)S(1)} %get-tuple-element.50), channel_id=1, source_target_pairs={{0,4},{1,5},{2,6},{3,7},{4,8},{5,9},{6,10},{7,11},{8,12},{9,13},{1... | collective-permute-start | bytes 884744 | tf_op jit(solution)/shard_map/ppermute | solution.py:48
  57.9 2.0 %collective-permute-done.15.r3 = bf16[264,1152]{1,0:T(8,128)(2,1)S(1)} collective-permute-done((bf16[264,1152]{1,0:T(8,128)(2,1)S(1)}, bf16[264,1152]{1,0:T(8,128)(2,1)S(1)}, u32[]{:S(2)}, u32[]{:S(2)}) %collective-permute-start.15) | collective-permute-done | bytes 608288 | tf_op jit(solution)/shard_map/ppermute | solution.py:42
  59.8 7.5 %collective-permute-done.13.r2 = bf16[264,1152]{1,0:T(8,128)(2,1)S(1)} collective-permute-done((bf16[264,1152]{1,0:T(8,128)(2,1)S(1)}, bf16[264,1152]{1,0:T(8,128)(2,1)S(1)}, u32[]{:S(2)}, u32[]{:S(2)}) %collective-permute-start.13) | collective-permute-done | bytes 608288 | tf_op jit(solution)/shard_map/ppermute | solution.py:42
  67.6 1.8 %collective-permute-start.16 = (bf16[72,1152]{1,0:T(8,128)(2,1)S(1)}, bf16[72,1152]{1,0:T(8,128)(2,1)S(1)}, u32[]{:S(2)}, u32[]{:S(2)}) collective-permute-start(bf16[72,1152]{1,0:T(8,128)(2,1)S(1)} %get-tuple-element.39), channel_id=1, source_target_pairs={{0,192},{1,193},{2,194},{3,195},{4,196},{5,197},{6,198},{7,199},{8... | collective-permute-start | bytes 497672 | tf_op jit(solution)/shard_map/ppermute | solution.py:36
  69.4 1.5 %collective-permute-start.17 = (bf16[72,1152]{1,0:T(8,128)(2,1)S(1)}, bf16[72,1152]{1,0:T(8,128)(2,1)S(1)}, u32[]{:S(2)}, u32[]{:S(2)}) collective-permute-start(bf16[72,1152]{1,0:T(8,128)(2,1)S(1)} %get-tuple-element.40), channel_id=1, source_target_pairs={{0,128},{1,129},{2,130},{3,131},{4,132},{5,133},{6,134},{7,135},{8... | collective-permute-start | bytes 497672 | tf_op jit(solution)/shard_map/ppermute | solution.py:36
  71.6 0.9 %collective-permute-start.23 = (bf16[64,1152]{1,0:T(8,128)(2,1)S(1)}, bf16[64,1152]{1,0:T(8,128)(2,1)S(1)}, u32[]{:S(2)}, u32[]{:S(2)}) collective-permute-start(bf16[64,1152]{1,0:T(8,128)(2,1)S(1)} %get-tuple-element.53), channel_id=1, source_target_pairs={{0,4},{1,5},{2,6},{3,7},{4,8},{5,9},{6,10},{7,11},{8,12},{9,13},{1... | collective-permute-start | bytes 442376 | tf_op jit(solution)/shard_map/ppermute | solution.py:48
  72.6 0.9 %collective-permute-done.16.r1 = bf16[72,1152]{1,0:T(8,128)(2,1)S(1)} collective-permute-done((bf16[72,1152]{1,0:T(8,128)(2,1)S(1)}, bf16[72,1152]{1,0:T(8,128)(2,1)S(1)}, u32[]{:S(2)}, u32[]{:S(2)}) %collective-permute-start.16) | collective-permute-done | bytes 165920 | tf_op jit(solution)/shard_map/ppermute | solution.py:36
  73.5 1.5 %collective-permute-start.24 = (bf16[64,1152]{1,0:T(8,128)(2,1)S(1)}, bf16[64,1152]{1,0:T(8,128)(2,1)S(1)}, u32[]{:S(2)}, u32[]{:S(2)}) collective-permute-start(bf16[64,1152]{1,0:T(8,128)(2,1)S(1)} %get-tuple-element.54), channel_id=1, source_target_pairs={{0,16},{1,17},{2,18},{3,19},{4,20},{5,21},{6,22},{7,23},{8,24},{9,... | collective-permute-start | bytes 442376 | tf_op jit(solution)/shard_map/ppermute | solution.py:48
  75.2 2.0 %collective-permute-done.18.r3 = bf16[72,1152]{1,0:T(8,128)(2,1)S(1)} collective-permute-done((bf16[72,1152]{1,0:T(8,128)(2,1)S(1)}, bf16[72,1152]{1,0:T(8,128)(2,1)S(1)}, u32[]{:S(2)}, u32[]{:S(2)}) %collective-permute-start.18) | collective-permute-done | bytes 165920 | tf_op jit(solution)/shard_map/ppermute | solution.py:36
  77.2 0.9 %finish_img.1 = (f32[64,1152]{1,0:T(8,128)}, f32[1,64]{1,0:T(1,128)}) custom-call(f32[64,1152]{1,0:T(8,128)S(1)} %get-tuple-element.37.g_ref, f32[8,256]{1,0:T(8,128)S(1)} %get-tuple-element.38.l_ref, bf16[72,1152]{1,0:T(8,128)(2,1)S(1)} %collective-permute-done.16.r1, bf16[72,1152]{1,0:T(8,128)(2,1)S(1)} %collective-permute-done.17.r2, ...), custom_call_target="tpu_custom_call" | custom-call | bytes 1179648 | tf_op jit(solution)/shard_map/finish_img/pallas_call | solution.py:269
  78.1 7.8 %collective-permute-done.24.r3 = bf16[64,1152]{1,0:T(8,128)(2,1)S(1)} collective-permute-done((bf16[64,1152]{1,0:T(8,128)(2,1)S(1)}, bf16[64,1152]{1,0:T(8,128)(2,1)S(1)}, u32[]{:S(2)}, u32[]{:S(2)}) %collective-permute-start.24) | collective-permute-done | bytes 147488 | tf_op jit(solution)/shard_map/ppermute | solution.py:48
  (53 shorter events, 7.4 us)
Async XLA Ops:
  0.6 0.9 %copy-start = (bf16[64,1152]{1,0:T(8,128)(2,1)S(1)}, bf16[64,1152]{1,0:T(8,128)(2,1)}, u32[]{:S(2)}) copy-start(bf16[64,1152]{1,0:T(8,128)(2,1)} %raw.3) | copy-start | bytes 442372
  1.5 0.9 %copy-start.2 = (bf16[64,1152]{1,0:T(8,128)(2,1)S(1)}, bf16[64,1152]{1,0:T(8,128)(2,1)}, u32[]{:S(2)}) copy-start(bf16[64,1152]{1,0:T(8,128)(2,1)} %raw.2) | copy-start | bytes 442372
  2.6 14.5 %collective-permute-start.2 = (bf16[64,1152]{1,0:T(8,128)(2,1)S(1)}, bf16[64,1152]{1,0:T(8,128)(2,1)S(1)}, u32[]{:S(2)}, u32[]{:S(2)}) collective-permute-start(bf16[64,1152]{1,0:T(8,128)(2,1)S(1)} %get-tuple-element.30), channel_id=1, source_target_pairs={{0,192},{1,193},{2,194},{3,195},{4,196},{5,197},{6,198},{7,199},{8... | collective-permute-start | bytes 442376 | tf_op jit(solution)/shard_map/ppermute | solution.py:36
  6.2 10.9 %collective-permute-start.1 = (bf16[64,1152]{1,0:T(8,128)(2,1)S(1)}, bf16[64,1152]{1,0:T(8,128)(2,1)S(1)}, u32[]{:S(2)}, u32[]{:S(2)}) collective-permute-start(bf16[64,1152]{1,0:T(8,128)(2,1)S(1)} %get-tuple-element.30), channel_id=1, source_target_pairs={{0,128},{1,129},{2,130},{3,131},{4,132},{5,133},{6,134},{7,135},{8... | collective-permute-start | bytes 442376 | tf_op jit(solution)/shard_map/ppermute | solution.py:36
  6.6 8.9 %collective-permute-start = (bf16[64,1152]{1,0:T(8,128)(2,1)S(1)}, bf16[64,1152]{1,0:T(8,128)(2,1)S(1)}, u32[]{:S(2)}, u32[]{:S(2)}) collective-permute-start(bf16[64,1152]{1,0:T(8,128)(2,1)S(1)} %get-tuple-element.30), channel_id=1, source_target_pairs={{0,64},{1,65},{2,66},{3,67},{4,68},{5,69},{6,70},{7,71},{8,72},{9,... | collective-permute-start | bytes 442376 | tf_op jit(solution)/shard_map/ppermute | solution.py:36
  7.3 13.0 %collective-permute-start.5 = (bf16[64,1152]{1,0:T(8,128)(2,1)S(1)}, bf16[64,1152]{1,0:T(8,128)(2,1)S(1)}, u32[]{:S(2)}, u32[]{:S(2)}) collective-permute-start(bf16[64,1152]{1,0:T(8,128)(2,1)S(1)} %get-tuple-element.31), channel_id=1, source_target_pairs={{0,16},{1,17},{2,18},{3,19},{4,20},{5,21},{6,22},{7,23},{8,24},{9,... | collective-permute-start | bytes 442376 | tf_op jit(solution)/shard_map/ppermute | solution.py:48
  14.2 9.9 %collective-permute-start.4 = (bf16[64,1152]{1,0:T(8,128)(2,1)S(1)}, bf16[64,1152]{1,0:T(8,128)(2,1)S(1)}, u32[]{:S(2)}, u32[]{:S(2)}) collective-permute-start(bf16[64,1152]{1,0:T(8,128)(2,1)S(1)} %get-tuple-element.31), channel_id=1, source_target_pairs={{0,28},{1,29},{2,30},{3,31},{4,0},{5,1},{6,2},{7,3},{8,4},{9,5},{1... | collective-permute-start | bytes 442376 | tf_op jit(solution)/shard_map/ppermute | solution.py:48
  15.5 8.6 %collective-permute-start.3 = (bf16[64,1152]{1,0:T(8,128)(2,1)S(1)}, bf16[64,1152]{1,0:T(8,128)(2,1)S(1)}, u32[]{:S(2)}, u32[]{:S(2)}) collective-permute-start(bf16[64,1152]{1,0:T(8,128)(2,1)S(1)} %get-tuple-element.31), channel_id=1, source_target_pairs={{0,4},{1,5},{2,6},{3,7},{4,8},{5,9},{6,10},{7,11},{8,12},{9,13},{1... | collective-permute-start | bytes 442376 | tf_op jit(solution)/shard_map/ppermute | solution.py:48
  17.2 24.5 %collective-permute-start.14 = (bf16[256,1152]{1,0:T(8,128)(2,1)S(1)}, bf16[256,1152]{1,0:T(8,128)(2,1)S(1)}, u32[]{:S(2)}, u32[]{:S(2)}) collective-permute-start(bf16[256,1152]{1,0:T(8,128)(2,1)S(1)} %constant_dynamic-update-slice_fusion.img_ref.s0), channel_id=1, source_target_pairs={{0,3},{1,0},{2,1},{3,2},{4,7},{5,4},{6,5},{7,6},{8,11},{9,8},{10,9... | collective-permute-start | bytes 1769480 | tf_op jit(solution)/shard_map/ppermute | solution.py:42
  19.7 23.8 %collective-permute-start.12 = (bf16[256,1152]{1,0:T(8,128)(2,1)S(1)}, bf16[256,1152]{1,0:T(8,128)(2,1)S(1)}, u32[]{:S(2)}, u32[]{:S(2)}) collective-permute-start(bf16[256,1152]{1,0:T(8,128)(2,1)S(1)} %constant_dynamic-update-slice_fusion.img_ref.s0), channel_id=1, source_target_pairs={{0,2},{1,3},{2,0},{3,1},{4,6},{5,7},{6,4},{7,5},{8,10},{9,11},{10,... | collective-permute-start | bytes 1769480 | tf_op jit(solution)/shard_map/ppermute | solution.py:42
  20.3 25.2 %collective-permute-start.10 = (bf16[256,1152]{1,0:T(8,128)(2,1)S(1)}, bf16[256,1152]{1,0:T(8,128)(2,1)S(1)}, u32[]{:S(2)}, u32[]{:S(2)}) collective-permute-start(bf16[256,1152]{1,0:T(8,128)(2,1)S(1)} %constant_dynamic-update-slice_fusion.img_ref.s0), channel_id=1, source_target_pairs={{0,1},{1,2},{2,3},{3,0},{4,5},{5,6},{6,7},{7,4},{8,9},{9,10},{10,1... | collective-permute-start | bytes 1769480 | tf_op jit(solution)/shard_map/ppermute | solution.py:42
  24.2 8.2 %collective-permute-start.7 = (bf16[128,1152]{1,0:T(8,128)(2,1)S(1)}, bf16[128,1152]{1,0:T(8,128)(2,1)S(1)}, u32[]{:S(2)}, u32[]{:S(2)}) collective-permute-start(bf16[128,1152]{1,0:T(8,128)(2,1)S(1)} %get-tuple-element.57), channel_id=1, source_target_pairs={{0,28},{1,29},{2,30},{3,31},{4,0},{5,1},{6,2},{7,3},{8,4},{9,5},{1... | collective-permute-start | bytes 884744 | tf_op jit(solution)/shard_map/ppermute | solution.py:48
  27.1 8.4 %collective-permute-start.6 = (bf16[128,1152]{1,0:T(8,128)(2,1)S(1)}, bf16[128,1152]{1,0:T(8,128)(2,1)S(1)}, u32[]{:S(2)}, u32[]{:S(2)}) collective-permute-start(bf16[128,1152]{1,0:T(8,128)(2,1)S(1)} %get-tuple-element.58), channel_id=1, source_target_pairs={{0,4},{1,5},{2,6},{3,7},{4,8},{5,9},{6,10},{7,11},{8,12},{9,13},{1... | collective-permute-start | bytes 884744 | tf_op jit(solution)/shard_map/ppermute | solution.py:48
  32.4 5.7 %collective-permute-start.8 = (bf16[256,1152]{1,0:T(8,128)(2,1)S(1)}, bf16[256,1152]{1,0:T(8,128)(2,1)S(1)}, u32[]{:S(2)}, u32[]{:S(2)}) collective-permute-start(bf16[256,1152]{1,0:T(8,128)(2,1)S(1)} %pad_maximum_fusion), channel_id=1, source_target_pairs={{0,32},{1,33},{2,34},{3,35},{4,36},{5,37},{6,38},{7,39},{8,40},{9,... | collective-permute-start | bytes 1769480 | tf_op jit(solution)/shard_map/ppermute | solution.py:52
  35.6 4.1 %collective-permute-start.9 = (bf16[256,1152]{1,0:T(8,128)(2,1)S(1)}, bf16[256,1152]{1,0:T(8,128)(2,1)S(1)}, u32[]{:S(2)}, u32[]{:S(2)}) collective-permute-start(bf16[256,1152]{1,0:T(8,128)(2,1)S(1)} %pad_maximum_fusion.1), channel_id=1, source_target_pairs={{0,32},{1,33},{2,34},{3,35},{4,36},{5,37},{6,38},{7,39},{8,40},{9,... | collective-permute-start | bytes 1769480 | tf_op jit(solution)/shard_map/ppermute | solution.py:52
  49.0 6.9 %collective-permute-start.19 = (bf16[512,1152]{1,0:T(8,128)(2,1)S(1)}, bf16[512,1152]{1,0:T(8,128)(2,1)S(1)}, u32[]{:S(2)}, u32[]{:S(2)}) collective-permute-start(bf16[512,1152]{1,0:T(8,128)(2,1)S(1)} %texts1.1), channel_id=1, source_target_pairs={{0,32},{1,33},{2,34},{3,35},{4,36},{5,37},{6,38},{7,39},{8,40},{9,... | collective-permute-start | bytes 3538952 | tf_op jit(solution)/shard_map/ppermute | solution.py:52
  49.4 10.4 %collective-permute-start.15 = (bf16[264,1152]{1,0:T(8,128)(2,1)S(1)}, bf16[264,1152]{1,0:T(8,128)(2,1)S(1)}, u32[]{:S(2)}, u32[]{:S(2)}) collective-permute-start(bf16[264,1152]{1,0:T(8,128)(2,1)S(1)} %get-tuple-element.36), channel_id=1, source_target_pairs={{0,1},{1,2},{2,3},{3,0},{4,5},{5,6},{6,7},{7,4},{8,9},{9,10},{10,1... | collective-permute-start | bytes 1824776 | tf_op jit(solution)/shard_map/ppermute | solution.py:42
  50.6 16.7 %collective-permute-start.13 = (bf16[264,1152]{1,0:T(8,128)(2,1)S(1)}, bf16[264,1152]{1,0:T(8,128)(2,1)S(1)}, u32[]{:S(2)}, u32[]{:S(2)}) collective-permute-start(bf16[264,1152]{1,0:T(8,128)(2,1)S(1)} %get-tuple-element.35), channel_id=1, source_target_pairs={{0,2},{1,3},{2,0},{3,1},{4,6},{5,7},{6,4},{7,5},{8,10},{9,11},{10,... | collective-permute-start | bytes 1824776 | tf_op jit(solution)/shard_map/ppermute | solution.py:42
  53.1 14.3 %collective-permute-start.11 = (bf16[264,1152]{1,0:T(8,128)(2,1)S(1)}, bf16[264,1152]{1,0:T(8,128)(2,1)S(1)}, u32[]{:S(2)}, u32[]{:S(2)}) collective-permute-start(bf16[264,1152]{1,0:T(8,128)(2,1)S(1)} %get-tuple-element.34), channel_id=1, source_target_pairs={{0,3},{1,0},{2,1},{3,2},{4,7},{5,4},{6,5},{7,6},{8,11},{9,8},{10,9... | collective-permute-start | bytes 1824776 | tf_op jit(solution)/shard_map/ppermute | solution.py:42
  56.1 14.8 %collective-permute-start.20 = (bf16[128,1152]{1,0:T(8,128)(2,1)S(1)}, bf16[128,1152]{1,0:T(8,128)(2,1)S(1)}, u32[]{:S(2)}, u32[]{:S(2)}) collective-permute-start(bf16[128,1152]{1,0:T(8,128)(2,1)S(1)} %get-tuple-element.49), channel_id=1, source_target_pairs={{0,28},{1,29},{2,30},{3,31},{4,0},{5,1},{6,2},{7,3},{8,4},{9,5},{1... | collective-permute-start | bytes 884744 | tf_op jit(solution)/shard_map/ppermute | solution.py:48
  56.9 13.9 %collective-permute-start.21 = (bf16[128,1152]{1,0:T(8,128)(2,1)S(1)}, bf16[128,1152]{1,0:T(8,128)(2,1)S(1)}, u32[]{:S(2)}, u32[]{:S(2)}) collective-permute-start(bf16[128,1152]{1,0:T(8,128)(2,1)S(1)} %get-tuple-element.50), channel_id=1, source_target_pairs={{0,4},{1,5},{2,6},{3,7},{4,8},{5,9},{6,10},{7,11},{8,12},{9,13},{1... | collective-permute-start | bytes 884744 | tf_op jit(solution)/shard_map/ppermute | solution.py:48
  67.4 9.8 %copy-start.3 = (bf16[64,1152]{1,0:T(8,128)(2,1)S(1)}, bf16[64,1152]{1,0:T(8,128)(2,1)}, u32[]{:S(2)}) copy-start(bf16[64,1152]{1,0:T(8,128)(2,1)} %raw.2) | copy-start | bytes 442372
  67.4 18.6 %copy-start.1 = (bf16[64,1152]{1,0:T(8,128)(2,1)S(1)}, bf16[64,1152]{1,0:T(8,128)(2,1)}, u32[]{:S(2)}) copy-start(bf16[64,1152]{1,0:T(8,128)(2,1)} %raw.3) | copy-start | bytes 442372
  67.6 5.8 %collective-permute-start.16 = (bf16[72,1152]{1,0:T(8,128)(2,1)S(1)}, bf16[72,1152]{1,0:T(8,128)(2,1)S(1)}, u32[]{:S(2)}, u32[]{:S(2)}) collective-permute-start(bf16[72,1152]{1,0:T(8,128)(2,1)S(1)} %get-tuple-element.39), channel_id=1, source_target_pairs={{0,192},{1,193},{2,194},{3,195},{4,196},{5,197},{6,198},{7,199},{8... | collective-permute-start | bytes 497672 | tf_op jit(solution)/shard_map/ppermute | solution.py:36
  69.4 5.8 %collective-permute-start.17 = (bf16[72,1152]{1,0:T(8,128)(2,1)S(1)}, bf16[72,1152]{1,0:T(8,128)(2,1)S(1)}, u32[]{:S(2)}, u32[]{:S(2)}) collective-permute-start(bf16[72,1152]{1,0:T(8,128)(2,1)S(1)} %get-tuple-element.40), channel_id=1, source_target_pairs={{0,128},{1,129},{2,130},{3,131},{4,132},{5,133},{6,134},{7,135},{8... | collective-permute-start | bytes 497672 | tf_op jit(solution)/shard_map/ppermute | solution.py:36
  70.9 6.3 %collective-permute-start.18 = (bf16[72,1152]{1,0:T(8,128)(2,1)S(1)}, bf16[72,1152]{1,0:T(8,128)(2,1)S(1)}, u32[]{:S(2)}, u32[]{:S(2)}) collective-permute-start(bf16[72,1152]{1,0:T(8,128)(2,1)S(1)} %get-tuple-element.41), channel_id=1, source_target_pairs={{0,64},{1,65},{2,66},{3,67},{4,68},{5,69},{6,70},{7,71},{8,72},{9,... | collective-permute-start | bytes 497672 | tf_op jit(solution)/shard_map/ppermute | solution.py:36
  71.0 7.1 %collective-permute-start.22 = (bf16[64,1152]{1,0:T(8,128)(2,1)S(1)}, bf16[64,1152]{1,0:T(8,128)(2,1)S(1)}, u32[]{:S(2)}, u32[]{:S(2)}) collective-permute-start(bf16[64,1152]{1,0:T(8,128)(2,1)S(1)} %get-tuple-element.52), channel_id=1, source_target_pairs={{0,28},{1,29},{2,30},{3,31},{4,0},{5,1},{6,2},{7,3},{8,4},{9,5},{1... | collective-permute-start | bytes 442376 | tf_op jit(solution)/shard_map/ppermute | solution.py:48
  71.6 6.5 %collective-permute-start.23 = (bf16[64,1152]{1,0:T(8,128)(2,1)S(1)}, bf16[64,1152]{1,0:T(8,128)(2,1)S(1)}, u32[]{:S(2)}, u32[]{:S(2)}) collective-permute-start(bf16[64,1152]{1,0:T(8,128)(2,1)S(1)} %get-tuple-element.53), channel_id=1, source_target_pairs={{0,4},{1,5},{2,6},{3,7},{4,8},{5,9},{6,10},{7,11},{8,12},{9,13},{1... | collective-permute-start | bytes 442376 | tf_op jit(solution)/shard_map/ppermute | solution.py:48
  73.5 12.5 %collective-permute-start.24 = (bf16[64,1152]{1,0:T(8,128)(2,1)S(1)}, bf16[64,1152]{1,0:T(8,128)(2,1)S(1)}, u32[]{:S(2)}, u32[]{:S(2)}) collective-permute-start(bf16[64,1152]{1,0:T(8,128)(2,1)S(1)} %get-tuple-element.54), channel_id=1, source_target_pairs={{0,16},{1,17},{2,18},{3,19},{4,20},{5,21},{6,22},{7,23},{8,24},{9,... | collective-permute-start | bytes 442376 | tf_op jit(solution)/shard_map/ppermute | solution.py:48

commit v2 on v1

v2 whole, which is shorter than its diff:
```python
import functools

import jax
import jax.numpy as jnp
from jax import lax
from jax.experimental import pallas as pl
from jax.experimental.pallas import tpu as pltpu
from jax.sharding import Mesh
from jax.sharding import PartitionSpec as P

AXES = ("x", "core", "z", "y")
NX, NC, NZ, NY = 4, 2, 8, 4
U = 64
EPS = 1e-06
F32 = jnp.float32
BF16 = jnp.bfloat16
MIB = 1 << 20
VMEM = pl.BlockSpec(memory_space=pltpu.VMEM)
SMEM = pl.BlockSpec(memory_space=pltpu.SMEM)
ANY = pl.BlockSpec(memory_space=pl.ANY)
HBM = pl.BlockSpec(memory_space=pltpu.HBM)


def device(x, core, z, y):
    return ((x % NX * NC + core) * NZ + z % NZ) * NY + y % NY


def permutation(move):
    return [
        (device(x, c, z, y), device(*move(x, c, z, y)))
        for x in range(NX)
        for c in range(NC)
        for z in range(NZ)
        for y in range(NY)
    ]


def first(a, s):
    return lax.ppermute(
        a, AXES, permutation(lambda x, c, z, y: (x, c, z, y + s) if c else (x + s, c, z, y))
    )


def second(a, s):
    return lax.ppermute(
        a, AXES, permutation(lambda x, c, z, y: (x + s, c, z, y) if c else (x, c, z, y + s))
    )


def ring(a, s):
    return lax.ppermute(a, AXES, permutation(lambda x, c, z, y: (x, c, z - s if c else z + s, y)))


def swap(a):
    return lax.ppermute(a, AXES, permutation(lambda x, c, z, y: (x, 1 - c, z, y)))


def call(name, body, outs, ins, scalars=(), after=(), specs=None, scratch=()):
    n_out, n_in = len(outs), len(ins) + len(scalars)

    def kernel(*refs):
        used = refs[:n_in] + refs[n_in + len(after) :]
        body(*used)

    return pl.pallas_call(
        kernel,
        out_shape=outs,
        in_specs=[SMEM] * len(scalars) + (specs or [VMEM] * len(ins)) + [ANY] * len(after),
        out_specs=[VMEM] * n_out,
        scratch_shapes=list(scratch),
        name=name,
        cost_estimate=pl.CostEstimate(flops=1, bytes_accessed=1, transcendentals=0),
        compiler_params=pltpu.CompilerParams(vmem_limit_bytes=20 * MIB),
    )(*scalars, *ins, *after)


def shape(*dims, dtype=BF16):
    return jax.ShapeDtypeStruct(dims, dtype)


def up(ref, lo, hi):
    return ref[lo:hi, :].astype(F32)


def normalize_body(img_ref, txt_ref, img_unit, txt_unit, img_inv, txt_inv, raw_ref, sem):
    copies = [
        pltpu.make_async_copy(src, raw_ref.at[i], sem.at[i])
        for i, src in enumerate((img_ref, txt_ref))
    ]
    for copy in copies:
        copy.start()
    for i, (unit, inv) in enumerate(((img_unit, img_inv), (txt_unit, txt_inv))):
        copies[i].wait()
        v = raw_ref[i].astype(F32)
        r = lax.rsqrt(jnp.sum(v * v, axis=-1, keepdims=True) + EPS)
        unit[...] = (v * r).astype(BF16)
        inv[...] = r


def split3(v):
    hi = v.astype(BF16).astype(F32)
    mid = (v - hi).astype(BF16).astype(F32)
    return hi, mid, v - hi - mid


def loss_rows(total):
    hi, mid, low = split3(total)
    at = lax.broadcasted_iota(jnp.int32, total.shape, 0)
    return jnp.where(at == 0, hi, jnp.where(at == 1, mid, jnp.where(at == 2, low, 0.0))).astype(BF16)


def loss_sum(rows):
    return jnp.sum(rows.astype(F32), axis=0, keepdims=True)


def entry(img, txt, scale, bias, match=None):
    dots = lax.dot_general(img, txt, (((1,), (1,)), ((), ())), preferred_element_type=F32)
    logits = dots * scale + bias
    if match is not None:
        logits = jnp.where(match, -logits, logits)
    e = jnp.exp(logits)
    u = 1.0 + e
    inv = 1.0 / u
    softplus = jnp.log(u) + (e - (u - 1.0)) * inv
    weight = scale * (e * inv)
    if match is not None:
        weight = jnp.where(match, -weight, weight)
    return weight.astype(BF16), softplus


def fold(v):
    total = v[:, :128]
    for n in range(1, v.shape[1] // 128):
        total = total + v[:, 128 * n : 128 * (n + 1)]
    return total


def near_body(scale_ref, bias_ref, img_ref, txt_ref, coeff_ref, loss_ref):
    total = None
    for n in range(2):
        at = slice(256 * n, 256 * (n + 1))
        weight, softplus = entry(img_ref[...], txt_ref[at, :], scale_ref[0], bias_ref[0])
        coeff_ref[:, at] = weight
        total = fold(softplus) if total is None else total + fold(softplus)
    loss_ref[...] = total


def texts(coeffs, imgs, lo, hi):
    total = None
    for c, s in zip(coeffs, imgs):
        part = lax.dot_general(
            c[:, lo:hi], s[...], (((0,), (0,)), ((), ())), preferred_element_type=F32
        )
        total = part if total is None else total + part
    return total


def far_body(scale_ref, bias_ref, i0, i1, i2, i3, txt_ref, l0, l1, l2, l3, c0, c1, c2, c3, keep, send, pair, loss):
    scale, bias = scale_ref[0], bias_ref[0]
    imgs, coeffs, sums = (i0, i1, i2, i3), (c0, c1, c2, c3), (l0, l1, l2, l3)
    for k in range(4):
        total = sums[k][...]
        for n in range(2):
            at = slice(256 * n, 256 * (n + 1))
            match = None
            if k == 0 and n == 1:
                r = lax.broadcasted_iota(jnp.int32, (256, 256), 0)
                c = lax.broadcasted_iota(jnp.int32, (256, 256), 1)
                match = (r + 128 == c) & (r < U)
            weight, softplus = entry(imgs[k][...], txt_ref[at, :], scale, bias, match)
            coeffs[k][:, at] = weight
            total = total + fold(softplus)
        column = jnp.broadcast_to(jnp.sum(total, axis=1, keepdims=True), (256, 128))
        loss[:, 256 * k : 256 * (k + 1)] = jnp.transpose(column)[:8, :]
    g = texts(coeffs, imgs, 0, 256)
    keep[...] = g[:192, :]
    send[:64, :] = g[192:, :].astype(BF16)
    g = texts(coeffs, imgs, 256, 512)
    send[64:, :] = g[:128, :].astype(BF16)
    pair[...] = g[128:, :]


def near_texts_body(c0, c1, c2, c3, i0, i1, i2, i3, keep, send):
    coeffs, imgs = (c0, c1, c2, c3), (i0, i1, i2, i3)
    keep[...] = texts(coeffs, imgs, 0, 256)
    send[...] = texts(coeffs, imgs, 256, 512).astype(BF16)


def image_body(k, cf, cn, far, near, loss, out):
    g = jnp.dot(cf[...], far[...], preferred_element_type=F32)
    g = g + jnp.dot(cn[...], near[...], preferred_element_type=F32)
    if k == 0:
        out[...] = g
    else:
        out[:256, :] = g.astype(BF16)
        out[256:, :] = jnp.zeros((8, g.shape[1]), BF16)
        out[256:, :256] = loss_rows(loss[:, 256 * k : 256 * (k + 1)])


def merge_img_body(g_ref, l_ref, r1, r2, r3, own_ref, own_loss, m1, m2, m3):
    loss = l_ref[:, :256] + (
        loss_sum(r1[256:, :256]) + loss_sum(r2[256:, :256]) + loss_sum(r3[256:, :256])
    )
    own_loss[...] = loss
    marks = loss_rows(loss)
    for j, out in enumerate((own_ref, m1, m2, m3)):
        lo, hi = U * j, U * (j + 1)
        total = g_ref[lo:hi, :] + (up(r1, lo, hi) + up(r2, lo, hi) + up(r3, lo, hi))
        out[:U, :] = total.astype(out.dtype)
        if j:
            out[U:, :] = jnp.zeros((8, total.shape[1]), BF16)
            out[U:, :256] = marks


def step1_body(keep, got, out):
    out[...] = (keep[:64, :] + up(got, 0, 64)).astype(BF16)


def step2_body(keep, got, r, out):
    out[:64, :] = (keep[64:128, :] + (up(got, 64, 128) + up(r, 0, 64))).astype(BF16)
    out[64:, :] = (keep[128:192, :] + up(got, 128, 192)).astype(BF16)


def step_body(lo, keep, got, r, out):
    hi = lo + 128
    out[...] = (keep[lo:hi, :] + (up(got, lo, hi) + up(r, 0, 128))).astype(BF16)


def step5_body(pair, r, out):
    out[...] = (pair[64:, :] + up(r, 64, 128)).astype(BF16)


def back_norm(g, raw, inv):
    unit = raw[...].astype(F32) * inv[...]
    return inv[...] * (g - unit * jnp.sum(unit * g, axis=-1, keepdims=True))


def finish_img_body(g_ref, l_ref, r1, r2, r3, raw, inv, out_ref, loss_ref):
    g = g_ref[...] + (up(r1, 0, U) + up(r2, 0, U) + up(r3, 0, U))
    out_ref[...] = back_norm(g, raw, inv)
    loss = l_ref[:1, :U]
    for j, r in enumerate((r1, r2, r3)):
        loss = loss + loss_sum(r[U:, U * (j + 1) : U * (j + 2)])
    loss_ref[...] = loss


def finish_txt_body(pair, r, got, raw, inv, out_ref):
    g = pair[:64, :] + (up(r, 0, 64) + got[...].astype(F32))
    out_ref[...] = back_norm(g, raw, inv)


def on_device(picture, caption, scale, bias):
    rows, d = picture.shape
    img, txt, img_inv, txt_inv = call(
        "normalize", normalize_body,
        [shape(rows, d), shape(rows, d), shape(rows, 1, dtype=F32), shape(rows, 1, dtype=F32)],
        [pltpu.with_memory_space_constraint(a, pltpu.HBM) for a in (picture, caption)], specs=[HBM] * 2,
        scratch=[pltpu.VMEM((2, rows, d), BF16), pltpu.SemaphoreType.DMA((2,))],
    )

    pair = jnp.concatenate([txt, swap(txt)], axis=0)
    f1, f3, f2 = first(img, 1), first(img, 3), first(img, 2)
    b1 = ring(pair, 1)
    group = jnp.concatenate([img, f1, f2, f3], axis=0)
    g1, g3, g2 = second(group, 1), second(group, 3), second(group, 2)
    groups = (group, g1, g2, g3)
    b2 = ring(b1, 1)
    near_mine = jnp.concatenate([b2, b1], axis=0)
    near = jnp.concatenate([near_mine, swap(near_mine)], axis=0)
    b3 = ring(b2, 1)
    b4 = ring(b3[:U], 1)
    far_mine = jnp.concatenate([b4, b3], axis=0)
    far = jnp.concatenate([far_mine, swap(far_mine), pair], axis=0)

    sc = (scale, bias)
    near_c, near_l, last = [None] * 4, [None] * 4, ()
    for k in (0, 1, 3, 2):
        near_c[k], near_l[k] = call(
            f"near{k}", near_body, [shape(256, 512), shape(256, 128, dtype=F32)],
            (groups[k], near), sc, last,
        )
        last = (near_l[k],)
    *far_c, keep_a, send_a, own_pair, loss = call(
        "far", far_body,
        [shape(256, 512)] * 4
        + [shape(192, d, dtype=F32), shape(192, d), shape(128, d, dtype=F32), shape(8, 1024, dtype=F32)],
        (*groups, far, *near_l), sc,
    )
    got_a = swap(send_a)

    def image(k, after):
        out = shape(256, d, dtype=F32) if k == 0 else shape(264, d)
        return call(
            f"image{k}", functools.partial(image_body, k), [out],
            (far_c[k], near_c[k], far, near, loss), (), after,
        )[0]

    keep_b, send_b = call(
        "near_texts", near_texts_body, [shape(256, d, dtype=F32), shape(256, d)],
        (*near_c, *groups), (), (send_a,),
    )
    got_b = swap(send_b)
    z1 = call("step1", step1_body, [shape(64, d)], (keep_a, got_a), (), (send_b,))[0]
    w1 = ring(z1, -1)
    p1 = image(1, (z1,))
    r1 = second(p1, -1)
    p3 = image(3, (p1,))
    r3 = second(p3, -3)
    z2 = call("step2", step2_body, [shape(128, d)], (keep_a, got_a, w1), (), (p3, got_b))[0]
    w2 = ring(z2, -1)
    p2 = image(2, (z2,))
    r2 = second(p2, -2)
    p0 = image(0, (p2,))
    z3 = call("step3", functools.partial(step_body, 0), [shape(128, d)], (keep_b, got_b, w2), (), (p0,))[0]
    w3 = ring(z3, -1)
    own_img, own_loss, m1, m2, m3 = call(
        "merge_img", merge_img_body,
        [shape(rows, d, dtype=F32), shape(8, 256, dtype=F32)] + [shape(rows + 8, d)] * 3,
        (p0, loss, r1, r2, r3), (), (z3,),
    )
    q1, q3, q2 = first(m1, -1), first(m3, -3), first(m2, -2)
    z4 = call("step4", functools.partial(step_body, 128), [shape(128, d)], (keep_b, got_b, w3), (), (m3,))[0]
    w4 = ring(z4, -1)
    z5 = call("step5", step5_body, [shape(64, d)], (own_pair, w4))[0]
    got_c = swap(z5)
    grad_img, loss_out = call(
        "finish_img", finish_img_body,
        [shape(rows, d, dtype=F32), shape(1, rows, dtype=F32)],
        (own_img, own_loss, q1, q2, q3, picture, img_inv), (), (z5,),
    )
    grad_txt = call(
        "finish_txt", finish_txt_body, [shape(rows, d, dtype=F32)],
        (own_pair, w4, got_c, caption, txt_inv),
    )[0]
    return grad_img, grad_txt, loss_out.reshape(rows)


def solution(mesh):
    torus = Mesh(mesh.devices.reshape(NX, NC, NZ, NY), AXES)
    return jax.shard_map(
        on_device,
        mesh=torus,
        in_specs=(P(AXES, None), P(AXES, None), P(), P()),
        out_specs=(P(AXES, None), P(AXES, None), P(AXES)),
        check_vma=False,
    )
```

time: 87.2 us -> 87.8 us (level)
  the two profiles are of different devices: /device:TPU:1 before, /device:TPU:8 now
where the time goes in v2:
time: 87.8 us; the launch traced here: 87.6 us
  waiting for transfers between devices  40.4 us (46%)
  starting transfers between devices  29.7 us (34%)
  Pallas kernels  14.8 us (17%)
  between operations  2.21 us (3%)
    ppermute x8, waiting for transfers between devices, ring(): lax.ppermute(a, AXES, permutation(lambda x, c, z, y: (x, c, z - s if c el...  30.1 us
    pallas_call x19, Pallas kernels, call(): pl.pallas_call(kernel, out_shape=outs, in_specs=[SMEM] * len(scalars) + (...  14.8 us
    ppermute x6, waiting for transfers between devices, first(): lax.ppermute(a, AXES, permutation(lambda x, c, z, y: (x, c, z, y + s) if...  9.81 us
    ppermute x6, starting transfers between devices, second(): lax.ppermute(a, AXES, permutation(lambda x, c, z, y: (x + s, c, z, y) if...  9.78 us
    ppermute x8, starting transfers between devices, ring(): lax.ppermute(a, AXES, permutation(lambda x, c, z, y: (x, c, z - s if c el...  9.6 us
    ppermute x6, starting transfers between devices, first(): lax.ppermute(a, AXES, permutation(lambda x, c, z, y: (x, c, z, y + s) if...  8.4 us
    ppermute x6, starting transfers between devices, swap(): lax.ppermute(a, AXES, permutation(lambda x, c, z, y: (x, 1 - c, z, y)))  1.94 us
  transfers between devices with their start and end apart: 26, of which 13 were waited for; matrix products, arithmetic and copies ran while one was open for 0% of the time, Pallas kernels for 11%

profile of v2, /device:TPU:8, one launch (start us, length us, event | category | flops | bytes accessed | tf_op | source)
XLA Modules:
  0.0 87.6 jit_solution(9469976609950731031)
XLA Ops:
  0.6 1.2 %normalize.1 = (bf16[64,1152]{1,0:T(8,128)(2,1)S(1)}, bf16[64,1152]{1,0:T(8,128)(2,1)S(1)}, f32[64,1]{1,0:T(8,128)S(1)}, f32[64,1]{1,0:T(8,128)S(1)}) custom-call(bf16[64,1152]{1,0:T(8,128)(2,1)} %refs_5_.1, bf16[64,1152]{1,0:T(8,128)(2,1)} %refs_3_.1), custom_call_target="tpu_custom_call" | custom-call | flops 1 | bytes 1 | tf_op jit(solution)/shard_map/normalize/pallas_call | solution.py:65
  1.9 2.8 %collective-permute-start.2 = (bf16[64,1152]{1,0:T(8,128)(2,1)S(1)}, bf16[64,1152]{1,0:T(8,128)(2,1)S(1)}, u32[]{:S(2)}, u32[]{:S(2)}) collective-permute-start(bf16[64,1152]{1,0:T(8,128)(2,1)S(1)} %get-tuple-element.32), channel_id=1, source_target_pairs={{0,192},{1,193},{2,194},{3,195},{4,196},{5,197},{6,198},{7,199},{8... | collective-permute-start | bytes 442376 | tf_op jit(solution)/shard_map/ppermute | solution.py:39
  5.5 0.9 %collective-permute-start = (bf16[64,1152]{1,0:T(8,128)(2,1)S(1)}, bf16[64,1152]{1,0:T(8,128)(2,1)S(1)}, u32[]{:S(2)}, u32[]{:S(2)}) collective-permute-start(bf16[64,1152]{1,0:T(8,128)(2,1)S(1)} %get-tuple-element.32), channel_id=1, source_target_pairs={{0,64},{1,65},{2,66},{3,67},{4,68},{5,69},{6,70},{7,71},{8,72},{9,... | collective-permute-start | bytes 442376 | tf_op jit(solution)/shard_map/ppermute | solution.py:39
  6.5 2.0 %collective-permute-start.7 = (bf16[128,1152]{1,0:T(8,128)(2,1)S(1)}, bf16[128,1152]{1,0:T(8,128)(2,1)S(1)}, u32[]{:S(2)}, u32[]{:S(2)}) collective-permute-start(bf16[128,1152]{1,0:T(8,128)(2,1)S(1)} %pad_maximum_fusion.2), channel_id=1, source_target_pairs={{0,4},{1,5},{2,6},{3,7},{4,8},{5,9},{6,10},{7,11},{8,12},{9,13},{1... | collective-permute-start | bytes 884744 | tf_op jit(solution)/shard_map/ppermute | solution.py:51
  9.8 3.2 %collective-permute-done = bf16[64,1152]{1,0:T(8,128)(2,1)S(1)} collective-permute-done((bf16[64,1152]{1,0:T(8,128)(2,1)S(1)}, bf16[64,1152]{1,0:T(8,128)(2,1)S(1)}, u32[]{:S(2)}, u32[]{:S(2)}) %collective-permute-start) | collective-permute-done | bytes 147488 | tf_op jit(solution)/shard_map/ppermute | solution.py:39
  13.0 4.1 %collective-permute-done.7 = bf16[128,1152]{1,0:T(8,128)(2,1)S(1)} collective-permute-done((bf16[128,1152]{1,0:T(8,128)(2,1)S(1)}, bf16[128,1152]{1,0:T(8,128)(2,1)S(1)}, u32[]{:S(2)}, u32[]{:S(2)}) %collective-permute-start.7) | collective-permute-done | bytes 294944 | tf_op jit(solution)/shard_map/ppermute | solution.py:51
  17.7 2.6 %collective-permute-start.4 = (bf16[256,1152]{1,0:T(8,128)(2,1)S(1)}, bf16[256,1152]{1,0:T(8,128)(2,1)S(1)}, u32[]{:S(2)}, u32[]{:S(2)}) collective-permute-start(bf16[256,1152]{1,0:T(8,128)(2,1)S(1)} %constant_dynamic-update-slice_fusion.refs_2_.refs_4_), channel_id=1, source_target_pairs={{0,2},{1,3},{2,0},{3,1},{4,6},{5,7},{6,4},{7,5},{8,10},{9,11},{10,... | collective-permute-start | bytes 1769480 | tf_op jit(solution)/shard_map/ppermute | solution.py:45
  20.3 1.9 %collective-permute-start.3 = (bf16[256,1152]{1,0:T(8,128)(2,1)S(1)}, bf16[256,1152]{1,0:T(8,128)(2,1)S(1)}, u32[]{:S(2)}, u32[]{:S(2)}) collective-permute-start(bf16[256,1152]{1,0:T(8,128)(2,1)S(1)} %constant_dynamic-update-slice_fusion.refs_2_.refs_4_), channel_id=1, source_target_pairs={{0,1},{1,2},{2,3},{3,0},{4,5},{5,6},{6,7},{7,4},{8,9},{9,10},{10,1... | collective-permute-start | bytes 1769480 | tf_op jit(solution)/shard_map/ppermute | solution.py:45
  22.2 2.9 %collective-permute-done.8 = bf16[128,1152]{1,0:T(8,128)(2,1)S(1)} collective-permute-done((bf16[128,1152]{1,0:T(8,128)(2,1)S(1)}, bf16[128,1152]{1,0:T(8,128)(2,1)S(1)}, u32[]{:S(2)}, u32[]{:S(2)}) %collective-permute-start.8) | collective-permute-done | bytes 294944 | tf_op jit(solution)/shard_map/ppermute | solution.py:51
  25.9 7.1 %collective-permute-done.9 = bf16[128,1152]{1,0:T(8,128)(2,1)S(1)} collective-permute-done((bf16[128,1152]{1,0:T(8,128)(2,1)S(1)}, bf16[128,1152]{1,0:T(8,128)(2,1)S(1)}, u32[]{:S(2)}, u32[]{:S(2)}) %collective-permute-start.9) | collective-permute-done | bytes 294944 | tf_op jit(solution)/shard_map/ppermute | solution.py:51
  33.1 6.3 %collective-permute-done.10 = bf16[64,1152]{1,0:T(8,128)(2,1)S(1)} collective-permute-done((bf16[64,1152]{1,0:T(8,128)(2,1)S(1)}, bf16[64,1152]{1,0:T(8,128)(2,1)S(1)}, u32[]{:S(2)}, u32[]{:S(2)}) %collective-permute-start.10) | collective-permute-done | bytes 147488 | tf_op jit(solution)/shard_map/ppermute | solution.py:51
  43.1 3.3 %far.1 = (bf16[256,512]{1,0:T(8,128)(2,1)S(1)}, bf16[256,512]{1,0:T(8,128)(2,1)S(1)}, bf16[256,512]{1,0:T(8,128)(2,1)S(1)}, bf16[256,512]{1,0:T(8,128)(2,1)S(1)}...) custom-call(f32[1]{0:T(128)S(6)} %copy.16.refs_0_, ...), custom_call_target="tpu_custom_call" | custom-call | flops 1 | bytes 1 | tf_op jit(solution)/shard_map/far/pallas_call | solution.py:65
  46.9 1.5 %near_texts.1 = (f32[256,1152]{1,0:T(8,128)S(1)}, bf16[256,1152]{1,0:T(8,128)(2,1)S(1)}) custom-call(bf16[256,512]{1,0:T(8,128)(2,1)S(1)} %get-tuple-element.39.refs_0_.refs_1_, bf16[256,512]{1,0:T(8,128)(2,1)S(1)} %get-tuple-element.45.refs_1_, bf16[256,512]{1,0:T(8,128)(2,1)S(1)} %get-tuple-element.42.refs_2_.refs_1_, ...), custom_call_target="tpu_custom_call" | custom-call | flops 1 | bytes 1 | tf_op jit(solution)/shard_map/near_texts/pallas_call | solution.py:65
  48.7 0.9 image1.1.refs_5_
  49.5 1.0 %collective-permute-start.16 = (bf16[264,1152]{1,0:T(8,128)(2,1)S(1)}, bf16[264,1152]{1,0:T(8,128)(2,1)S(1)}, u32[]{:S(2)}, u32[]{:S(2)}) collective-permute-start(bf16[264,1152]{1,0:T(8,128)(2,1)S(1)} %image1.1.refs_5_), channel_id=1, source_target_pairs={{0,3},{1,0},{2,1},{3,2},{4,7},{5,4},{6,5},{7,6},{8,11},{9,8},{10,9... | collective-permute-start | bytes 1824776 | tf_op jit(solution)/shard_map/ppermute | solution.py:45
  50.6 0.8 image3.1.refs_3_
  51.4 1.1 %collective-permute-start.18 = (bf16[264,1152]{1,0:T(8,128)(2,1)S(1)}, bf16[264,1152]{1,0:T(8,128)(2,1)S(1)}, u32[]{:S(2)}, u32[]{:S(2)}) collective-permute-start(bf16[264,1152]{1,0:T(8,128)(2,1)S(1)} %image3.1.refs_3_), channel_id=1, source_target_pairs={{0,1},{1,2},{2,3},{3,0},{4,5},{5,6},{6,7},{7,4},{8,9},{9,10},{10,1... | collective-permute-start | bytes 1824776 | tf_op jit(solution)/shard_map/ppermute | solution.py:45
  52.6 1.2 %collective-permute-done.14.refs_2_ = bf16[64,1152]{1,0:T(8,128)(2,1)S(1)} collective-permute-done((bf16[64,1152]{1,0:T(8,128)(2,1)S(1)}, bf16[64,1152]{1,0:T(8,128)(2,1)S(1)}, u32[]{:S(2)}, u32[]{:S(2)}) %collective-permute-start.14) | collective-permute-done | bytes 147488 | tf_op jit(solution)/shard_map/ppermute | solution.py:51
  53.9 0.8 image2.1.refs_5_
  54.8 2.6 %collective-permute-start.17 = (bf16[264,1152]{1,0:T(8,128)(2,1)S(1)}, bf16[264,1152]{1,0:T(8,128)(2,1)S(1)}, u32[]{:S(2)}, u32[]{:S(2)}) collective-permute-start(bf16[264,1152]{1,0:T(8,128)(2,1)S(1)} %image2.1.refs_5_), channel_id=1, source_target_pairs={{0,2},{1,3},{2,0},{3,1},{4,6},{5,7},{6,4},{7,5},{8,10},{9,11},{10,... | collective-permute-start | bytes 1824776 | tf_op jit(solution)/shard_map/ppermute | solution.py:45
  57.4 1.2 %collective-permute-start.19 = (bf16[128,1152]{1,0:T(8,128)(2,1)S(1)}, bf16[128,1152]{1,0:T(8,128)(2,1)S(1)}, u32[]{:S(2)}, u32[]{:S(2)}) collective-permute-start(bf16[128,1152]{1,0:T(8,128)(2,1)S(1)} %step2.1.refs_5_), channel_id=1, source_target_pairs={{0,28},{1,29},{2,30},{3,31},{4,0},{5,1},{6,2},{7,3},{8,4},{9,5},{1... | collective-permute-start | bytes 884744 | tf_op jit(solution)/shard_map/ppermute | solution.py:51
  59.4 4.7 %collective-permute-done.19.refs_2_ = bf16[128,1152]{1,0:T(8,128)(2,1)S(1)} collective-permute-done((bf16[128,1152]{1,0:T(8,128)(2,1)S(1)}, bf16[128,1152]{1,0:T(8,128)(2,1)S(1)}, u32[]{:S(2)}, u32[]{:S(2)}) %collective-permute-start.19) | collective-permute-done | bytes 294944 | tf_op jit(solution)/shard_map/ppermute | solution.py:51
  64.2 2.5 %collective-permute-start.23 = (bf16[128,1152]{1,0:T(8,128)(2,1)S(1)}, bf16[128,1152]{1,0:T(8,128)(2,1)S(1)}, u32[]{:S(2)}, u32[]{:S(2)}) collective-permute-start(bf16[128,1152]{1,0:T(8,128)(2,1)S(1)} %step3.1.refs_5_), channel_id=1, source_target_pairs={{0,28},{1,29},{2,30},{3,31},{4,0},{5,1},{6,2},{7,3},{8,4},{9,5},{1... | collective-permute-start | bytes 884744 | tf_op jit(solution)/shard_map/ppermute | solution.py:51
  67.5 3.5 %collective-permute-done.23.refs_2_ = bf16[128,1152]{1,0:T(8,128)(2,1)S(1)} collective-permute-done((bf16[128,1152]{1,0:T(8,128)(2,1)S(1)}, bf16[128,1152]{1,0:T(8,128)(2,1)S(1)}, u32[]{:S(2)}, u32[]{:S(2)}) %collective-permute-start.23) | collective-permute-done | bytes 294944 | tf_op jit(solution)/shard_map/ppermute | solution.py:51
  71.1 3.7 %collective-permute-start.24 = (bf16[128,1152]{1,0:T(8,128)(2,1)S(1)}, bf16[128,1152]{1,0:T(8,128)(2,1)S(1)}, u32[]{:S(2)}, u32[]{:S(2)}) collective-permute-start(bf16[128,1152]{1,0:T(8,128)(2,1)S(1)} %step4.1), channel_id=1, source_target_pairs={{0,28},{1,29},{2,30},{3,31},{4,0},{5,1},{6,2},{7,3},{8,4},{9,5},{1... | collective-permute-start | bytes 884744 | tf_op jit(solution)/shard_map/ppermute | solution.py:51
  74.8 2.4 %collective-permute-start.20 = (bf16[72,1152]{1,0:T(8,128)(2,1)S(1)}, bf16[72,1152]{1,0:T(8,128)(2,1)S(1)}, u32[]{:S(2)}, u32[]{:S(2)}) collective-permute-start(bf16[72,1152]{1,0:T(8,128)(2,1)S(1)} %get-tuple-element.53), channel_id=1, source_target_pairs={{0,192},{1,193},{2,194},{3,195},{4,196},{5,197},{6,198},{7,199},{8... | collective-permute-start | bytes 497672 | tf_op jit(solution)/shard_map/ppermute | solution.py:39
  77.2 1.5 %collective-permute-start.21 = (bf16[72,1152]{1,0:T(8,128)(2,1)S(1)}, bf16[72,1152]{1,0:T(8,128)(2,1)S(1)}, u32[]{:S(2)}, u32[]{:S(2)}) collective-permute-start(bf16[72,1152]{1,0:T(8,128)(2,1)S(1)} %get-tuple-element.54), channel_id=1, source_target_pairs={{0,128},{1,129},{2,130},{3,131},{4,132},{5,133},{6,134},{7,135},{8... | collective-permute-start | bytes 497672 | tf_op jit(solution)/shard_map/ppermute | solution.py:39
  79.2 2.7 %collective-permute-done.20.refs_2_ = bf16[72,1152]{1,0:T(8,128)(2,1)S(1)} collective-permute-done((bf16[72,1152]{1,0:T(8,128)(2,1)S(1)}, bf16[72,1152]{1,0:T(8,128)(2,1)S(1)}, u32[]{:S(2)}, u32[]{:S(2)}) %collective-permute-start.20) | collective-permute-done | bytes 165920 | tf_op jit(solution)/shard_map/ppermute | solution.py:39
  81.9 2.2 %collective-permute-done.21.refs_3_ = bf16[72,1152]{1,0:T(8,128)(2,1)S(1)} collective-permute-done((bf16[72,1152]{1,0:T(8,128)(2,1)S(1)}, bf16[72,1152]{1,0:T(8,128)(2,1)S(1)}, u32[]{:S(2)}, u32[]{:S(2)}) %collective-permute-start.21) | collective-permute-done | bytes 165920 | tf_op jit(solution)/shard_map/ppermute | solution.py:39
  84.1 1.7 %collective-permute-done.22.refs_4_ = bf16[72,1152]{1,0:T(8,128)(2,1)S(1)} collective-permute-done((bf16[72,1152]{1,0:T(8,128)(2,1)S(1)}, bf16[72,1152]{1,0:T(8,128)(2,1)S(1)}, u32[]{:S(2)}, u32[]{:S(2)}) %collective-permute-start.22) | collective-permute-done | bytes 165920 | tf_op jit(solution)/shard_map/ppermute | solution.py:39
  85.8 0.9 %finish_img.1 = (f32[64,1152]{1,0:T(8,128)}, f32[1,64]{1,0:T(1,128)}) custom-call(f32[64,1152]{1,0:T(8,128)S(1)} %get-tuple-element.51.refs_0_, f32[8,256]{1,0:T(8,128)S(1)} %get-tuple-element.52.refs_1_, bf16[72,1152]{1,0:T(8,128)(2,1)S(1)} %collective-permute-done.20.refs_2_, bf16[72,1152]{1,0:T(8,128)(2,1)S(1)} %collective-permute-done.21.refs_3_, ...), custom_call_target="tpu_custom_call" | custom-call | flops 1 | bytes 1 | tf_op jit(solution)/shard_map/finish_img/pallas_call | solution.py:65
  86.7 0.9 %finish_txt.1 = f32[64,1152]{1,0:T(8,128)} custom-call(f32[128,1152]{1,0:T(8,128)S(1)} %get-tuple-element.57.refs_0_, bf16[128,1152]{1,0:T(8,128)(2,1)S(1)} %collective-permute-done.24.refs_1_, bf16[64,1152]{1,0:T(8,128)(2,1)S(1)} %collective-permute-done.25.refs_2_, bf16[64,1152]{1,0:T(8,128)(2,1)S(1)} %copy-done.1, f32[64,1]{1,0:T(8,128)S(1)} %get-tuple-element.59.refs_4_), custom_call_target="tpu_custom_call" | custom-call | flops 1 | bytes 1 | tf_op jit(solution)/shard_map/finish_txt/pallas_call | solution.py:65
  (59 shorter events, 9.3 us)
Async XLA Ops:
  1.8 4.6 %collective-permute-start.6 = (bf16[64,1152]{1,0:T(8,128)(2,1)S(1)}, bf16[64,1152]{1,0:T(8,128)(2,1)S(1)}, u32[]{:S(2)}, u32[]{:S(2)}) collective-permute-start(bf16[64,1152]{1,0:T(8,128)(2,1)S(1)} %get-tuple-element.33), channel_id=1, source_target_pairs={{0,32},{1,33},{2,34},{3,35},{4,36},{5,37},{6,38},{7,39},{8,40},{9,... | collective-permute-start | bytes 442376 | tf_op jit(solution)/shard_map/ppermute | solution.py:55
  1.9 15.2 %collective-permute-start.2 = (bf16[64,1152]{1,0:T(8,128)(2,1)S(1)}, bf16[64,1152]{1,0:T(8,128)(2,1)S(1)}, u32[]{:S(2)}, u32[]{:S(2)}) collective-permute-start(bf16[64,1152]{1,0:T(8,128)(2,1)S(1)} %get-tuple-element.32), channel_id=1, source_target_pairs={{0,192},{1,193},{2,194},{3,195},{4,196},{5,197},{6,198},{7,199},{8... | collective-permute-start | bytes 442376 | tf_op jit(solution)/shard_map/ppermute | solution.py:39
  4.7 12.4 %collective-permute-start.1 = (bf16[64,1152]{1,0:T(8,128)(2,1)S(1)}, bf16[64,1152]{1,0:T(8,128)(2,1)S(1)}, u32[]{:S(2)}, u32[]{:S(2)}) collective-permute-start(bf16[64,1152]{1,0:T(8,128)(2,1)S(1)} %get-tuple-element.32), channel_id=1, source_target_pairs={{0,128},{1,129},{2,130},{3,131},{4,132},{5,133},{6,134},{7,135},{8... | collective-permute-start | bytes 442376 | tf_op jit(solution)/shard_map/ppermute | solution.py:39
  5.5 7.4 %collective-permute-start = (bf16[64,1152]{1,0:T(8,128)(2,1)S(1)}, bf16[64,1152]{1,0:T(8,128)(2,1)S(1)}, u32[]{:S(2)}, u32[]{:S(2)}) collective-permute-start(bf16[64,1152]{1,0:T(8,128)(2,1)S(1)} %get-tuple-element.32), channel_id=1, source_target_pairs={{0,64},{1,65},{2,66},{3,67},{4,68},{5,69},{6,70},{7,71},{8,72},{9,... | collective-permute-start | bytes 442376 | tf_op jit(solution)/shard_map/ppermute | solution.py:39
  6.5 10.6 %collective-permute-start.7 = (bf16[128,1152]{1,0:T(8,128)(2,1)S(1)}, bf16[128,1152]{1,0:T(8,128)(2,1)S(1)}, u32[]{:S(2)}, u32[]{:S(2)}) collective-permute-start(bf16[128,1152]{1,0:T(8,128)(2,1)S(1)} %pad_maximum_fusion.2), channel_id=1, source_target_pairs={{0,4},{1,5},{2,6},{3,7},{4,8},{5,9},{6,10},{7,11},{8,12},{9,13},{1... | collective-permute-start | bytes 884744 | tf_op jit(solution)/shard_map/ppermute | solution.py:51
  17.1 7.9 %collective-permute-start.8 = (bf16[128,1152]{1,0:T(8,128)(2,1)S(1)}, bf16[128,1152]{1,0:T(8,128)(2,1)S(1)}, u32[]{:S(2)}, u32[]{:S(2)}) collective-permute-start(bf16[128,1152]{1,0:T(8,128)(2,1)S(1)} %collective-permute-done.7), channel_id=1, source_target_pairs={{0,4},{1,5},{2,6},{3,7},{4,8},{5,9},{6,10},{7,11},{8,12},{9,13},{1... | collective-permute-start | bytes 884744 | tf_op jit(solution)/shard_map/ppermute | solution.py:51
  17.2 24.3 %collective-permute-start.5 = (bf16[256,1152]{1,0:T(8,128)(2,1)S(1)}, bf16[256,1152]{1,0:T(8,128)(2,1)S(1)}, u32[]{:S(2)}, u32[]{:S(2)}) collective-permute-start(bf16[256,1152]{1,0:T(8,128)(2,1)S(1)} %constant_dynamic-update-slice_fusion.refs_2_.refs_4_), channel_id=1, source_target_pairs={{0,3},{1,0},{2,1},{3,2},{4,7},{5,4},{6,5},{7,6},{8,11},{9,8},{10,9... | collective-permute-start | bytes 1769480 | tf_op jit(solution)/shard_map/ppermute | solution.py:45
  17.7 24.5 %collective-permute-start.4 = (bf16[256,1152]{1,0:T(8,128)(2,1)S(1)}, bf16[256,1152]{1,0:T(8,128)(2,1)S(1)}, u32[]{:S(2)}, u32[]{:S(2)}) collective-permute-start(bf16[256,1152]{1,0:T(8,128)(2,1)S(1)} %constant_dynamic-update-slice_fusion.refs_2_.refs_4_), channel_id=1, source_target_pairs={{0,2},{1,3},{2,0},{3,1},{4,6},{5,7},{6,4},{7,5},{8,10},{9,11},{10,... | collective-permute-start | bytes 1769480 | tf_op jit(solution)/shard_map/ppermute | solution.py:45
  20.3 20.4 %collective-permute-start.3 = (bf16[256,1152]{1,0:T(8,128)(2,1)S(1)}, bf16[256,1152]{1,0:T(8,128)(2,1)S(1)}, u32[]{:S(2)}, u32[]{:S(2)}) collective-permute-start(bf16[256,1152]{1,0:T(8,128)(2,1)S(1)} %constant_dynamic-update-slice_fusion.refs_2_.refs_4_), channel_id=1, source_target_pairs={{0,1},{1,2},{2,3},{3,0},{4,5},{5,6},{6,7},{7,4},{8,9},{9,10},{10,1... | collective-permute-start | bytes 1769480 | tf_op jit(solution)/shard_map/ppermute | solution.py:45
  25.0 7.9 %collective-permute-start.9 = (bf16[128,1152]{1,0:T(8,128)(2,1)S(1)}, bf16[128,1152]{1,0:T(8,128)(2,1)S(1)}, u32[]{:S(2)}, u32[]{:S(2)}) collective-permute-start(bf16[128,1152]{1,0:T(8,128)(2,1)S(1)} %collective-permute-done.8), channel_id=1, source_target_pairs={{0,4},{1,5},{2,6},{3,7},{4,8},{5,9},{6,10},{7,11},{8,12},{9,13},{1... | collective-permute-start | bytes 884744 | tf_op jit(solution)/shard_map/ppermute | solution.py:51
  25.1 14.7 %collective-permute-start.12 = (bf16[256,1152]{1,0:T(8,128)(2,1)S(1)}, bf16[256,1152]{1,0:T(8,128)(2,1)S(1)}, u32[]{:S(2)}, u32[]{:S(2)}) collective-permute-start(bf16[256,1152]{1,0:T(8,128)(2,1)S(1)} %pad_maximum_fusion), channel_id=1, source_target_pairs={{0,32},{1,33},{2,34},{3,35},{4,36},{5,37},{6,38},{7,39},{8,40},{9,... | collective-permute-start | bytes 1769480 | tf_op jit(solution)/shard_map/ppermute | solution.py:55
  33.0 6.4 %collective-permute-start.10 = (bf16[64,1152]{1,0:T(8,128)(2,1)S(1)}, bf16[64,1152]{1,0:T(8,128)(2,1)S(1)}, u32[]{:S(2)}, u32[]{:S(2)}) collective-permute-start(bf16[64,1152]{1,0:T(8,128)(2,1)S(1)} %slice.4), channel_id=1, source_target_pairs={{0,4},{1,5},{2,6},{3,7},{4,8},{5,9},{6,10},{7,11},{8,12},{9,13},{1... | collective-permute-start | bytes 442376 | tf_op jit(solution)/shard_map/ppermute | solution.py:51
  39.5 3.5 %collective-permute-start.11 = (bf16[192,1152]{1,0:T(8,128)(2,1)S(1)}, bf16[192,1152]{1,0:T(8,128)(2,1)S(1)}, u32[]{:S(2)}, u32[]{:S(2)}) collective-permute-start(bf16[192,1152]{1,0:T(8,128)(2,1)S(1)} %pad_maximum_fusion.1), channel_id=1, source_target_pairs={{0,32},{1,33},{2,34},{3,35},{4,36},{5,37},{6,38},{7,39},{8,40},{9,... | collective-permute-start | bytes 1327112 | tf_op jit(solution)/shard_map/ppermute | solution.py:55
  46.3 2.2 %collective-permute-start.13 = (bf16[192,1152]{1,0:T(8,128)(2,1)S(1)}, bf16[192,1152]{1,0:T(8,128)(2,1)S(1)}, u32[]{:S(2)}, u32[]{:S(2)}) collective-permute-start(bf16[192,1152]{1,0:T(8,128)(2,1)S(1)} %get-tuple-element.44.refs_8_), channel_id=1, source_target_pairs={{0,32},{1,33},{2,34},{3,35},{4,36},{5,37},{6,38},{7,39},{8,40},{9,... | collective-permute-start | bytes 1327112 | tf_op jit(solution)/shard_map/ppermute | solution.py:55
  48.4 5.4 %collective-permute-start.15 = (bf16[256,1152]{1,0:T(8,128)(2,1)S(1)}, bf16[256,1152]{1,0:T(8,128)(2,1)S(1)}, u32[]{:S(2)}, u32[]{:S(2)}) collective-permute-start(bf16[256,1152]{1,0:T(8,128)(2,1)S(1)} %get-tuple-element.47.refs_2_), channel_id=1, source_target_pairs={{0,32},{1,33},{2,34},{3,35},{4,36},{5,37},{6,38},{7,39},{8,40},{9,... | collective-permute-start | bytes 1769480 | tf_op jit(solution)/shard_map/ppermute | solution.py:55
  48.6 5.2 %collective-permute-start.14 = (bf16[64,1152]{1,0:T(8,128)(2,1)S(1)}, bf16[64,1152]{1,0:T(8,128)(2,1)S(1)}, u32[]{:S(2)}, u32[]{:S(2)}) collective-permute-start(bf16[64,1152]{1,0:T(8,128)(2,1)S(1)} %step1.1.refs_5_), channel_id=1, source_target_pairs={{0,28},{1,29},{2,30},{3,31},{4,0},{5,1},{6,2},{7,3},{8,4},{9,5},{1... | collective-permute-start | bytes 442376 | tf_op jit(solution)/shard_map/ppermute | solution.py:51
  49.5 17.2 %collective-permute-start.16 = (bf16[264,1152]{1,0:T(8,128)(2,1)S(1)}, bf16[264,1152]{1,0:T(8,128)(2,1)S(1)}, u32[]{:S(2)}, u32[]{:S(2)}) collective-permute-start(bf16[264,1152]{1,0:T(8,128)(2,1)S(1)} %image1.1.refs_5_), channel_id=1, source_target_pairs={{0,3},{1,0},{2,1},{3,2},{4,7},{5,4},{6,5},{7,6},{8,11},{9,8},{10,9... | collective-permute-start | bytes 1824776 | tf_op jit(solution)/shard_map/ppermute | solution.py:45
  51.4 15.3 %collective-permute-start.18 = (bf16[264,1152]{1,0:T(8,128)(2,1)S(1)}, bf16[264,1152]{1,0:T(8,128)(2,1)S(1)}, u32[]{:S(2)}, u32[]{:S(2)}) collective-permute-start(bf16[264,1152]{1,0:T(8,128)(2,1)S(1)} %image3.1.refs_3_), channel_id=1, source_target_pairs={{0,1},{1,2},{2,3},{3,0},{4,5},{5,6},{6,7},{7,4},{8,9},{9,10},{10,1... | collective-permute-start | bytes 1824776 | tf_op jit(solution)/shard_map/ppermute | solution.py:45
  54.8 12.5 %collective-permute-start.17 = (bf16[264,1152]{1,0:T(8,128)(2,1)S(1)}, bf16[264,1152]{1,0:T(8,128)(2,1)S(1)}, u32[]{:S(2)}, u32[]{:S(2)}) collective-permute-start(bf16[264,1152]{1,0:T(8,128)(2,1)S(1)} %image2.1.refs_5_), channel_id=1, source_target_pairs={{0,2},{1,3},{2,0},{3,1},{4,6},{5,7},{6,4},{7,5},{8,10},{9,11},{10,... | collective-permute-start | bytes 1824776 | tf_op jit(solution)/shard_map/ppermute | solution.py:45
  57.4 6.7 %collective-permute-start.19 = (bf16[128,1152]{1,0:T(8,128)(2,1)S(1)}, bf16[128,1152]{1,0:T(8,128)(2,1)S(1)}, u32[]{:S(2)}, u32[]{:S(2)}) collective-permute-start(bf16[128,1152]{1,0:T(8,128)(2,1)S(1)} %step2.1.refs_5_), channel_id=1, source_target_pairs={{0,28},{1,29},{2,30},{3,31},{4,0},{5,1},{6,2},{7,3},{8,4},{9,5},{1... | collective-permute-start | bytes 884744 | tf_op jit(solution)/shard_map/ppermute | solution.py:51
  64.2 6.8 %collective-permute-start.23 = (bf16[128,1152]{1,0:T(8,128)(2,1)S(1)}, bf16[128,1152]{1,0:T(8,128)(2,1)S(1)}, u32[]{:S(2)}, u32[]{:S(2)}) collective-permute-start(bf16[128,1152]{1,0:T(8,128)(2,1)S(1)} %step3.1.refs_5_), channel_id=1, source_target_pairs={{0,28},{1,29},{2,30},{3,31},{4,0},{5,1},{6,2},{7,3},{8,4},{9,5},{1... | collective-permute-start | bytes 884744 | tf_op jit(solution)/shard_map/ppermute | solution.py:51
  71.0 14.8 %copy-start = (bf16[64,1152]{1,0:T(8,128)(2,1)S(1)}, bf16[64,1152]{1,0:T(8,128)(2,1)}, u32[]{:S(2)}) copy-start(bf16[64,1152]{1,0:T(8,128)(2,1)} %refs_5_.1) | copy-start | bytes 442372
  71.1 15.6 %copy-start.1 = (bf16[64,1152]{1,0:T(8,128)(2,1)S(1)}, bf16[64,1152]{1,0:T(8,128)(2,1)}, u32[]{:S(2)}) copy-start(bf16[64,1152]{1,0:T(8,128)(2,1)} %refs_3_.1) | copy-start | bytes 442372
  71.1 8.0 %collective-permute-start.24 = (bf16[128,1152]{1,0:T(8,128)(2,1)S(1)}, bf16[128,1152]{1,0:T(8,128)(2,1)S(1)}, u32[]{:S(2)}, u32[]{:S(2)}) collective-permute-start(bf16[128,1152]{1,0:T(8,128)(2,1)S(1)} %step4.1), channel_id=1, source_target_pairs={{0,28},{1,29},{2,30},{3,31},{4,0},{5,1},{6,2},{7,3},{8,4},{9,5},{1... | collective-permute-start | bytes 884744 | tf_op jit(solution)/shard_map/ppermute | solution.py:51
  74.8 7.0 %collective-permute-start.20 = (bf16[72,1152]{1,0:T(8,128)(2,1)S(1)}, bf16[72,1152]{1,0:T(8,128)(2,1)S(1)}, u32[]{:S(2)}, u32[]{:S(2)}) collective-permute-start(bf16[72,1152]{1,0:T(8,128)(2,1)S(1)} %get-tuple-element.53), channel_id=1, source_target_pairs={{0,192},{1,193},{2,194},{3,195},{4,196},{5,197},{6,198},{7,199},{8... | collective-permute-start | bytes 497672 | tf_op jit(solution)/shard_map/ppermute | solution.py:39
  77.2 6.9 %collective-permute-start.21 = (bf16[72,1152]{1,0:T(8,128)(2,1)S(1)}, bf16[72,1152]{1,0:T(8,128)(2,1)S(1)}, u32[]{:S(2)}, u32[]{:S(2)}) collective-permute-start(bf16[72,1152]{1,0:T(8,128)(2,1)S(1)} %get-tuple-element.54), channel_id=1, source_target_pairs={{0,128},{1,129},{2,130},{3,131},{4,132},{5,133},{6,134},{7,135},{8... | collective-permute-start | bytes 497672 | tf_op jit(solution)/shard_map/ppermute | solution.py:39
  78.7 7.1 %collective-permute-start.22 = (bf16[72,1152]{1,0:T(8,128)(2,1)S(1)}, bf16[72,1152]{1,0:T(8,128)(2,1)S(1)}, u32[]{:S(2)}, u32[]{:S(2)}) collective-permute-start(bf16[72,1152]{1,0:T(8,128)(2,1)S(1)} %get-tuple-element.55.refs_3_), channel_id=1, source_target_pairs={{0,64},{1,65},{2,66},{3,67},{4,68},{5,69},{6,70},{7,71},{8,72},{9,... | collective-permute-start | bytes 497672 | tf_op jit(solution)/shard_map/ppermute | solution.py:39
  79.1 7.6 %collective-permute-start.25 = (bf16[64,1152]{1,0:T(8,128)(2,1)S(1)}, bf16[64,1152]{1,0:T(8,128)(2,1)S(1)}, u32[]{:S(2)}, u32[]{:S(2)}) collective-permute-start(bf16[64,1152]{1,0:T(8,128)(2,1)S(1)} %step5.1.refs_7_), channel_id=1, source_target_pairs={{0,32},{1,33},{2,34},{3,35},{4,36},{5,37},{6,38},{7,39},{8,40},{9,... | collective-permute-start | bytes 442376 | tf_op jit(solution)/shard_map/ppermute | solution.py:55

commit v3 on v2

--- a/solution.py
+++ b/solution.py
@@ -135,14 +135,10 @@
     return total
 
 
-def near_body(scale_ref, bias_ref, img_ref, txt_ref, coeff_ref, loss_ref):
-    total = None
-    for n in range(2):
-        at = slice(256 * n, 256 * (n + 1))
-        weight, softplus = entry(img_ref[...], txt_ref[at, :], scale_ref[0], bias_ref[0])
-        coeff_ref[:, at] = weight
-        total = fold(softplus) if total is None else total + fold(softplus)
-    loss_ref[...] = total
+def mine_body(scale_ref, bias_ref, img_ref, txt_ref, coeff_ref, loss_ref):
+    weight, softplus = entry(img_ref[...], txt_ref[...], scale_ref[0], bias_ref[0])
+    coeff_ref[...] = weight
+    loss_ref[...] = fold(softplus)
 
 
 def texts(coeffs, imgs, lo, hi):
@@ -155,11 +151,11 @@
     return total
 
 
-def far_body(scale_ref, bias_ref, i0, i1, i2, i3, txt_ref, l0, l1, l2, l3, c0, c1, c2, c3, keep, send, pair, loss):
+def far_body(scale_ref, bias_ref, i0, i1, i2, i3, txt_ref, near_loss, c0, c1, c2, c3, keep, send, pair, loss):
     scale, bias = scale_ref[0], bias_ref[0]
-    imgs, coeffs, sums = (i0, i1, i2, i3), (c0, c1, c2, c3), (l0, l1, l2, l3)
+    imgs, coeffs = (i0, i1, i2, i3), (c0, c1, c2, c3)
     for k in range(4):
-        total = sums[k][...]
+        total = near_loss[256 * k : 256 * (k + 1), :]
         for n in range(2):
             at = slice(256 * n, 256 * (n + 1))
             match = None
@@ -180,15 +176,24 @@
     pair[...] = g[128:, :]
 
 
-def near_texts_body(c0, c1, c2, c3, i0, i1, i2, i3, keep, send):
-    coeffs, imgs = (c0, c1, c2, c3), (i0, i1, i2, i3)
-    keep[...] = texts(coeffs, imgs, 0, 256)
-    send[...] = texts(coeffs, imgs, 256, 512).astype(BF16)
-
-
-def image_body(k, cf, cn, far, near, loss, out):
+def other_body(scale_ref, bias_ref, i0, i1, i2, i3, c0, c1, c2, c3, txt_ref, l0, l1, l2, l3, o0, o1, o2, o3, keep, send, loss):
+    imgs, sums, mine, other = (i0, i1, i2, i3), (l0, l1, l2, l3), (c0, c1, c2, c3), (o0, o1, o2, o3)
+    for k in range(4):
+        weight, softplus = entry(imgs[k][...], txt_ref[...], scale_ref[0], bias_ref[0])
+        other[k][...] = weight
+        loss[256 * k : 256 * (k + 1), :] = sums[k][...] + fold(softplus)
+    send[...] = texts(other, imgs, 0, 256).astype(BF16)
+    keep[...] = texts(mine, imgs, 0, 256)
+
+
+def copy_body(src, dst):
+    dst[...] = src[...]
+
+
+def image_body(k, cf, cm, co, far, mine, other, loss, out):
     g = jnp.dot(cf[...], far[...], preferred_element_type=F32)
-    g = g + jnp.dot(cn[...], near[...], preferred_element_type=F32)
+    g = g + jnp.dot(cm[...], mine[...], preferred_element_type=F32)
+    g = g + jnp.dot(co[...], other[...], preferred_element_type=F32)
     if k == 0:
         out[...] = g
     else:
@@ -212,22 +217,25 @@
             out[U:, :256] = marks
 
 
+def pack_body(b1, b2, far, near):
+    far[:U, :] = b2[:U, :]
+    far[U:, :] = b1[...]
+    near[:128, :] = b2[...]
+    near[128:, :] = b1[...]
+
+
 def step1_body(keep, got, out):
-    out[...] = (keep[:64, :] + up(got, 0, 64)).astype(BF16)
-
-
-def step2_body(keep, got, r, out):
-    out[:64, :] = (keep[64:128, :] + (up(got, 64, 128) + up(r, 0, 64))).astype(BF16)
-    out[64:, :] = (keep[128:192, :] + up(got, 128, 192)).astype(BF16)
-
-
-def step_body(lo, keep, got, r, out):
-    hi = lo + 128
-    out[...] = (keep[lo:hi, :] + (up(got, lo, hi) + up(r, 0, 128))).astype(BF16)
-
-
-def step5_body(pair, r, out):
-    out[...] = (pair[64:, :] + up(r, 64, 128)).astype(BF16)
+    out[...] = (keep[...] + got[...].astype(F32)).astype(BF16)
+
+
+def step2_body(keep, got, w, two, one):
+    two[:64, :] = (keep[:64, :] + (up(got, 0, 64) + up(w, 0, 64))).astype(BF16)
+    two[64:, :] = (keep[64:128, :] + up(got, 64, 128)).astype(BF16)
+    one[...] = (keep[128:, :] + (up(got, 128, 256) + up(w, 64, 192))).astype(BF16)
+
+
+def step3_body(pair, v1, v2, out):
+    out[...] = (pair[64:, :] + (up(v1, 64, 128) + up(v2, 64, 128))).astype(BF16)
 
 
 def back_norm(g, raw, inv):
@@ -244,8 +252,8 @@
     loss_ref[...] = loss
 
 
-def finish_txt_body(pair, r, got, raw, inv, out_ref):
-    g = pair[:64, :] + (up(r, 0, 64) + got[...].astype(F32))
+def finish_txt_body(pair, v1, v2, got, raw, inv, out_ref):
+    g = pair[:64, :] + (up(v1, 0, 64) + up(v2, 0, 64) + got[...].astype(F32))
     out_ref[...] = back_norm(g, raw, inv)
 
 
@@ -260,31 +268,37 @@
 
     pair = jnp.concatenate([txt, swap(txt)], axis=0)
     f1, f3, f2 = first(img, 1), first(img, 3), first(img, 2)
-    b1 = ring(pair, 1)
+    b1, b2 = ring(pair, 1), ring(pair, 2)
     group = jnp.concatenate([img, f1, f2, f3], axis=0)
     g1, g3, g2 = second(group, 1), second(group, 3), second(group, 2)
     groups = (group, g1, g2, g3)
-    b2 = ring(b1, 1)
-    near_mine = jnp.concatenate([b2, b1], axis=0)
-    near = jnp.concatenate([near_mine, swap(near_mine)], axis=0)
-    b3 = ring(b2, 1)
-    b4 = ring(b3[:U], 1)
-    far_mine = jnp.concatenate([b4, b3], axis=0)
+    far_pack, near_mine = call(
+        "pack", pack_body, [shape(192, d), shape(256, d)], (b1, b2), (), (group,)
+    )
+    far_got = ring(far_pack, 2)
+    near_other = swap(near_mine)
+
+    sc = (scale, bias)
+    mine_c, mine_l, last = [None] * 4, [None] * 4, ()
+    for k in (0, 1, 3, 2):
+        mine_c[k], mine_l[k] = call(
+            f"mine{k}", mine_body, [shape(256, 256), shape(256, 128, dtype=F32)],
+            (groups[k], near_mine), sc, last,
+        )
+        last = (mine_l[k],)
+    *other_c, keep_b, send_b, near_loss = call(
+        "other", other_body,
+        [shape(256, 256)] * 4 + [shape(256, d, dtype=F32), shape(256, d), shape(1024, 128, dtype=F32)],
+        (*groups, *mine_c, near_other, *mine_l), sc, last,
+    )
+    got_b = swap(send_b)
+    far_mine = call("arrived", copy_body, [shape(192, d)], (far_got,), (), (send_b,))[0]
     far = jnp.concatenate([far_mine, swap(far_mine), pair], axis=0)
-
-    sc = (scale, bias)
-    near_c, near_l, last = [None] * 4, [None] * 4, ()
-    for k in (0, 1, 3, 2):
-        near_c[k], near_l[k] = call(
-            f"near{k}", near_body, [shape(256, 512), shape(256, 128, dtype=F32)],
-            (groups[k], near), sc, last,
-        )
-        last = (near_l[k],)
     *far_c, keep_a, send_a, own_pair, loss = call(
         "far", far_body,
         [shape(256, 512)] * 4
         + [shape(192, d, dtype=F32), shape(192, d), shape(128, d, dtype=F32), shape(8, 1024, dtype=F32)],
-        (*groups, far, *near_l), sc,
+        (*groups, far, near_loss), sc,
     )
     got_a = swap(send_a)
 
@@ -292,45 +306,36 @@
         out = shape(256, d, dtype=F32) if k == 0 else shape(264, d)
         return call(
             f"image{k}", functools.partial(image_body, k), [out],
-            (far_c[k], near_c[k], far, near, loss), (), after,
+            (far_c[k], mine_c[k], other_c[k], far, near_mine, near_other, loss), (), after,
         )[0]
 
-    keep_b, send_b = call(
-        "near_texts", near_texts_body, [shape(256, d, dtype=F32), shape(256, d)],
-        (*near_c, *groups), (), (send_a,),
-    )
-    got_b = swap(send_b)
-    z1 = call("step1", step1_body, [shape(64, d)], (keep_a, got_a), (), (send_b,))[0]
-    w1 = ring(z1, -1)
-    p1 = image(1, (z1,))
+    p1 = image(1, ())
     r1 = second(p1, -1)
-    p3 = image(3, (p1,))
+    z1 = call("step1", step1_body, [shape(192, d)], (keep_a, got_a), (), (p1, got_b))[0]
+    w = ring(z1, -2)
+    p3 = image(3, (z1,))
     r3 = second(p3, -3)
-    z2 = call("step2", step2_body, [shape(128, d)], (keep_a, got_a, w1), (), (p3, got_b))[0]
-    w2 = ring(z2, -1)
-    p2 = image(2, (z2,))
+    p2 = image(2, (p3,))
     r2 = second(p2, -2)
     p0 = image(0, (p2,))
-    z3 = call("step3", functools.partial(step_body, 0), [shape(128, d)], (keep_b, got_b, w2), (), (p0,))[0]
-    w3 = ring(z3, -1)
+    two, one = call("step2", step2_body, [shape(128, d)] * 2, (keep_b, got_b, w), (), (p0,))
+    v1, v2 = ring(one, -1), ring(two, -2)
     own_img, own_loss, m1, m2, m3 = call(
         "merge_img", merge_img_body,
         [shape(rows, d, dtype=F32), shape(8, 256, dtype=F32)] + [shape(rows + 8, d)] * 3,
-        (p0, loss, r1, r2, r3), (), (z3,),
+        (p0, loss, r1, r2, r3), (), (one,),
     )
     q1, q3, q2 = first(m1, -1), first(m3, -3), first(m2, -2)
-    z4 = call("step4", functools.partial(step_body, 128), [shape(128, d)], (keep_b, got_b, w3), (), (m3,))[0]
-    w4 = ring(z4, -1)
-    z5 = call("step5", step5_body, [shape(64, d)], (own_pair, w4))[0]
-    got_c = swap(z5)
+    z3 = call("step3", step3_body, [shape(64, d)], (own_pair, v1, v2), (), (m3,))[0]
+    got_c = swap(z3)
     grad_img, loss_out = call(
         "finish_img", finish_img_body,
         [shape(rows, d, dtype=F32), shape(1, rows, dtype=F32)],
-        (own_img, own_loss, q1, q2, q3, picture, img_inv), (), (z5,),
+        (own_img, own_loss, q1, q2, q3, picture, img_inv), (), (z3,),
     )
     grad_txt = call(
         "finish_txt", finish_txt_body, [shape(rows, d, dtype=F32)],
-        (own_pair, w4, got_c, caption, txt_inv),
+        (own_pair, v1, v2, got_c, caption, txt_inv),
     )[0]
     return grad_img, grad_txt, loss_out.reshape(rows)
 

time: 87.8 us -> 84.4 us (0.961)
  the two profiles are of different devices: /device:TPU:8 before, /device:TPU:32 now
where the time goes in v3:
time: 84.4 us; the launch traced here: 84.3 us
  starting transfers between devices  38.2 us (45%)
  waiting for transfers between devices  29 us (34%)
  Pallas kernels  14.7 us (17%)
  between operations  2.16 us (3%)
    ppermute x6, starting transfers between devices, ring(): lax.ppermute(a, AXES, permutation(lambda x, c, z, y: (x, c, z - s if c el...  19.2 us
    pallas_call x19, Pallas kernels, call(): pl.pallas_call(kernel, out_shape=outs, in_specs=[SMEM] * len(scalars) + (...  14.7 us
    ppermute x6, waiting for transfers between devices, second(): lax.ppermute(a, AXES, permutation(lambda x, c, z, y: (x + s, c, z, y) if...  9.78 us
    ppermute x6, starting transfers between devices, second(): lax.ppermute(a, AXES, permutation(lambda x, c, z, y: (x + s, c, z, y) if...  9.5 us
    ppermute x6, waiting for transfers between devices, ring(): lax.ppermute(a, AXES, permutation(lambda x, c, z, y: (x, c, z - s if c el...  8.89 us
    ppermute x6, starting transfers between devices, first(): lax.ppermute(a, AXES, permutation(lambda x, c, z, y: (x, c, z, y + s) if...  8.47 us
    ppermute x6, waiting for transfers between devices, first(): lax.ppermute(a, AXES, permutation(lambda x, c, z, y: (x, c, z, y + s) if...  6.92 us
    ppermute x6, waiting for transfers between devices, swap(): lax.ppermute(a, AXES, permutation(lambda x, c, z, y: (x, 1 - c, z, y)))  3.42 us
  transfers between devices with their start and end apart: 24, of which 13 were waited for; matrix products, arithmetic and copies ran while one was open for 0% of the time, Pallas kernels for 15%

profile of v3, /device:TPU:32, one launch (start us, length us, event | category | flops | bytes accessed | tf_op | source)
XLA Modules:
  0.0 84.3 jit_solution(7978181084939619972)
XLA Ops:
  0.6 1.2 %normalize.1 = (bf16[64,1152]{1,0:T(8,128)(2,1)S(1)}, bf16[64,1152]{1,0:T(8,128)(2,1)S(1)}, f32[64,1]{1,0:T(8,128)S(1)}, f32[64,1]{1,0:T(8,128)S(1)}) custom-call(bf16[64,1152]{1,0:T(8,128)(2,1)} %refs_5_.1, bf16[64,1152]{1,0:T(8,128)(2,1)} %refs_4_.1), custom_call_target="tpu_custom_call" | custom-call | flops 1 | bytes 1 | tf_op jit(solution)/shard_map/normalize/pallas_call | solution.py:65
  1.8 2.8 %collective-permute-start.2 = (bf16[64,1152]{1,0:T(8,128)(2,1)S(1)}, bf16[64,1152]{1,0:T(8,128)(2,1)S(1)}, u32[]{:S(2)}, u32[]{:S(2)}) collective-permute-start(bf16[64,1152]{1,0:T(8,128)(2,1)S(1)} %get-tuple-element.41), channel_id=1, source_target_pairs={{0,192},{1,193},{2,194},{3,195},{4,196},{5,197},{6,198},{7,199},{8... | collective-permute-start | bytes 442376 | tf_op jit(solution)/shard_map/ppermute | solution.py:39
  5.4 0.9 %collective-permute-start = (bf16[64,1152]{1,0:T(8,128)(2,1)S(1)}, bf16[64,1152]{1,0:T(8,128)(2,1)S(1)}, u32[]{:S(2)}, u32[]{:S(2)}) collective-permute-start(bf16[64,1152]{1,0:T(8,128)(2,1)S(1)} %get-tuple-element.41), channel_id=1, source_target_pairs={{0,64},{1,65},{2,66},{3,67},{4,68},{5,69},{6,70},{7,71},{8,72},{9,... | collective-permute-start | bytes 442376 | tf_op jit(solution)/shard_map/ppermute | solution.py:39
  6.4 1.3 %collective-permute-done.6 = bf16[64,1152]{1,0:T(8,128)(2,1)S(1)} collective-permute-done((bf16[64,1152]{1,0:T(8,128)(2,1)S(1)}, bf16[64,1152]{1,0:T(8,128)(2,1)S(1)}, u32[]{:S(2)}, u32[]{:S(2)}) %collective-permute-start.6) | collective-permute-done | bytes 147488 | tf_op jit(solution)/shard_map/ppermute | solution.py:55
  7.7 3.3 %collective-permute-start.8 = (bf16[128,1152]{1,0:T(8,128)(2,1)S(1)}, bf16[128,1152]{1,0:T(8,128)(2,1)S(1)}, u32[]{:S(2)}, u32[]{:S(2)}) collective-permute-start(bf16[128,1152]{1,0:T(8,128)(2,1)S(1)} %constant_dynamic-update-slice_fusion.4), channel_id=1, source_target_pairs={{0,8},{1,9},{2,10},{3,11},{4,12},{5,13},{6,14},{7,15},{8,16},{9,17... | collective-permute-start | bytes 884744 | tf_op jit(solution)/shard_map/ppermute | solution.py:51
  11.1 3.1 %collective-permute-start.7 = (bf16[128,1152]{1,0:T(8,128)(2,1)S(1)}, bf16[128,1152]{1,0:T(8,128)(2,1)S(1)}, u32[]{:S(2)}, u32[]{:S(2)}) collective-permute-start(bf16[128,1152]{1,0:T(8,128)(2,1)S(1)} %constant_dynamic-update-slice_fusion.4), channel_id=1, source_target_pairs={{0,4},{1,5},{2,6},{3,7},{4,8},{5,9},{6,10},{7,11},{8,12},{9,13},{1... | collective-permute-start | bytes 884744 | tf_op jit(solution)/shard_map/ppermute | solution.py:51
  14.3 1.7 %collective-permute-start.3 = (bf16[256,1152]{1,0:T(8,128)(2,1)S(1)}, bf16[256,1152]{1,0:T(8,128)(2,1)S(1)}, u32[]{:S(2)}, u32[]{:S(2)}) collective-permute-start(bf16[256,1152]{1,0:T(8,128)(2,1)S(1)} %constant_dynamic-update-slice_fusion.refs_2_), channel_id=1, source_target_pairs={{0,1},{1,2},{2,3},{3,0},{4,5},{5,6},{6,7},{7,4},{8,9},{9,10},{10,1... | collective-permute-start | bytes 1769480 | tf_op jit(solution)/shard_map/ppermute | solution.py:45
  15.9 1.7 %collective-permute-start.5 = (bf16[256,1152]{1,0:T(8,128)(2,1)S(1)}, bf16[256,1152]{1,0:T(8,128)(2,1)S(1)}, u32[]{:S(2)}, u32[]{:S(2)}) collective-permute-start(bf16[256,1152]{1,0:T(8,128)(2,1)S(1)} %constant_dynamic-update-slice_fusion.refs_2_), channel_id=1, source_target_pairs={{0,3},{1,0},{2,1},{3,2},{4,7},{5,4},{6,5},{7,6},{8,11},{9,8},{10,9... | collective-permute-start | bytes 1769480 | tf_op jit(solution)/shard_map/ppermute | solution.py:45
  17.6 2.0 %collective-permute-start.4 = (bf16[256,1152]{1,0:T(8,128)(2,1)S(1)}, bf16[256,1152]{1,0:T(8,128)(2,1)S(1)}, u32[]{:S(2)}, u32[]{:S(2)}) collective-permute-start(bf16[256,1152]{1,0:T(8,128)(2,1)S(1)} %constant_dynamic-update-slice_fusion.refs_2_), channel_id=1, source_target_pairs={{0,2},{1,3},{2,0},{3,1},{4,6},{5,7},{6,4},{7,5},{8,10},{9,11},{10,... | collective-permute-start | bytes 1769480 | tf_op jit(solution)/shard_map/ppermute | solution.py:45
  19.6 1.6 %collective-permute-done.8.refs_1_ = bf16[128,1152]{1,0:T(8,128)(2,1)S(1)} collective-permute-done((bf16[128,1152]{1,0:T(8,128)(2,1)S(1)}, bf16[128,1152]{1,0:T(8,128)(2,1)S(1)}, u32[]{:S(2)}, u32[]{:S(2)}) %collective-permute-start.8) | collective-permute-done | bytes 294944 | tf_op jit(solution)/shard_map/ppermute | solution.py:51
  21.2 1.1 %collective-permute-done.7.refs_0_ = bf16[128,1152]{1,0:T(8,128)(2,1)S(1)} collective-permute-done((bf16[128,1152]{1,0:T(8,128)(2,1)S(1)}, bf16[128,1152]{1,0:T(8,128)(2,1)S(1)}, u32[]{:S(2)}, u32[]{:S(2)}) %collective-permute-start.7) | collective-permute-done | bytes 294944 | tf_op jit(solution)/shard_map/ppermute | solution.py:51
  22.4 4.5 %collective-permute-start.9 = (bf16[192,1152]{1,0:T(8,128)(2,1)S(1)}, bf16[192,1152]{1,0:T(8,128)(2,1)S(1)}, u32[]{:S(2)}, u32[]{:S(2)}) collective-permute-start(bf16[192,1152]{1,0:T(8,128)(2,1)S(1)} %get-tuple-element.43), channel_id=1, source_target_pairs={{0,8},{1,9},{2,10},{3,11},{4,12},{5,13},{6,14},{7,15},{8,16},{9,17... | collective-permute-start | bytes 1327112 | tf_op jit(solution)/shard_map/ppermute | solution.py:51
  29.6 3.4 %collective-permute-done.4.refs_2_.refs_4_ = bf16[256,1152]{1,0:T(8,128)(2,1)S(1)} collective-permute-done((bf16[256,1152]{1,0:T(8,128)(2,1)S(1)}, bf16[256,1152]{1,0:T(8,128)(2,1)S(1)}, u32[]{:S(2)}, u32[]{:S(2)}) %collective-permute-start.4) | collective-permute-done | bytes 589856 | tf_op jit(solution)/shard_map/ppermute | solution.py:45
  33.5 2.6 %other.1 = (bf16[256,256]{1,0:T(8,128)(2,1)S(1)}, bf16[256,256]{1,0:T(8,128)(2,1)S(1)}, bf16[256,256]{1,0:T(8,128)(2,1)S(1)}, bf16[256,256]{1,0:T(8,128)(2,1)S(1...) custom-call(f32[1]{0:T(128)S(6)} %copy.11.refs_0_, f32[1]{0:T(128)S(6)} %copy.12.refs_1_, ...), custom_call_target="tpu_custom_call" | custom-call | flops 1 | bytes 1 | tf_op jit(solution)/shard_map/other/pallas_call | solution.py:65
  36.1 2.3 %collective-permute-done.9.refs_0_ = bf16[192,1152]{1,0:T(8,128)(2,1)S(1)} collective-permute-done((bf16[192,1152]{1,0:T(8,128)(2,1)S(1)}, bf16[192,1152]{1,0:T(8,128)(2,1)S(1)}, u32[]{:S(2)}, u32[]{:S(2)}) %collective-permute-start.9) | collective-permute-done | bytes 442400 | tf_op jit(solution)/shard_map/ppermute | solution.py:51
  39.0 1.3 %collective-permute-done.11 = bf16[192,1152]{1,0:T(8,128)(2,1)S(1)} collective-permute-done((bf16[192,1152]{1,0:T(8,128)(2,1)S(1)}, bf16[192,1152]{1,0:T(8,128)(2,1)S(1)}, u32[]{:S(2)}, u32[]{:S(2)}) %collective-permute-start.11) | collective-permute-done | bytes 442400 | tf_op jit(solution)/shard_map/ppermute | solution.py:55
  40.4 3.2 %far.1 = (bf16[256,512]{1,0:T(8,128)(2,1)S(1)}, bf16[256,512]{1,0:T(8,128)(2,1)S(1)}, bf16[256,512]{1,0:T(8,128)(2,1)S(1)}, bf16[256,512]{1,0:T(8,128)(2,1)S(1)}...) custom-call(f32[1]{0:T(128)S(6)} %copy.11.refs_0_, ...), custom_call_target="tpu_custom_call" | custom-call | flops 1 | bytes 1 | tf_op jit(solution)/shard_map/far/pallas_call | solution.py:65
  45.6 2.8 %collective-permute-start.17 = (bf16[192,1152]{1,0:T(8,128)(2,1)S(1)}, bf16[192,1152]{1,0:T(8,128)(2,1)S(1)}, u32[]{:S(2)}, u32[]{:S(2)}) collective-permute-start(bf16[192,1152]{1,0:T(8,128)(2,1)S(1)} %step1.1.refs_7_), channel_id=1, source_target_pairs={{0,24},{1,25},{2,26},{3,27},{4,28},{5,29},{6,30},{7,31},{8,0},{9,1... | collective-permute-start | bytes 1327112 | tf_op jit(solution)/shard_map/ppermute | solution.py:51
  48.4 3.0 %collective-permute-start.14 = (bf16[264,1152]{1,0:T(8,128)(2,1)S(1)}, bf16[264,1152]{1,0:T(8,128)(2,1)S(1)}, u32[]{:S(2)}, u32[]{:S(2)}) collective-permute-start(bf16[264,1152]{1,0:T(8,128)(2,1)S(1)} %image1.1.refs_2_), channel_id=1, source_target_pairs={{0,3},{1,0},{2,1},{3,2},{4,7},{5,4},{6,5},{7,6},{8,11},{9,8},{10,9... | collective-permute-start | bytes 1824776 | tf_op jit(solution)/shard_map/ppermute | solution.py:45
  52.2 0.8 %image2.1.refs_7_ = bf16[264,1152]{1,0:T(8,128)(2,1)S(1)} custom-call(bf16[256,512]{1,0:T(8,128)(2,1)S(1)} %get-tuple-element.58.refs_0_, bf16[256,256]{1,0:T(8,128)(2,1)S(1)} %get-tuple-element.50.refs_8_.refs_1_, bf16[256,256]{1,0:T(8,128)(2,1)S(1)} %get-tuple-element.59.refs_2_, bf16[512,1152]{1,0:T(8,128)(2,1)S(1)} %pad_maximum_fusion.refs_6_.refs_3_, ...), custom_call_target="tpu_custom_call" | custom-call | flops 1 | bytes 1 | tf_op jit(solution)/shard_map/image2/pallas_call | solution.py:65
  53.3 1.0 %collective-permute-start.16 = (bf16[264,1152]{1,0:T(8,128)(2,1)S(1)}, bf16[264,1152]{1,0:T(8,128)(2,1)S(1)}, u32[]{:S(2)}, u32[]{:S(2)}) collective-permute-start(bf16[264,1152]{1,0:T(8,128)(2,1)S(1)} %image3.1.refs_7_), channel_id=1, source_target_pairs={{0,1},{1,2},{2,3},{3,0},{4,5},{5,6},{6,7},{7,4},{8,9},{9,10},{10,1... | collective-permute-start | bytes 1824776 | tf_op jit(solution)/shard_map/ppermute | solution.py:45
  55.1 3.9 %collective-permute-done.17.refs_2_ = bf16[192,1152]{1,0:T(8,128)(2,1)S(1)} collective-permute-done((bf16[192,1152]{1,0:T(8,128)(2,1)S(1)}, bf16[192,1152]{1,0:T(8,128)(2,1)S(1)}, u32[]{:S(2)}, u32[]{:S(2)}) %collective-permute-start.17) | collective-permute-done | bytes 442400 | tf_op jit(solution)/shard_map/ppermute | solution.py:51
  59.2 2.8 %collective-permute-start.22 = (bf16[128,1152]{1,0:T(8,128)(2,1)S(1)}, bf16[128,1152]{1,0:T(8,128)(2,1)S(1)}, u32[]{:S(2)}, u32[]{:S(2)}) collective-permute-start(bf16[128,1152]{1,0:T(8,128)(2,1)S(1)} %get-tuple-element.75), channel_id=1, source_target_pairs={{0,24},{1,25},{2,26},{3,27},{4,28},{5,29},{6,30},{7,31},{8,0},{9,1... | collective-permute-start | bytes 884744 | tf_op jit(solution)/shard_map/ppermute | solution.py:51
  62.0 2.7 %collective-permute-start.21 = (bf16[128,1152]{1,0:T(8,128)(2,1)S(1)}, bf16[128,1152]{1,0:T(8,128)(2,1)S(1)}, u32[]{:S(2)}, u32[]{:S(2)}) collective-permute-start(bf16[128,1152]{1,0:T(8,128)(2,1)S(1)} %get-tuple-element.67.refs_5_), channel_id=1, source_target_pairs={{0,28},{1,29},{2,30},{3,31},{4,0},{5,1},{6,2},{7,3},{8,4},{9,5},{1... | collective-permute-start | bytes 884744 | tf_op jit(solution)/shard_map/ppermute | solution.py:51
  65.5 5.6 %collective-permute-done.16.refs_4_ = bf16[264,1152]{1,0:T(8,128)(2,1)S(1)} collective-permute-done((bf16[264,1152]{1,0:T(8,128)(2,1)S(1)}, bf16[264,1152]{1,0:T(8,128)(2,1)S(1)}, u32[]{:S(2)}, u32[]{:S(2)}) %collective-permute-start.16) | collective-permute-done | bytes 608288 | tf_op jit(solution)/shard_map/ppermute | solution.py:45
  71.4 2.4 %collective-permute-start.18 = (bf16[72,1152]{1,0:T(8,128)(2,1)S(1)}, bf16[72,1152]{1,0:T(8,128)(2,1)S(1)}, u32[]{:S(2)}, u32[]{:S(2)}) collective-permute-start(bf16[72,1152]{1,0:T(8,128)(2,1)S(1)} %get-tuple-element.70), channel_id=1, source_target_pairs={{0,192},{1,193},{2,194},{3,195},{4,196},{5,197},{6,198},{7,199},{8... | collective-permute-start | bytes 497672 | tf_op jit(solution)/shard_map/ppermute | solution.py:39
  73.8 1.5 %collective-permute-start.19 = (bf16[72,1152]{1,0:T(8,128)(2,1)S(1)}, bf16[72,1152]{1,0:T(8,128)(2,1)S(1)}, u32[]{:S(2)}, u32[]{:S(2)}) collective-permute-start(bf16[72,1152]{1,0:T(8,128)(2,1)S(1)} %get-tuple-element.71), channel_id=1, source_target_pairs={{0,128},{1,129},{2,130},{3,131},{4,132},{5,133},{6,134},{7,135},{8... | collective-permute-start | bytes 497672 | tf_op jit(solution)/shard_map/ppermute | solution.py:39
  75.5 3.0 %collective-permute-done.18.refs_2_ = bf16[72,1152]{1,0:T(8,128)(2,1)S(1)} collective-permute-done((bf16[72,1152]{1,0:T(8,128)(2,1)S(1)}, bf16[72,1152]{1,0:T(8,128)(2,1)S(1)}, u32[]{:S(2)}, u32[]{:S(2)}) %collective-permute-start.18) | collective-permute-done | bytes 165920 | tf_op jit(solution)/shard_map/ppermute | solution.py:39
  78.5 2.2 %collective-permute-done.19.refs_3_ = bf16[72,1152]{1,0:T(8,128)(2,1)S(1)} collective-permute-done((bf16[72,1152]{1,0:T(8,128)(2,1)S(1)}, bf16[72,1152]{1,0:T(8,128)(2,1)S(1)}, u32[]{:S(2)}, u32[]{:S(2)}) %collective-permute-start.19) | collective-permute-done | bytes 165920 | tf_op jit(solution)/shard_map/ppermute | solution.py:39
  80.7 1.7 %collective-permute-done.20.refs_4_ = bf16[72,1152]{1,0:T(8,128)(2,1)S(1)} collective-permute-done((bf16[72,1152]{1,0:T(8,128)(2,1)S(1)}, bf16[72,1152]{1,0:T(8,128)(2,1)S(1)}, u32[]{:S(2)}, u32[]{:S(2)}) %collective-permute-start.20) | collective-permute-done | bytes 165920 | tf_op jit(solution)/shard_map/ppermute | solution.py:39
  82.4 0.9 %finish_img.1 = (f32[64,1152]{1,0:T(8,128)}, f32[1,64]{1,0:T(1,128)}) custom-call(f32[64,1152]{1,0:T(8,128)S(1)} %get-tuple-element.68.refs_0_, f32[8,256]{1,0:T(8,128)S(1)} %get-tuple-element.69.refs_1_, bf16[72,1152]{1,0:T(8,128)(2,1)S(1)} %collective-permute-done.18.refs_2_, bf16[72,1152]{1,0:T(8,128)(2,1)S(1)} %collective-permute-done.19.refs_3_, ...), custom_call_target="tpu_custom_call" | custom-call | flops 1 | bytes 1 | tf_op jit(solution)/shard_map/finish_img/pallas_call | solution.py:65
  83.3 0.9 %finish_txt.1 = f32[64,1152]{1,0:T(8,128)} custom-call(f32[128,1152]{1,0:T(8,128)S(1)} %get-tuple-element.74.refs_0_, bf16[128,1152]{1,0:T(8,128)(2,1)S(1)} %collective-permute-done.21.refs_1_, bf16[128,1152]{1,0:T(8,128)(2,1)S(1)} %collective-permute-done.22.refs_2_, bf16[64,1152]{1,0:T(8,128)(2,1)S(1)} %collective-permute-done.23.refs_3_, ...), custom_call_target="tpu_custom_call" | custom-call | flops 1 | bytes 1 | tf_op jit(solution)/shard_map/finish_txt/pallas_call | solution.py:65
  (46 shorter events, 8.8 us)
Async XLA Ops:
  1.8 12.5 %collective-permute-start.2 = (bf16[64,1152]{1,0:T(8,128)(2,1)S(1)}, bf16[64,1152]{1,0:T(8,128)(2,1)S(1)}, u32[]{:S(2)}, u32[]{:S(2)}) collective-permute-start(bf16[64,1152]{1,0:T(8,128)(2,1)S(1)} %get-tuple-element.41), channel_id=1, source_target_pairs={{0,192},{1,193},{2,194},{3,195},{4,196},{5,197},{6,198},{7,199},{8... | collective-permute-start | bytes 442376 | tf_op jit(solution)/shard_map/ppermute | solution.py:39
  4.6 9.6 %collective-permute-start.1 = (bf16[64,1152]{1,0:T(8,128)(2,1)S(1)}, bf16[64,1152]{1,0:T(8,128)(2,1)S(1)}, u32[]{:S(2)}, u32[]{:S(2)}) collective-permute-start(bf16[64,1152]{1,0:T(8,128)(2,1)S(1)} %get-tuple-element.41), channel_id=1, source_target_pairs={{0,128},{1,129},{2,130},{3,131},{4,132},{5,133},{6,134},{7,135},{8... | collective-permute-start | bytes 442376 | tf_op jit(solution)/shard_map/ppermute | solution.py:39
  5.4 8.8 %collective-permute-start = (bf16[64,1152]{1,0:T(8,128)(2,1)S(1)}, bf16[64,1152]{1,0:T(8,128)(2,1)S(1)}, u32[]{:S(2)}, u32[]{:S(2)}) collective-permute-start(bf16[64,1152]{1,0:T(8,128)(2,1)S(1)} %get-tuple-element.41), channel_id=1, source_target_pairs={{0,64},{1,65},{2,66},{3,67},{4,68},{5,69},{6,70},{7,71},{8,72},{9,... | collective-permute-start | bytes 442376 | tf_op jit(solution)/shard_map/ppermute | solution.py:39
  6.3 1.4 %collective-permute-start.6 = (bf16[64,1152]{1,0:T(8,128)(2,1)S(1)}, bf16[64,1152]{1,0:T(8,128)(2,1)S(1)}, u32[]{:S(2)}, u32[]{:S(2)}) collective-permute-start(bf16[64,1152]{1,0:T(8,128)(2,1)S(1)} %get-tuple-element.42), channel_id=1, source_target_pairs={{0,32},{1,33},{2,34},{3,35},{4,36},{5,37},{6,38},{7,39},{8,40},{9,... | collective-permute-start | bytes 442376 | tf_op jit(solution)/shard_map/ppermute | solution.py:55
  7.7 13.4 %collective-permute-start.8 = (bf16[128,1152]{1,0:T(8,128)(2,1)S(1)}, bf16[128,1152]{1,0:T(8,128)(2,1)S(1)}, u32[]{:S(2)}, u32[]{:S(2)}) collective-permute-start(bf16[128,1152]{1,0:T(8,128)(2,1)S(1)} %constant_dynamic-update-slice_fusion.4), channel_id=1, source_target_pairs={{0,8},{1,9},{2,10},{3,11},{4,12},{5,13},{6,14},{7,15},{8,16},{9,17... | collective-permute-start | bytes 884744 | tf_op jit(solution)/shard_map/ppermute | solution.py:51
  11.1 11.2 %collective-permute-start.7 = (bf16[128,1152]{1,0:T(8,128)(2,1)S(1)}, bf16[128,1152]{1,0:T(8,128)(2,1)S(1)}, u32[]{:S(2)}, u32[]{:S(2)}) collective-permute-start(bf16[128,1152]{1,0:T(8,128)(2,1)S(1)} %constant_dynamic-update-slice_fusion.4), channel_id=1, source_target_pairs={{0,4},{1,5},{2,6},{3,7},{4,8},{5,9},{6,10},{7,11},{8,12},{9,13},{1... | collective-permute-start | bytes 884744 | tf_op jit(solution)/shard_map/ppermute | solution.py:51
  14.3 14.4 %collective-permute-start.3 = (bf16[256,1152]{1,0:T(8,128)(2,1)S(1)}, bf16[256,1152]{1,0:T(8,128)(2,1)S(1)}, u32[]{:S(2)}, u32[]{:S(2)}) collective-permute-start(bf16[256,1152]{1,0:T(8,128)(2,1)S(1)} %constant_dynamic-update-slice_fusion.refs_2_), channel_id=1, source_target_pairs={{0,1},{1,2},{2,3},{3,0},{4,5},{5,6},{6,7},{7,4},{8,9},{9,10},{10,1... | collective-permute-start | bytes 1769480 | tf_op jit(solution)/shard_map/ppermute | solution.py:45
  15.9 13.2 %collective-permute-start.5 = (bf16[256,1152]{1,0:T(8,128)(2,1)S(1)}, bf16[256,1152]{1,0:T(8,128)(2,1)S(1)}, u32[]{:S(2)}, u32[]{:S(2)}) collective-permute-start(bf16[256,1152]{1,0:T(8,128)(2,1)S(1)} %constant_dynamic-update-slice_fusion.refs_2_), channel_id=1, source_target_pairs={{0,3},{1,0},{2,1},{3,2},{4,7},{5,4},{6,5},{7,6},{8,11},{9,8},{10,9... | collective-permute-start | bytes 1769480 | tf_op jit(solution)/shard_map/ppermute | solution.py:45
  17.6 15.4 %collective-permute-start.4 = (bf16[256,1152]{1,0:T(8,128)(2,1)S(1)}, bf16[256,1152]{1,0:T(8,128)(2,1)S(1)}, u32[]{:S(2)}, u32[]{:S(2)}) collective-permute-start(bf16[256,1152]{1,0:T(8,128)(2,1)S(1)} %constant_dynamic-update-slice_fusion.refs_2_), channel_id=1, source_target_pairs={{0,2},{1,3},{2,0},{3,1},{4,6},{5,7},{6,4},{7,5},{8,10},{9,11},{10,... | collective-permute-start | bytes 1769480 | tf_op jit(solution)/shard_map/ppermute | solution.py:45
  22.3 11.2 %collective-permute-start.10 = (bf16[256,1152]{1,0:T(8,128)(2,1)S(1)}, bf16[256,1152]{1,0:T(8,128)(2,1)S(1)}, u32[]{:S(2)}, u32[]{:S(2)}) collective-permute-start(bf16[256,1152]{1,0:T(8,128)(2,1)S(1)} %get-tuple-element.44.refs_3_.refs_4_), channel_id=1, source_target_pairs={{0,32},{1,33},{2,34},{3,35},{4,36},{5,37},{6,38},{7,39},{8,40},{9,... | collective-permute-start | bytes 1769480 | tf_op jit(solution)/shard_map/ppermute | solution.py:55
  22.4 15.9 %collective-permute-start.9 = (bf16[192,1152]{1,0:T(8,128)(2,1)S(1)}, bf16[192,1152]{1,0:T(8,128)(2,1)S(1)}, u32[]{:S(2)}, u32[]{:S(2)}) collective-permute-start(bf16[192,1152]{1,0:T(8,128)(2,1)S(1)} %get-tuple-element.43), channel_id=1, source_target_pairs={{0,8},{1,9},{2,10},{3,11},{4,12},{5,13},{6,14},{7,15},{8,16},{9,17... | collective-permute-start | bytes 1327112 | tf_op jit(solution)/shard_map/ppermute | solution.py:51
  38.4 1.9 %collective-permute-start.11 = (bf16[192,1152]{1,0:T(8,128)(2,1)S(1)}, bf16[192,1152]{1,0:T(8,128)(2,1)S(1)}, u32[]{:S(2)}, u32[]{:S(2)}) collective-permute-start(bf16[192,1152]{1,0:T(8,128)(2,1)S(1)} %arrived.1), channel_id=1, source_target_pairs={{0,32},{1,33},{2,34},{3,35},{4,36},{5,37},{6,38},{7,39},{8,40},{9,... | collective-permute-start | bytes 1327112 | tf_op jit(solution)/shard_map/ppermute | solution.py:55
  38.5 6.2 %collective-permute-start.13 = (bf16[256,1152]{1,0:T(8,128)(2,1)S(1)}, bf16[256,1152]{1,0:T(8,128)(2,1)S(1)}, u32[]{:S(2)}, u32[]{:S(2)}) collective-permute-start(bf16[256,1152]{1,0:T(8,128)(2,1)S(1)} %get-tuple-element.53.refs_1_), channel_id=1, source_target_pairs={{0,32},{1,33},{2,34},{3,35},{4,36},{5,37},{6,38},{7,39},{8,40},{9,... | collective-permute-start | bytes 1769480 | tf_op jit(solution)/shard_map/ppermute | solution.py:55
  43.6 1.9 %collective-permute-start.12 = (bf16[192,1152]{1,0:T(8,128)(2,1)S(1)}, bf16[192,1152]{1,0:T(8,128)(2,1)S(1)}, u32[]{:S(2)}, u32[]{:S(2)}) collective-permute-start(bf16[192,1152]{1,0:T(8,128)(2,1)S(1)} %get-tuple-element.63), channel_id=1, source_target_pairs={{0,32},{1,33},{2,34},{3,35},{4,36},{5,37},{6,38},{7,39},{8,40},{9,... | collective-permute-start | bytes 1327112 | tf_op jit(solution)/shard_map/ppermute | solution.py:55
  45.6 13.4 %collective-permute-start.17 = (bf16[192,1152]{1,0:T(8,128)(2,1)S(1)}, bf16[192,1152]{1,0:T(8,128)(2,1)S(1)}, u32[]{:S(2)}, u32[]{:S(2)}) collective-permute-start(bf16[192,1152]{1,0:T(8,128)(2,1)S(1)} %step1.1.refs_7_), channel_id=1, source_target_pairs={{0,24},{1,25},{2,26},{3,27},{4,28},{5,29},{6,30},{7,31},{8,0},{9,1... | collective-permute-start | bytes 1327112 | tf_op jit(solution)/shard_map/ppermute | solution.py:51
  48.4 17.1 %collective-permute-start.14 = (bf16[264,1152]{1,0:T(8,128)(2,1)S(1)}, bf16[264,1152]{1,0:T(8,128)(2,1)S(1)}, u32[]{:S(2)}, u32[]{:S(2)}) collective-permute-start(bf16[264,1152]{1,0:T(8,128)(2,1)S(1)} %image1.1.refs_2_), channel_id=1, source_target_pairs={{0,3},{1,0},{2,1},{3,2},{4,7},{5,4},{6,5},{7,6},{8,11},{9,8},{10,9... | collective-permute-start | bytes 1824776 | tf_op jit(solution)/shard_map/ppermute | solution.py:45
  53.1 12.4 %collective-permute-start.15 = (bf16[264,1152]{1,0:T(8,128)(2,1)S(1)}, bf16[264,1152]{1,0:T(8,128)(2,1)S(1)}, u32[]{:S(2)}, u32[]{:S(2)}) collective-permute-start(bf16[264,1152]{1,0:T(8,128)(2,1)S(1)} %image2.1.refs_7_), channel_id=1, source_target_pairs={{0,2},{1,3},{2,0},{3,1},{4,6},{5,7},{6,4},{7,5},{8,10},{9,11},{10,... | collective-permute-start | bytes 1824776 | tf_op jit(solution)/shard_map/ppermute | solution.py:45
  53.3 17.8 %collective-permute-start.16 = (bf16[264,1152]{1,0:T(8,128)(2,1)S(1)}, bf16[264,1152]{1,0:T(8,128)(2,1)S(1)}, u32[]{:S(2)}, u32[]{:S(2)}) collective-permute-start(bf16[264,1152]{1,0:T(8,128)(2,1)S(1)} %image3.1.refs_7_), channel_id=1, source_target_pairs={{0,1},{1,2},{2,3},{3,0},{4,5},{5,6},{6,7},{7,4},{8,9},{9,10},{10,1... | collective-permute-start | bytes 1824776 | tf_op jit(solution)/shard_map/ppermute | solution.py:45
  59.2 16.1 %collective-permute-start.22 = (bf16[128,1152]{1,0:T(8,128)(2,1)S(1)}, bf16[128,1152]{1,0:T(8,128)(2,1)S(1)}, u32[]{:S(2)}, u32[]{:S(2)}) collective-permute-start(bf16[128,1152]{1,0:T(8,128)(2,1)S(1)} %get-tuple-element.75), channel_id=1, source_target_pairs={{0,24},{1,25},{2,26},{3,27},{4,28},{5,29},{6,30},{7,31},{8,0},{9,1... | collective-permute-start | bytes 884744 | tf_op jit(solution)/shard_map/ppermute | solution.py:51
  62.0 13.3 %collective-permute-start.21 = (bf16[128,1152]{1,0:T(8,128)(2,1)S(1)}, bf16[128,1152]{1,0:T(8,128)(2,1)S(1)}, u32[]{:S(2)}, u32[]{:S(2)}) collective-permute-start(bf16[128,1152]{1,0:T(8,128)(2,1)S(1)} %get-tuple-element.67.refs_5_), channel_id=1, source_target_pairs={{0,28},{1,29},{2,30},{3,31},{4,0},{5,1},{6,2},{7,3},{8,4},{9,5},{1... | collective-permute-start | bytes 884744 | tf_op jit(solution)/shard_map/ppermute | solution.py:51
  71.4 11.1 %copy-start = (bf16[64,1152]{1,0:T(8,128)(2,1)S(1)}, bf16[64,1152]{1,0:T(8,128)(2,1)}, u32[]{:S(2)}) copy-start(bf16[64,1152]{1,0:T(8,128)(2,1)} %refs_5_.1) | copy-start | bytes 442372
  71.4 7.1 %collective-permute-start.18 = (bf16[72,1152]{1,0:T(8,128)(2,1)S(1)}, bf16[72,1152]{1,0:T(8,128)(2,1)S(1)}, u32[]{:S(2)}, u32[]{:S(2)}) collective-permute-start(bf16[72,1152]{1,0:T(8,128)(2,1)S(1)} %get-tuple-element.70), channel_id=1, source_target_pairs={{0,192},{1,193},{2,194},{3,195},{4,196},{5,197},{6,198},{7,199},{8... | collective-permute-start | bytes 497672 | tf_op jit(solution)/shard_map/ppermute | solution.py:39
  73.8 6.9 %collective-permute-start.19 = (bf16[72,1152]{1,0:T(8,128)(2,1)S(1)}, bf16[72,1152]{1,0:T(8,128)(2,1)S(1)}, u32[]{:S(2)}, u32[]{:S(2)}) collective-permute-start(bf16[72,1152]{1,0:T(8,128)(2,1)S(1)} %get-tuple-element.71), channel_id=1, source_target_pairs={{0,128},{1,129},{2,130},{3,131},{4,132},{5,133},{6,134},{7,135},{8... | collective-permute-start | bytes 497672 | tf_op jit(solution)/shard_map/ppermute | solution.py:39
  75.3 7.1 %collective-permute-start.20 = (bf16[72,1152]{1,0:T(8,128)(2,1)S(1)}, bf16[72,1152]{1,0:T(8,128)(2,1)S(1)}, u32[]{:S(2)}, u32[]{:S(2)}) collective-permute-start(bf16[72,1152]{1,0:T(8,128)(2,1)S(1)} %get-tuple-element.72.refs_3_), channel_id=1, source_target_pairs={{0,64},{1,65},{2,66},{3,67},{4,68},{5,69},{6,70},{7,71},{8,72},{9,... | collective-permute-start | bytes 497672 | tf_op jit(solution)/shard_map/ppermute | solution.py:39
  75.3 8.0 %copy-start.1 = (bf16[64,1152]{1,0:T(8,128)(2,1)S(1)}, bf16[64,1152]{1,0:T(8,128)(2,1)}, u32[]{:S(2)}) copy-start(bf16[64,1152]{1,0:T(8,128)(2,1)} %refs_4_.1) | copy-start | bytes 442372
  75.4 7.9 %collective-permute-start.23 = (bf16[64,1152]{1,0:T(8,128)(2,1)S(1)}, bf16[64,1152]{1,0:T(8,128)(2,1)S(1)}, u32[]{:S(2)}, u32[]{:S(2)}) collective-permute-start(bf16[64,1152]{1,0:T(8,128)(2,1)S(1)} %step3.1.refs_7_), channel_id=1, source_target_pairs={{0,32},{1,33},{2,34},{3,35},{4,36},{5,37},{6,38},{7,39},{8,40},{9,... | collective-permute-start | bytes 442376 | tf_op jit(solution)/shard_map/ppermute | solution.py:55

commit v4 on v3

--- a/solution.py
+++ b/solution.py
@@ -151,43 +151,41 @@
     return total
 
 
-def far_body(scale_ref, bias_ref, i0, i1, i2, i3, txt_ref, near_loss, c0, c1, c2, c3, keep, send, pair, loss):
+def far_body(scale_ref, bias_ref, i0, i1, i2, i3, txt_ref, near_loss, c0, c1, c2, c3, keep, send, loss):
     scale, bias = scale_ref[0], bias_ref[0]
     imgs, coeffs = (i0, i1, i2, i3), (c0, c1, c2, c3)
     for k in range(4):
         total = near_loss[256 * k : 256 * (k + 1), :]
-        for n in range(2):
-            at = slice(256 * n, 256 * (n + 1))
-            match = None
-            if k == 0 and n == 1:
-                r = lax.broadcasted_iota(jnp.int32, (256, 256), 0)
-                c = lax.broadcasted_iota(jnp.int32, (256, 256), 1)
-                match = (r + 128 == c) & (r < U)
-            weight, softplus = entry(imgs[k][...], txt_ref[at, :], scale, bias, match)
-            coeffs[k][:, at] = weight
+        for lo, hi in ((0, 256), (256, 384)):
+            weight, softplus = entry(imgs[k][...], txt_ref[lo:hi, :], scale, bias)
+            coeffs[k][:, lo:hi] = weight
             total = total + fold(softplus)
         column = jnp.broadcast_to(jnp.sum(total, axis=1, keepdims=True), (256, 128))
         loss[:, 256 * k : 256 * (k + 1)] = jnp.transpose(column)[:8, :]
-    g = texts(coeffs, imgs, 0, 256)
+    g = texts(coeffs, imgs, 0, 384)
     keep[...] = g[:192, :]
-    send[:64, :] = g[192:, :].astype(BF16)
-    g = texts(coeffs, imgs, 256, 512)
-    send[64:, :] = g[:128, :].astype(BF16)
-    pair[...] = g[128:, :]
-
-
-def other_body(scale_ref, bias_ref, i0, i1, i2, i3, c0, c1, c2, c3, txt_ref, l0, l1, l2, l3, o0, o1, o2, o3, keep, send, loss):
+    send[...] = g[192:, :].astype(BF16)
+
+
+def other_body(scale_ref, bias_ref, i0, i1, i2, i3, c0, c1, c2, c3, txt_ref, l0, l1, l2, l3, o0, o1, o2, o3, keep, send, pair, loss):
+    scale, bias = scale_ref[0], bias_ref[0]
     imgs, sums, mine, other = (i0, i1, i2, i3), (l0, l1, l2, l3), (c0, c1, c2, c3), (o0, o1, o2, o3)
     for k in range(4):
-        weight, softplus = entry(imgs[k][...], txt_ref[...], scale_ref[0], bias_ref[0])
-        other[k][...] = weight
-        loss[256 * k : 256 * (k + 1), :] = sums[k][...] + fold(softplus)
-    send[...] = texts(other, imgs, 0, 256).astype(BF16)
+        total = sums[k][...]
+        for lo, hi in ((0, 256), (256, 384)):
+            match = None
+            if k == 0 and lo == 256:
+                r = lax.broadcasted_iota(jnp.int32, (256, 128), 0)
+                c = lax.broadcasted_iota(jnp.int32, (256, 128), 1)
+                match = (r == c) & (r < U)
+            weight, softplus = entry(imgs[k][...], txt_ref[lo:hi, :], scale, bias, match)
+            other[k][:, lo:hi] = weight
+            total = total + fold(softplus)
+        loss[256 * k : 256 * (k + 1), :] = total
+    g = texts(other, imgs, 0, 384)
+    send[...] = g[:256, :].astype(BF16)
+    pair[...] = g[256:, :]
     keep[...] = texts(mine, imgs, 0, 256)
-
-
-def copy_body(src, dst):
-    dst[...] = src[...]
 
 
 def image_body(k, cf, cm, co, far, mine, other, loss, out):
@@ -217,25 +215,31 @@
             out[U:, :256] = marks
 
 
-def pack_body(b1, b2, far, near):
-    far[:U, :] = b2[:U, :]
-    far[U:, :] = b1[...]
-    near[:128, :] = b2[...]
-    near[128:, :] = b1[...]
-
-
-def step1_body(keep, got, out):
-    out[...] = (keep[...] + got[...].astype(F32)).astype(BF16)
-
-
-def step2_body(keep, got, w, two, one):
-    two[:64, :] = (keep[:64, :] + (up(got, 0, 64) + up(w, 0, 64))).astype(BF16)
-    two[64:, :] = (keep[64:128, :] + up(got, 64, 128)).astype(BF16)
-    one[...] = (keep[128:, :] + (up(got, 128, 256) + up(w, 64, 192))).astype(BF16)
-
-
-def step3_body(pair, v1, v2, out):
-    out[...] = (pair[64:, :] + (up(v1, 64, 128) + up(v2, 64, 128))).astype(BF16)
+def pack_body(*refs):
+    out, at = refs[-1], 0
+    for ref in refs[:-1]:
+        n = min(ref.shape[0], out.shape[0] - at)
+        out[at : at + n, :] = ref[:n, :]
+        at += n
+
+
+def step1_body(keep, got, two, one):
+    two[...] = (keep[:64, :] + up(got, 0, 64)).astype(BF16)
+    one[...] = (keep[64:, :] + up(got, 64, 192)).astype(BF16)
+
+
+def step2_body(keep, got, v2, v1, out):
+    total = keep[:128, :] + (up(got, 0, 128) + up(v1, 0, 128))
+    out[:64, :] = (total[:64, :] + up(v2, 0, 64)).astype(BF16)
+    out[64:, :] = total[64:, :].astype(BF16)
+
+
+def step3_body(keep, got, w, out):
+    out[...] = (keep[128:, :] + (up(got, 128, 256) + up(w, 0, 128))).astype(BF16)
+
+
+def step4_body(pair, w, out):
+    out[...] = (pair[64:, :] + up(w, 64, 128)).astype(BF16)
 
 
 def back_norm(g, raw, inv):
@@ -243,7 +247,8 @@
     return inv[...] * (g - unit * jnp.sum(unit * g, axis=-1, keepdims=True))
 
 
-def finish_img_body(g_ref, l_ref, r1, r2, r3, raw, inv, out_ref, loss_ref):
+def finish_img_body(g_ref, l_ref, r1, r2, r3, raw, inv, out_ref, loss_ref, done_ref):
+    done_ref[...] = l_ref[:, :128]
     g = g_ref[...] + (up(r1, 0, U) + up(r2, 0, U) + up(r3, 0, U))
     out_ref[...] = back_norm(g, raw, inv)
     loss = l_ref[:1, :U]
@@ -252,8 +257,8 @@
     loss_ref[...] = loss
 
 
-def finish_txt_body(pair, v1, v2, got, raw, inv, out_ref):
-    g = pair[:64, :] + (up(v1, 0, 64) + up(v2, 0, 64) + got[...].astype(F32))
+def finish_txt_body(pair, w, got, raw, inv, out_ref):
+    g = pair[:64, :] + (up(w, 0, 64) + got[...].astype(F32))
     out_ref[...] = back_norm(g, raw, inv)
 
 
@@ -266,38 +271,44 @@
         scratch=[pltpu.VMEM((2, rows, d), BF16), pltpu.SemaphoreType.DMA((2,))],
     )
 
-    pair = jnp.concatenate([txt, swap(txt)], axis=0)
+    def pack(name, n, parts, after=()):
+        return call(name, pack_body, [shape(n, d)], parts, (), after)[0]
+
+    pair = pack("pair", 128, (txt, swap(txt)))
+    b1 = ring(pair, 1)
     f1, f3, f2 = first(img, 1), first(img, 3), first(img, 2)
-    b1, b2 = ring(pair, 1), ring(pair, 2)
-    group = jnp.concatenate([img, f1, f2, f3], axis=0)
+    group = pack("group", 256, (img, f1, f2, f3))
     g1, g3, g2 = second(group, 1), second(group, 3), second(group, 2)
     groups = (group, g1, g2, g3)
-    far_pack, near_mine = call(
-        "pack", pack_body, [shape(192, d), shape(256, d)], (b1, b2), (), (group,)
-    )
-    far_got = ring(far_pack, 2)
-    near_other = swap(near_mine)
+    b1 = pack("behind1", 128, (b1,), (group,))
+    b2, a1 = ring(b1, 1), swap(b1)
+    b2 = pack("behind2", 128, (b2,), (a1,))
+    b3, a2 = ring(b2, 1), swap(b2)
+    far_first = pack("far_first", 64, (b3,), (a2,))
+    b4 = ring(far_first, 1)
+    near_mine = pack("near_mine", 256, (b2, b1), (far_first,))
+    other = pack("other_texts", 384, (a2, a1, pair), (near_mine,))
 
     sc = (scale, bias)
-    mine_c, mine_l, last = [None] * 4, [None] * 4, ()
+    mine_c, mine_l, last = [None] * 4, [None] * 4, (other,)
     for k in (0, 1, 3, 2):
         mine_c[k], mine_l[k] = call(
             f"mine{k}", mine_body, [shape(256, 256), shape(256, 128, dtype=F32)],
             (groups[k], near_mine), sc, last,
         )
         last = (mine_l[k],)
-    *other_c, keep_b, send_b, near_loss = call(
+    *other_c, keep_b, send_b, own_pair, near_loss = call(
         "other", other_body,
-        [shape(256, 256)] * 4 + [shape(256, d, dtype=F32), shape(256, d), shape(1024, 128, dtype=F32)],
-        (*groups, *mine_c, near_other, *mine_l), sc, last,
+        [shape(256, 384)] * 4
+        + [shape(256, d, dtype=F32), shape(256, d), shape(128, d, dtype=F32), shape(1024, 128, dtype=F32)],
+        (*groups, *mine_c, other, *mine_l), sc, last,
     )
     got_b = swap(send_b)
-    far_mine = call("arrived", copy_body, [shape(192, d)], (far_got,), (), (send_b,))[0]
-    far = jnp.concatenate([far_mine, swap(far_mine), pair], axis=0)
-    *far_c, keep_a, send_a, own_pair, loss = call(
+    far_mine = pack("far_mine", 192, (b4, b3), (send_b,))
+    far = pack("far_texts", 384, (far_mine, swap(far_mine)))
+    *far_c, keep_a, send_a, loss = call(
         "far", far_body,
-        [shape(256, 512)] * 4
-        + [shape(192, d, dtype=F32), shape(192, d), shape(128, d, dtype=F32), shape(8, 1024, dtype=F32)],
+        [shape(256, 384)] * 4 + [shape(192, d, dtype=F32), shape(192, d), shape(8, 1024, dtype=F32)],
         (*groups, far, near_loss), sc,
     )
     got_a = swap(send_a)
@@ -306,36 +317,38 @@
         out = shape(256, d, dtype=F32) if k == 0 else shape(264, d)
         return call(
             f"image{k}", functools.partial(image_body, k), [out],
-            (far_c[k], mine_c[k], other_c[k], far, near_mine, near_other, loss), (), after,
+            (far_c[k], mine_c[k], other_c[k], far, near_mine, other, loss), (), after,
         )[0]
 
     p1 = image(1, ())
     r1 = second(p1, -1)
-    z1 = call("step1", step1_body, [shape(192, d)], (keep_a, got_a), (), (p1, got_b))[0]
-    w = ring(z1, -2)
-    p3 = image(3, (z1,))
+    two, one = call("step1", step1_body, [shape(64, d), shape(128, d)], (keep_a, got_a), (), (p1, got_b))
+    v2, v1 = ring(two, -2), ring(one, -1)
+    p3 = image(3, (one,))
     r3 = second(p3, -3)
     p2 = image(2, (p3,))
     r2 = second(p2, -2)
     p0 = image(0, (p2,))
-    two, one = call("step2", step2_body, [shape(128, d)] * 2, (keep_b, got_b, w), (), (p0,))
-    v1, v2 = ring(one, -1), ring(two, -2)
+    z2 = call("step2", step2_body, [shape(128, d)], (keep_b, got_b, v2, v1), (), (p0,))[0]
+    w2 = ring(z2, -1)
     own_img, own_loss, m1, m2, m3 = call(
         "merge_img", merge_img_body,
         [shape(rows, d, dtype=F32), shape(8, 256, dtype=F32)] + [shape(rows + 8, d)] * 3,
-        (p0, loss, r1, r2, r3), (), (one,),
+        (p0, loss, r1, r2, r3), (), (z2,),
     )
     q1, q3, q2 = first(m1, -1), first(m3, -3), first(m2, -2)
-    z3 = call("step3", step3_body, [shape(64, d)], (own_pair, v1, v2), (), (m3,))[0]
-    got_c = swap(z3)
-    grad_img, loss_out = call(
+    z3 = call("step3", step3_body, [shape(128, d)], (keep_b, got_b, w2), (), (m3,))[0]
+    w3 = ring(z3, -1)
+    grad_img, loss_out, done = call(
         "finish_img", finish_img_body,
-        [shape(rows, d, dtype=F32), shape(1, rows, dtype=F32)],
+        [shape(rows, d, dtype=F32), shape(1, rows, dtype=F32), shape(8, 128, dtype=F32)],
         (own_img, own_loss, q1, q2, q3, picture, img_inv), (), (z3,),
     )
+    z4 = call("step4", step4_body, [shape(64, d)], (own_pair, w3), (), (done,))[0]
+    got_c = swap(z4)
     grad_txt = call(
         "finish_txt", finish_txt_body, [shape(rows, d, dtype=F32)],
-        (own_pair, v1, v2, got_c, caption, txt_inv),
+        (own_pair, w3, got_c, caption, txt_inv),
     )[0]
     return grad_img, grad_txt, loss_out.reshape(rows)
 

time: 84.4 us -> 90.6 us (1.073)
  the two profiles are of different devices: /device:TPU:32 before, /device:TPU:1 now
where the time goes in v4:
time: 90.6 us; the launch traced here: 90.5 us
  waiting for transfers between devices  36.7 us (41%)
  starting transfers between devices  35.9 us (40%)
  Pallas kernels  15.7 us (17%)
  between operations  2.18 us (2%)
    pallas_call x27, Pallas kernels, call(): pl.pallas_call(kernel, out_shape=outs, in_specs=[SMEM] * len(scalars) + (...  15.7 us
    ppermute x8, waiting for transfers between devices, ring(): lax.ppermute(a, AXES, permutation(lambda x, c, z, y: (x, c, z - s if c el...  15.5 us
    ppermute x6, waiting for transfers between devices, first(): lax.ppermute(a, AXES, permutation(lambda x, c, z, y: (x, c, z, y + s) if...  12.5 us
    ppermute x7, starting transfers between devices, swap(): lax.ppermute(a, AXES, permutation(lambda x, c, z, y: (x, 1 - c, z, y)))  12.2 us
    ppermute x8, starting transfers between devices, ring(): lax.ppermute(a, AXES, permutation(lambda x, c, z, y: (x, c, z - s if c el...  10.4 us
    ppermute x6, starting transfers between devices, second(): lax.ppermute(a, AXES, permutation(lambda x, c, z, y: (x + s, c, z, y) if...  7.16 us
    ppermute x6, starting transfers between devices, first(): lax.ppermute(a, AXES, permutation(lambda x, c, z, y: (x, c, z, y + s) if...  6.17 us
    ppermute x6, waiting for transfers between devices, second(): lax.ppermute(a, AXES, permutation(lambda x, c, z, y: (x + s, c, z, y) if...  4.5 us
  transfers between devices with their start and end apart: 27, of which 15 were waited for; matrix products, arithmetic and copies ran while one was open for 0% of the time, Pallas kernels for 15%

profile of v4, /device:TPU:1, one launch (start us, length us, event | category | flops | bytes accessed | tf_op | source)
XLA Modules:
  0.0 90.5 jit_solution(5269633684508416924)
XLA Ops:
  0.6 1.2 %normalize.1 = (bf16[64,1152]{1,0:T(8,128)(2,1)S(1)}, bf16[64,1152]{1,0:T(8,128)(2,1)S(1)}, f32[64,1]{1,0:T(8,128)S(1)}, f32[64,1]{1,0:T(8,128)S(1)}) custom-call(bf16[64,1152]{1,0:T(8,128)(2,1)} %refs_5_.1, bf16[64,1152]{1,0:T(8,128)(2,1)} %refs_3_.1), custom_call_target="tpu_custom_call" | custom-call | flops 1 | bytes 1 | tf_op jit(solution)/shard_map/normalize/pallas_call | solution.py:65
  1.8 3.3 %collective-permute-start.6 = (bf16[64,1152]{1,0:T(8,128)(2,1)S(1)}, bf16[64,1152]{1,0:T(8,128)(2,1)S(1)}, u32[]{:S(2)}, u32[]{:S(2)}) collective-permute-start(bf16[64,1152]{1,0:T(8,128)(2,1)S(1)} %get-tuple-element.41.refs_0_), channel_id=1, source_target_pairs={{0,32},{1,33},{2,34},{3,35},{4,36},{5,37},{6,38},{7,39},{8,40},{9,... | collective-permute-start | bytes 442376 | tf_op jit(solution)/shard_map/ppermute | solution.py:55
  5.1 1.0 %collective-permute-done.6.refs_1_ = bf16[64,1152]{1,0:T(8,128)(2,1)S(1)} collective-permute-done((bf16[64,1152]{1,0:T(8,128)(2,1)S(1)}, bf16[64,1152]{1,0:T(8,128)(2,1)S(1)}, u32[]{:S(2)}, u32[]{:S(2)}) %collective-permute-start.6) | collective-permute-done | bytes 147488 | tf_op jit(solution)/shard_map/ppermute | solution.py:55
  6.2 3.9 %collective-permute-start.7 = (bf16[128,1152]{1,0:T(8,128)(2,1)S(1)}, bf16[128,1152]{1,0:T(8,128)(2,1)S(1)}, u32[]{:S(2)}, u32[]{:S(2)}) collective-permute-start(bf16[128,1152]{1,0:T(8,128)(2,1)S(1)} %pair.1.refs_2_), channel_id=1, source_target_pairs={{0,4},{1,5},{2,6},{3,7},{4,8},{5,9},{6,10},{7,11},{8,12},{9,13},{1... | collective-permute-start | bytes 884744 | tf_op jit(solution)/shard_map/ppermute | solution.py:51
  10.1 2.7 %collective-permute-start.2 = (bf16[64,1152]{1,0:T(8,128)(2,1)S(1)}, bf16[64,1152]{1,0:T(8,128)(2,1)S(1)}, u32[]{:S(2)}, u32[]{:S(2)}) collective-permute-start(bf16[64,1152]{1,0:T(8,128)(2,1)S(1)} %get-tuple-element.40.refs_0_), channel_id=1, source_target_pairs={{0,192},{1,193},{2,194},{3,195},{4,196},{5,197},{6,198},{7,199},{8... | collective-permute-start | bytes 442376 | tf_op jit(solution)/shard_map/ppermute | solution.py:39
  13.9 2.6 %collective-permute-done.2.refs_3_ = bf16[64,1152]{1,0:T(8,128)(2,1)S(1)} collective-permute-done((bf16[64,1152]{1,0:T(8,128)(2,1)S(1)}, bf16[64,1152]{1,0:T(8,128)(2,1)S(1)}, u32[]{:S(2)}, u32[]{:S(2)}) %collective-permute-start.2) | collective-permute-done | bytes 147488 | tf_op jit(solution)/shard_map/ppermute | solution.py:39
  16.5 1.9 %collective-permute-done.1.refs_2_ = bf16[64,1152]{1,0:T(8,128)(2,1)S(1)} collective-permute-done((bf16[64,1152]{1,0:T(8,128)(2,1)S(1)}, bf16[64,1152]{1,0:T(8,128)(2,1)S(1)}, u32[]{:S(2)}, u32[]{:S(2)}) %collective-permute-start.1) | collective-permute-done | bytes 147488 | tf_op jit(solution)/shard_map/ppermute | solution.py:39
  18.4 1.5 %collective-permute-done.refs_1_ = bf16[64,1152]{1,0:T(8,128)(2,1)S(1)} collective-permute-done((bf16[64,1152]{1,0:T(8,128)(2,1)S(1)}, bf16[64,1152]{1,0:T(8,128)(2,1)S(1)}, u32[]{:S(2)}, u32[]{:S(2)}) %collective-permute-start) | collective-permute-done | bytes 147488 | tf_op jit(solution)/shard_map/ppermute | solution.py:39
  20.1 1.6 %collective-permute-start.8 = (bf16[128,1152]{1,0:T(8,128)(2,1)S(1)}, bf16[128,1152]{1,0:T(8,128)(2,1)S(1)}, u32[]{:S(2)}, u32[]{:S(2)}) collective-permute-start(bf16[128,1152]{1,0:T(8,128)(2,1)S(1)} %behind1.1.refs_1_), channel_id=1, source_target_pairs={{0,4},{1,5},{2,6},{3,7},{4,8},{5,9},{6,10},{7,11},{8,12},{9,13},{1... | collective-permute-start | bytes 884744 | tf_op jit(solution)/shard_map/ppermute | solution.py:51
  22.1 2.3 %collective-permute-start.5 = (bf16[256,1152]{1,0:T(8,128)(2,1)S(1)}, bf16[256,1152]{1,0:T(8,128)(2,1)S(1)}, u32[]{:S(2)}, u32[]{:S(2)}) collective-permute-start(bf16[256,1152]{1,0:T(8,128)(2,1)S(1)} %group.1.refs_1_.refs_2_), channel_id=1, source_target_pairs={{0,3},{1,0},{2,1},{3,2},{4,7},{5,4},{6,5},{7,6},{8,11},{9,8},{10,9... | collective-permute-start | bytes 1769480 | tf_op jit(solution)/shard_map/ppermute | solution.py:45
  25.1 0.9 %collective-permute-done.8.refs_0_ = bf16[128,1152]{1,0:T(8,128)(2,1)S(1)} collective-permute-done((bf16[128,1152]{1,0:T(8,128)(2,1)S(1)}, bf16[128,1152]{1,0:T(8,128)(2,1)S(1)}, u32[]{:S(2)}, u32[]{:S(2)}) %collective-permute-start.8) | collective-permute-done | bytes 294944 | tf_op jit(solution)/shard_map/ppermute | solution.py:51
  26.1 2.6 %collective-permute-start.11 = (bf16[128,1152]{1,0:T(8,128)(2,1)S(1)}, bf16[128,1152]{1,0:T(8,128)(2,1)S(1)}, u32[]{:S(2)}, u32[]{:S(2)}) collective-permute-start(bf16[128,1152]{1,0:T(8,128)(2,1)S(1)} %behind2.1.refs_0_), channel_id=1, source_target_pairs={{0,32},{1,33},{2,34},{3,35},{4,36},{5,37},{6,38},{7,39},{8,40},{9,... | collective-permute-start | bytes 884744 | tf_op jit(solution)/shard_map/ppermute | solution.py:55
  29.8 4.7 %collective-permute-done.10.refs_0_.refs_1_ = bf16[128,1152]{1,0:T(8,128)(2,1)S(1)} collective-permute-done((bf16[128,1152]{1,0:T(8,128)(2,1)S(1)}, bf16[128,1152]{1,0:T(8,128)(2,1)S(1)}, u32[]{:S(2)}, u32[]{:S(2)}) %collective-permute-start.10) | collective-permute-done | bytes 294944 | tf_op jit(solution)/shard_map/ppermute | solution.py:51
  34.5 1.8 %collective-permute-start.12 = (bf16[64,1152]{1,0:T(8,128)(2,1)S(1)}, bf16[64,1152]{1,0:T(8,128)(2,1)S(1)}, u32[]{:S(2)}, u32[]{:S(2)}) collective-permute-start(bf16[64,1152]{1,0:T(8,128)(2,1)S(1)} %far_first.1.refs_2_), channel_id=1, source_target_pairs={{0,4},{1,5},{2,6},{3,7},{4,8},{5,9},{6,10},{7,11},{8,12},{9,13},{1... | collective-permute-start | bytes 442376 | tf_op jit(solution)/shard_map/ppermute | solution.py:51
  39.7 3.4 %other.1 = (bf16[256,384]{1,0:T(8,128)(2,1)S(1)}, bf16[256,384]{1,0:T(8,128)(2,1)S(1)}, bf16[256,384]{1,0:T(8,128)(2,1)S(1)}, bf16[256,384]{1,0:T(8,128)(2,1)S(1...) custom-call(f32[1]{0:T(128)S(6)} %copy.7.refs_0_, ...), custom_call_target="tpu_custom_call" | custom-call | flops 1 | bytes 1 | tf_op jit(solution)/shard_map/other/pallas_call | solution.py:65
  43.9 1.3 %collective-permute-done.13.refs_1_ = bf16[192,1152]{1,0:T(8,128)(2,1)S(1)} collective-permute-done((bf16[192,1152]{1,0:T(8,128)(2,1)S(1)}, bf16[192,1152]{1,0:T(8,128)(2,1)S(1)}, u32[]{:S(2)}, u32[]{:S(2)}) %collective-permute-start.13) | collective-permute-done | bytes 442400 | tf_op jit(solution)/shard_map/ppermute | solution.py:55
  45.3 2.7 %far.1 = (bf16[256,384]{1,0:T(8,128)(2,1)S(1)}, bf16[256,384]{1,0:T(8,128)(2,1)S(1)}, bf16[256,384]{1,0:T(8,128)(2,1)S(1)}, bf16[256,384]{1,0:T(8,128)(2,1)S(1)}...) custom-call(f32[1]{0:T(128)S(6)} %copy.7.refs_0_, f32[1]{0:T(128)S(6)} %copy.8.refs_1_, ...), custom_call_target="tpu_custom_call" | custom-call | flops 1 | bytes 1 | tf_op jit(solution)/shard_map/far/pallas_call | solution.py:65
  48.4 1.0 %image1.1.refs_2_ = bf16[264,1152]{1,0:T(8,128)(2,1)S(1)} custom-call(bf16[256,384]{1,0:T(8,128)(2,1)S(1)} %get-tuple-element.61.refs_0_, bf16[256,256]{1,0:T(8,128)(2,1)S(1)} %get-tuple-element.44.refs_7_.refs_1_, bf16[256,384]{1,0:T(8,128)(2,1)S(1)} %get-tuple-element.62.refs_2_, bf16[384,1152]{1,0:T(8,128)(2,1)S(1)} %far_texts.1.refs_6_.refs_3_, ...), custom_call_target="tpu_custom_call" | custom-call | flops 1 | bytes 1 | tf_op jit(solution)/shard_map/image1/pallas_call | solution.py:65
  49.4 2.5 %collective-permute-start.16 = (bf16[264,1152]{1,0:T(8,128)(2,1)S(1)}, bf16[264,1152]{1,0:T(8,128)(2,1)S(1)}, u32[]{:S(2)}, u32[]{:S(2)}) collective-permute-start(bf16[264,1152]{1,0:T(8,128)(2,1)S(1)} %image1.1.refs_2_), channel_id=1, source_target_pairs={{0,3},{1,0},{2,1},{3,2},{4,7},{5,4},{6,5},{7,6},{8,11},{9,8},{10,9... | collective-permute-start | bytes 1824776 | tf_op jit(solution)/shard_map/ppermute | solution.py:45
  52.0 1.0 %image3.1.refs_7_ = bf16[264,1152]{1,0:T(8,128)(2,1)S(1)} custom-call(bf16[256,384]{1,0:T(8,128)(2,1)S(1)} %get-tuple-element.57.refs_0_, bf16[256,256]{1,0:T(8,128)(2,1)S(1)} %get-tuple-element.48.refs_9_.refs_1_, bf16[256,384]{1,0:T(8,128)(2,1)S(1)} %get-tuple-element.58.refs_2_, bf16[384,1152]{1,0:T(8,128)(2,1)S(1)} %far_texts.1.refs_6_.refs_3_, ...), custom_call_target="tpu_custom_call" | custom-call | flops 1 | bytes 1 | tf_op jit(solution)/shard_map/image3/pallas_call | solution.py:65
  53.0 1.0 %image2.1.refs_7_ = bf16[264,1152]{1,0:T(8,128)(2,1)S(1)} custom-call(bf16[256,384]{1,0:T(8,128)(2,1)S(1)} %get-tuple-element.55.refs_0_, bf16[256,256]{1,0:T(8,128)(2,1)S(1)} %get-tuple-element.47.refs_8_.refs_1_, bf16[256,384]{1,0:T(8,128)(2,1)S(1)} %get-tuple-element.56.refs_2_, bf16[384,1152]{1,0:T(8,128)(2,1)S(1)} %far_texts.1.refs_6_.refs_3_, ...), custom_call_target="tpu_custom_call" | custom-call | flops 1 | bytes 1 | tf_op jit(solution)/shard_map/image2/pallas_call | solution.py:65
  55.2 2.5 %collective-permute-start.19 = (bf16[64,1152]{1,0:T(8,128)(2,1)S(1)}, bf16[64,1152]{1,0:T(8,128)(2,1)S(1)}, u32[]{:S(2)}, u32[]{:S(2)}) collective-permute-start(bf16[64,1152]{1,0:T(8,128)(2,1)S(1)} %get-tuple-element.65), channel_id=1, source_target_pairs={{0,24},{1,25},{2,26},{3,27},{4,28},{5,29},{6,30},{7,31},{8,0},{9,1... | collective-permute-start | bytes 442376 | tf_op jit(solution)/shard_map/ppermute | solution.py:51
  57.7 1.0 %image0.1.refs_4_.refs_0_ = f32[256,1152]{1,0:T(8,128)S(1)} custom-call(bf16[256,384]{1,0:T(8,128)(2,1)S(1)} %get-tuple-element.52.refs_0_, bf16[256,256]{1,0:T(8,128)(2,1)S(1)} %get-tuple-element.42.refs_6_.refs_1_, bf16[256,384]{1,0:T(8,128)(2,1)S(1)} %get-tuple-element.53.refs_2_, bf16[384,1152]{1,0:T(8,128)(2,1)S(1)} %far_texts.1.refs_6_.refs_3_, ...), custom_call_target="tpu_custom_call" | custom-call | flops 1 | bytes 1 | tf_op jit(solution)/shard_map/image0/pallas_call | solution.py:65
  58.7 7.9 %collective-permute-done.19.refs_2_ = bf16[64,1152]{1,0:T(8,128)(2,1)S(1)} collective-permute-done((bf16[64,1152]{1,0:T(8,128)(2,1)S(1)}, bf16[64,1152]{1,0:T(8,128)(2,1)S(1)}, u32[]{:S(2)}, u32[]{:S(2)}) %collective-permute-start.19) | collective-permute-done | bytes 147488 | tf_op jit(solution)/shard_map/ppermute | solution.py:51
  66.8 4.5 %collective-permute-done.18.refs_4_ = bf16[264,1152]{1,0:T(8,128)(2,1)S(1)} collective-permute-done((bf16[264,1152]{1,0:T(8,128)(2,1)S(1)}, bf16[264,1152]{1,0:T(8,128)(2,1)S(1)}, u32[]{:S(2)}, u32[]{:S(2)}) %collective-permute-start.18) | collective-permute-done | bytes 608288 | tf_op jit(solution)/shard_map/ppermute | solution.py:45
  71.6 2.0 %collective-permute-done.24.refs_2_ = bf16[128,1152]{1,0:T(8,128)(2,1)S(1)} collective-permute-done((bf16[128,1152]{1,0:T(8,128)(2,1)S(1)}, bf16[128,1152]{1,0:T(8,128)(2,1)S(1)}, u32[]{:S(2)}, u32[]{:S(2)}) %collective-permute-start.24) | collective-permute-done | bytes 294944 | tf_op jit(solution)/shard_map/ppermute | solution.py:51
  73.8 1.7 %collective-permute-start.21 = (bf16[72,1152]{1,0:T(8,128)(2,1)S(1)}, bf16[72,1152]{1,0:T(8,128)(2,1)S(1)}, u32[]{:S(2)}, u32[]{:S(2)}) collective-permute-start(bf16[72,1152]{1,0:T(8,128)(2,1)S(1)} %get-tuple-element.68), channel_id=1, source_target_pairs={{0,192},{1,193},{2,194},{3,195},{4,196},{5,197},{6,198},{7,199},{8... | collective-permute-start | bytes 497672 | tf_op jit(solution)/shard_map/ppermute | solution.py:39
  76.2 3.4 %collective-permute-done.21.refs_2_ = bf16[72,1152]{1,0:T(8,128)(2,1)S(1)} collective-permute-done((bf16[72,1152]{1,0:T(8,128)(2,1)S(1)}, bf16[72,1152]{1,0:T(8,128)(2,1)S(1)}, u32[]{:S(2)}, u32[]{:S(2)}) %collective-permute-start.21) | collective-permute-done | bytes 165920 | tf_op jit(solution)/shard_map/ppermute | solution.py:39
  79.6 1.7 %collective-permute-done.22.refs_3_ = bf16[72,1152]{1,0:T(8,128)(2,1)S(1)} collective-permute-done((bf16[72,1152]{1,0:T(8,128)(2,1)S(1)}, bf16[72,1152]{1,0:T(8,128)(2,1)S(1)}, u32[]{:S(2)}, u32[]{:S(2)}) %collective-permute-start.22) | collective-permute-done | bytes 165920 | tf_op jit(solution)/shard_map/ppermute | solution.py:39
  81.3 1.4 %collective-permute-done.23.refs_4_ = bf16[72,1152]{1,0:T(8,128)(2,1)S(1)} collective-permute-done((bf16[72,1152]{1,0:T(8,128)(2,1)S(1)}, bf16[72,1152]{1,0:T(8,128)(2,1)S(1)}, u32[]{:S(2)}, u32[]{:S(2)}) %collective-permute-start.23) | collective-permute-done | bytes 165920 | tf_op jit(solution)/shard_map/ppermute | solution.py:39
  83.7 4.9 %collective-permute-start.26 = (bf16[64,1152]{1,0:T(8,128)(2,1)S(1)}, bf16[64,1152]{1,0:T(8,128)(2,1)S(1)}, u32[]{:S(2)}, u32[]{:S(2)}) collective-permute-start(bf16[64,1152]{1,0:T(8,128)(2,1)S(1)} %step4.1), channel_id=1, source_target_pairs={{0,32},{1,33},{2,34},{3,35},{4,36},{5,37},{6,38},{7,39},{8,40},{9,... | collective-permute-start | bytes 442376 | tf_op jit(solution)/shard_map/ppermute | solution.py:55
  88.6 1.0 %collective-permute-done.26.refs_2_ = bf16[64,1152]{1,0:T(8,128)(2,1)S(1)} collective-permute-done((bf16[64,1152]{1,0:T(8,128)(2,1)S(1)}, bf16[64,1152]{1,0:T(8,128)(2,1)S(1)}, u32[]{:S(2)}, u32[]{:S(2)}) %collective-permute-start.26) | collective-permute-done | bytes 147488 | tf_op jit(solution)/shard_map/ppermute | solution.py:55
  (53 shorter events, 11.4 us)
Async XLA Ops:
  1.8 4.3 %collective-permute-start.6 = (bf16[64,1152]{1,0:T(8,128)(2,1)S(1)}, bf16[64,1152]{1,0:T(8,128)(2,1)S(1)}, u32[]{:S(2)}, u32[]{:S(2)}) collective-permute-start(bf16[64,1152]{1,0:T(8,128)(2,1)S(1)} %get-tuple-element.41.refs_0_), channel_id=1, source_target_pairs={{0,32},{1,33},{2,34},{3,35},{4,36},{5,37},{6,38},{7,39},{8,40},{9,... | collective-permute-start | bytes 442376 | tf_op jit(solution)/shard_map/ppermute | solution.py:55
  6.2 13.8 %collective-permute-start.7 = (bf16[128,1152]{1,0:T(8,128)(2,1)S(1)}, bf16[128,1152]{1,0:T(8,128)(2,1)S(1)}, u32[]{:S(2)}, u32[]{:S(2)}) collective-permute-start(bf16[128,1152]{1,0:T(8,128)(2,1)S(1)} %pair.1.refs_2_), channel_id=1, source_target_pairs={{0,4},{1,5},{2,6},{3,7},{4,8},{5,9},{6,10},{7,11},{8,12},{9,13},{1... | collective-permute-start | bytes 884744 | tf_op jit(solution)/shard_map/ppermute | solution.py:51
  10.1 6.4 %collective-permute-start.2 = (bf16[64,1152]{1,0:T(8,128)(2,1)S(1)}, bf16[64,1152]{1,0:T(8,128)(2,1)S(1)}, u32[]{:S(2)}, u32[]{:S(2)}) collective-permute-start(bf16[64,1152]{1,0:T(8,128)(2,1)S(1)} %get-tuple-element.40.refs_0_), channel_id=1, source_target_pairs={{0,192},{1,193},{2,194},{3,195},{4,196},{5,197},{6,198},{7,199},{8... | collective-permute-start | bytes 442376 | tf_op jit(solution)/shard_map/ppermute | solution.py:39
  12.8 5.6 %collective-permute-start.1 = (bf16[64,1152]{1,0:T(8,128)(2,1)S(1)}, bf16[64,1152]{1,0:T(8,128)(2,1)S(1)}, u32[]{:S(2)}, u32[]{:S(2)}) collective-permute-start(bf16[64,1152]{1,0:T(8,128)(2,1)S(1)} %get-tuple-element.40.refs_0_), channel_id=1, source_target_pairs={{0,128},{1,129},{2,130},{3,131},{4,132},{5,133},{6,134},{7,135},{8... | collective-permute-start | bytes 442376 | tf_op jit(solution)/shard_map/ppermute | solution.py:39
  13.2 6.7 %collective-permute-start = (bf16[64,1152]{1,0:T(8,128)(2,1)S(1)}, bf16[64,1152]{1,0:T(8,128)(2,1)S(1)}, u32[]{:S(2)}, u32[]{:S(2)}) collective-permute-start(bf16[64,1152]{1,0:T(8,128)(2,1)S(1)} %get-tuple-element.40.refs_0_), channel_id=1, source_target_pairs={{0,64},{1,65},{2,66},{3,67},{4,68},{5,69},{6,70},{7,71},{8,72},{9,... | collective-permute-start | bytes 442376 | tf_op jit(solution)/shard_map/ppermute | solution.py:39
  20.0 5.1 %collective-permute-start.9 = (bf16[128,1152]{1,0:T(8,128)(2,1)S(1)}, bf16[128,1152]{1,0:T(8,128)(2,1)S(1)}, u32[]{:S(2)}, u32[]{:S(2)}) collective-permute-start(bf16[128,1152]{1,0:T(8,128)(2,1)S(1)} %behind1.1.refs_1_), channel_id=1, source_target_pairs={{0,32},{1,33},{2,34},{3,35},{4,36},{5,37},{6,38},{7,39},{8,40},{9,... | collective-permute-start | bytes 884744 | tf_op jit(solution)/shard_map/ppermute | solution.py:55
  20.1 5.9 %collective-permute-start.8 = (bf16[128,1152]{1,0:T(8,128)(2,1)S(1)}, bf16[128,1152]{1,0:T(8,128)(2,1)S(1)}, u32[]{:S(2)}, u32[]{:S(2)}) collective-permute-start(bf16[128,1152]{1,0:T(8,128)(2,1)S(1)} %behind1.1.refs_1_), channel_id=1, source_target_pairs={{0,4},{1,5},{2,6},{3,7},{4,8},{5,9},{6,10},{7,11},{8,12},{9,13},{1... | collective-permute-start | bytes 884744 | tf_op jit(solution)/shard_map/ppermute | solution.py:51
  21.7 16.5 %collective-permute-start.3 = (bf16[256,1152]{1,0:T(8,128)(2,1)S(1)}, bf16[256,1152]{1,0:T(8,128)(2,1)S(1)}, u32[]{:S(2)}, u32[]{:S(2)}) collective-permute-start(bf16[256,1152]{1,0:T(8,128)(2,1)S(1)} %group.1.refs_1_.refs_2_), channel_id=1, source_target_pairs={{0,1},{1,2},{2,3},{3,0},{4,5},{5,6},{6,7},{7,4},{8,9},{9,10},{10,1... | collective-permute-start | bytes 1769480 | tf_op jit(solution)/shard_map/ppermute | solution.py:45
  22.1 16.6 %collective-permute-start.5 = (bf16[256,1152]{1,0:T(8,128)(2,1)S(1)}, bf16[256,1152]{1,0:T(8,128)(2,1)S(1)}, u32[]{:S(2)}, u32[]{:S(2)}) collective-permute-start(bf16[256,1152]{1,0:T(8,128)(2,1)S(1)} %group.1.refs_1_.refs_2_), channel_id=1, source_target_pairs={{0,3},{1,0},{2,1},{3,2},{4,7},{5,4},{6,5},{7,6},{8,11},{9,8},{10,9... | collective-permute-start | bytes 1769480 | tf_op jit(solution)/shard_map/ppermute | solution.py:45
  24.4 14.8 %collective-permute-start.4 = (bf16[256,1152]{1,0:T(8,128)(2,1)S(1)}, bf16[256,1152]{1,0:T(8,128)(2,1)S(1)}, u32[]{:S(2)}, u32[]{:S(2)}) collective-permute-start(bf16[256,1152]{1,0:T(8,128)(2,1)S(1)} %group.1.refs_1_.refs_2_), channel_id=1, source_target_pairs={{0,2},{1,3},{2,0},{3,1},{4,6},{5,7},{6,4},{7,5},{8,10},{9,11},{10,... | collective-permute-start | bytes 1769480 | tf_op jit(solution)/shard_map/ppermute | solution.py:45
  26.1 3.8 %collective-permute-start.11 = (bf16[128,1152]{1,0:T(8,128)(2,1)S(1)}, bf16[128,1152]{1,0:T(8,128)(2,1)S(1)}, u32[]{:S(2)}, u32[]{:S(2)}) collective-permute-start(bf16[128,1152]{1,0:T(8,128)(2,1)S(1)} %behind2.1.refs_0_), channel_id=1, source_target_pairs={{0,32},{1,33},{2,34},{3,35},{4,36},{5,37},{6,38},{7,39},{8,40},{9,... | collective-permute-start | bytes 884744 | tf_op jit(solution)/shard_map/ppermute | solution.py:55
  28.6 5.9 %collective-permute-start.10 = (bf16[128,1152]{1,0:T(8,128)(2,1)S(1)}, bf16[128,1152]{1,0:T(8,128)(2,1)S(1)}, u32[]{:S(2)}, u32[]{:S(2)}) collective-permute-start(bf16[128,1152]{1,0:T(8,128)(2,1)S(1)} %behind2.1.refs_0_), channel_id=1, source_target_pairs={{0,4},{1,5},{2,6},{3,7},{4,8},{5,9},{6,10},{7,11},{8,12},{9,13},{1... | collective-permute-start | bytes 884744 | tf_op jit(solution)/shard_map/ppermute | solution.py:51
  34.5 8.5 %collective-permute-start.12 = (bf16[64,1152]{1,0:T(8,128)(2,1)S(1)}, bf16[64,1152]{1,0:T(8,128)(2,1)S(1)}, u32[]{:S(2)}, u32[]{:S(2)}) collective-permute-start(bf16[64,1152]{1,0:T(8,128)(2,1)S(1)} %far_first.1.refs_2_), channel_id=1, source_target_pairs={{0,4},{1,5},{2,6},{3,7},{4,8},{5,9},{6,10},{7,11},{8,12},{9,13},{1... | collective-permute-start | bytes 442376 | tf_op jit(solution)/shard_map/ppermute | solution.py:51
  43.1 2.1 %collective-permute-start.13 = (bf16[192,1152]{1,0:T(8,128)(2,1)S(1)}, bf16[192,1152]{1,0:T(8,128)(2,1)S(1)}, u32[]{:S(2)}, u32[]{:S(2)}) collective-permute-start(bf16[192,1152]{1,0:T(8,128)(2,1)S(1)} %far_mine.1.refs_0_), channel_id=1, source_target_pairs={{0,32},{1,33},{2,34},{3,35},{4,36},{5,37},{6,38},{7,39},{8,40},{9,... | collective-permute-start | bytes 1327112 | tf_op jit(solution)/shard_map/ppermute | solution.py:55
  43.8 8.2 %collective-permute-start.15 = (bf16[256,1152]{1,0:T(8,128)(2,1)S(1)}, bf16[256,1152]{1,0:T(8,128)(2,1)S(1)}, u32[]{:S(2)}, u32[]{:S(2)}) collective-permute-start(bf16[256,1152]{1,0:T(8,128)(2,1)S(1)} %get-tuple-element.50.refs_2_), channel_id=1, source_target_pairs={{0,32},{1,33},{2,34},{3,35},{4,36},{5,37},{6,38},{7,39},{8,40},{9,... | collective-permute-start | bytes 1769480 | tf_op jit(solution)/shard_map/ppermute | solution.py:55
  47.9 4.0 %collective-permute-start.14 = (bf16[192,1152]{1,0:T(8,128)(2,1)S(1)}, bf16[192,1152]{1,0:T(8,128)(2,1)S(1)}, u32[]{:S(2)}, u32[]{:S(2)}) collective-permute-start(bf16[192,1152]{1,0:T(8,128)(2,1)S(1)} %get-tuple-element.60), channel_id=1, source_target_pairs={{0,32},{1,33},{2,34},{3,35},{4,36},{5,37},{6,38},{7,39},{8,40},{9,... | collective-permute-start | bytes 1327112 | tf_op jit(solution)/shard_map/ppermute | solution.py:55
  49.4 17.4 %collective-permute-start.16 = (bf16[264,1152]{1,0:T(8,128)(2,1)S(1)}, bf16[264,1152]{1,0:T(8,128)(2,1)S(1)}, u32[]{:S(2)}, u32[]{:S(2)}) collective-permute-start(bf16[264,1152]{1,0:T(8,128)(2,1)S(1)} %image1.1.refs_2_), channel_id=1, source_target_pairs={{0,3},{1,0},{2,1},{3,2},{4,7},{5,4},{6,5},{7,6},{8,11},{9,8},{10,9... | collective-permute-start | bytes 1824776 | tf_op jit(solution)/shard_map/ppermute | solution.py:45
  54.0 12.8 %collective-permute-start.17 = (bf16[264,1152]{1,0:T(8,128)(2,1)S(1)}, bf16[264,1152]{1,0:T(8,128)(2,1)S(1)}, u32[]{:S(2)}, u32[]{:S(2)}) collective-permute-start(bf16[264,1152]{1,0:T(8,128)(2,1)S(1)} %image2.1.refs_7_), channel_id=1, source_target_pairs={{0,2},{1,3},{2,0},{3,1},{4,6},{5,7},{6,4},{7,5},{8,10},{9,11},{10,... | collective-permute-start | bytes 1824776 | tf_op jit(solution)/shard_map/ppermute | solution.py:45
  54.7 16.6 %collective-permute-start.18 = (bf16[264,1152]{1,0:T(8,128)(2,1)S(1)}, bf16[264,1152]{1,0:T(8,128)(2,1)S(1)}, u32[]{:S(2)}, u32[]{:S(2)}) collective-permute-start(bf16[264,1152]{1,0:T(8,128)(2,1)S(1)} %image3.1.refs_7_), channel_id=1, source_target_pairs={{0,1},{1,2},{2,3},{3,0},{4,5},{5,6},{6,7},{7,4},{8,9},{9,10},{10,1... | collective-permute-start | bytes 1824776 | tf_op jit(solution)/shard_map/ppermute | solution.py:45
  55.2 11.4 %collective-permute-start.20 = (bf16[128,1152]{1,0:T(8,128)(2,1)S(1)}, bf16[128,1152]{1,0:T(8,128)(2,1)S(1)}, u32[]{:S(2)}, u32[]{:S(2)}) collective-permute-start(bf16[128,1152]{1,0:T(8,128)(2,1)S(1)} %get-tuple-element.63.refs_7_), channel_id=1, source_target_pairs={{0,28},{1,29},{2,30},{3,31},{4,0},{5,1},{6,2},{7,3},{8,4},{9,5},{1... | collective-permute-start | bytes 884744 | tf_op jit(solution)/shard_map/ppermute | solution.py:51
  55.2 11.4 %collective-permute-start.19 = (bf16[64,1152]{1,0:T(8,128)(2,1)S(1)}, bf16[64,1152]{1,0:T(8,128)(2,1)S(1)}, u32[]{:S(2)}, u32[]{:S(2)}) collective-permute-start(bf16[64,1152]{1,0:T(8,128)(2,1)S(1)} %get-tuple-element.65), channel_id=1, source_target_pairs={{0,24},{1,25},{2,26},{3,27},{4,28},{5,29},{6,30},{7,31},{8,0},{9,1... | collective-permute-start | bytes 442376 | tf_op jit(solution)/shard_map/ppermute | solution.py:51
  66.7 6.9 %collective-permute-start.24 = (bf16[128,1152]{1,0:T(8,128)(2,1)S(1)}, bf16[128,1152]{1,0:T(8,128)(2,1)S(1)}, u32[]{:S(2)}, u32[]{:S(2)}) collective-permute-start(bf16[128,1152]{1,0:T(8,128)(2,1)S(1)} %step2.1.refs_5_), channel_id=1, source_target_pairs={{0,28},{1,29},{2,30},{3,31},{4,0},{5,1},{6,2},{7,3},{8,4},{9,5},{1... | collective-permute-start | bytes 884744 | tf_op jit(solution)/shard_map/ppermute | solution.py:51
  73.6 9.1 %copy-start = (bf16[64,1152]{1,0:T(8,128)(2,1)S(1)}, bf16[64,1152]{1,0:T(8,128)(2,1)}, u32[]{:S(2)}) copy-start(bf16[64,1152]{1,0:T(8,128)(2,1)} %refs_5_.1) | copy-start | bytes 442372
  73.7 15.9 %copy-start.1 = (bf16[64,1152]{1,0:T(8,128)(2,1)S(1)}, bf16[64,1152]{1,0:T(8,128)(2,1)}, u32[]{:S(2)}) copy-start(bf16[64,1152]{1,0:T(8,128)(2,1)} %refs_3_.1) | copy-start | bytes 442372
  73.7 9.9 %collective-permute-start.25 = (bf16[128,1152]{1,0:T(8,128)(2,1)S(1)}, bf16[128,1152]{1,0:T(8,128)(2,1)S(1)}, u32[]{:S(2)}, u32[]{:S(2)}) collective-permute-start(bf16[128,1152]{1,0:T(8,128)(2,1)S(1)} %step3.1.refs_7_), channel_id=1, source_target_pairs={{0,28},{1,29},{2,30},{3,31},{4,0},{5,1},{6,2},{7,3},{8,4},{9,5},{1... | collective-permute-start | bytes 884744 | tf_op jit(solution)/shard_map/ppermute | solution.py:51
  73.8 5.8 %collective-permute-start.21 = (bf16[72,1152]{1,0:T(8,128)(2,1)S(1)}, bf16[72,1152]{1,0:T(8,128)(2,1)S(1)}, u32[]{:S(2)}, u32[]{:S(2)}) collective-permute-start(bf16[72,1152]{1,0:T(8,128)(2,1)S(1)} %get-tuple-element.68), channel_id=1, source_target_pairs={{0,192},{1,193},{2,194},{3,195},{4,196},{5,197},{6,198},{7,199},{8... | collective-permute-start | bytes 497672 | tf_op jit(solution)/shard_map/ppermute | solution.py:39
  75.5 5.8 %collective-permute-start.22 = (bf16[72,1152]{1,0:T(8,128)(2,1)S(1)}, bf16[72,1152]{1,0:T(8,128)(2,1)S(1)}, u32[]{:S(2)}, u32[]{:S(2)}) collective-permute-start(bf16[72,1152]{1,0:T(8,128)(2,1)S(1)} %get-tuple-element.69), channel_id=1, source_target_pairs={{0,128},{1,129},{2,130},{3,131},{4,132},{5,133},{6,134},{7,135},{8... | collective-permute-start | bytes 497672 | tf_op jit(solution)/shard_map/ppermute | solution.py:39
  75.5 7.2 %collective-permute-start.23 = (bf16[72,1152]{1,0:T(8,128)(2,1)S(1)}, bf16[72,1152]{1,0:T(8,128)(2,1)S(1)}, u32[]{:S(2)}, u32[]{:S(2)}) collective-permute-start(bf16[72,1152]{1,0:T(8,128)(2,1)S(1)} %get-tuple-element.70.refs_3_), channel_id=1, source_target_pairs={{0,64},{1,65},{2,66},{3,67},{4,68},{5,69},{6,70},{7,71},{8,72},{9,... | collective-permute-start | bytes 497672 | tf_op jit(solution)/shard_map/ppermute | solution.py:39
  83.7 5.9 %collective-permute-start.26 = (bf16[64,1152]{1,0:T(8,128)(2,1)S(1)}, bf16[64,1152]{1,0:T(8,128)(2,1)S(1)}, u32[]{:S(2)}, u32[]{:S(2)}) collective-permute-start(bf16[64,1152]{1,0:T(8,128)(2,1)S(1)} %step4.1), channel_id=1, source_target_pairs={{0,32},{1,33},{2,34},{3,35},{4,36},{5,37},{6,38},{7,39},{8,40},{9,... | collective-permute-start | bytes 442376 | tf_op jit(solution)/shard_map/ppermute | solution.py:55

commit v5 on v3

--- a/solution.py
+++ b/solution.py
@@ -136,7 +136,7 @@
 
 
 def mine_body(scale_ref, bias_ref, img_ref, txt_ref, coeff_ref, loss_ref):
-    weight, softplus = entry(img_ref[...], txt_ref[...], scale_ref[0], bias_ref[0])
+    weight, softplus = entry(img_ref[:256, :], txt_ref[...], scale_ref[0], bias_ref[0])
     coeff_ref[...] = weight
     loss_ref[...] = fold(softplus)
 
@@ -145,49 +145,54 @@
     total = None
     for c, s in zip(coeffs, imgs):
         part = lax.dot_general(
-            c[:, lo:hi], s[...], (((0,), (0,)), ((), ())), preferred_element_type=F32
+            c[:, lo:hi], s[:256, :], (((0,), (0,)), ((), ())), preferred_element_type=F32
         )
         total = part if total is None else total + part
     return total
 
 
-def far_body(scale_ref, bias_ref, i0, i1, i2, i3, txt_ref, near_loss, c0, c1, c2, c3, keep, send, pair, loss):
+def tile(img, txt_ref, coeff_ref, total, scale, bias, own=False):
+    for lo, hi in ((0, 256), (256, 384)):
+        match = None
+        if own and lo == 256:
+            r = lax.broadcasted_iota(jnp.int32, (256, 128), 0)
+            c = lax.broadcasted_iota(jnp.int32, (256, 128), 1)
+            match = (r == c) & (r < U)
+        weight, softplus = entry(img[:256, :], txt_ref[lo:hi, :], scale, bias, match)
+        coeff_ref[:, lo:hi] = weight
+        total = total + fold(softplus)
+    return total
+
+
+def other_body(scale_ref, bias_ref, i0, i1, i3, txt_ref, l0, l1, l3, o0, o1, o3, loss):
+    for n, (i, o, l) in enumerate(((i0, o0, l0), (i1, o1, l1), (i3, o3, l3))):
+        loss[256 * n : 256 * (n + 1), :] = tile(
+            i, txt_ref, o, l[...], scale_ref[0], bias_ref[0], n == 0
+        )
+
+
+def last_body(scale_ref, bias_ref, i0, i1, i2, i3, near, other, m0, m1, m3, o0, o1, o3, m2, o2, loss, keep, send, pair):
     scale, bias = scale_ref[0], bias_ref[0]
+    imgs = (i0, i1, i2, i3)
+    weight, softplus = entry(i2[:256, :], near[...], scale, bias)
+    m2[...] = weight
+    loss[...] = tile(i2, other, o2, fold(softplus), scale, bias)
+    g = texts((o0, o1, o2, o3), imgs, 0, 384)
+    send[...] = g[:256, :].astype(BF16)
+    pair[...] = g[256:, :]
+    keep[...] = texts((m0, m1, m2, m3), imgs, 0, 256)
+
+
+def far_body(scale_ref, bias_ref, i0, i1, i2, i3, txt_ref, l013, l2, c0, c1, c2, c3, keep, send, loss):
     imgs, coeffs = (i0, i1, i2, i3), (c0, c1, c2, c3)
+    before = (l013[:256, :], l013[256:512, :], l2[...], l013[512:, :])
     for k in range(4):
-        total = near_loss[256 * k : 256 * (k + 1), :]
-        for n in range(2):
-            at = slice(256 * n, 256 * (n + 1))
-            match = None
-            if k == 0 and n == 1:
-                r = lax.broadcasted_iota(jnp.int32, (256, 256), 0)
-                c = lax.broadcasted_iota(jnp.int32, (256, 256), 1)
-                match = (r + 128 == c) & (r < U)
-            weight, softplus = entry(imgs[k][...], txt_ref[at, :], scale, bias, match)
-            coeffs[k][:, at] = weight
-            total = total + fold(softplus)
+        total = tile(imgs[k], txt_ref, coeffs[k], before[k], scale_ref[0], bias_ref[0])
         column = jnp.broadcast_to(jnp.sum(total, axis=1, keepdims=True), (256, 128))
         loss[:, 256 * k : 256 * (k + 1)] = jnp.transpose(column)[:8, :]
-    g = texts(coeffs, imgs, 0, 256)
+    g = texts(coeffs, imgs, 0, 384)
     keep[...] = g[:192, :]
-    send[:64, :] = g[192:, :].astype(BF16)
-    g = texts(coeffs, imgs, 256, 512)
-    send[64:, :] = g[:128, :].astype(BF16)
-    pair[...] = g[128:, :]
-
-
-def other_body(scale_ref, bias_ref, i0, i1, i2, i3, c0, c1, c2, c3, txt_ref, l0, l1, l2, l3, o0, o1, o2, o3, keep, send, loss):
-    imgs, sums, mine, other = (i0, i1, i2, i3), (l0, l1, l2, l3), (c0, c1, c2, c3), (o0, o1, o2, o3)
-    for k in range(4):
-        weight, softplus = entry(imgs[k][...], txt_ref[...], scale_ref[0], bias_ref[0])
-        other[k][...] = weight
-        loss[256 * k : 256 * (k + 1), :] = sums[k][...] + fold(softplus)
-    send[...] = texts(other, imgs, 0, 256).astype(BF16)
-    keep[...] = texts(mine, imgs, 0, 256)
-
-
-def copy_body(src, dst):
-    dst[...] = src[...]
+    send[...] = g[192:, :].astype(BF16)
 
 
 def image_body(k, cf, cm, co, far, mine, other, loss, out):
@@ -217,7 +222,17 @@
             out[U:, :256] = marks
 
 
-def pack_body(b1, b2, far, near):
+def pack_body(*refs):
+    out, at = refs[-1], 0
+    for ref in refs[:-1]:
+        n = min(ref.shape[0], out.shape[0] - at)
+        out[at : at + n, :] = ref[:n, :]
+        at += n
+    if at < out.shape[0]:
+        out[at:, :] = jnp.zeros((out.shape[0] - at, out.shape[1]), out.dtype)
+
+
+def split_body(b1, b2, far, near):
     far[:U, :] = b2[:U, :]
     far[U:, :] = b1[...]
     near[:128, :] = b2[...]
@@ -243,18 +258,15 @@
     return inv[...] * (g - unit * jnp.sum(unit * g, axis=-1, keepdims=True))
 
 
-def finish_img_body(g_ref, l_ref, r1, r2, r3, raw, inv, out_ref, loss_ref):
+def finish_body(g_ref, l_ref, r1, r2, r3, raw_i, inv_i, pair, v1, v2, got, raw_t, inv_t, img_ref, txt_ref, loss_ref):
     g = g_ref[...] + (up(r1, 0, U) + up(r2, 0, U) + up(r3, 0, U))
-    out_ref[...] = back_norm(g, raw, inv)
+    img_ref[...] = back_norm(g, raw_i, inv_i)
     loss = l_ref[:1, :U]
     for j, r in enumerate((r1, r2, r3)):
         loss = loss + loss_sum(r[U:, U * (j + 1) : U * (j + 2)])
     loss_ref[...] = loss
-
-
-def finish_txt_body(pair, v1, v2, got, raw, inv, out_ref):
     g = pair[:64, :] + (up(v1, 0, 64) + up(v2, 0, 64) + got[...].astype(F32))
-    out_ref[...] = back_norm(g, raw, inv)
+    txt_ref[...] = back_norm(g, raw_t, inv_t)
 
 
 def on_device(picture, caption, scale, bias):
@@ -266,39 +278,48 @@
         scratch=[pltpu.VMEM((2, rows, d), BF16), pltpu.SemaphoreType.DMA((2,))],
     )
 
-    pair = jnp.concatenate([txt, swap(txt)], axis=0)
-    f1, f3, f2 = first(img, 1), first(img, 3), first(img, 2)
-    b1, b2 = ring(pair, 1), ring(pair, 2)
-    group = jnp.concatenate([img, f1, f2, f3], axis=0)
+    def pack(name, n, parts, after=()):
+        return call(name, pack_body, [shape(n, d)], parts, (), after)[0]
+
+    pair = pack("pair", 128, (txt, swap(txt)))
+    b2, b1 = ring(pair, 2), ring(pair, 1)
+    f2, f1, f3 = first(img, 2), first(img, 1), first(img, 3)
+    group = pack("group", 264, (img, f1, f2, f3))
     g1, g3, g2 = second(group, 1), second(group, 3), second(group, 2)
     groups = (group, g1, g2, g3)
     far_pack, near_mine = call(
-        "pack", pack_body, [shape(192, d), shape(256, d)], (b1, b2), (), (group,)
+        "pack", split_body, [shape(192, d), shape(256, d)], (b1, b2), (), (group,)
     )
     far_got = ring(far_pack, 2)
     near_other = swap(near_mine)
 
     sc = (scale, bias)
-    mine_c, mine_l, last = [None] * 4, [None] * 4, ()
-    for k in (0, 1, 3, 2):
+    mine_c, mine_l, other_c, last = [None] * 4, [None] * 4, [None] * 4, ()
+    for k in (0, 1, 3):
         mine_c[k], mine_l[k] = call(
             f"mine{k}", mine_body, [shape(256, 256), shape(256, 128, dtype=F32)],
             (groups[k], near_mine), sc, last,
         )
         last = (mine_l[k],)
-    *other_c, keep_b, send_b, near_loss = call(
-        "other", other_body,
-        [shape(256, 256)] * 4 + [shape(256, d, dtype=F32), shape(256, d), shape(1024, 128, dtype=F32)],
-        (*groups, *mine_c, near_other, *mine_l), sc, last,
+    other = pack("other_texts", 384, (near_other, pair), last)
+    other_c[0], other_c[1], other_c[3], near_loss = call(
+        "other", other_body, [shape(256, 384)] * 3 + [shape(768, 128, dtype=F32)],
+        (groups[0], groups[1], groups[3], other, mine_l[0], mine_l[1], mine_l[3]), sc,
+    )
+    mine_c[2], other_c[2], last_loss, keep_b, send_b, own_pair = call(
+        "last", last_body,
+        [shape(256, 256), shape(256, 384), shape(256, 128, dtype=F32)]
+        + [shape(256, d, dtype=F32), shape(256, d), shape(128, d, dtype=F32)],
+        (*groups, near_mine, other, mine_c[0], mine_c[1], mine_c[3], other_c[0], other_c[1], other_c[3]),
+        sc, (near_loss,),
     )
     got_b = swap(send_b)
-    far_mine = call("arrived", copy_body, [shape(192, d)], (far_got,), (), (send_b,))[0]
-    far = jnp.concatenate([far_mine, swap(far_mine), pair], axis=0)
-    *far_c, keep_a, send_a, own_pair, loss = call(
+    far_mine = pack("far_mine", 192, (far_got,), (send_b,))
+    far = pack("far_texts", 384, (far_mine, swap(far_mine)))
+    *far_c, keep_a, send_a, loss = call(
         "far", far_body,
-        [shape(256, 512)] * 4
-        + [shape(192, d, dtype=F32), shape(192, d), shape(128, d, dtype=F32), shape(8, 1024, dtype=F32)],
-        (*groups, far, near_loss), sc,
+        [shape(256, 384)] * 4 + [shape(192, d, dtype=F32), shape(192, d), shape(8, 1024, dtype=F32)],
+        (*groups, far, near_loss, last_loss), sc,
     )
     got_a = swap(send_a)
 
@@ -306,7 +327,7 @@
         out = shape(256, d, dtype=F32) if k == 0 else shape(264, d)
         return call(
             f"image{k}", functools.partial(image_body, k), [out],
-            (far_c[k], mine_c[k], other_c[k], far, near_mine, near_other, loss), (), after,
+            (far_c[k], mine_c[k], other_c[k], far, near_mine, other, loss), (), after,
         )[0]
 
     p1 = image(1, ())
@@ -319,7 +340,7 @@
     r2 = second(p2, -2)
     p0 = image(0, (p2,))
     two, one = call("step2", step2_body, [shape(128, d)] * 2, (keep_b, got_b, w), (), (p0,))
-    v1, v2 = ring(one, -1), ring(two, -2)
+    v2, v1 = ring(two, -2), ring(one, -1)
     own_img, own_loss, m1, m2, m3 = call(
         "merge_img", merge_img_body,
         [shape(rows, d, dtype=F32), shape(8, 256, dtype=F32)] + [shape(rows + 8, d)] * 3,
@@ -328,15 +349,11 @@
     q1, q3, q2 = first(m1, -1), first(m3, -3), first(m2, -2)
     z3 = call("step3", step3_body, [shape(64, d)], (own_pair, v1, v2), (), (m3,))[0]
     got_c = swap(z3)
-    grad_img, loss_out = call(
-        "finish_img", finish_img_body,
-        [shape(rows, d, dtype=F32), shape(1, rows, dtype=F32)],
-        (own_img, own_loss, q1, q2, q3, picture, img_inv), (), (z3,),
-    )
-    grad_txt = call(
-        "finish_txt", finish_txt_body, [shape(rows, d, dtype=F32)],
-        (own_pair, v1, v2, got_c, caption, txt_inv),
-    )[0]
+    grad_img, grad_txt, loss_out = call(
+        "finish", finish_body,
+        [shape(rows, d, dtype=F32), shape(rows, d, dtype=F32), shape(1, rows, dtype=F32)],
+        (own_img, own_loss, q1, q2, q3, picture, img_inv, own_pair, v1, v2, got_c, caption, txt_inv),
+    )
     return grad_img, grad_txt, loss_out.reshape(rows)
 
 

time: 84.4 us -> 85.8 us (1.017)
  the two profiles are of different devices: /device:TPU:32 before, /device:TPU:1 now
where the time goes in v5:
time: 85.8 us; the launch traced here: 84.8 us
  waiting for transfers between devices  33.9 us (40%)
  starting transfers between devices  33.4 us (39%)
  Pallas kernels  15.3 us (18%)
  between operations  2.13 us (2%)
    pallas_call x22, Pallas kernels, call(): pl.pallas_call(kernel, out_shape=outs, in_specs=[SMEM] * len(scalars) + (...  15.3 us
    ppermute x6, starting transfers between devices, ring(): lax.ppermute(a, AXES, permutation(lambda x, c, z, y: (x, c, z - s if c el...  14.2 us
    ppermute x6, waiting for transfers between devices, second(): lax.ppermute(a, AXES, permutation(lambda x, c, z, y: (x + s, c, z, y) if...  12.4 us
    ppermute x6, waiting for transfers between devices, first(): lax.ppermute(a, AXES, permutation(lambda x, c, z, y: (x, c, z, y + s) if...  11.1 us
    ppermute x6, waiting for transfers between devices, ring(): lax.ppermute(a, AXES, permutation(lambda x, c, z, y: (x, c, z - s if c el...  7.67 us
    ppermute x6, starting transfers between devices, first(): lax.ppermute(a, AXES, permutation(lambda x, c, z, y: (x, c, z, y + s) if...  7.41 us
    ppermute x6, starting transfers between devices, second(): lax.ppermute(a, AXES, permutation(lambda x, c, z, y: (x + s, c, z, y) if...  6.17 us
    ppermute x6, starting transfers between devices, swap(): lax.ppermute(a, AXES, permutation(lambda x, c, z, y: (x, 1 - c, z, y)))  5.66 us
  transfers between devices with their start and end apart: 24, of which 14 were waited for; matrix products, arithmetic and copies ran while one was open for 0% of the time, Pallas kernels for 15%

profile of v5, /device:TPU:1, one launch (start us, length us, event | category | flops | bytes accessed | tf_op | source)
XLA Modules:
  0.0 84.8 jit_solution(1942314683157731070)
XLA Ops:
  0.6 1.2 %normalize.1 = (bf16[64,1152]{1,0:T(8,128)(2,1)S(1)}, bf16[64,1152]{1,0:T(8,128)(2,1)S(1)}, f32[64,1]{1,0:T(8,128)S(1)}, f32[64,1]{1,0:T(8,128)S(1)}) custom-call(bf16[64,1152]{1,0:T(8,128)(2,1)} %refs_5_.1, bf16[64,1152]{1,0:T(8,128)(2,1)} %refs_11_.1), custom_call_target="tpu_custom_call" | custom-call | flops 1 | bytes 1 | tf_op jit(solution)/shard_map/normalize/pallas_call | solution.py:65
  1.8 3.3 %collective-permute-start.6 = (bf16[64,1152]{1,0:T(8,128)(2,1)S(1)}, bf16[64,1152]{1,0:T(8,128)(2,1)S(1)}, u32[]{:S(2)}, u32[]{:S(2)}) collective-permute-start(bf16[64,1152]{1,0:T(8,128)(2,1)S(1)} %get-tuple-element.43.refs_0_), channel_id=1, source_target_pairs={{0,32},{1,33},{2,34},{3,35},{4,36},{5,37},{6,38},{7,39},{8,40},{9,... | collective-permute-start | bytes 442376 | tf_op jit(solution)/shard_map/ppermute | solution.py:55
  5.1 1.0 %collective-permute-done.6.refs_1_ = bf16[64,1152]{1,0:T(8,128)(2,1)S(1)} collective-permute-done((bf16[64,1152]{1,0:T(8,128)(2,1)S(1)}, bf16[64,1152]{1,0:T(8,128)(2,1)S(1)}, u32[]{:S(2)}, u32[]{:S(2)}) %collective-permute-start.6) | collective-permute-done | bytes 147488 | tf_op jit(solution)/shard_map/ppermute | solution.py:55
  6.2 4.4 %collective-permute-start.8 = (bf16[128,1152]{1,0:T(8,128)(2,1)S(1)}, bf16[128,1152]{1,0:T(8,128)(2,1)S(1)}, u32[]{:S(2)}, u32[]{:S(2)}) collective-permute-start(bf16[128,1152]{1,0:T(8,128)(2,1)S(1)} %pair.1.refs_1_), channel_id=1, source_target_pairs={{0,8},{1,9},{2,10},{3,11},{4,12},{5,13},{6,14},{7,15},{8,16},{9,17... | collective-permute-start | bytes 884744 | tf_op jit(solution)/shard_map/ppermute | solution.py:51
  11.3 2.7 %collective-permute-start.2 = (bf16[64,1152]{1,0:T(8,128)(2,1)S(1)}, bf16[64,1152]{1,0:T(8,128)(2,1)S(1)}, u32[]{:S(2)}, u32[]{:S(2)}) collective-permute-start(bf16[64,1152]{1,0:T(8,128)(2,1)S(1)} %get-tuple-element.42.refs_0_), channel_id=1, source_target_pairs={{0,192},{1,193},{2,194},{3,195},{4,196},{5,197},{6,198},{7,199},{8... | collective-permute-start | bytes 442376 | tf_op jit(solution)/shard_map/ppermute | solution.py:39
  15.0 2.6 %collective-permute-done.2.refs_3_ = bf16[64,1152]{1,0:T(8,128)(2,1)S(1)} collective-permute-done((bf16[64,1152]{1,0:T(8,128)(2,1)S(1)}, bf16[64,1152]{1,0:T(8,128)(2,1)S(1)}, u32[]{:S(2)}, u32[]{:S(2)}) %collective-permute-start.2) | collective-permute-done | bytes 147488 | tf_op jit(solution)/shard_map/ppermute | solution.py:39
  17.7 1.9 %collective-permute-done.1.refs_2_ = bf16[64,1152]{1,0:T(8,128)(2,1)S(1)} collective-permute-done((bf16[64,1152]{1,0:T(8,128)(2,1)S(1)}, bf16[64,1152]{1,0:T(8,128)(2,1)S(1)}, u32[]{:S(2)}, u32[]{:S(2)}) %collective-permute-start.1) | collective-permute-done | bytes 147488 | tf_op jit(solution)/shard_map/ppermute | solution.py:39
  19.6 1.8 %collective-permute-done.refs_1_ = bf16[64,1152]{1,0:T(8,128)(2,1)S(1)} collective-permute-done((bf16[64,1152]{1,0:T(8,128)(2,1)S(1)}, bf16[64,1152]{1,0:T(8,128)(2,1)S(1)}, u32[]{:S(2)}, u32[]{:S(2)}) %collective-permute-start) | collective-permute-done | bytes 147488 | tf_op jit(solution)/shard_map/ppermute | solution.py:39
  21.4 1.3 %collective-permute-start.3 = (bf16[264,1152]{1,0:T(8,128)(2,1)S(1)}, bf16[264,1152]{1,0:T(8,128)(2,1)S(1)}, u32[]{:S(2)}, u32[]{:S(2)}) collective-permute-start(bf16[264,1152]{1,0:T(8,128)(2,1)S(1)} %group.1.refs_2_), channel_id=1, source_target_pairs={{0,1},{1,2},{2,3},{3,0},{4,5},{5,6},{6,7},{7,4},{8,9},{9,10},{10,1... | collective-permute-start | bytes 1824776 | tf_op jit(solution)/shard_map/ppermute | solution.py:45
  22.7 1.5 %collective-permute-start.5 = (bf16[264,1152]{1,0:T(8,128)(2,1)S(1)}, bf16[264,1152]{1,0:T(8,128)(2,1)S(1)}, u32[]{:S(2)}, u32[]{:S(2)}) collective-permute-start(bf16[264,1152]{1,0:T(8,128)(2,1)S(1)} %group.1.refs_2_), channel_id=1, source_target_pairs={{0,3},{1,0},{2,1},{3,2},{4,7},{5,4},{6,5},{7,6},{8,11},{9,8},{10,9... | collective-permute-start | bytes 1824776 | tf_op jit(solution)/shard_map/ppermute | solution.py:45
  24.2 1.5 %collective-permute-start.4 = (bf16[264,1152]{1,0:T(8,128)(2,1)S(1)}, bf16[264,1152]{1,0:T(8,128)(2,1)S(1)}, u32[]{:S(2)}, u32[]{:S(2)}) collective-permute-start(bf16[264,1152]{1,0:T(8,128)(2,1)S(1)} %group.1.refs_2_), channel_id=1, source_target_pairs={{0,2},{1,3},{2,0},{3,1},{4,6},{5,7},{6,4},{7,5},{8,10},{9,11},{10,... | collective-permute-start | bytes 1824776 | tf_op jit(solution)/shard_map/ppermute | solution.py:45
  26.6 1.9 %collective-permute-start.9 = (bf16[192,1152]{1,0:T(8,128)(2,1)S(1)}, bf16[192,1152]{1,0:T(8,128)(2,1)S(1)}, u32[]{:S(2)}, u32[]{:S(2)}) collective-permute-start(bf16[192,1152]{1,0:T(8,128)(2,1)S(1)} %get-tuple-element.44), channel_id=1, source_target_pairs={{0,8},{1,9},{2,10},{3,11},{4,12},{5,13},{6,14},{7,15},{8,16},{9,17... | collective-permute-start | bytes 1327112 | tf_op jit(solution)/shard_map/ppermute | solution.py:51
  30.3 1.7 %collective-permute-done.3.refs_2_.refs_3_ = bf16[264,1152]{1,0:T(8,128)(2,1)S(1)} collective-permute-done((bf16[264,1152]{1,0:T(8,128)(2,1)S(1)}, bf16[264,1152]{1,0:T(8,128)(2,1)S(1)}, u32[]{:S(2)}, u32[]{:S(2)}) %collective-permute-start.3) | collective-permute-done | bytes 608288 | tf_op jit(solution)/shard_map/ppermute | solution.py:45
  33.0 1.5 %other.1 = (bf16[256,384]{1,0:T(8,128)(2,1)S(1)}, bf16[256,384]{1,0:T(8,128)(2,1)S(1)}, bf16[256,384]{1,0:T(8,128)(2,1)S(1)}, f32[768,128]{1,0:T(8,128)S(1)}) custom-call(f32[1]{0:T(128)S(6)} %copy.7.refs_0_, f32[1]{0:T(128)S(6)} %copy.8.refs_1_, bf16[264,1152]{1,0:T(8,128)(2,1)S(1)} %group.1.refs_2_, ...), custom_call_target="tpu_custom_call" | custom-call | flops 1 | bytes 1 | tf_op jit(solution)/shard_map/other/pallas_call | solution.py:65
  34.4 5.0 %collective-permute-done.4.refs_4_ = bf16[264,1152]{1,0:T(8,128)(2,1)S(1)} collective-permute-done((bf16[264,1152]{1,0:T(8,128)(2,1)S(1)}, bf16[264,1152]{1,0:T(8,128)(2,1)S(1)}, u32[]{:S(2)}, u32[]{:S(2)}) %collective-permute-start.4) | collective-permute-done | bytes 608288 | tf_op jit(solution)/shard_map/ppermute | solution.py:45
  39.4 2.7 %last.1 = (bf16[256,256]{1,0:T(8,128)(2,1)S(1)}, bf16[256,384]{1,0:T(8,128)(2,1)S(1)}, f32[256,128]{1,0:T(8,128)S(1)}, f32[256,1152]{1,0:T(8,128)S(1)}, bf16[256...) custom-call(f32[1]{0:T(128)S(6)} %copy.7.refs_0_, f32[1]{0:T(128)S(6)} %copy.8.refs_1_, ...), custom_call_target="tpu_custom_call" | custom-call | flops 1 | bytes 1 | tf_op jit(solution)/shard_map/last/pallas_call | solution.py:65
  43.1 1.3 %collective-permute-done.11.refs_1_ = bf16[192,1152]{1,0:T(8,128)(2,1)S(1)} collective-permute-done((bf16[192,1152]{1,0:T(8,128)(2,1)S(1)}, bf16[192,1152]{1,0:T(8,128)(2,1)S(1)}, u32[]{:S(2)}, u32[]{:S(2)}) %collective-permute-start.11) | collective-permute-done | bytes 442400 | tf_op jit(solution)/shard_map/ppermute | solution.py:55
  44.5 2.7 %far.1 = (bf16[256,384]{1,0:T(8,128)(2,1)S(1)}, bf16[256,384]{1,0:T(8,128)(2,1)S(1)}, bf16[256,384]{1,0:T(8,128)(2,1)S(1)}, bf16[256,384]{1,0:T(8,128)(2,1)S(1)}...) custom-call(f32[1]{0:T(128)S(6)} %copy.7.refs_0_, f32[1]{0:T(128)S(6)} %copy.8.refs_1_, ...), custom_call_target="tpu_custom_call" | custom-call | flops 1 | bytes 1 | tf_op jit(solution)/shard_map/far/pallas_call | solution.py:65
  47.7 1.0 %image1.1.refs_2_ = bf16[264,1152]{1,0:T(8,128)(2,1)S(1)} custom-call(bf16[256,384]{1,0:T(8,128)(2,1)S(1)} %get-tuple-element.66.refs_0_, bf16[256,256]{1,0:T(8,128)(2,1)S(1)} %get-tuple-element.50.refs_9_.refs_1_, bf16[256,384]{1,0:T(8,128)(2,1)S(1)} %get-tuple-element.53.refs_12_.refs_2_, bf16[384,1152]{1,0:T(8,128)(2,1)S(1)} %far_texts.1.refs_6_.refs_3_, ...), custom_call_target="tpu_custom_call" | custom-call | flops 1 | bytes 1 | tf_op jit(solution)/shard_map/image1/pallas_call | solution.py:65
  49.2 3.4 %collective-permute-start.17 = (bf16[192,1152]{1,0:T(8,128)(2,1)S(1)}, bf16[192,1152]{1,0:T(8,128)(2,1)S(1)}, u32[]{:S(2)}, u32[]{:S(2)}) collective-permute-start(bf16[192,1152]{1,0:T(8,128)(2,1)S(1)} %step1.1.refs_7_), channel_id=1, source_target_pairs={{0,24},{1,25},{2,26},{3,27},{4,28},{5,29},{6,30},{7,31},{8,0},{9,1... | collective-permute-start | bytes 1327112 | tf_op jit(solution)/shard_map/ppermute | solution.py:51
  52.6 1.2 %collective-permute-start.14 = (bf16[264,1152]{1,0:T(8,128)(2,1)S(1)}, bf16[264,1152]{1,0:T(8,128)(2,1)S(1)}, u32[]{:S(2)}, u32[]{:S(2)}) collective-permute-start(bf16[264,1152]{1,0:T(8,128)(2,1)S(1)} %image1.1.refs_2_), channel_id=1, source_target_pairs={{0,3},{1,0},{2,1},{3,2},{4,7},{5,4},{6,5},{7,6},{8,11},{9,8},{10,9... | collective-permute-start | bytes 1824776 | tf_op jit(solution)/shard_map/ppermute | solution.py:45
  53.9 1.0 %image3.1.refs_7_ = bf16[264,1152]{1,0:T(8,128)(2,1)S(1)} custom-call(bf16[256,384]{1,0:T(8,128)(2,1)S(1)} %get-tuple-element.63.refs_0_, bf16[256,256]{1,0:T(8,128)(2,1)S(1)} %get-tuple-element.51.refs_10_.refs_1_, bf16[256,384]{1,0:T(8,128)(2,1)S(1)} %get-tuple-element.54.refs_13_.refs_2_, bf16[384,1152]{1,0:T(8,128)(2,1)S(1)} %far_texts.1.refs_6_.refs_3_, ...), custom_call_target="tpu_custom_call" | custom-call | flops 1 | bytes 1 | tf_op jit(solution)/shard_map/image3/pallas_call | solution.py:65
  57.5 5.8 %collective-permute-done.17.refs_2_ = bf16[192,1152]{1,0:T(8,128)(2,1)S(1)} collective-permute-done((bf16[192,1152]{1,0:T(8,128)(2,1)S(1)}, bf16[192,1152]{1,0:T(8,128)(2,1)S(1)}, u32[]{:S(2)}, u32[]{:S(2)}) %collective-permute-start.17) | collective-permute-done | bytes 442400 | tf_op jit(solution)/shard_map/ppermute | solution.py:51
  63.4 2.2 %collective-permute-start.22 = (bf16[128,1152]{1,0:T(8,128)(2,1)S(1)}, bf16[128,1152]{1,0:T(8,128)(2,1)S(1)}, u32[]{:S(2)}, u32[]{:S(2)}) collective-permute-start(bf16[128,1152]{1,0:T(8,128)(2,1)S(1)} %get-tuple-element.76), channel_id=1, source_target_pairs={{0,24},{1,25},{2,26},{3,27},{4,28},{5,29},{6,30},{7,31},{8,0},{9,1... | collective-permute-start | bytes 884744 | tf_op jit(solution)/shard_map/ppermute | solution.py:51
  65.6 1.6 %collective-permute-start.21 = (bf16[128,1152]{1,0:T(8,128)(2,1)S(1)}, bf16[128,1152]{1,0:T(8,128)(2,1)S(1)}, u32[]{:S(2)}, u32[]{:S(2)}) collective-permute-start(bf16[128,1152]{1,0:T(8,128)(2,1)S(1)} %get-tuple-element.68.refs_5_), channel_id=1, source_target_pairs={{0,28},{1,29},{2,30},{3,31},{4,0},{5,1},{6,2},{7,3},{8,4},{9,5},{1... | collective-permute-start | bytes 884744 | tf_op jit(solution)/shard_map/ppermute | solution.py:51
  67.2 5.8 %collective-permute-done.16.refs_4_ = bf16[264,1152]{1,0:T(8,128)(2,1)S(1)} collective-permute-done((bf16[264,1152]{1,0:T(8,128)(2,1)S(1)}, bf16[264,1152]{1,0:T(8,128)(2,1)S(1)}, u32[]{:S(2)}, u32[]{:S(2)}) %collective-permute-start.16) | collective-permute-done | bytes 608288 | tf_op jit(solution)/shard_map/ppermute | solution.py:45
  73.3 3.0 %collective-permute-start.18 = (bf16[72,1152]{1,0:T(8,128)(2,1)S(1)}, bf16[72,1152]{1,0:T(8,128)(2,1)S(1)}, u32[]{:S(2)}, u32[]{:S(2)}) collective-permute-start(bf16[72,1152]{1,0:T(8,128)(2,1)S(1)} %get-tuple-element.71), channel_id=1, source_target_pairs={{0,192},{1,193},{2,194},{3,195},{4,196},{5,197},{6,198},{7,199},{8... | collective-permute-start | bytes 497672 | tf_op jit(solution)/shard_map/ppermute | solution.py:39
  76.9 1.9 %collective-permute-done.21.refs_1_.refs_8_ = bf16[128,1152]{1,0:T(8,128)(2,1)S(1)} collective-permute-done((bf16[128,1152]{1,0:T(8,128)(2,1)S(1)}, bf16[128,1152]{1,0:T(8,128)(2,1)S(1)}, u32[]{:S(2)}, u32[]{:S(2)}) %collective-permute-start.21) | collective-permute-done | bytes 294944 | tf_op jit(solution)/shard_map/ppermute | solution.py:51
  79.0 1.3 %collective-permute-done.18.refs_2_ = bf16[72,1152]{1,0:T(8,128)(2,1)S(1)} collective-permute-done((bf16[72,1152]{1,0:T(8,128)(2,1)S(1)}, bf16[72,1152]{1,0:T(8,128)(2,1)S(1)}, u32[]{:S(2)}, u32[]{:S(2)}) %collective-permute-start.18) | collective-permute-done | bytes 165920 | tf_op jit(solution)/shard_map/ppermute | solution.py:39
  80.3 2.0 %collective-permute-done.19.refs_3_ = bf16[72,1152]{1,0:T(8,128)(2,1)S(1)} collective-permute-done((bf16[72,1152]{1,0:T(8,128)(2,1)S(1)}, bf16[72,1152]{1,0:T(8,128)(2,1)S(1)}, u32[]{:S(2)}, u32[]{:S(2)}) %collective-permute-start.19) | collective-permute-done | bytes 165920 | tf_op jit(solution)/shard_map/ppermute | solution.py:39
  82.3 1.4 %collective-permute-done.20.refs_4_ = bf16[72,1152]{1,0:T(8,128)(2,1)S(1)} collective-permute-done((bf16[72,1152]{1,0:T(8,128)(2,1)S(1)}, bf16[72,1152]{1,0:T(8,128)(2,1)S(1)}, u32[]{:S(2)}, u32[]{:S(2)}) %collective-permute-start.20) | collective-permute-done | bytes 165920 | tf_op jit(solution)/shard_map/ppermute | solution.py:39
  83.8 1.1 %finish.1 = (f32[64,1152]{1,0:T(8,128)}, f32[64,1152]{1,0:T(8,128)}, f32[1,64]{1,0:T(1,128)}) custom-call(f32[64,1152]{1,0:T(8,128)S(1)} %get-tuple-element.69.refs_0_, f32[8,256]{1,0:T(8,128)S(1)} %get-tuple-element.70.refs_1_, bf16[72,1152]{1,0:T(8,128)(2,1)S(1)} %collective-permute-done.18.refs_2_, bf16[72,1152]{1,0:T(8,128)(2,1)S(1)} %collective-permute-done.19.refs_3_, ...), custom_call_target="tpu_custom_call" | custom-call | flops 1 | bytes 1 | tf_op jit(solution)/shard_map/finish/pallas_call | solution.py:65
  (42 shorter events, 10.1 us)
Async XLA Ops:
  1.8 4.3 %collective-permute-start.6 = (bf16[64,1152]{1,0:T(8,128)(2,1)S(1)}, bf16[64,1152]{1,0:T(8,128)(2,1)S(1)}, u32[]{:S(2)}, u32[]{:S(2)}) collective-permute-start(bf16[64,1152]{1,0:T(8,128)(2,1)S(1)} %get-tuple-element.43.refs_0_), channel_id=1, source_target_pairs={{0,32},{1,33},{2,34},{3,35},{4,36},{5,37},{6,38},{7,39},{8,40},{9,... | collective-permute-start | bytes 442376 | tf_op jit(solution)/shard_map/ppermute | solution.py:55
  6.2 19.5 %collective-permute-start.8 = (bf16[128,1152]{1,0:T(8,128)(2,1)S(1)}, bf16[128,1152]{1,0:T(8,128)(2,1)S(1)}, u32[]{:S(2)}, u32[]{:S(2)}) collective-permute-start(bf16[128,1152]{1,0:T(8,128)(2,1)S(1)} %pair.1.refs_1_), channel_id=1, source_target_pairs={{0,8},{1,9},{2,10},{3,11},{4,12},{5,13},{6,14},{7,15},{8,16},{9,17... | collective-permute-start | bytes 884744 | tf_op jit(solution)/shard_map/ppermute | solution.py:51
  10.5 15.2 %collective-permute-start.7 = (bf16[128,1152]{1,0:T(8,128)(2,1)S(1)}, bf16[128,1152]{1,0:T(8,128)(2,1)S(1)}, u32[]{:S(2)}, u32[]{:S(2)}) collective-permute-start(bf16[128,1152]{1,0:T(8,128)(2,1)S(1)} %pair.1.refs_1_), channel_id=1, source_target_pairs={{0,4},{1,5},{2,6},{3,7},{4,8},{5,9},{6,10},{7,11},{8,12},{9,13},{1... | collective-permute-start | bytes 884744 | tf_op jit(solution)/shard_map/ppermute | solution.py:51
  11.3 6.4 %collective-permute-start.2 = (bf16[64,1152]{1,0:T(8,128)(2,1)S(1)}, bf16[64,1152]{1,0:T(8,128)(2,1)S(1)}, u32[]{:S(2)}, u32[]{:S(2)}) collective-permute-start(bf16[64,1152]{1,0:T(8,128)(2,1)S(1)} %get-tuple-element.42.refs_0_), channel_id=1, source_target_pairs={{0,192},{1,193},{2,194},{3,195},{4,196},{5,197},{6,198},{7,199},{8... | collective-permute-start | bytes 442376 | tf_op jit(solution)/shard_map/ppermute | solution.py:39
  14.0 5.6 %collective-permute-start.1 = (bf16[64,1152]{1,0:T(8,128)(2,1)S(1)}, bf16[64,1152]{1,0:T(8,128)(2,1)S(1)}, u32[]{:S(2)}, u32[]{:S(2)}) collective-permute-start(bf16[64,1152]{1,0:T(8,128)(2,1)S(1)} %get-tuple-element.42.refs_0_), channel_id=1, source_target_pairs={{0,128},{1,129},{2,130},{3,131},{4,132},{5,133},{6,134},{7,135},{8... | collective-permute-start | bytes 442376 | tf_op jit(solution)/shard_map/ppermute | solution.py:39
  14.3 7.0 %collective-permute-start = (bf16[64,1152]{1,0:T(8,128)(2,1)S(1)}, bf16[64,1152]{1,0:T(8,128)(2,1)S(1)}, u32[]{:S(2)}, u32[]{:S(2)}) collective-permute-start(bf16[64,1152]{1,0:T(8,128)(2,1)S(1)} %get-tuple-element.42.refs_0_), channel_id=1, source_target_pairs={{0,64},{1,65},{2,66},{3,67},{4,68},{5,69},{6,70},{7,71},{8,72},{9,... | collective-permute-start | bytes 442376 | tf_op jit(solution)/shard_map/ppermute | solution.py:39
  21.4 10.5 %collective-permute-start.3 = (bf16[264,1152]{1,0:T(8,128)(2,1)S(1)}, bf16[264,1152]{1,0:T(8,128)(2,1)S(1)}, u32[]{:S(2)}, u32[]{:S(2)}) collective-permute-start(bf16[264,1152]{1,0:T(8,128)(2,1)S(1)} %group.1.refs_2_), channel_id=1, source_target_pairs={{0,1},{1,2},{2,3},{3,0},{4,5},{5,6},{6,7},{7,4},{8,9},{9,10},{10,1... | collective-permute-start | bytes 1824776 | tf_op jit(solution)/shard_map/ppermute | solution.py:45
  22.7 9.7 %collective-permute-start.5 = (bf16[264,1152]{1,0:T(8,128)(2,1)S(1)}, bf16[264,1152]{1,0:T(8,128)(2,1)S(1)}, u32[]{:S(2)}, u32[]{:S(2)}) collective-permute-start(bf16[264,1152]{1,0:T(8,128)(2,1)S(1)} %group.1.refs_2_), channel_id=1, source_target_pairs={{0,3},{1,0},{2,1},{3,2},{4,7},{5,4},{6,5},{7,6},{8,11},{9,8},{10,9... | collective-permute-start | bytes 1824776 | tf_op jit(solution)/shard_map/ppermute | solution.py:45
  24.2 15.3 %collective-permute-start.4 = (bf16[264,1152]{1,0:T(8,128)(2,1)S(1)}, bf16[264,1152]{1,0:T(8,128)(2,1)S(1)}, u32[]{:S(2)}, u32[]{:S(2)}) collective-permute-start(bf16[264,1152]{1,0:T(8,128)(2,1)S(1)} %group.1.refs_2_), channel_id=1, source_target_pairs={{0,2},{1,3},{2,0},{3,1},{4,6},{5,7},{6,4},{7,5},{8,10},{9,11},{10,... | collective-permute-start | bytes 1824776 | tf_op jit(solution)/shard_map/ppermute | solution.py:45
  25.8 7.1 %collective-permute-start.10 = (bf16[256,1152]{1,0:T(8,128)(2,1)S(1)}, bf16[256,1152]{1,0:T(8,128)(2,1)S(1)}, u32[]{:S(2)}, u32[]{:S(2)}) collective-permute-start(bf16[256,1152]{1,0:T(8,128)(2,1)S(1)} %get-tuple-element.45.refs_3_.refs_6_.refs_4_), channel_id=1, source_target_pairs={{0,32},{1,33},{2,34},{3,35},{4,36},{5,37},{6,38},{7,39},{8,40},{9,... | collective-permute-start | bytes 1769480 | tf_op jit(solution)/shard_map/ppermute | solution.py:55
  26.6 15.5 %collective-permute-start.9 = (bf16[192,1152]{1,0:T(8,128)(2,1)S(1)}, bf16[192,1152]{1,0:T(8,128)(2,1)S(1)}, u32[]{:S(2)}, u32[]{:S(2)}) collective-permute-start(bf16[192,1152]{1,0:T(8,128)(2,1)S(1)} %get-tuple-element.44), channel_id=1, source_target_pairs={{0,8},{1,9},{2,10},{3,11},{4,12},{5,13},{6,14},{7,15},{8,16},{9,17... | collective-permute-start | bytes 1327112 | tf_op jit(solution)/shard_map/ppermute | solution.py:51
  42.2 2.3 %collective-permute-start.11 = (bf16[192,1152]{1,0:T(8,128)(2,1)S(1)}, bf16[192,1152]{1,0:T(8,128)(2,1)S(1)}, u32[]{:S(2)}, u32[]{:S(2)}) collective-permute-start(bf16[192,1152]{1,0:T(8,128)(2,1)S(1)} %far_mine.1.refs_0_), channel_id=1, source_target_pairs={{0,32},{1,33},{2,34},{3,35},{4,36},{5,37},{6,38},{7,39},{8,40},{9,... | collective-permute-start | bytes 1327112 | tf_op jit(solution)/shard_map/ppermute | solution.py:55
  43.0 5.7 %collective-permute-start.13 = (bf16[256,1152]{1,0:T(8,128)(2,1)S(1)}, bf16[256,1152]{1,0:T(8,128)(2,1)S(1)}, u32[]{:S(2)}, u32[]{:S(2)}) collective-permute-start(bf16[256,1152]{1,0:T(8,128)(2,1)S(1)} %get-tuple-element.56.refs_1_), channel_id=1, source_target_pairs={{0,32},{1,33},{2,34},{3,35},{4,36},{5,37},{6,38},{7,39},{8,40},{9,... | collective-permute-start | bytes 1769480 | tf_op jit(solution)/shard_map/ppermute | solution.py:55
  47.3 1.9 %collective-permute-start.12 = (bf16[192,1152]{1,0:T(8,128)(2,1)S(1)}, bf16[192,1152]{1,0:T(8,128)(2,1)S(1)}, u32[]{:S(2)}, u32[]{:S(2)}) collective-permute-start(bf16[192,1152]{1,0:T(8,128)(2,1)S(1)} %get-tuple-element.65), channel_id=1, source_target_pairs={{0,32},{1,33},{2,34},{3,35},{4,36},{5,37},{6,38},{7,39},{8,40},{9,... | collective-permute-start | bytes 1327112 | tf_op jit(solution)/shard_map/ppermute | solution.py:55
  49.2 14.0 %collective-permute-start.17 = (bf16[192,1152]{1,0:T(8,128)(2,1)S(1)}, bf16[192,1152]{1,0:T(8,128)(2,1)S(1)}, u32[]{:S(2)}, u32[]{:S(2)}) collective-permute-start(bf16[192,1152]{1,0:T(8,128)(2,1)S(1)} %step1.1.refs_7_), channel_id=1, source_target_pairs={{0,24},{1,25},{2,26},{3,27},{4,28},{5,29},{6,30},{7,31},{8,0},{9,1... | collective-permute-start | bytes 1327112 | tf_op jit(solution)/shard_map/ppermute | solution.py:51
  52.6 14.6 %collective-permute-start.14 = (bf16[264,1152]{1,0:T(8,128)(2,1)S(1)}, bf16[264,1152]{1,0:T(8,128)(2,1)S(1)}, u32[]{:S(2)}, u32[]{:S(2)}) collective-permute-start(bf16[264,1152]{1,0:T(8,128)(2,1)S(1)} %image1.1.refs_2_), channel_id=1, source_target_pairs={{0,3},{1,0},{2,1},{3,2},{4,7},{5,4},{6,5},{7,6},{8,11},{9,8},{10,9... | collective-permute-start | bytes 1824776 | tf_op jit(solution)/shard_map/ppermute | solution.py:45
  55.8 11.4 %collective-permute-start.15 = (bf16[264,1152]{1,0:T(8,128)(2,1)S(1)}, bf16[264,1152]{1,0:T(8,128)(2,1)S(1)}, u32[]{:S(2)}, u32[]{:S(2)}) collective-permute-start(bf16[264,1152]{1,0:T(8,128)(2,1)S(1)} %image2.1.refs_7_), channel_id=1, source_target_pairs={{0,2},{1,3},{2,0},{3,1},{4,6},{5,7},{6,4},{7,5},{8,10},{9,11},{10,... | collective-permute-start | bytes 1824776 | tf_op jit(solution)/shard_map/ppermute | solution.py:45
  55.9 17.0 %collective-permute-start.16 = (bf16[264,1152]{1,0:T(8,128)(2,1)S(1)}, bf16[264,1152]{1,0:T(8,128)(2,1)S(1)}, u32[]{:S(2)}, u32[]{:S(2)}) collective-permute-start(bf16[264,1152]{1,0:T(8,128)(2,1)S(1)} %image3.1.refs_7_), channel_id=1, source_target_pairs={{0,1},{1,2},{2,3},{3,0},{4,5},{5,6},{6,7},{7,4},{8,9},{9,10},{10,1... | collective-permute-start | bytes 1824776 | tf_op jit(solution)/shard_map/ppermute | solution.py:45
  63.4 13.5 %collective-permute-start.22 = (bf16[128,1152]{1,0:T(8,128)(2,1)S(1)}, bf16[128,1152]{1,0:T(8,128)(2,1)S(1)}, u32[]{:S(2)}, u32[]{:S(2)}) collective-permute-start(bf16[128,1152]{1,0:T(8,128)(2,1)S(1)} %get-tuple-element.76), channel_id=1, source_target_pairs={{0,24},{1,25},{2,26},{3,27},{4,28},{5,29},{6,30},{7,31},{8,0},{9,1... | collective-permute-start | bytes 884744 | tf_op jit(solution)/shard_map/ppermute | solution.py:51
  65.6 13.3 %collective-permute-start.21 = (bf16[128,1152]{1,0:T(8,128)(2,1)S(1)}, bf16[128,1152]{1,0:T(8,128)(2,1)S(1)}, u32[]{:S(2)}, u32[]{:S(2)}) collective-permute-start(bf16[128,1152]{1,0:T(8,128)(2,1)S(1)} %get-tuple-element.68.refs_5_), channel_id=1, source_target_pairs={{0,28},{1,29},{2,30},{3,31},{4,0},{5,1},{6,2},{7,3},{8,4},{9,5},{1... | collective-permute-start | bytes 884744 | tf_op jit(solution)/shard_map/ppermute | solution.py:51
  73.3 10.5 %copy-start = (bf16[64,1152]{1,0:T(8,128)(2,1)S(1)}, bf16[64,1152]{1,0:T(8,128)(2,1)}, u32[]{:S(2)}) copy-start(bf16[64,1152]{1,0:T(8,128)(2,1)} %refs_5_.1) | copy-start | bytes 442372
  73.3 10.5 %copy-start.1 = (bf16[64,1152]{1,0:T(8,128)(2,1)S(1)}, bf16[64,1152]{1,0:T(8,128)(2,1)}, u32[]{:S(2)}) copy-start(bf16[64,1152]{1,0:T(8,128)(2,1)} %refs_11_.1) | copy-start | bytes 442372
  73.3 7.0 %collective-permute-start.18 = (bf16[72,1152]{1,0:T(8,128)(2,1)S(1)}, bf16[72,1152]{1,0:T(8,128)(2,1)S(1)}, u32[]{:S(2)}, u32[]{:S(2)}) collective-permute-start(bf16[72,1152]{1,0:T(8,128)(2,1)S(1)} %get-tuple-element.71), channel_id=1, source_target_pairs={{0,192},{1,193},{2,194},{3,195},{4,196},{5,197},{6,198},{7,199},{8... | collective-permute-start | bytes 497672 | tf_op jit(solution)/shard_map/ppermute | solution.py:39
  76.3 6.0 %collective-permute-start.19 = (bf16[72,1152]{1,0:T(8,128)(2,1)S(1)}, bf16[72,1152]{1,0:T(8,128)(2,1)S(1)}, u32[]{:S(2)}, u32[]{:S(2)}) collective-permute-start(bf16[72,1152]{1,0:T(8,128)(2,1)S(1)} %get-tuple-element.72), channel_id=1, source_target_pairs={{0,128},{1,129},{2,130},{3,131},{4,132},{5,133},{6,134},{7,135},{8... | collective-permute-start | bytes 497672 | tf_op jit(solution)/shard_map/ppermute | solution.py:39
  76.3 7.5 %collective-permute-start.20 = (bf16[72,1152]{1,0:T(8,128)(2,1)S(1)}, bf16[72,1152]{1,0:T(8,128)(2,1)S(1)}, u32[]{:S(2)}, u32[]{:S(2)}) collective-permute-start(bf16[72,1152]{1,0:T(8,128)(2,1)S(1)} %get-tuple-element.73.refs_3_), channel_id=1, source_target_pairs={{0,64},{1,65},{2,66},{3,67},{4,68},{5,69},{6,70},{7,71},{8,72},{9,... | collective-permute-start | bytes 497672 | tf_op jit(solution)/shard_map/ppermute | solution.py:39
  78.9 4.8 %collective-permute-start.23 = (bf16[64,1152]{1,0:T(8,128)(2,1)S(1)}, bf16[64,1152]{1,0:T(8,128)(2,1)S(1)}, u32[]{:S(2)}, u32[]{:S(2)}) collective-permute-start(bf16[64,1152]{1,0:T(8,128)(2,1)S(1)} %step3.1), channel_id=1, source_target_pairs={{0,32},{1,33},{2,34},{3,35},{4,36},{5,37},{6,38},{7,39},{8,40},{9,... | collective-permute-start | bytes 442376 | tf_op jit(solution)/shard_map/ppermute | solution.py:55

commit v6 on v5

--- a/solution.py
+++ b/solution.py
@@ -135,12 +135,6 @@
     return total
 
 
-def mine_body(scale_ref, bias_ref, img_ref, txt_ref, coeff_ref, loss_ref):
-    weight, softplus = entry(img_ref[:256, :], txt_ref[...], scale_ref[0], bias_ref[0])
-    coeff_ref[...] = weight
-    loss_ref[...] = fold(softplus)
-
-
 def texts(coeffs, imgs, lo, hi):
     total = None
     for c, s in zip(coeffs, imgs):
@@ -164,58 +158,80 @@
     return total
 
 
-def other_body(scale_ref, bias_ref, i0, i1, i3, txt_ref, l0, l1, l3, o0, o1, o3, loss):
-    for n, (i, o, l) in enumerate(((i0, o0, l0), (i1, o1, l1), (i3, o3, l3))):
-        loss[256 * n : 256 * (n + 1), :] = tile(
-            i, txt_ref, o, l[...], scale_ref[0], bias_ref[0], n == 0
-        )
-
-
-def last_body(scale_ref, bias_ref, i0, i1, i2, i3, near, other, m0, m1, m3, o0, o1, o3, m2, o2, loss, keep, send, pair):
+def near_tile(img, mine_ref, other_ref, coeff_ref, total, scale, bias, own=False):
+    weight, softplus = entry(img[:256, :], mine_ref[...], scale, bias)
+    coeff_ref[:, :256] = weight
+    total = total + fold(softplus)
+    return tile(img, other_ref, coeff_ref.at[:, 256:], total, scale, bias, own)
+
+
+def near_body(own, scale_ref, bias_ref, img, mine, other, coeff, loss):
+    zero = jnp.zeros((256, 128), F32)
+    loss[...] = near_tile(img, mine, other, coeff, zero, scale_ref[0], bias_ref[0], own)
+
+
+def loss_row(total):
+    column = jnp.broadcast_to(jnp.sum(total, axis=1, keepdims=True), (256, 128))
+    return jnp.transpose(column)[:8, :]
+
+
+def image(cn, cf, mine, other, far):
+    g = jnp.dot(cf[...], far[...], preferred_element_type=F32)
+    g = g + jnp.dot(cn[:, :256], mine[...], preferred_element_type=F32)
+    return g + jnp.dot(cn[:, 256:], other[...], preferred_element_type=F32)
+
+
+def send_image(out, g, loss):
+    out[:256, :] = g.astype(BF16)
+    out[256:, :] = jnp.zeros((8, g.shape[1]), BF16)
+    out[256:, :256] = loss_rows(loss)
+
+
+def far_image_body(scale_ref, bias_ref, img, mine, other, far, cn, loss, cf, out):
+    total = tile(img, far, cf, loss[...], scale_ref[0], bias_ref[0])
+    send_image(out, image(cn, cf, mine, other, far), loss_row(total))
+
+
+def far_own_body(scale_ref, bias_ref, img, far, loss, cf, row):
+    row[...] = loss_row(tile(img, far, cf, loss[...], scale_ref[0], bias_ref[0]))
+
+
+def last_body(scale_ref, bias_ref, img, mine, other, far, cn, cf, row):
     scale, bias = scale_ref[0], bias_ref[0]
-    imgs = (i0, i1, i2, i3)
-    weight, softplus = entry(i2[:256, :], near[...], scale, bias)
-    m2[...] = weight
-    loss[...] = tile(i2, other, o2, fold(softplus), scale, bias)
-    g = texts((o0, o1, o2, o3), imgs, 0, 384)
-    send[...] = g[:256, :].astype(BF16)
-    pair[...] = g[256:, :]
-    keep[...] = texts((m0, m1, m2, m3), imgs, 0, 256)
-
-
-def far_body(scale_ref, bias_ref, i0, i1, i2, i3, txt_ref, l013, l2, c0, c1, c2, c3, keep, send, loss):
-    imgs, coeffs = (i0, i1, i2, i3), (c0, c1, c2, c3)
-    before = (l013[:256, :], l013[256:512, :], l2[...], l013[512:, :])
-    for k in range(4):
-        total = tile(imgs[k], txt_ref, coeffs[k], before[k], scale_ref[0], bias_ref[0])
-        column = jnp.broadcast_to(jnp.sum(total, axis=1, keepdims=True), (256, 128))
-        loss[:, 256 * k : 256 * (k + 1)] = jnp.transpose(column)[:8, :]
-    g = texts(coeffs, imgs, 0, 384)
-    keep[...] = g[:192, :]
-    send[...] = g[192:, :].astype(BF16)
-
-
-def image_body(k, cf, cm, co, far, mine, other, loss, out):
-    g = jnp.dot(cf[...], far[...], preferred_element_type=F32)
-    g = g + jnp.dot(cm[...], mine[...], preferred_element_type=F32)
-    g = g + jnp.dot(co[...], other[...], preferred_element_type=F32)
-    if k == 0:
-        out[...] = g
-    else:
-        out[:256, :] = g.astype(BF16)
-        out[256:, :] = jnp.zeros((8, g.shape[1]), BF16)
-        out[256:, :256] = loss_rows(loss[:, 256 * k : 256 * (k + 1)])
-
-
-def merge_img_body(g_ref, l_ref, r1, r2, r3, own_ref, own_loss, m1, m2, m3):
-    loss = l_ref[:, :256] + (
-        loss_sum(r1[256:, :256]) + loss_sum(r2[256:, :256]) + loss_sum(r3[256:, :256])
-    )
+    total = near_tile(img, mine, other, cn, jnp.zeros((256, 128), F32), scale, bias)
+    row[...] = loss_row(tile(img, far, cf, total, scale, bias))
+
+
+def near_part_body(c0, c1, c3, i0, i1, i3, part):
+    part[...] = texts((c0, c1, c3), (i0, i1, i3), 0, 640)
+
+
+def texts_body(c0, c1, c2, c3, n2, i0, i1, i2, i3, part, keep_a, send_a, keep_b, send_b, pair):
+    g = texts((c0, c1, c2, c3), (i0, i1, i2, i3), 0, 384)
+    keep_a[...] = g[:192, :]
+    send_a[...] = g[192:, :].astype(BF16)
+    g = part[...] + texts((n2,), (i2,), 0, 640)
+    keep_b[...] = g[:256, :]
+    send_b[...] = g[256:512, :].astype(BF16)
+    pair[...] = g[512:, :]
+
+
+def last_image_body(cn, cf, mine, other, far, row, out):
+    send_image(out, image(cn, cf, mine, other, far), row[...])
+
+
+def own_image_body(cn, cf, mine, other, far, row, r1, r3, out, loss):
+    out[...] = image(cn, cf, mine, other, far) + (up(r1, 0, 256) + up(r3, 0, 256))
+    loss[...] = row[...] + (loss_sum(r1[256:, :256]) + loss_sum(r3[256:, :256]))
+
+
+def merge_img_body(g_ref, l_ref, r2, own_ref, own_loss, m1, m2, m3):
+    loss = l_ref[...] + loss_sum(r2[256:, :256])
     own_loss[...] = loss
     marks = loss_rows(loss)
     for j, out in enumerate((own_ref, m1, m2, m3)):
         lo, hi = U * j, U * (j + 1)
-        total = g_ref[lo:hi, :] + (up(r1, lo, hi) + up(r2, lo, hi) + up(r3, lo, hi))
+        total = g_ref[lo:hi, :] + up(r2, lo, hi)
         out[:U, :] = total.astype(out.dtype)
         if j:
             out[U:, :] = jnp.zeros((8, total.shape[1]), BF16)
@@ -294,57 +310,61 @@
     near_other = swap(near_mine)
 
     sc = (scale, bias)
-    mine_c, mine_l, other_c, last = [None] * 4, [None] * 4, [None] * 4, ()
+    other = pack("other_texts", 384, (near_other, pair))
+    near_c, near_l, last = [None] * 4, [None] * 4, ()
     for k in (0, 1, 3):
-        mine_c[k], mine_l[k] = call(
-            f"mine{k}", mine_body, [shape(256, 256), shape(256, 128, dtype=F32)],
-            (groups[k], near_mine), sc, last,
+        near_c[k], near_l[k] = call(
+            f"near{k}", functools.partial(near_body, k == 0), [shape(256, 640), shape(256, 128, dtype=F32)],
+            (groups[k], near_mine, other), sc, last,
         )
-        last = (mine_l[k],)
-    other = pack("other_texts", 384, (near_other, pair), last)
-    other_c[0], other_c[1], other_c[3], near_loss = call(
-        "other", other_body, [shape(256, 384)] * 3 + [shape(768, 128, dtype=F32)],
-        (groups[0], groups[1], groups[3], other, mine_l[0], mine_l[1], mine_l[3]), sc,
-    )
-    mine_c[2], other_c[2], last_loss, keep_b, send_b, own_pair = call(
-        "last", last_body,
-        [shape(256, 256), shape(256, 384), shape(256, 128, dtype=F32)]
-        + [shape(256, d, dtype=F32), shape(256, d), shape(128, d, dtype=F32)],
-        (*groups, near_mine, other, mine_c[0], mine_c[1], mine_c[3], other_c[0], other_c[1], other_c[3]),
-        sc, (near_loss,),
-    )
+        last = (near_l[k],)
+    part = call(
+        "near_part", near_part_body, [shape(640, d, dtype=F32)],
+        (near_c[0], near_c[1], near_c[3], groups[0], groups[1], groups[3]), (), last,
+    )[0]
+    far_mine = pack("far_mine", 192, (far_got,), (part,))
+    far = pack("far_texts", 384, (far_mine, swap(far_mine)))
+    far_c, sent, last = [None] * 4, [None] * 4, ()
+    for k in (1, 3):
+        far_c[k], sent[k] = call(
+            f"far_image{k}", far_image_body, [shape(256, 384), shape(264, d)],
+            (groups[k], near_mine, other, far, near_c[k], near_l[k]), sc, last,
+        )
+        last = (sent[k],)
+    r1, r3 = second(sent[1], -1), second(sent[3], -3)
+    far_c[0], row0 = call(
+        "far_own", far_own_body, [shape(256, 384), shape(8, 256, dtype=F32)],
+        (groups[0], far, near_l[0]), sc, last,
+    )
+    near_c[2], far_c[2], row2 = call(
+        "last", last_body, [shape(256, 640), shape(256, 384), shape(8, 256, dtype=F32)],
+        (groups[2], near_mine, other, far), sc, (row0,),
+    )
+    keep_a, send_a, keep_b, send_b, own_pair = call(
+        "texts_grad", texts_body,
+        [shape(192, d, dtype=F32), shape(192, d), shape(256, d, dtype=F32), shape(256, d), shape(128, d, dtype=F32)],
+        (*far_c, near_c[2], *groups, part),
+    )
+    got_a = swap(send_a)
+    sent[2] = call(
+        "last_image", last_image_body, [shape(264, d)],
+        (near_c[2], far_c[2], near_mine, other, far, row2), (), (send_a,),
+    )[0]
+    r2 = second(sent[2], -2)
+
+    z1 = call("step1", step1_body, [shape(192, d)], (keep_a, got_a), (), (sent[2],))[0]
+    w = ring(z1, -2)
     got_b = swap(send_b)
-    far_mine = pack("far_mine", 192, (far_got,), (send_b,))
-    far = pack("far_texts", 384, (far_mine, swap(far_mine)))
-    *far_c, keep_a, send_a, loss = call(
-        "far", far_body,
-        [shape(256, 384)] * 4 + [shape(192, d, dtype=F32), shape(192, d), shape(8, 1024, dtype=F32)],
-        (*groups, far, near_loss, last_loss), sc,
-    )
-    got_a = swap(send_a)
-
-    def image(k, after):
-        out = shape(256, d, dtype=F32) if k == 0 else shape(264, d)
-        return call(
-            f"image{k}", functools.partial(image_body, k), [out],
-            (far_c[k], mine_c[k], other_c[k], far, near_mine, other, loss), (), after,
-        )[0]
-
-    p1 = image(1, ())
-    r1 = second(p1, -1)
-    z1 = call("step1", step1_body, [shape(192, d)], (keep_a, got_a), (), (p1, got_b))[0]
-    w = ring(z1, -2)
-    p3 = image(3, (z1,))
-    r3 = second(p3, -3)
-    p2 = image(2, (p3,))
-    r2 = second(p2, -2)
-    p0 = image(0, (p2,))
+    p0, loss = call(
+        "own_image", own_image_body, [shape(256, d, dtype=F32), shape(8, 256, dtype=F32)],
+        (near_c[0], far_c[0], near_mine, other, far, row0, r1, r3), (), (z1,),
+    )
     two, one = call("step2", step2_body, [shape(128, d)] * 2, (keep_b, got_b, w), (), (p0,))
     v2, v1 = ring(two, -2), ring(one, -1)
     own_img, own_loss, m1, m2, m3 = call(
         "merge_img", merge_img_body,
         [shape(rows, d, dtype=F32), shape(8, 256, dtype=F32)] + [shape(rows + 8, d)] * 3,
-        (p0, loss, r1, r2, r3), (), (one,),
+        (p0, loss, r2), (), (one,),
     )
     q1, q3, q2 = first(m1, -1), first(m3, -3), first(m2, -2)
     z3 = call("step3", step3_body, [shape(64, d)], (own_pair, v1, v2), (), (m3,))[0]

time: 85.8 us -> 86 us (level); the launches traced: 84.8 us -> 85.9 us
  starting transfers between devices: 33.4 us -> 42.1 us
  waiting for transfers between devices: 33.9 us -> 26.4 us
    ppermute x6, waiting for transfers between devices: 12.4 us -> 3.77 us  [second(): lax.ppermute(a, AXES, permutation(lambda x, c, z, y: (x + s, c, z, y) if...]
    ppermute x6, waiting for transfers between devices: 7.67 us -> 12.8 us  [ring(): lax.ppermute(a, AXES, permutation(lambda x, c, z, y: (x, c, z - s if c el...]
    ppermute x6, starting transfers between devices: 5.66 us -> 10.4 us  [swap(): lax.ppermute(a, AXES, permutation(lambda x, c, z, y: (x, 1 - c, z, y)))]
    ppermute x6, waiting for transfers between devices: 11.1 us -> 6.33 us  [first(): lax.ppermute(a, AXES, permutation(lambda x, c, z, y: (x, c, z, y + s) if...]
    ppermute x6, starting transfers between devices: 6.17 us -> 8.33 us  [second(): lax.ppermute(a, AXES, permutation(lambda x, c, z, y: (x + s, c, z, y) if...]
    ppermute x6, starting transfers between devices: 7.41 us -> 9.16 us  [first(): lax.ppermute(a, AXES, permutation(lambda x, c, z, y: (x, c, z, y + s) if...]
    pallas_call x22 -> x23, Pallas kernels: 15.3 us -> 15.3 us  [call(): pl.pallas_call(kernel, out_shape=outs, in_specs=[SMEM] * len(scalars) + (...]
  transfers between devices with their start and end apart: 24 -> 24, of which waited for: 14 -> 12; matrix products, arithmetic and copies ran while one was open for 0% -> 0% of each run, Pallas kernels for 15% -> 12%
where the time goes in v6:
time: 86 us; the launch traced here: 85.9 us
  starting transfers between devices  42.1 us (49%)
  waiting for transfers between devices  26.4 us (31%)
  Pallas kernels  15.3 us (18%)
  between operations  2.12 us (2%)
    pallas_call x23, Pallas kernels, call(): pl.pallas_call(kernel, out_shape=outs, in_specs=[SMEM] * len(scalars) + (...  15.3 us
    ppermute x6, starting transfers between devices, ring(): lax.ppermute(a, AXES, permutation(lambda x, c, z, y: (x, c, z - s if c el...  14.3 us
    ppermute x6, waiting for transfers between devices, ring(): lax.ppermute(a, AXES, permutation(lambda x, c, z, y: (x, c, z - s if c el...  12.8 us
    ppermute x6, starting transfers between devices, swap(): lax.ppermute(a, AXES, permutation(lambda x, c, z, y: (x, 1 - c, z, y)))  10.4 us
    ppermute x6, starting transfers between devices, first(): lax.ppermute(a, AXES, permutation(lambda x, c, z, y: (x, c, z, y + s) if...  9.16 us
    ppermute x6, starting transfers between devices, second(): lax.ppermute(a, AXES, permutation(lambda x, c, z, y: (x + s, c, z, y) if...  8.33 us
    ppermute x6, waiting for transfers between devices, first(): lax.ppermute(a, AXES, permutation(lambda x, c, z, y: (x, c, z, y + s) if...  6.33 us
    ppermute x6, waiting for transfers between devices, second(): lax.ppermute(a, AXES, permutation(lambda x, c, z, y: (x + s, c, z, y) if...  3.77 us
  transfers between devices with their start and end apart: 24, of which 12 were waited for; matrix products, arithmetic and copies ran while one was open for 0% of the time, Pallas kernels for 12%

profile of v6, /device:TPU:1, one launch (start us, length us, event | category | flops | bytes accessed | tf_op | source)
XLA Modules:
  0.0 85.9 jit_solution(10010870474038659897)
XLA Ops:
  0.6 1.2 %normalize.1 = (bf16[64,1152]{1,0:T(8,128)(2,1)S(1)}, bf16[64,1152]{1,0:T(8,128)(2,1)S(1)}, f32[64,1]{1,0:T(8,128)S(1)}, f32[64,1]{1,0:T(8,128)S(1)}) custom-call(bf16[64,1152]{1,0:T(8,128)(2,1)} %refs_5_.1, bf16[64,1152]{1,0:T(8,128)(2,1)} %refs_11_.1), custom_call_target="tpu_custom_call" | custom-call | flops 1 | bytes 1 | tf_op jit(solution)/shard_map/normalize/pallas_call | solution.py:65
  1.8 3.3 %collective-permute-start.3 = (bf16[64,1152]{1,0:T(8,128)(2,1)S(1)}, bf16[64,1152]{1,0:T(8,128)(2,1)S(1)}, u32[]{:S(2)}, u32[]{:S(2)}) collective-permute-start(bf16[64,1152]{1,0:T(8,128)(2,1)S(1)} %get-tuple-element.42.refs_0_), channel_id=1, source_target_pairs={{0,32},{1,33},{2,34},{3,35},{4,36},{5,37},{6,38},{7,39},{8,40},{9,... | collective-permute-start | bytes 442376 | tf_op jit(solution)/shard_map/ppermute | solution.py:55
  5.1 1.0 %collective-permute-done.3.refs_1_ = bf16[64,1152]{1,0:T(8,128)(2,1)S(1)} collective-permute-done((bf16[64,1152]{1,0:T(8,128)(2,1)S(1)}, bf16[64,1152]{1,0:T(8,128)(2,1)S(1)}, u32[]{:S(2)}, u32[]{:S(2)}) %collective-permute-start.3) | collective-permute-done | bytes 147488 | tf_op jit(solution)/shard_map/ppermute | solution.py:55
  6.2 4.4 %collective-permute-start.5 = (bf16[128,1152]{1,0:T(8,128)(2,1)S(1)}, bf16[128,1152]{1,0:T(8,128)(2,1)S(1)}, u32[]{:S(2)}, u32[]{:S(2)}) collective-permute-start(bf16[128,1152]{1,0:T(8,128)(2,1)S(1)} %pair.1.refs_1_), channel_id=1, source_target_pairs={{0,8},{1,9},{2,10},{3,11},{4,12},{5,13},{6,14},{7,15},{8,16},{9,17... | collective-permute-start | bytes 884744 | tf_op jit(solution)/shard_map/ppermute | solution.py:51
  11.3 2.7 %collective-permute-start.2 = (bf16[64,1152]{1,0:T(8,128)(2,1)S(1)}, bf16[64,1152]{1,0:T(8,128)(2,1)S(1)}, u32[]{:S(2)}, u32[]{:S(2)}) collective-permute-start(bf16[64,1152]{1,0:T(8,128)(2,1)S(1)} %get-tuple-element.41.refs_0_), channel_id=1, source_target_pairs={{0,192},{1,193},{2,194},{3,195},{4,196},{5,197},{6,198},{7,199},{8... | collective-permute-start | bytes 442376 | tf_op jit(solution)/shard_map/ppermute | solution.py:39
  15.0 2.6 %collective-permute-done.2.refs_3_ = bf16[64,1152]{1,0:T(8,128)(2,1)S(1)} collective-permute-done((bf16[64,1152]{1,0:T(8,128)(2,1)S(1)}, bf16[64,1152]{1,0:T(8,128)(2,1)S(1)}, u32[]{:S(2)}, u32[]{:S(2)}) %collective-permute-start.2) | collective-permute-done | bytes 147488 | tf_op jit(solution)/shard_map/ppermute | solution.py:39
  17.7 1.9 %collective-permute-done.1.refs_2_ = bf16[64,1152]{1,0:T(8,128)(2,1)S(1)} collective-permute-done((bf16[64,1152]{1,0:T(8,128)(2,1)S(1)}, bf16[64,1152]{1,0:T(8,128)(2,1)S(1)}, u32[]{:S(2)}, u32[]{:S(2)}) %collective-permute-start.1) | collective-permute-done | bytes 147488 | tf_op jit(solution)/shard_map/ppermute | solution.py:39
  19.6 1.8 %collective-permute-done.refs_1_ = bf16[64,1152]{1,0:T(8,128)(2,1)S(1)} collective-permute-done((bf16[64,1152]{1,0:T(8,128)(2,1)S(1)}, bf16[64,1152]{1,0:T(8,128)(2,1)S(1)}, u32[]{:S(2)}, u32[]{:S(2)}) %collective-permute-start) | collective-permute-done | bytes 147488 | tf_op jit(solution)/shard_map/ppermute | solution.py:39
  21.4 1.3 %collective-permute-start.8 = (bf16[264,1152]{1,0:T(8,128)(2,1)S(1)}, bf16[264,1152]{1,0:T(8,128)(2,1)S(1)}, u32[]{:S(2)}, u32[]{:S(2)}) collective-permute-start(bf16[264,1152]{1,0:T(8,128)(2,1)S(1)} %group.1.refs_2_.refs_3_.refs_5_), channel_id=1, source_target_pairs={{0,1},{1,2},{2,3},{3,0},{4,5},{5,6},{6,7},{7,4},{8,9},{9,10},{10,1... | collective-permute-start | bytes 1824776 | tf_op jit(solution)/shard_map/ppermute | solution.py:45
  22.7 1.5 %collective-permute-start.9 = (bf16[264,1152]{1,0:T(8,128)(2,1)S(1)}, bf16[264,1152]{1,0:T(8,128)(2,1)S(1)}, u32[]{:S(2)}, u32[]{:S(2)}) collective-permute-start(bf16[264,1152]{1,0:T(8,128)(2,1)S(1)} %group.1.refs_2_.refs_3_.refs_5_), channel_id=1, source_target_pairs={{0,3},{1,0},{2,1},{3,2},{4,7},{5,4},{6,5},{7,6},{8,11},{9,8},{10,9... | collective-permute-start | bytes 1824776 | tf_op jit(solution)/shard_map/ppermute | solution.py:45
  24.6 1.9 %collective-permute-start.7 = (bf16[192,1152]{1,0:T(8,128)(2,1)S(1)}, bf16[192,1152]{1,0:T(8,128)(2,1)S(1)}, u32[]{:S(2)}, u32[]{:S(2)}) collective-permute-start(bf16[192,1152]{1,0:T(8,128)(2,1)S(1)} %get-tuple-element.45), channel_id=1, source_target_pairs={{0,8},{1,9},{2,10},{3,11},{4,12},{5,13},{6,14},{7,15},{8,16},{9,17... | collective-permute-start | bytes 1327112 | tf_op jit(solution)/shard_map/ppermute | solution.py:51
  29.5 2.5 %collective-permute-done.8.refs_2_.refs_4_.refs_6_ = bf16[264,1152]{1,0:T(8,128)(2,1)S(1)} collective-permute-done((bf16[264,1152]{1,0:T(8,128)(2,1)S(1)}, bf16[264,1152]{1,0:T(8,128)(2,1)S(1)}, u32[]{:S(2)}, u32[]{:S(2)}) %collective-permute-start.8) | collective-permute-done | bytes 608288 | tf_op jit(solution)/shard_map/ppermute | solution.py:45
  33.5 1.5 %near_part.1.refs_1_.refs_9_ = f32[640,1152]{1,0:T(8,128)S(1)} custom-call(bf16[256,640]{1,0:T(8,128)(2,1)S(1)} %get-tuple-element.44.refs_0_, bf16[256,640]{1,0:T(8,128)(2,1)S(1)} %get-tuple-element.47.refs_1_.refs_6_, bf16[256,640]{1,0:T(8,128)(2,1)S(1)} %get-tuple-element.49.refs_2_.refs_6_, bf16[264,1152]{1,0:T(8,128)(2,1)S(1)} %group.1.refs_2_.refs_3_.refs_5_, ...), custom_call_target="tpu_custom_call" | custom-call | flops 1 | bytes 1 | tf_op jit(solution)/shard_map/near_part/pallas_call | solution.py:65
  35.4 4.0 %collective-permute-start.10 = (bf16[192,1152]{1,0:T(8,128)(2,1)S(1)}, bf16[192,1152]{1,0:T(8,128)(2,1)S(1)}, u32[]{:S(2)}, u32[]{:S(2)}) collective-permute-start(bf16[192,1152]{1,0:T(8,128)(2,1)S(1)} %far_mine.1.refs_0_), channel_id=1, source_target_pairs={{0,32},{1,33},{2,34},{3,35},{4,36},{5,37},{6,38},{7,39},{8,40},{9,... | collective-permute-start | bytes 1327112 | tf_op jit(solution)/shard_map/ppermute | solution.py:55
  39.3 1.4 %collective-permute-done.10.refs_1_ = bf16[192,1152]{1,0:T(8,128)(2,1)S(1)} collective-permute-done((bf16[192,1152]{1,0:T(8,128)(2,1)S(1)}, bf16[192,1152]{1,0:T(8,128)(2,1)S(1)}, u32[]{:S(2)}, u32[]{:S(2)}) %collective-permute-start.10) | collective-permute-done | bytes 442400 | tf_op jit(solution)/shard_map/ppermute | solution.py:55
  40.8 1.4 %far_image1.1 = (bf16[256,384]{1,0:T(8,128)(2,1)S(1)}, bf16[264,1152]{1,0:T(8,128)(2,1)S(1)}) custom-call(f32[1]{0:T(128)S(6)} %copy.7.refs_0_, f32[1]{0:T(128)S(6)} %copy.8.refs_1_, bf16[264,1152]{1,0:T(8,128)(2,1)S(1)} %collective-permute-done.8.refs_2_.refs_4_.refs_6_, bf16[256,1152]{1,0:T(8,128)(2,1)S(1)} %get-tuple-element.43.refs_3_.refs_2_, ...), custom_call_target="tpu_custom_call" | custom-call | flops 1 | bytes 1 | tf_op jit(solution)/shard_map/far_image1/pallas_call | solution.py:65
  42.2 1.4 %far_image3.1 = (bf16[256,384]{1,0:T(8,128)(2,1)S(1)}, bf16[264,1152]{1,0:T(8,128)(2,1)S(1)}) custom-call(f32[1]{0:T(128)S(6)} %copy.7.refs_0_, f32[1]{0:T(128)S(6)} %copy.8.refs_1_, bf16[264,1152]{1,0:T(8,128)(2,1)S(1)} %collective-permute-done.9.refs_2_.refs_5_.refs_8_, bf16[256,1152]{1,0:T(8,128)(2,1)S(1)} %get-tuple-element.43.refs_3_.refs_2_, ...), custom_call_target="tpu_custom_call" | custom-call | flops 1 | bytes 1 | tf_op jit(solution)/shard_map/far_image3/pallas_call | solution.py:65
  44.4 1.3 %last.1 = (bf16[256,640]{1,0:T(8,128)(2,1)S(1)}, bf16[256,384]{1,0:T(8,128)(2,1)S(1)}, f32[8,256]{1,0:T(8,128)S(1)}) custom-call(f32[1]{0:T(128)S(6)} %copy.7.refs_0_, f32[1]{0:T(128)S(6)} %copy.8.refs_1_, bf16[264,1152]{1,0:T(8,128)(2,1)S(1)} %collective-permute-done.13.refs_2_.refs_7_, bf16[256,1152]{1,0:T(8,128)(2,1)S(1)} %get-tuple-element.43.refs_3_.refs_2_, ...), custom_call_target="tpu_custom_call" | custom-call | flops 1 | bytes 1 | tf_op jit(solution)/shard_map/last/pallas_call | solution.py:65
  45.6 1.7 %texts_grad.1 = (f32[192,1152]{1,0:T(8,128)S(1)}, bf16[192,1152]{1,0:T(8,128)(2,1)S(1)}, f32[256,1152]{1,0:T(8,128)S(1)}, bf16[256,1152]{1,0:T(8,128)(2,1)S(1)}, f32[128,1152]{1,0:T(8,128)S(1)}) custom-call(bf16[256,384]{1,0:T(8,128)(2,1)S(1)} %get-tuple-element.53.refs_0_.refs_1_, bf16[256,384]{1,0:T(8,128)(2,1)S(1)} %get-tuple-element.55.refs_1_, ...), custom_call_target="tpu_custom_call" | custom-call | flops 1 | bytes 1 | tf_op jit(solution)/shard_map/texts_grad/pallas_call | solution.py:65
  48.4 3.7 %collective-permute-start.11 = (bf16[264,1152]{1,0:T(8,128)(2,1)S(1)}, bf16[264,1152]{1,0:T(8,128)(2,1)S(1)}, u32[]{:S(2)}, u32[]{:S(2)}) collective-permute-start(bf16[264,1152]{1,0:T(8,128)(2,1)S(1)} %get-tuple-element.51.refs_8_), channel_id=1, source_target_pairs={{0,3},{1,0},{2,1},{3,2},{4,7},{5,4},{6,5},{7,6},{8,11},{9,8},{10,9... | collective-permute-start | bytes 1824776 | tf_op jit(solution)/shard_map/ppermute | solution.py:45
  52.1 1.4 %collective-permute-start.16 = (bf16[256,1152]{1,0:T(8,128)(2,1)S(1)}, bf16[256,1152]{1,0:T(8,128)(2,1)S(1)}, u32[]{:S(2)}, u32[]{:S(2)}) collective-permute-start(bf16[256,1152]{1,0:T(8,128)(2,1)S(1)} %get-tuple-element.65), channel_id=1, source_target_pairs={{0,32},{1,33},{2,34},{3,35},{4,36},{5,37},{6,38},{7,39},{8,40},{9,... | collective-permute-start | bytes 1769480 | tf_op jit(solution)/shard_map/ppermute | solution.py:55
  54.6 3.4 %collective-permute-start.17 = (bf16[192,1152]{1,0:T(8,128)(2,1)S(1)}, bf16[192,1152]{1,0:T(8,128)(2,1)S(1)}, u32[]{:S(2)}, u32[]{:S(2)}) collective-permute-start(bf16[192,1152]{1,0:T(8,128)(2,1)S(1)} %step1.1.refs_8_), channel_id=1, source_target_pairs={{0,24},{1,25},{2,26},{3,27},{4,28},{5,29},{6,30},{7,31},{8,0},{9,1... | collective-permute-start | bytes 1327112 | tf_op jit(solution)/shard_map/ppermute | solution.py:51
  58.5 1.3 %collective-permute-done.12.refs_7_ = bf16[264,1152]{1,0:T(8,128)(2,1)S(1)} collective-permute-done((bf16[264,1152]{1,0:T(8,128)(2,1)S(1)}, bf16[264,1152]{1,0:T(8,128)(2,1)S(1)}, u32[]{:S(2)}, u32[]{:S(2)}) %collective-permute-start.12) | collective-permute-done | bytes 608288 | tf_op jit(solution)/shard_map/ppermute | solution.py:45
  60.8 6.5 %collective-permute-done.17.refs_2_ = bf16[192,1152]{1,0:T(8,128)(2,1)S(1)} collective-permute-done((bf16[192,1152]{1,0:T(8,128)(2,1)S(1)}, bf16[192,1152]{1,0:T(8,128)(2,1)S(1)}, u32[]{:S(2)}, u32[]{:S(2)}) %collective-permute-start.17) | collective-permute-done | bytes 442400 | tf_op jit(solution)/shard_map/ppermute | solution.py:51
  67.5 1.6 %collective-permute-start.22 = (bf16[128,1152]{1,0:T(8,128)(2,1)S(1)}, bf16[128,1152]{1,0:T(8,128)(2,1)S(1)}, u32[]{:S(2)}, u32[]{:S(2)}) collective-permute-start(bf16[128,1152]{1,0:T(8,128)(2,1)S(1)} %get-tuple-element.74), channel_id=1, source_target_pairs={{0,24},{1,25},{2,26},{3,27},{4,28},{5,29},{6,30},{7,31},{8,0},{9,1... | collective-permute-start | bytes 884744 | tf_op jit(solution)/shard_map/ppermute | solution.py:51
  69.2 2.2 %collective-permute-start.21 = (bf16[128,1152]{1,0:T(8,128)(2,1)S(1)}, bf16[128,1152]{1,0:T(8,128)(2,1)S(1)}, u32[]{:S(2)}, u32[]{:S(2)}) collective-permute-start(bf16[128,1152]{1,0:T(8,128)(2,1)S(1)} %get-tuple-element.66.refs_3_), channel_id=1, source_target_pairs={{0,28},{1,29},{2,30},{3,31},{4,0},{5,1},{6,2},{7,3},{8,4},{9,5},{1... | collective-permute-start | bytes 884744 | tf_op jit(solution)/shard_map/ppermute | solution.py:51
  71.5 3.3 %collective-permute-start.18 = (bf16[72,1152]{1,0:T(8,128)(2,1)S(1)}, bf16[72,1152]{1,0:T(8,128)(2,1)S(1)}, u32[]{:S(2)}, u32[]{:S(2)}) collective-permute-start(bf16[72,1152]{1,0:T(8,128)(2,1)S(1)} %get-tuple-element.69), channel_id=1, source_target_pairs={{0,192},{1,193},{2,194},{3,195},{4,196},{5,197},{6,198},{7,199},{8... | collective-permute-start | bytes 497672 | tf_op jit(solution)/shard_map/ppermute | solution.py:39
  74.8 1.4 %collective-permute-start.19 = (bf16[72,1152]{1,0:T(8,128)(2,1)S(1)}, bf16[72,1152]{1,0:T(8,128)(2,1)S(1)}, u32[]{:S(2)}, u32[]{:S(2)}) collective-permute-start(bf16[72,1152]{1,0:T(8,128)(2,1)S(1)} %get-tuple-element.70), channel_id=1, source_target_pairs={{0,128},{1,129},{2,130},{3,131},{4,132},{5,133},{6,134},{7,135},{8... | collective-permute-start | bytes 497672 | tf_op jit(solution)/shard_map/ppermute | solution.py:39
  76.9 1.9 %collective-permute-done.22.refs_2_.refs_9_ = bf16[128,1152]{1,0:T(8,128)(2,1)S(1)} collective-permute-done((bf16[128,1152]{1,0:T(8,128)(2,1)S(1)}, bf16[128,1152]{1,0:T(8,128)(2,1)S(1)}, u32[]{:S(2)}, u32[]{:S(2)}) %collective-permute-start.22) | collective-permute-done | bytes 294944 | tf_op jit(solution)/shard_map/ppermute | solution.py:51
  78.8 4.1 %collective-permute-done.21.refs_1_.refs_8_ = bf16[128,1152]{1,0:T(8,128)(2,1)S(1)} collective-permute-done((bf16[128,1152]{1,0:T(8,128)(2,1)S(1)}, bf16[128,1152]{1,0:T(8,128)(2,1)S(1)}, u32[]{:S(2)}, u32[]{:S(2)}) %collective-permute-start.21) | collective-permute-done | bytes 294944 | tf_op jit(solution)/shard_map/ppermute | solution.py:51
  83.9 1.0 %collective-permute-done.23.refs_10_ = bf16[64,1152]{1,0:T(8,128)(2,1)S(1)} collective-permute-done((bf16[64,1152]{1,0:T(8,128)(2,1)S(1)}, bf16[64,1152]{1,0:T(8,128)(2,1)S(1)}, u32[]{:S(2)}, u32[]{:S(2)}) %collective-permute-start.23) | collective-permute-done | bytes 147488 | tf_op jit(solution)/shard_map/ppermute | solution.py:55
  84.9 1.1 %finish.1 = (f32[64,1152]{1,0:T(8,128)}, f32[64,1152]{1,0:T(8,128)}, f32[1,64]{1,0:T(1,128)}) custom-call(f32[64,1152]{1,0:T(8,128)S(1)} %get-tuple-element.67.refs_0_, f32[8,256]{1,0:T(8,128)S(1)} %get-tuple-element.68.refs_1_, bf16[72,1152]{1,0:T(8,128)(2,1)S(1)} %collective-permute-done.18.refs_2_, bf16[72,1152]{1,0:T(8,128)(2,1)S(1)} %collective-permute-done.19.refs_3_, ...), custom_call_target="tpu_custom_call" | custom-call | flops 1 | bytes 1 | tf_op jit(solution)/shard_map/finish/pallas_call | solution.py:65
  (43 shorter events, 12.3 us)
Async XLA Ops:
  1.8 4.3 %collective-permute-start.3 = (bf16[64,1152]{1,0:T(8,128)(2,1)S(1)}, bf16[64,1152]{1,0:T(8,128)(2,1)S(1)}, u32[]{:S(2)}, u32[]{:S(2)}) collective-permute-start(bf16[64,1152]{1,0:T(8,128)(2,1)S(1)} %get-tuple-element.42.refs_0_), channel_id=1, source_target_pairs={{0,32},{1,33},{2,34},{3,35},{4,36},{5,37},{6,38},{7,39},{8,40},{9,... | collective-permute-start | bytes 442376 | tf_op jit(solution)/shard_map/ppermute | solution.py:55
  6.2 18.0 %collective-permute-start.5 = (bf16[128,1152]{1,0:T(8,128)(2,1)S(1)}, bf16[128,1152]{1,0:T(8,128)(2,1)S(1)}, u32[]{:S(2)}, u32[]{:S(2)}) collective-permute-start(bf16[128,1152]{1,0:T(8,128)(2,1)S(1)} %pair.1.refs_1_), channel_id=1, source_target_pairs={{0,8},{1,9},{2,10},{3,11},{4,12},{5,13},{6,14},{7,15},{8,16},{9,17... | collective-permute-start | bytes 884744 | tf_op jit(solution)/shard_map/ppermute | solution.py:51
  10.5 13.6 %collective-permute-start.4 = (bf16[128,1152]{1,0:T(8,128)(2,1)S(1)}, bf16[128,1152]{1,0:T(8,128)(2,1)S(1)}, u32[]{:S(2)}, u32[]{:S(2)}) collective-permute-start(bf16[128,1152]{1,0:T(8,128)(2,1)S(1)} %pair.1.refs_1_), channel_id=1, source_target_pairs={{0,4},{1,5},{2,6},{3,7},{4,8},{5,9},{6,10},{7,11},{8,12},{9,13},{1... | collective-permute-start | bytes 884744 | tf_op jit(solution)/shard_map/ppermute | solution.py:51
  11.3 6.4 %collective-permute-start.2 = (bf16[64,1152]{1,0:T(8,128)(2,1)S(1)}, bf16[64,1152]{1,0:T(8,128)(2,1)S(1)}, u32[]{:S(2)}, u32[]{:S(2)}) collective-permute-start(bf16[64,1152]{1,0:T(8,128)(2,1)S(1)} %get-tuple-element.41.refs_0_), channel_id=1, source_target_pairs={{0,192},{1,193},{2,194},{3,195},{4,196},{5,197},{6,198},{7,199},{8... | collective-permute-start | bytes 442376 | tf_op jit(solution)/shard_map/ppermute | solution.py:39
  14.0 5.6 %collective-permute-start.1 = (bf16[64,1152]{1,0:T(8,128)(2,1)S(1)}, bf16[64,1152]{1,0:T(8,128)(2,1)S(1)}, u32[]{:S(2)}, u32[]{:S(2)}) collective-permute-start(bf16[64,1152]{1,0:T(8,128)(2,1)S(1)} %get-tuple-element.41.refs_0_), channel_id=1, source_target_pairs={{0,128},{1,129},{2,130},{3,131},{4,132},{5,133},{6,134},{7,135},{8... | collective-permute-start | bytes 442376 | tf_op jit(solution)/shard_map/ppermute | solution.py:39
  14.3 7.0 %collective-permute-start = (bf16[64,1152]{1,0:T(8,128)(2,1)S(1)}, bf16[64,1152]{1,0:T(8,128)(2,1)S(1)}, u32[]{:S(2)}, u32[]{:S(2)}) collective-permute-start(bf16[64,1152]{1,0:T(8,128)(2,1)S(1)} %get-tuple-element.41.refs_0_), channel_id=1, source_target_pairs={{0,64},{1,65},{2,66},{3,67},{4,68},{5,69},{6,70},{7,71},{8,72},{9,... | collective-permute-start | bytes 442376 | tf_op jit(solution)/shard_map/ppermute | solution.py:39
  21.4 10.5 %collective-permute-start.8 = (bf16[264,1152]{1,0:T(8,128)(2,1)S(1)}, bf16[264,1152]{1,0:T(8,128)(2,1)S(1)}, u32[]{:S(2)}, u32[]{:S(2)}) collective-permute-start(bf16[264,1152]{1,0:T(8,128)(2,1)S(1)} %group.1.refs_2_.refs_3_.refs_5_), channel_id=1, source_target_pairs={{0,1},{1,2},{2,3},{3,0},{4,5},{5,6},{6,7},{7,4},{8,9},{9,10},{10,1... | collective-permute-start | bytes 1824776 | tf_op jit(solution)/shard_map/ppermute | solution.py:45
  22.7 10.0 %collective-permute-start.9 = (bf16[264,1152]{1,0:T(8,128)(2,1)S(1)}, bf16[264,1152]{1,0:T(8,128)(2,1)S(1)}, u32[]{:S(2)}, u32[]{:S(2)}) collective-permute-start(bf16[264,1152]{1,0:T(8,128)(2,1)S(1)} %group.1.refs_2_.refs_3_.refs_5_), channel_id=1, source_target_pairs={{0,3},{1,0},{2,1},{3,2},{4,7},{5,4},{6,5},{7,6},{8,11},{9,8},{10,9... | collective-permute-start | bytes 1824776 | tf_op jit(solution)/shard_map/ppermute | solution.py:45
  24.2 4.4 %collective-permute-start.6 = (bf16[256,1152]{1,0:T(8,128)(2,1)S(1)}, bf16[256,1152]{1,0:T(8,128)(2,1)S(1)}, u32[]{:S(2)}, u32[]{:S(2)}) collective-permute-start(bf16[256,1152]{1,0:T(8,128)(2,1)S(1)} %get-tuple-element.43.refs_3_.refs_2_), channel_id=1, source_target_pairs={{0,32},{1,33},{2,34},{3,35},{4,36},{5,37},{6,38},{7,39},{8,40},{9,... | collective-permute-start | bytes 1769480 | tf_op jit(solution)/shard_map/ppermute | solution.py:55
  24.6 10.7 %collective-permute-start.7 = (bf16[192,1152]{1,0:T(8,128)(2,1)S(1)}, bf16[192,1152]{1,0:T(8,128)(2,1)S(1)}, u32[]{:S(2)}, u32[]{:S(2)}) collective-permute-start(bf16[192,1152]{1,0:T(8,128)(2,1)S(1)} %get-tuple-element.45), channel_id=1, source_target_pairs={{0,8},{1,9},{2,10},{3,11},{4,12},{5,13},{6,14},{7,15},{8,16},{9,17... | collective-permute-start | bytes 1327112 | tf_op jit(solution)/shard_map/ppermute | solution.py:51
  26.5 17.8 %collective-permute-start.13 = (bf16[264,1152]{1,0:T(8,128)(2,1)S(1)}, bf16[264,1152]{1,0:T(8,128)(2,1)S(1)}, u32[]{:S(2)}, u32[]{:S(2)}) collective-permute-start(bf16[264,1152]{1,0:T(8,128)(2,1)S(1)} %group.1.refs_2_.refs_3_.refs_5_), channel_id=1, source_target_pairs={{0,2},{1,3},{2,0},{3,1},{4,6},{5,7},{6,4},{7,5},{8,10},{9,11},{10,... | collective-permute-start | bytes 1824776 | tf_op jit(solution)/shard_map/ppermute | solution.py:45
  35.4 5.4 %collective-permute-start.10 = (bf16[192,1152]{1,0:T(8,128)(2,1)S(1)}, bf16[192,1152]{1,0:T(8,128)(2,1)S(1)}, u32[]{:S(2)}, u32[]{:S(2)}) collective-permute-start(bf16[192,1152]{1,0:T(8,128)(2,1)S(1)} %far_mine.1.refs_0_), channel_id=1, source_target_pairs={{0,32},{1,33},{2,34},{3,35},{4,36},{5,37},{6,38},{7,39},{8,40},{9,... | collective-permute-start | bytes 1327112 | tf_op jit(solution)/shard_map/ppermute | solution.py:55
  47.4 7.1 %collective-permute-start.14 = (bf16[192,1152]{1,0:T(8,128)(2,1)S(1)}, bf16[192,1152]{1,0:T(8,128)(2,1)S(1)}, u32[]{:S(2)}, u32[]{:S(2)}) collective-permute-start(bf16[192,1152]{1,0:T(8,128)(2,1)S(1)} %get-tuple-element.60.refs_6_), channel_id=1, source_target_pairs={{0,32},{1,33},{2,34},{3,35},{4,36},{5,37},{6,38},{7,39},{8,40},{9,... | collective-permute-start | bytes 1327112 | tf_op jit(solution)/shard_map/ppermute | solution.py:55
  47.8 12.0 %collective-permute-start.12 = (bf16[264,1152]{1,0:T(8,128)(2,1)S(1)}, bf16[264,1152]{1,0:T(8,128)(2,1)S(1)}, u32[]{:S(2)}, u32[]{:S(2)}) collective-permute-start(bf16[264,1152]{1,0:T(8,128)(2,1)S(1)} %get-tuple-element.52.refs_5_), channel_id=1, source_target_pairs={{0,1},{1,2},{2,3},{3,0},{4,5},{5,6},{6,7},{7,4},{8,9},{9,10},{10,1... | collective-permute-start | bytes 1824776 | tf_op jit(solution)/shard_map/ppermute | solution.py:45
  48.4 11.4 %collective-permute-start.11 = (bf16[264,1152]{1,0:T(8,128)(2,1)S(1)}, bf16[264,1152]{1,0:T(8,128)(2,1)S(1)}, u32[]{:S(2)}, u32[]{:S(2)}) collective-permute-start(bf16[264,1152]{1,0:T(8,128)(2,1)S(1)} %get-tuple-element.51.refs_8_), channel_id=1, source_target_pairs={{0,3},{1,0},{2,1},{3,2},{4,7},{5,4},{6,5},{7,6},{8,11},{9,8},{10,9... | collective-permute-start | bytes 1824776 | tf_op jit(solution)/shard_map/ppermute | solution.py:45
  52.1 8.7 %collective-permute-start.16 = (bf16[256,1152]{1,0:T(8,128)(2,1)S(1)}, bf16[256,1152]{1,0:T(8,128)(2,1)S(1)}, u32[]{:S(2)}, u32[]{:S(2)}) collective-permute-start(bf16[256,1152]{1,0:T(8,128)(2,1)S(1)} %get-tuple-element.65), channel_id=1, source_target_pairs={{0,32},{1,33},{2,34},{3,35},{4,36},{5,37},{6,38},{7,39},{8,40},{9,... | collective-permute-start | bytes 1769480 | tf_op jit(solution)/shard_map/ppermute | solution.py:55
  54.6 12.8 %collective-permute-start.17 = (bf16[192,1152]{1,0:T(8,128)(2,1)S(1)}, bf16[192,1152]{1,0:T(8,128)(2,1)S(1)}, u32[]{:S(2)}, u32[]{:S(2)}) collective-permute-start(bf16[192,1152]{1,0:T(8,128)(2,1)S(1)} %step1.1.refs_8_), channel_id=1, source_target_pairs={{0,24},{1,25},{2,26},{3,27},{4,28},{5,29},{6,30},{7,31},{8,0},{9,1... | collective-permute-start | bytes 1327112 | tf_op jit(solution)/shard_map/ppermute | solution.py:51
  58.0 13.4 %collective-permute-start.15 = (bf16[264,1152]{1,0:T(8,128)(2,1)S(1)}, bf16[264,1152]{1,0:T(8,128)(2,1)S(1)}, u32[]{:S(2)}, u32[]{:S(2)}) collective-permute-start(bf16[264,1152]{1,0:T(8,128)(2,1)S(1)} %last_image.1.refs_2_), channel_id=1, source_target_pairs={{0,2},{1,3},{2,0},{3,1},{4,6},{5,7},{6,4},{7,5},{8,10},{9,11},{10,... | collective-permute-start | bytes 1824776 | tf_op jit(solution)/shard_map/ppermute | solution.py:45
  67.5 11.3 %collective-permute-start.22 = (bf16[128,1152]{1,0:T(8,128)(2,1)S(1)}, bf16[128,1152]{1,0:T(8,128)(2,1)S(1)}, u32[]{:S(2)}, u32[]{:S(2)}) collective-permute-start(bf16[128,1152]{1,0:T(8,128)(2,1)S(1)} %get-tuple-element.74), channel_id=1, source_target_pairs={{0,24},{1,25},{2,26},{3,27},{4,28},{5,29},{6,30},{7,31},{8,0},{9,1... | collective-permute-start | bytes 884744 | tf_op jit(solution)/shard_map/ppermute | solution.py:51
  69.2 13.7 %collective-permute-start.21 = (bf16[128,1152]{1,0:T(8,128)(2,1)S(1)}, bf16[128,1152]{1,0:T(8,128)(2,1)S(1)}, u32[]{:S(2)}, u32[]{:S(2)}) collective-permute-start(bf16[128,1152]{1,0:T(8,128)(2,1)S(1)} %get-tuple-element.66.refs_3_), channel_id=1, source_target_pairs={{0,28},{1,29},{2,30},{3,31},{4,0},{5,1},{6,2},{7,3},{8,4},{9,5},{1... | collective-permute-start | bytes 884744 | tf_op jit(solution)/shard_map/ppermute | solution.py:51
  71.5 13.4 %copy-start = (bf16[64,1152]{1,0:T(8,128)(2,1)S(1)}, bf16[64,1152]{1,0:T(8,128)(2,1)}, u32[]{:S(2)}) copy-start(bf16[64,1152]{1,0:T(8,128)(2,1)} %refs_5_.1) | copy-start | bytes 442372
  71.5 13.4 %copy-start.1 = (bf16[64,1152]{1,0:T(8,128)(2,1)S(1)}, bf16[64,1152]{1,0:T(8,128)(2,1)}, u32[]{:S(2)}) copy-start(bf16[64,1152]{1,0:T(8,128)(2,1)} %refs_11_.1) | copy-start | bytes 442372
  71.5 12.3 %collective-permute-start.18 = (bf16[72,1152]{1,0:T(8,128)(2,1)S(1)}, bf16[72,1152]{1,0:T(8,128)(2,1)S(1)}, u32[]{:S(2)}, u32[]{:S(2)}) collective-permute-start(bf16[72,1152]{1,0:T(8,128)(2,1)S(1)} %get-tuple-element.69), channel_id=1, source_target_pairs={{0,192},{1,193},{2,194},{3,195},{4,196},{5,197},{6,198},{7,199},{8... | collective-permute-start | bytes 497672 | tf_op jit(solution)/shard_map/ppermute | solution.py:39
  74.8 9.1 %collective-permute-start.19 = (bf16[72,1152]{1,0:T(8,128)(2,1)S(1)}, bf16[72,1152]{1,0:T(8,128)(2,1)S(1)}, u32[]{:S(2)}, u32[]{:S(2)}) collective-permute-start(bf16[72,1152]{1,0:T(8,128)(2,1)S(1)} %get-tuple-element.70), channel_id=1, source_target_pairs={{0,128},{1,129},{2,130},{3,131},{4,132},{5,133},{6,134},{7,135},{8... | collective-permute-start | bytes 497672 | tf_op jit(solution)/shard_map/ppermute | solution.py:39
  76.1 7.7 %collective-permute-start.20 = (bf16[72,1152]{1,0:T(8,128)(2,1)S(1)}, bf16[72,1152]{1,0:T(8,128)(2,1)S(1)}, u32[]{:S(2)}, u32[]{:S(2)}) collective-permute-start(bf16[72,1152]{1,0:T(8,128)(2,1)S(1)} %get-tuple-element.71.refs_3_), channel_id=1, source_target_pairs={{0,64},{1,65},{2,66},{3,67},{4,68},{5,69},{6,70},{7,71},{8,72},{9,... | collective-permute-start | bytes 497672 | tf_op jit(solution)/shard_map/ppermute | solution.py:39
  82.9 1.9 %collective-permute-start.23 = (bf16[64,1152]{1,0:T(8,128)(2,1)S(1)}, bf16[64,1152]{1,0:T(8,128)(2,1)S(1)}, u32[]{:S(2)}, u32[]{:S(2)}) collective-permute-start(bf16[64,1152]{1,0:T(8,128)(2,1)S(1)} %step3.1), channel_id=1, source_target_pairs={{0,32},{1,33},{2,34},{3,35},{4,36},{5,37},{6,38},{7,39},{8,40},{9,... | collective-permute-start | bytes 442376 | tf_op jit(solution)/shard_map/ppermute | solution.py:55

commit v7 on v6

--- a/solution.py
+++ b/solution.py
@@ -220,18 +220,19 @@
     send_image(out, image(cn, cf, mine, other, far), row[...])
 
 
-def own_image_body(cn, cf, mine, other, far, row, r1, r3, out, loss):
-    out[...] = image(cn, cf, mine, other, far) + (up(r1, 0, 256) + up(r3, 0, 256))
-    loss[...] = row[...] + (loss_sum(r1[256:, :256]) + loss_sum(r3[256:, :256]))
-
-
-def merge_img_body(g_ref, l_ref, r2, own_ref, own_loss, m1, m2, m3):
-    loss = l_ref[...] + loss_sum(r2[256:, :256])
+def own_image_body(cn, cf, mine, other, far, out):
+    out[...] = image(cn, cf, mine, other, far)
+
+
+def merge_img_body(g_ref, l_ref, r1, r2, r3, own_ref, own_loss, m1, m2, m3):
+    loss = l_ref[...] + (
+        loss_sum(r1[256:, :256]) + loss_sum(r2[256:, :256]) + loss_sum(r3[256:, :256])
+    )
     own_loss[...] = loss
     marks = loss_rows(loss)
     for j, out in enumerate((own_ref, m1, m2, m3)):
         lo, hi = U * j, U * (j + 1)
-        total = g_ref[lo:hi, :] + up(r2, lo, hi)
+        total = g_ref[lo:hi, :] + (up(r1, lo, hi) + up(r2, lo, hi) + up(r3, lo, hi))
         out[:U, :] = total.astype(out.dtype)
         if j:
             out[U:, :] = jnp.zeros((8, total.shape[1]), BF16)
@@ -310,7 +311,9 @@
     near_other = swap(near_mine)
 
     sc = (scale, bias)
-    other = pack("other_texts", 384, (near_other, pair))
+    far_mine = pack("far_mine", 192, (far_got,))
+    far_other = swap(far_mine)
+    other = pack("other_texts", 384, (near_other, pair), (far_mine,))
     near_c, near_l, last = [None] * 4, [None] * 4, ()
     for k in (0, 1, 3):
         near_c[k], near_l[k] = call(
@@ -322,8 +325,7 @@
         "near_part", near_part_body, [shape(640, d, dtype=F32)],
         (near_c[0], near_c[1], near_c[3], groups[0], groups[1], groups[3]), (), last,
     )[0]
-    far_mine = pack("far_mine", 192, (far_got,), (part,))
-    far = pack("far_texts", 384, (far_mine, swap(far_mine)))
+    far = pack("far_texts", 384, (far_mine, far_other), (part,))
     far_c, sent, last = [None] * 4, [None] * 4, ()
     for k in (1, 3):
         far_c[k], sent[k] = call(
@@ -355,16 +357,16 @@
     z1 = call("step1", step1_body, [shape(192, d)], (keep_a, got_a), (), (sent[2],))[0]
     w = ring(z1, -2)
     got_b = swap(send_b)
-    p0, loss = call(
-        "own_image", own_image_body, [shape(256, d, dtype=F32), shape(8, 256, dtype=F32)],
-        (near_c[0], far_c[0], near_mine, other, far, row0, r1, r3), (), (z1,),
-    )
+    p0 = call(
+        "own_image", own_image_body, [shape(256, d, dtype=F32)],
+        (near_c[0], far_c[0], near_mine, other, far), (), (z1,),
+    )[0]
     two, one = call("step2", step2_body, [shape(128, d)] * 2, (keep_b, got_b, w), (), (p0,))
     v2, v1 = ring(two, -2), ring(one, -1)
     own_img, own_loss, m1, m2, m3 = call(
         "merge_img", merge_img_body,
         [shape(rows, d, dtype=F32), shape(8, 256, dtype=F32)] + [shape(rows + 8, d)] * 3,
-        (p0, loss, r2), (), (one,),
+        (p0, row0, r1, r2, r3), (), (one,),
     )
     q1, q3, q2 = first(m1, -1), first(m3, -3), first(m2, -2)
     z3 = call("step3", step3_body, [shape(64, d)], (own_pair, v1, v2), (), (m3,))[0]

time: 86 us -> 85 us (0.988)
  waiting for transfers between devices: 26.4 us -> 25 us
    ppermute x6, waiting for transfers between devices: 6.33 us -> 10.1 us  [first(): lax.ppermute(a, AXES, permutation(lambda x, c, z, y: (x, c, z, y + s) if...]
    ppermute x6, waiting for transfers between devices: 3.43 us -> 1.3 us  [swap(): lax.ppermute(a, AXES, permutation(lambda x, c, z, y: (x, 1 - c, z, y)))]
    ppermute x6, starting transfers between devices: 10.4 us -> 8.47 us  [swap(): lax.ppermute(a, AXES, permutation(lambda x, c, z, y: (x, 1 - c, z, y)))]
    ppermute x6, starting transfers between devices: 9.16 us -> 11 us  [first(): lax.ppermute(a, AXES, permutation(lambda x, c, z, y: (x, c, z, y + s) if...]
    ppermute x6, waiting for transfers between devices: 12.8 us -> 11 us  [ring(): lax.ppermute(a, AXES, permutation(lambda x, c, z, y: (x, c, z - s if c el...]
    ppermute x6, starting transfers between devices: 8.33 us -> 9.82 us  [second(): lax.ppermute(a, AXES, permutation(lambda x, c, z, y: (x + s, c, z, y) if...]
    ppermute x6, waiting for transfers between devices: 3.77 us -> 2.51 us  [second(): lax.ppermute(a, AXES, permutation(lambda x, c, z, y: (x + s, c, z, y) if...]
    ppermute x6, starting transfers between devices: 14.3 us -> 13 us  [ring(): lax.ppermute(a, AXES, permutation(lambda x, c, z, y: (x, c, z - s if c el...]
  transfers between devices with their start and end apart: 24 -> 24, of which waited for: 12 -> 13; matrix products, arithmetic and copies ran while one was open for 0% -> 0% of each run, Pallas kernels for 12% -> 12%
where the time goes in v7:
time: 85 us; the launch traced here: 84.9 us
  starting transfers between devices  42.3 us (50%)
  waiting for transfers between devices  25 us (29%)
  Pallas kernels  15.5 us (18%)
  between operations  2.14 us (3%)
    pallas_call x23, Pallas kernels, call(): pl.pallas_call(kernel, out_shape=outs, in_specs=[SMEM] * len(scalars) + (...  15.5 us
    ppermute x6, starting transfers between devices, ring(): lax.ppermute(a, AXES, permutation(lambda x, c, z, y: (x, c, z - s if c el...  13 us
    ppermute x6, starting transfers between devices, first(): lax.ppermute(a, AXES, permutation(lambda x, c, z, y: (x, c, z, y + s) if...  11 us
    ppermute x6, waiting for transfers between devices, ring(): lax.ppermute(a, AXES, permutation(lambda x, c, z, y: (x, c, z - s if c el...  11 us
    ppermute x6, waiting for transfers between devices, first(): lax.ppermute(a, AXES, permutation(lambda x, c, z, y: (x, c, z, y + s) if...  10.1 us
    ppermute x6, starting transfers between devices, second(): lax.ppermute(a, AXES, permutation(lambda x, c, z, y: (x + s, c, z, y) if...  9.82 us
    ppermute x6, starting transfers between devices, swap(): lax.ppermute(a, AXES, permutation(lambda x, c, z, y: (x, 1 - c, z, y)))  8.47 us
    ppermute x6, waiting for transfers between devices, second(): lax.ppermute(a, AXES, permutation(lambda x, c, z, y: (x + s, c, z, y) if...  2.51 us
  transfers between devices with their start and end apart: 24, of which 13 were waited for; matrix products, arithmetic and copies ran while one was open for 0% of the time, Pallas kernels for 12%

profile of v7, /device:TPU:1, one launch (start us, length us, event | category | flops | bytes accessed | tf_op | source)
XLA Modules:
  0.0 84.9 jit_solution(17666201852899447191)
XLA Ops:
  0.6 1.2 %normalize.1 = (bf16[64,1152]{1,0:T(8,128)(2,1)S(1)}, bf16[64,1152]{1,0:T(8,128)(2,1)S(1)}, f32[64,1]{1,0:T(8,128)S(1)}, f32[64,1]{1,0:T(8,128)S(1)}) custom-call(bf16[64,1152]{1,0:T(8,128)(2,1)} %refs_5_.1, bf16[64,1152]{1,0:T(8,128)(2,1)} %refs_11_.1), custom_call_target="tpu_custom_call" | custom-call | flops 1 | bytes 1 | tf_op jit(solution)/shard_map/normalize/pallas_call | solution.py:65
  1.8 3.3 %collective-permute-start.3 = (bf16[64,1152]{1,0:T(8,128)(2,1)S(1)}, bf16[64,1152]{1,0:T(8,128)(2,1)S(1)}, u32[]{:S(2)}, u32[]{:S(2)}) collective-permute-start(bf16[64,1152]{1,0:T(8,128)(2,1)S(1)} %get-tuple-element.40.refs_0_), channel_id=1, source_target_pairs={{0,32},{1,33},{2,34},{3,35},{4,36},{5,37},{6,38},{7,39},{8,40},{9,... | collective-permute-start | bytes 442376 | tf_op jit(solution)/shard_map/ppermute | solution.py:55
  6.2 4.4 %collective-permute-start.5 = (bf16[128,1152]{1,0:T(8,128)(2,1)S(1)}, bf16[128,1152]{1,0:T(8,128)(2,1)S(1)}, u32[]{:S(2)}, u32[]{:S(2)}) collective-permute-start(bf16[128,1152]{1,0:T(8,128)(2,1)S(1)} %pair.1.refs_1_), channel_id=1, source_target_pairs={{0,8},{1,9},{2,10},{3,11},{4,12},{5,13},{6,14},{7,15},{8,16},{9,17... | collective-permute-start | bytes 884744 | tf_op jit(solution)/shard_map/ppermute | solution.py:51
  11.3 2.7 %collective-permute-start.2 = (bf16[64,1152]{1,0:T(8,128)(2,1)S(1)}, bf16[64,1152]{1,0:T(8,128)(2,1)S(1)}, u32[]{:S(2)}, u32[]{:S(2)}) collective-permute-start(bf16[64,1152]{1,0:T(8,128)(2,1)S(1)} %get-tuple-element.39.refs_0_), channel_id=1, source_target_pairs={{0,192},{1,193},{2,194},{3,195},{4,196},{5,197},{6,198},{7,199},{8... | collective-permute-start | bytes 442376 | tf_op jit(solution)/shard_map/ppermute | solution.py:39
  15.0 2.6 %collective-permute-done.2.refs_3_ = bf16[64,1152]{1,0:T(8,128)(2,1)S(1)} collective-permute-done((bf16[64,1152]{1,0:T(8,128)(2,1)S(1)}, bf16[64,1152]{1,0:T(8,128)(2,1)S(1)}, u32[]{:S(2)}, u32[]{:S(2)}) %collective-permute-start.2) | collective-permute-done | bytes 147488 | tf_op jit(solution)/shard_map/ppermute | solution.py:39
  17.7 1.9 %collective-permute-done.1.refs_2_ = bf16[64,1152]{1,0:T(8,128)(2,1)S(1)} collective-permute-done((bf16[64,1152]{1,0:T(8,128)(2,1)S(1)}, bf16[64,1152]{1,0:T(8,128)(2,1)S(1)}, u32[]{:S(2)}, u32[]{:S(2)}) %collective-permute-start.1) | collective-permute-done | bytes 147488 | tf_op jit(solution)/shard_map/ppermute | solution.py:39
  19.6 1.8 %collective-permute-done.refs_1_ = bf16[64,1152]{1,0:T(8,128)(2,1)S(1)} collective-permute-done((bf16[64,1152]{1,0:T(8,128)(2,1)S(1)}, bf16[64,1152]{1,0:T(8,128)(2,1)S(1)}, u32[]{:S(2)}, u32[]{:S(2)}) %collective-permute-start) | collective-permute-done | bytes 147488 | tf_op jit(solution)/shard_map/ppermute | solution.py:39
  21.5 1.9 %collective-permute-start.7 = (bf16[192,1152]{1,0:T(8,128)(2,1)S(1)}, bf16[192,1152]{1,0:T(8,128)(2,1)S(1)}, u32[]{:S(2)}, u32[]{:S(2)}) collective-permute-start(bf16[192,1152]{1,0:T(8,128)(2,1)S(1)} %get-tuple-element.42), channel_id=1, source_target_pairs={{0,8},{1,9},{2,10},{3,11},{4,12},{5,13},{6,14},{7,15},{8,16},{9,17... | collective-permute-start | bytes 1327112 | tf_op jit(solution)/shard_map/ppermute | solution.py:51
  23.4 1.2 %collective-permute-start.9 = (bf16[264,1152]{1,0:T(8,128)(2,1)S(1)}, bf16[264,1152]{1,0:T(8,128)(2,1)S(1)}, u32[]{:S(2)}, u32[]{:S(2)}) collective-permute-start(bf16[264,1152]{1,0:T(8,128)(2,1)S(1)} %group.1.refs_2_.refs_3_.refs_5_), channel_id=1, source_target_pairs={{0,1},{1,2},{2,3},{3,0},{4,5},{5,6},{6,7},{7,4},{8,9},{9,10},{10,1... | collective-permute-start | bytes 1824776 | tf_op jit(solution)/shard_map/ppermute | solution.py:45
  24.6 1.5 %collective-permute-start.10 = (bf16[264,1152]{1,0:T(8,128)(2,1)S(1)}, bf16[264,1152]{1,0:T(8,128)(2,1)S(1)}, u32[]{:S(2)}, u32[]{:S(2)}) collective-permute-start(bf16[264,1152]{1,0:T(8,128)(2,1)S(1)} %group.1.refs_2_.refs_3_.refs_5_), channel_id=1, source_target_pairs={{0,3},{1,0},{2,1},{3,2},{4,7},{5,4},{6,5},{7,6},{8,11},{9,8},{10,9... | collective-permute-start | bytes 1824776 | tf_op jit(solution)/shard_map/ppermute | solution.py:45
  26.0 1.5 %collective-permute-start.11 = (bf16[264,1152]{1,0:T(8,128)(2,1)S(1)}, bf16[264,1152]{1,0:T(8,128)(2,1)S(1)}, u32[]{:S(2)}, u32[]{:S(2)}) collective-permute-start(bf16[264,1152]{1,0:T(8,128)(2,1)S(1)} %group.1.refs_2_.refs_3_.refs_5_), channel_id=1, source_target_pairs={{0,2},{1,3},{2,0},{3,1},{4,6},{5,7},{6,4},{7,5},{8,10},{9,11},{10,... | collective-permute-start | bytes 1824776 | tf_op jit(solution)/shard_map/ppermute | solution.py:45
  27.6 2.5 %collective-permute-start.6 = (bf16[256,1152]{1,0:T(8,128)(2,1)S(1)}, bf16[256,1152]{1,0:T(8,128)(2,1)S(1)}, u32[]{:S(2)}, u32[]{:S(2)}) collective-permute-start(bf16[256,1152]{1,0:T(8,128)(2,1)S(1)} %get-tuple-element.41.refs_3_.refs_2_), channel_id=1, source_target_pairs={{0,32},{1,33},{2,34},{3,35},{4,36},{5,37},{6,38},{7,39},{8,40},{9,... | collective-permute-start | bytes 1769480 | tf_op jit(solution)/shard_map/ppermute | solution.py:55
  30.1 4.6 %collective-permute-done.7.refs_0_ = bf16[192,1152]{1,0:T(8,128)(2,1)S(1)} collective-permute-done((bf16[192,1152]{1,0:T(8,128)(2,1)S(1)}, bf16[192,1152]{1,0:T(8,128)(2,1)S(1)}, u32[]{:S(2)}, u32[]{:S(2)}) %collective-permute-start.7) | collective-permute-done | bytes 442400 | tf_op jit(solution)/shard_map/ppermute | solution.py:51
  34.8 1.2 %collective-permute-start.8 = (bf16[192,1152]{1,0:T(8,128)(2,1)S(1)}, bf16[192,1152]{1,0:T(8,128)(2,1)S(1)}, u32[]{:S(2)}, u32[]{:S(2)}) collective-permute-start(bf16[192,1152]{1,0:T(8,128)(2,1)S(1)} %far_mine.1.refs_2_.refs_0_), channel_id=1, source_target_pairs={{0,32},{1,33},{2,34},{3,35},{4,36},{5,37},{6,38},{7,39},{8,40},{9,... | collective-permute-start | bytes 1327112 | tf_op jit(solution)/shard_map/ppermute | solution.py:55
  39.7 1.5 %near_part.1.refs_2_.refs_9_ = f32[640,1152]{1,0:T(8,128)S(1)} custom-call(bf16[256,640]{1,0:T(8,128)(2,1)S(1)} %get-tuple-element.43.refs_0_, bf16[256,640]{1,0:T(8,128)(2,1)S(1)} %get-tuple-element.45.refs_1_.refs_6_, bf16[256,640]{1,0:T(8,128)(2,1)S(1)} %get-tuple-element.47.refs_2_.refs_6_, bf16[264,1152]{1,0:T(8,128)(2,1)S(1)} %group.1.refs_2_.refs_3_.refs_5_, ...), custom_call_target="tpu_custom_call" | custom-call | flops 1 | bytes 1 | tf_op jit(solution)/shard_map/near_part/pallas_call | solution.py:65
  41.3 1.4 %far_image1.1 = (bf16[256,384]{1,0:T(8,128)(2,1)S(1)}, bf16[264,1152]{1,0:T(8,128)(2,1)S(1)}) custom-call(f32[1]{0:T(128)S(6)} %copy.7.refs_0_, f32[1]{0:T(128)S(6)} %copy.8.refs_1_, bf16[264,1152]{1,0:T(8,128)(2,1)S(1)} %collective-permute-done.9.refs_2_.refs_4_.refs_6_, bf16[256,1152]{1,0:T(8,128)(2,1)S(1)} %get-tuple-element.41.refs_3_.refs_2_, ...), custom_call_target="tpu_custom_call" | custom-call | flops 1 | bytes 1 | tf_op jit(solution)/shard_map/far_image1/pallas_call | solution.py:65
  42.7 1.4 %far_image3.1 = (bf16[256,384]{1,0:T(8,128)(2,1)S(1)}, bf16[264,1152]{1,0:T(8,128)(2,1)S(1)}) custom-call(f32[1]{0:T(128)S(6)} %copy.7.refs_0_, f32[1]{0:T(128)S(6)} %copy.8.refs_1_, bf16[264,1152]{1,0:T(8,128)(2,1)S(1)} %collective-permute-done.10.refs_2_.refs_5_.refs_8_, bf16[256,1152]{1,0:T(8,128)(2,1)S(1)} %get-tuple-element.41.refs_3_.refs_2_, ...), custom_call_target="tpu_custom_call" | custom-call | flops 1 | bytes 1 | tf_op jit(solution)/shard_map/far_image3/pallas_call | solution.py:65
  44.8 1.3 %last.1 = (bf16[256,640]{1,0:T(8,128)(2,1)S(1)}, bf16[256,384]{1,0:T(8,128)(2,1)S(1)}, f32[8,256]{1,0:T(8,128)S(1)}) custom-call(f32[1]{0:T(128)S(6)} %copy.7.refs_0_, f32[1]{0:T(128)S(6)} %copy.8.refs_1_, bf16[264,1152]{1,0:T(8,128)(2,1)S(1)} %collective-permute-done.11.refs_2_.refs_7_, bf16[256,1152]{1,0:T(8,128)(2,1)S(1)} %get-tuple-element.41.refs_3_.refs_2_, ...), custom_call_target="tpu_custom_call" | custom-call | flops 1 | bytes 1 | tf_op jit(solution)/shard_map/last/pallas_call | solution.py:65
  46.1 1.7 %texts_grad.1 = (f32[192,1152]{1,0:T(8,128)S(1)}, bf16[192,1152]{1,0:T(8,128)(2,1)S(1)}, f32[256,1152]{1,0:T(8,128)S(1)}, bf16[256,1152]{1,0:T(8,128)(2,1)S(1)}, f32[128,1152]{1,0:T(8,128)S(1)}) custom-call(bf16[256,384]{1,0:T(8,128)(2,1)S(1)} %get-tuple-element.51.refs_0_.refs_1_, bf16[256,384]{1,0:T(8,128)(2,1)S(1)} %get-tuple-element.52.refs_1_, ...), custom_call_target="tpu_custom_call" | custom-call | flops 1 | bytes 1 | tf_op jit(solution)/shard_map/texts_grad/pallas_call | solution.py:65
  49.8 1.4 %collective-permute-start.17 = (bf16[192,1152]{1,0:T(8,128)(2,1)S(1)}, bf16[192,1152]{1,0:T(8,128)(2,1)S(1)}, u32[]{:S(2)}, u32[]{:S(2)}) collective-permute-start(bf16[192,1152]{1,0:T(8,128)(2,1)S(1)} %step1.1.refs_5_), channel_id=1, source_target_pairs={{0,24},{1,25},{2,26},{3,27},{4,28},{5,29},{6,30},{7,31},{8,0},{9,1... | collective-permute-start | bytes 1327112 | tf_op jit(solution)/shard_map/ppermute | solution.py:51
  51.2 2.9 %collective-permute-start.14 = (bf16[264,1152]{1,0:T(8,128)(2,1)S(1)}, bf16[264,1152]{1,0:T(8,128)(2,1)S(1)}, u32[]{:S(2)}, u32[]{:S(2)}) collective-permute-start(bf16[264,1152]{1,0:T(8,128)(2,1)S(1)} %last_image.1.refs_2_), channel_id=1, source_target_pairs={{0,2},{1,3},{2,0},{3,1},{4,6},{5,7},{6,4},{7,5},{8,10},{9,11},{10,... | collective-permute-start | bytes 1824776 | tf_op jit(solution)/shard_map/ppermute | solution.py:45
  54.1 1.0 %collective-permute-start.15 = (bf16[264,1152]{1,0:T(8,128)(2,1)S(1)}, bf16[264,1152]{1,0:T(8,128)(2,1)S(1)}, u32[]{:S(2)}, u32[]{:S(2)}) collective-permute-start(bf16[264,1152]{1,0:T(8,128)(2,1)S(1)} %get-tuple-element.50.refs_5_), channel_id=1, source_target_pairs={{0,1},{1,2},{2,3},{3,0},{4,5},{5,6},{6,7},{7,4},{8,9},{9,10},{10,1... | collective-permute-start | bytes 1824776 | tf_op jit(solution)/shard_map/ppermute | solution.py:45
  55.2 1.6 %collective-permute-start.13 = (bf16[264,1152]{1,0:T(8,128)(2,1)S(1)}, bf16[264,1152]{1,0:T(8,128)(2,1)S(1)}, u32[]{:S(2)}, u32[]{:S(2)}) collective-permute-start(bf16[264,1152]{1,0:T(8,128)(2,1)S(1)} %get-tuple-element.49.refs_8_), channel_id=1, source_target_pairs={{0,3},{1,0},{2,1},{3,2},{4,7},{5,4},{6,5},{7,6},{8,11},{9,8},{10,9... | collective-permute-start | bytes 1824776 | tf_op jit(solution)/shard_map/ppermute | solution.py:45
  57.8 4.3 %collective-permute-done.17.refs_2_ = bf16[192,1152]{1,0:T(8,128)(2,1)S(1)} collective-permute-done((bf16[192,1152]{1,0:T(8,128)(2,1)S(1)}, bf16[192,1152]{1,0:T(8,128)(2,1)S(1)}, u32[]{:S(2)}, u32[]{:S(2)}) %collective-permute-start.17) | collective-permute-done | bytes 442400 | tf_op jit(solution)/shard_map/ppermute | solution.py:51
  62.3 3.8 %collective-permute-start.22 = (bf16[128,1152]{1,0:T(8,128)(2,1)S(1)}, bf16[128,1152]{1,0:T(8,128)(2,1)S(1)}, u32[]{:S(2)}, u32[]{:S(2)}) collective-permute-start(bf16[128,1152]{1,0:T(8,128)(2,1)S(1)} %get-tuple-element.70), channel_id=1, source_target_pairs={{0,24},{1,25},{2,26},{3,27},{4,28},{5,29},{6,30},{7,31},{8,0},{9,1... | collective-permute-start | bytes 884744 | tf_op jit(solution)/shard_map/ppermute | solution.py:51
  67.0 1.5 %collective-permute-done.15.refs_4_ = bf16[264,1152]{1,0:T(8,128)(2,1)S(1)} collective-permute-done((bf16[264,1152]{1,0:T(8,128)(2,1)S(1)}, bf16[264,1152]{1,0:T(8,128)(2,1)S(1)}, u32[]{:S(2)}, u32[]{:S(2)}) %collective-permute-start.15) | collective-permute-done | bytes 608288 | tf_op jit(solution)/shard_map/ppermute | solution.py:45
  68.4 1.1 %collective-permute-done.13.refs_2_ = bf16[264,1152]{1,0:T(8,128)(2,1)S(1)} collective-permute-done((bf16[264,1152]{1,0:T(8,128)(2,1)S(1)}, bf16[264,1152]{1,0:T(8,128)(2,1)S(1)}, u32[]{:S(2)}, u32[]{:S(2)}) %collective-permute-start.13) | collective-permute-done | bytes 608288 | tf_op jit(solution)/shard_map/ppermute | solution.py:45
  69.8 6.6 %collective-permute-start.18 = (bf16[72,1152]{1,0:T(8,128)(2,1)S(1)}, bf16[72,1152]{1,0:T(8,128)(2,1)S(1)}, u32[]{:S(2)}, u32[]{:S(2)}) collective-permute-start(bf16[72,1152]{1,0:T(8,128)(2,1)S(1)} %get-tuple-element.65), channel_id=1, source_target_pairs={{0,192},{1,193},{2,194},{3,195},{4,196},{5,197},{6,198},{7,199},{8... | collective-permute-start | bytes 497672 | tf_op jit(solution)/shard_map/ppermute | solution.py:39
  77.0 2.1 %collective-permute-done.21.refs_1_.refs_8_ = bf16[128,1152]{1,0:T(8,128)(2,1)S(1)} collective-permute-done((bf16[128,1152]{1,0:T(8,128)(2,1)S(1)}, bf16[128,1152]{1,0:T(8,128)(2,1)S(1)}, u32[]{:S(2)}, u32[]{:S(2)}) %collective-permute-start.21) | collective-permute-done | bytes 294944 | tf_op jit(solution)/shard_map/ppermute | solution.py:51
  80.4 2.0 %collective-permute-done.19.refs_3_ = bf16[72,1152]{1,0:T(8,128)(2,1)S(1)} collective-permute-done((bf16[72,1152]{1,0:T(8,128)(2,1)S(1)}, bf16[72,1152]{1,0:T(8,128)(2,1)S(1)}, u32[]{:S(2)}, u32[]{:S(2)}) %collective-permute-start.19) | collective-permute-done | bytes 165920 | tf_op jit(solution)/shard_map/ppermute | solution.py:39
  82.4 1.4 %collective-permute-done.20.refs_4_ = bf16[72,1152]{1,0:T(8,128)(2,1)S(1)} collective-permute-done((bf16[72,1152]{1,0:T(8,128)(2,1)S(1)}, bf16[72,1152]{1,0:T(8,128)(2,1)S(1)}, u32[]{:S(2)}, u32[]{:S(2)}) %collective-permute-start.20) | collective-permute-done | bytes 165920 | tf_op jit(solution)/shard_map/ppermute | solution.py:39
  83.9 1.1 %finish.1 = (f32[64,1152]{1,0:T(8,128)}, f32[64,1152]{1,0:T(8,128)}, f32[1,64]{1,0:T(1,128)}) custom-call(f32[64,1152]{1,0:T(8,128)S(1)} %get-tuple-element.63.refs_0_, f32[8,256]{1,0:T(8,128)S(1)} %get-tuple-element.64.refs_1_, bf16[72,1152]{1,0:T(8,128)(2,1)S(1)} %collective-permute-done.18.refs_2_, bf16[72,1152]{1,0:T(8,128)(2,1)S(1)} %collective-permute-done.19.refs_3_, ...), custom_call_target="tpu_custom_call" | custom-call | flops 1 | bytes 1 | tf_op jit(solution)/shard_map/finish/pallas_call | solution.py:65
  (43 shorter events, 12.5 us)
Async XLA Ops:
  1.8 4.3 %collective-permute-start.3 = (bf16[64,1152]{1,0:T(8,128)(2,1)S(1)}, bf16[64,1152]{1,0:T(8,128)(2,1)S(1)}, u32[]{:S(2)}, u32[]{:S(2)}) collective-permute-start(bf16[64,1152]{1,0:T(8,128)(2,1)S(1)} %get-tuple-element.40.refs_0_), channel_id=1, source_target_pairs={{0,32},{1,33},{2,34},{3,35},{4,36},{5,37},{6,38},{7,39},{8,40},{9,... | collective-permute-start | bytes 442376 | tf_op jit(solution)/shard_map/ppermute | solution.py:55
  6.2 15.2 %collective-permute-start.5 = (bf16[128,1152]{1,0:T(8,128)(2,1)S(1)}, bf16[128,1152]{1,0:T(8,128)(2,1)S(1)}, u32[]{:S(2)}, u32[]{:S(2)}) collective-permute-start(bf16[128,1152]{1,0:T(8,128)(2,1)S(1)} %pair.1.refs_1_), channel_id=1, source_target_pairs={{0,8},{1,9},{2,10},{3,11},{4,12},{5,13},{6,14},{7,15},{8,16},{9,17... | collective-permute-start | bytes 884744 | tf_op jit(solution)/shard_map/ppermute | solution.py:51
  10.5 10.9 %collective-permute-start.4 = (bf16[128,1152]{1,0:T(8,128)(2,1)S(1)}, bf16[128,1152]{1,0:T(8,128)(2,1)S(1)}, u32[]{:S(2)}, u32[]{:S(2)}) collective-permute-start(bf16[128,1152]{1,0:T(8,128)(2,1)S(1)} %pair.1.refs_1_), channel_id=1, source_target_pairs={{0,4},{1,5},{2,6},{3,7},{4,8},{5,9},{6,10},{7,11},{8,12},{9,13},{1... | collective-permute-start | bytes 884744 | tf_op jit(solution)/shard_map/ppermute | solution.py:51
  11.3 6.4 %collective-permute-start.2 = (bf16[64,1152]{1,0:T(8,128)(2,1)S(1)}, bf16[64,1152]{1,0:T(8,128)(2,1)S(1)}, u32[]{:S(2)}, u32[]{:S(2)}) collective-permute-start(bf16[64,1152]{1,0:T(8,128)(2,1)S(1)} %get-tuple-element.39.refs_0_), channel_id=1, source_target_pairs={{0,192},{1,193},{2,194},{3,195},{4,196},{5,197},{6,198},{7,199},{8... | collective-permute-start | bytes 442376 | tf_op jit(solution)/shard_map/ppermute | solution.py:39
  14.0 5.6 %collective-permute-start.1 = (bf16[64,1152]{1,0:T(8,128)(2,1)S(1)}, bf16[64,1152]{1,0:T(8,128)(2,1)S(1)}, u32[]{:S(2)}, u32[]{:S(2)}) collective-permute-start(bf16[64,1152]{1,0:T(8,128)(2,1)S(1)} %get-tuple-element.39.refs_0_), channel_id=1, source_target_pairs={{0,128},{1,129},{2,130},{3,131},{4,132},{5,133},{6,134},{7,135},{8... | collective-permute-start | bytes 442376 | tf_op jit(solution)/shard_map/ppermute | solution.py:39
  14.3 7.0 %collective-permute-start = (bf16[64,1152]{1,0:T(8,128)(2,1)S(1)}, bf16[64,1152]{1,0:T(8,128)(2,1)S(1)}, u32[]{:S(2)}, u32[]{:S(2)}) collective-permute-start(bf16[64,1152]{1,0:T(8,128)(2,1)S(1)} %get-tuple-element.39.refs_0_), channel_id=1, source_target_pairs={{0,64},{1,65},{2,66},{3,67},{4,68},{5,69},{6,70},{7,71},{8,72},{9,... | collective-permute-start | bytes 442376 | tf_op jit(solution)/shard_map/ppermute | solution.py:39
  21.5 13.2 %collective-permute-start.7 = (bf16[192,1152]{1,0:T(8,128)(2,1)S(1)}, bf16[192,1152]{1,0:T(8,128)(2,1)S(1)}, u32[]{:S(2)}, u32[]{:S(2)}) collective-permute-start(bf16[192,1152]{1,0:T(8,128)(2,1)S(1)} %get-tuple-element.42), channel_id=1, source_target_pairs={{0,8},{1,9},{2,10},{3,11},{4,12},{5,13},{6,14},{7,15},{8,16},{9,17... | collective-permute-start | bytes 1327112 | tf_op jit(solution)/shard_map/ppermute | solution.py:51
  23.4 14.7 %collective-permute-start.9 = (bf16[264,1152]{1,0:T(8,128)(2,1)S(1)}, bf16[264,1152]{1,0:T(8,128)(2,1)S(1)}, u32[]{:S(2)}, u32[]{:S(2)}) collective-permute-start(bf16[264,1152]{1,0:T(8,128)(2,1)S(1)} %group.1.refs_2_.refs_3_.refs_5_), channel_id=1, source_target_pairs={{0,1},{1,2},{2,3},{3,0},{4,5},{5,6},{6,7},{7,4},{8,9},{9,10},{10,1... | collective-permute-start | bytes 1824776 | tf_op jit(solution)/shard_map/ppermute | solution.py:45
  24.6 14.3 %collective-permute-start.10 = (bf16[264,1152]{1,0:T(8,128)(2,1)S(1)}, bf16[264,1152]{1,0:T(8,128)(2,1)S(1)}, u32[]{:S(2)}, u32[]{:S(2)}) collective-permute-start(bf16[264,1152]{1,0:T(8,128)(2,1)S(1)} %group.1.refs_2_.refs_3_.refs_5_), channel_id=1, source_target_pairs={{0,3},{1,0},{2,1},{3,2},{4,7},{5,4},{6,5},{7,6},{8,11},{9,8},{10,9... | collective-permute-start | bytes 1824776 | tf_op jit(solution)/shard_map/ppermute | solution.py:45
  26.0 18.8 %collective-permute-start.11 = (bf16[264,1152]{1,0:T(8,128)(2,1)S(1)}, bf16[264,1152]{1,0:T(8,128)(2,1)S(1)}, u32[]{:S(2)}, u32[]{:S(2)}) collective-permute-start(bf16[264,1152]{1,0:T(8,128)(2,1)S(1)} %group.1.refs_2_.refs_3_.refs_5_), channel_id=1, source_target_pairs={{0,2},{1,3},{2,0},{3,1},{4,6},{5,7},{6,4},{7,5},{8,10},{9,11},{10,... | collective-permute-start | bytes 1824776 | tf_op jit(solution)/shard_map/ppermute | solution.py:45
  27.6 9.6 %collective-permute-start.6 = (bf16[256,1152]{1,0:T(8,128)(2,1)S(1)}, bf16[256,1152]{1,0:T(8,128)(2,1)S(1)}, u32[]{:S(2)}, u32[]{:S(2)}) collective-permute-start(bf16[256,1152]{1,0:T(8,128)(2,1)S(1)} %get-tuple-element.41.refs_3_.refs_2_), channel_id=1, source_target_pairs={{0,32},{1,33},{2,34},{3,35},{4,36},{5,37},{6,38},{7,39},{8,40},{9,... | collective-permute-start | bytes 1769480 | tf_op jit(solution)/shard_map/ppermute | solution.py:55
  34.8 6.4 %collective-permute-start.8 = (bf16[192,1152]{1,0:T(8,128)(2,1)S(1)}, bf16[192,1152]{1,0:T(8,128)(2,1)S(1)}, u32[]{:S(2)}, u32[]{:S(2)}) collective-permute-start(bf16[192,1152]{1,0:T(8,128)(2,1)S(1)} %far_mine.1.refs_2_.refs_0_), channel_id=1, source_target_pairs={{0,32},{1,33},{2,34},{3,35},{4,36},{5,37},{6,38},{7,39},{8,40},{9,... | collective-permute-start | bytes 1327112 | tf_op jit(solution)/shard_map/ppermute | solution.py:55
  47.8 1.9 %collective-permute-start.12 = (bf16[192,1152]{1,0:T(8,128)(2,1)S(1)}, bf16[192,1152]{1,0:T(8,128)(2,1)S(1)}, u32[]{:S(2)}, u32[]{:S(2)}) collective-permute-start(bf16[192,1152]{1,0:T(8,128)(2,1)S(1)} %get-tuple-element.58.refs_6_), channel_id=1, source_target_pairs={{0,32},{1,33},{2,34},{3,35},{4,36},{5,37},{6,38},{7,39},{8,40},{9,... | collective-permute-start | bytes 1327112 | tf_op jit(solution)/shard_map/ppermute | solution.py:55
  47.9 9.9 %collective-permute-start.16 = (bf16[256,1152]{1,0:T(8,128)(2,1)S(1)}, bf16[256,1152]{1,0:T(8,128)(2,1)S(1)}, u32[]{:S(2)}, u32[]{:S(2)}) collective-permute-start(bf16[256,1152]{1,0:T(8,128)(2,1)S(1)} %get-tuple-element.61), channel_id=1, source_target_pairs={{0,32},{1,33},{2,34},{3,35},{4,36},{5,37},{6,38},{7,39},{8,40},{9,... | collective-permute-start | bytes 1769480 | tf_op jit(solution)/shard_map/ppermute | solution.py:55
  49.8 12.3 %collective-permute-start.17 = (bf16[192,1152]{1,0:T(8,128)(2,1)S(1)}, bf16[192,1152]{1,0:T(8,128)(2,1)S(1)}, u32[]{:S(2)}, u32[]{:S(2)}) collective-permute-start(bf16[192,1152]{1,0:T(8,128)(2,1)S(1)} %step1.1.refs_5_), channel_id=1, source_target_pairs={{0,24},{1,25},{2,26},{3,27},{4,28},{5,29},{6,30},{7,31},{8,0},{9,1... | collective-permute-start | bytes 1327112 | tf_op jit(solution)/shard_map/ppermute | solution.py:51
  51.2 15.8 %collective-permute-start.14 = (bf16[264,1152]{1,0:T(8,128)(2,1)S(1)}, bf16[264,1152]{1,0:T(8,128)(2,1)S(1)}, u32[]{:S(2)}, u32[]{:S(2)}) collective-permute-start(bf16[264,1152]{1,0:T(8,128)(2,1)S(1)} %last_image.1.refs_2_), channel_id=1, source_target_pairs={{0,2},{1,3},{2,0},{3,1},{4,6},{5,7},{6,4},{7,5},{8,10},{9,11},{10,... | collective-permute-start | bytes 1824776 | tf_op jit(solution)/shard_map/ppermute | solution.py:45
  54.1 14.3 %collective-permute-start.15 = (bf16[264,1152]{1,0:T(8,128)(2,1)S(1)}, bf16[264,1152]{1,0:T(8,128)(2,1)S(1)}, u32[]{:S(2)}, u32[]{:S(2)}) collective-permute-start(bf16[264,1152]{1,0:T(8,128)(2,1)S(1)} %get-tuple-element.50.refs_5_), channel_id=1, source_target_pairs={{0,1},{1,2},{2,3},{3,0},{4,5},{5,6},{6,7},{7,4},{8,9},{9,10},{10,1... | collective-permute-start | bytes 1824776 | tf_op jit(solution)/shard_map/ppermute | solution.py:45
  55.2 14.3 %collective-permute-start.13 = (bf16[264,1152]{1,0:T(8,128)(2,1)S(1)}, bf16[264,1152]{1,0:T(8,128)(2,1)S(1)}, u32[]{:S(2)}, u32[]{:S(2)}) collective-permute-start(bf16[264,1152]{1,0:T(8,128)(2,1)S(1)} %get-tuple-element.49.refs_8_), channel_id=1, source_target_pairs={{0,3},{1,0},{2,1},{3,2},{4,7},{5,4},{6,5},{7,6},{8,11},{9,8},{10,9... | collective-permute-start | bytes 1824776 | tf_op jit(solution)/shard_map/ppermute | solution.py:45
  62.3 14.8 %collective-permute-start.22 = (bf16[128,1152]{1,0:T(8,128)(2,1)S(1)}, bf16[128,1152]{1,0:T(8,128)(2,1)S(1)}, u32[]{:S(2)}, u32[]{:S(2)}) collective-permute-start(bf16[128,1152]{1,0:T(8,128)(2,1)S(1)} %get-tuple-element.70), channel_id=1, source_target_pairs={{0,24},{1,25},{2,26},{3,27},{4,28},{5,29},{6,30},{7,31},{8,0},{9,1... | collective-permute-start | bytes 884744 | tf_op jit(solution)/shard_map/ppermute | solution.py:51
  66.1 13.0 %collective-permute-start.21 = (bf16[128,1152]{1,0:T(8,128)(2,1)S(1)}, bf16[128,1152]{1,0:T(8,128)(2,1)S(1)}, u32[]{:S(2)}, u32[]{:S(2)}) collective-permute-start(bf16[128,1152]{1,0:T(8,128)(2,1)S(1)} %get-tuple-element.62.refs_5_), channel_id=1, source_target_pairs={{0,28},{1,29},{2,30},{3,31},{4,0},{5,1},{6,2},{7,3},{8,4},{9,5},{1... | collective-permute-start | bytes 884744 | tf_op jit(solution)/shard_map/ppermute | solution.py:51
  69.8 14.1 %copy-start = (bf16[64,1152]{1,0:T(8,128)(2,1)S(1)}, bf16[64,1152]{1,0:T(8,128)(2,1)}, u32[]{:S(2)}) copy-start(bf16[64,1152]{1,0:T(8,128)(2,1)} %refs_5_.1) | copy-start | bytes 442372
  69.8 14.1 %copy-start.1 = (bf16[64,1152]{1,0:T(8,128)(2,1)S(1)}, bf16[64,1152]{1,0:T(8,128)(2,1)}, u32[]{:S(2)}) copy-start(bf16[64,1152]{1,0:T(8,128)(2,1)} %refs_11_.1) | copy-start | bytes 442372
  69.8 10.6 %collective-permute-start.18 = (bf16[72,1152]{1,0:T(8,128)(2,1)S(1)}, bf16[72,1152]{1,0:T(8,128)(2,1)S(1)}, u32[]{:S(2)}, u32[]{:S(2)}) collective-permute-start(bf16[72,1152]{1,0:T(8,128)(2,1)S(1)} %get-tuple-element.65), channel_id=1, source_target_pairs={{0,192},{1,193},{2,194},{3,195},{4,196},{5,197},{6,198},{7,199},{8... | collective-permute-start | bytes 497672 | tf_op jit(solution)/shard_map/ppermute | solution.py:39
  76.4 6.0 %collective-permute-start.19 = (bf16[72,1152]{1,0:T(8,128)(2,1)S(1)}, bf16[72,1152]{1,0:T(8,128)(2,1)S(1)}, u32[]{:S(2)}, u32[]{:S(2)}) collective-permute-start(bf16[72,1152]{1,0:T(8,128)(2,1)S(1)} %get-tuple-element.66), channel_id=1, source_target_pairs={{0,128},{1,129},{2,130},{3,131},{4,132},{5,133},{6,134},{7,135},{8... | collective-permute-start | bytes 497672 | tf_op jit(solution)/shard_map/ppermute | solution.py:39
  76.4 7.5 %collective-permute-start.20 = (bf16[72,1152]{1,0:T(8,128)(2,1)S(1)}, bf16[72,1152]{1,0:T(8,128)(2,1)S(1)}, u32[]{:S(2)}, u32[]{:S(2)}) collective-permute-start(bf16[72,1152]{1,0:T(8,128)(2,1)S(1)} %get-tuple-element.67.refs_3_), channel_id=1, source_target_pairs={{0,64},{1,65},{2,66},{3,67},{4,68},{5,69},{6,70},{7,71},{8,72},{9,... | collective-permute-start | bytes 497672 | tf_op jit(solution)/shard_map/ppermute | solution.py:39
  79.2 4.7 %collective-permute-start.23 = (bf16[64,1152]{1,0:T(8,128)(2,1)S(1)}, bf16[64,1152]{1,0:T(8,128)(2,1)S(1)}, u32[]{:S(2)}, u32[]{:S(2)}) collective-permute-start(bf16[64,1152]{1,0:T(8,128)(2,1)S(1)} %step3.1), channel_id=1, source_target_pairs={{0,32},{1,33},{2,34},{3,35},{4,36},{5,37},{6,38},{7,39},{8,40},{9,... | collective-permute-start | bytes 442376 | tf_op jit(solution)/shard_map/ppermute | solution.py:55

commit v8 on v7

--- a/solution.py
+++ b/solution.py
@@ -165,48 +165,44 @@
     return tile(img, other_ref, coeff_ref.at[:, 256:], total, scale, bias, own)
 
 
-def near_body(own, scale_ref, bias_ref, img, mine, other, coeff, loss):
-    zero = jnp.zeros((256, 128), F32)
-    loss[...] = near_tile(img, mine, other, coeff, zero, scale_ref[0], bias_ref[0], own)
-
-
 def loss_row(total):
     column = jnp.broadcast_to(jnp.sum(total, axis=1, keepdims=True), (256, 128))
     return jnp.transpose(column)[:8, :]
 
 
-def image(cn, cf, mine, other, far):
-    g = jnp.dot(cf[...], far[...], preferred_element_type=F32)
-    g = g + jnp.dot(cn[:, :256], mine[...], preferred_element_type=F32)
+def near_image(cn, mine, other):
+    g = jnp.dot(cn[:, :256], mine[...], preferred_element_type=F32)
     return g + jnp.dot(cn[:, 256:], other[...], preferred_element_type=F32)
 
 
-def send_image(out, g, loss):
-    out[:256, :] = g.astype(BF16)
-    out[256:, :] = jnp.zeros((8, g.shape[1]), BF16)
-    out[256:, :256] = loss_rows(loss)
-
-
-def far_image_body(scale_ref, bias_ref, img, mine, other, far, cn, loss, cf, out):
-    total = tile(img, far, cf, loss[...], scale_ref[0], bias_ref[0])
-    send_image(out, image(cn, cf, mine, other, far), loss_row(total))
-
-
-def far_own_body(scale_ref, bias_ref, img, far, loss, cf, row):
-    row[...] = loss_row(tile(img, far, cf, loss[...], scale_ref[0], bias_ref[0]))
-
-
-def last_body(scale_ref, bias_ref, img, mine, other, far, cn, cf, row):
+def far_image(cf, far):
+    return jnp.dot(cf[...], far[...], preferred_element_type=F32)
+
+
+def own_near_body(scale_ref, bias_ref, img, mine, other, cn, loss, part, g):
+    zero = jnp.zeros((256, 128), F32)
+    loss[...] = near_tile(img, mine, other, cn, zero, scale_ref[0], bias_ref[0], True)
+    part[...] = texts((cn,), (img,), 0, 640)
+    g[...] = near_image(cn, mine, other)
+
+
+def near_pair_body(scale_ref, bias_ref, i1, i3, mine, other, part0, n1, n3, l1, l3, part):
+    zero = jnp.zeros((256, 128), F32)
+    for i, n, l in ((i1, n1, l1), (i3, n3, l3)):
+        l[...] = near_tile(i, mine, other, n, zero, scale_ref[0], bias_ref[0])
+    part[...] = part0[...] + texts((n1, n3), (i1, i3), 0, 640)
+
+
+def far_body(scale_ref, bias_ref, i0, i1, i3, far, l0, l1, l3, c0, c1, c3, rows):
+    for n, (i, l, c) in enumerate(((i0, l0, c0), (i1, l1, c1), (i3, l3, c3))):
+        total = tile(i, far, c, l[...], scale_ref[0], bias_ref[0])
+        rows[:, 256 * n : 256 * (n + 1)] = loss_row(total)
+
+
+def last_body(scale_ref, bias_ref, i0, i1, i2, i3, mine, other, far, c0, c1, c3, part, n2, c2, row, keep_a, send_a, keep_b, send_b, pair):
     scale, bias = scale_ref[0], bias_ref[0]
-    total = near_tile(img, mine, other, cn, jnp.zeros((256, 128), F32), scale, bias)
-    row[...] = loss_row(tile(img, far, cf, total, scale, bias))
-
-
-def near_part_body(c0, c1, c3, i0, i1, i3, part):
-    part[...] = texts((c0, c1, c3), (i0, i1, i3), 0, 640)
-
-
-def texts_body(c0, c1, c2, c3, n2, i0, i1, i2, i3, part, keep_a, send_a, keep_b, send_b, pair):
+    total = near_tile(i2, mine, other, n2, jnp.zeros((256, 128), F32), scale, bias)
+    row[...] = loss_row(tile(i2, far, c2, total, scale, bias))
     g = texts((c0, c1, c2, c3), (i0, i1, i2, i3), 0, 384)
     keep_a[...] = g[:192, :]
     send_a[...] = g[192:, :].astype(BF16)
@@ -216,16 +212,19 @@
     pair[...] = g[512:, :]
 
 
-def last_image_body(cn, cf, mine, other, far, row, out):
-    send_image(out, image(cn, cf, mine, other, far), row[...])
-
-
-def own_image_body(cn, cf, mine, other, far, out):
-    out[...] = image(cn, cf, mine, other, far)
+def image_body(at, cn, cf, mine, other, far, row, out):
+    g = near_image(cn, mine, other) + far_image(cf, far)
+    out[:256, :] = g.astype(BF16)
+    out[256:, :] = jnp.zeros((8, g.shape[1]), BF16)
+    out[256:, :256] = loss_rows(row[:, 256 * at : 256 * (at + 1)])
+
+
+def own_image_body(near, cf, far, out):
+    out[...] = near[...] + far_image(cf, far)
 
 
 def merge_img_body(g_ref, l_ref, r1, r2, r3, own_ref, own_loss, m1, m2, m3):
-    loss = l_ref[...] + (
+    loss = l_ref[:, :256] + (
         loss_sum(r1[256:, :256]) + loss_sum(r2[256:, :256]) + loss_sum(r3[256:, :256])
     )
     own_loss[...] = loss
@@ -311,62 +310,52 @@
     near_other = swap(near_mine)
 
     sc = (scale, bias)
-    far_mine = pack("far_mine", 192, (far_got,))
-    far_other = swap(far_mine)
-    other = pack("other_texts", 384, (near_other, pair), (far_mine,))
-    near_c, near_l, last = [None] * 4, [None] * 4, ()
-    for k in (0, 1, 3):
-        near_c[k], near_l[k] = call(
-            f"near{k}", functools.partial(near_body, k == 0), [shape(256, 640), shape(256, 128, dtype=F32)],
-            (groups[k], near_mine, other), sc, last,
-        )
-        last = (near_l[k],)
-    part = call(
-        "near_part", near_part_body, [shape(640, d, dtype=F32)],
-        (near_c[0], near_c[1], near_c[3], groups[0], groups[1], groups[3]), (), last,
-    )[0]
-    far = pack("far_texts", 384, (far_mine, far_other), (part,))
-    far_c, sent, last = [None] * 4, [None] * 4, ()
-    for k in (1, 3):
-        far_c[k], sent[k] = call(
-            f"far_image{k}", far_image_body, [shape(256, 384), shape(264, d)],
-            (groups[k], near_mine, other, far, near_c[k], near_l[k]), sc, last,
-        )
-        last = (sent[k],)
-    r1, r3 = second(sent[1], -1), second(sent[3], -3)
-    far_c[0], row0 = call(
-        "far_own", far_own_body, [shape(256, 384), shape(8, 256, dtype=F32)],
-        (groups[0], far, near_l[0]), sc, last,
-    )
-    near_c[2], far_c[2], row2 = call(
-        "last", last_body, [shape(256, 640), shape(256, 384), shape(8, 256, dtype=F32)],
-        (groups[2], near_mine, other, far), sc, (row0,),
-    )
-    keep_a, send_a, keep_b, send_b, own_pair = call(
-        "texts_grad", texts_body,
-        [shape(192, d, dtype=F32), shape(192, d), shape(256, d, dtype=F32), shape(256, d), shape(128, d, dtype=F32)],
-        (*far_c, near_c[2], *groups, part),
-    )
-    got_a = swap(send_a)
-    sent[2] = call(
-        "last_image", last_image_body, [shape(264, d)],
-        (near_c[2], far_c[2], near_mine, other, far, row2), (), (send_a,),
-    )[0]
-    r2 = second(sent[2], -2)
-
-    z1 = call("step1", step1_body, [shape(192, d)], (keep_a, got_a), (), (sent[2],))[0]
+    other = pack("other_texts", 384, (near_other, pair))
+    own_c, own_l, part0, own_near = call(
+        "own_near", own_near_body,
+        [shape(256, 640), shape(256, 128, dtype=F32), shape(640, d, dtype=F32), shape(256, d, dtype=F32)],
+        (group, near_mine, other), sc,
+    )
+    far_mine = pack("far_mine", 192, (far_got,), (own_l,))
+    n1, n3, l1, l3, part = call(
+        "near_pair", near_pair_body,
+        [shape(256, 640)] * 2 + [shape(256, 128, dtype=F32)] * 2 + [shape(640, d, dtype=F32)],
+        (g1, g3, near_mine, other, part0), sc, (far_mine,),
+    )
+    far = pack("far_texts", 384, (far_mine, swap(far_mine)), (l1,))
+    c0, c1, c3, rows013 = call(
+        "far", far_body, [shape(256, 384)] * 3 + [shape(8, 768, dtype=F32)],
+        (group, g1, g3, far, own_l, l1, l3), sc,
+    )
+    n2, c2, row2, keep_a, send_a, keep_b, send_b, own_pair = call(
+        "last", last_body,
+        [shape(256, 640), shape(256, 384), shape(8, 256, dtype=F32)]
+        + [shape(192, d, dtype=F32), shape(192, d), shape(256, d, dtype=F32), shape(256, d), shape(128, d, dtype=F32)],
+        (*groups, near_mine, other, far, c0, c1, c3, part), sc,
+    )
+    got_a, got_b = swap(send_a), swap(send_b)
+
+    def sent(name, at, cn, cf, row, after):
+        return call(
+            name, functools.partial(image_body, at), [shape(264, d)],
+            (cn, cf, near_mine, other, far, row), (), after,
+        )[0]
+
+    p1 = sent("image1", 1, n1, c1, rows013, (send_a,))
+    z1 = call("step1", step1_body, [shape(192, d)], (keep_a, got_a), (), (p1, got_b))[0]
     w = ring(z1, -2)
-    got_b = swap(send_b)
+    p3 = sent("image3", 2, n3, c3, rows013, (z1,))
+    p2 = sent("image2", 0, n2, c2, row2, (p3,))
+    r1, r3, r2 = second(p1, -1), second(p3, -3), second(p2, -2)
     p0 = call(
-        "own_image", own_image_body, [shape(256, d, dtype=F32)],
-        (near_c[0], far_c[0], near_mine, other, far), (), (z1,),
+        "own_image", own_image_body, [shape(256, d, dtype=F32)], (own_near, c0, far), (), (p2,)
     )[0]
     two, one = call("step2", step2_body, [shape(128, d)] * 2, (keep_b, got_b, w), (), (p0,))
     v2, v1 = ring(two, -2), ring(one, -1)
     own_img, own_loss, m1, m2, m3 = call(
         "merge_img", merge_img_body,
         [shape(rows, d, dtype=F32), shape(8, 256, dtype=F32)] + [shape(rows + 8, d)] * 3,
-        (p0, row0, r1, r2, r3), (), (one,),
+        (p0, rows013, r1, r2, r3), (), (one,),
     )
     q1, q3, q2 = first(m1, -1), first(m3, -3), first(m2, -2)
     z3 = call("step3", step3_body, [shape(64, d)], (own_pair, v1, v2), (), (m3,))[0]

time: 85 us -> 88.6 us (1.042)
  waiting for transfers between devices: 25 us -> 37.8 us
  starting transfers between devices: 42.3 us -> 33.1 us
    ppermute x6, waiting for transfers between devices: 2.51 us -> 16.5 us  [second(): lax.ppermute(a, AXES, permutation(lambda x, c, z, y: (x + s, c, z, y) if...]
    ppermute x6, starting transfers between devices: 11 us -> 5.31 us  [first(): lax.ppermute(a, AXES, permutation(lambda x, c, z, y: (x, c, z, y + s) if...]
    ppermute x6, starting transfers between devices: 9.82 us -> 7.9 us  [second(): lax.ppermute(a, AXES, permutation(lambda x, c, z, y: (x + s, c, z, y) if...]
    ppermute x6, waiting for transfers between devices: 10.1 us -> 8.45 us  [first(): lax.ppermute(a, AXES, permutation(lambda x, c, z, y: (x, c, z, y + s) if...]
    ppermute x6, starting transfers between devices: 13 us -> 11.4 us  [ring(): lax.ppermute(a, AXES, permutation(lambda x, c, z, y: (x, c, z - s if c el...]
    ppermute x6, waiting for transfers between devices: 1.3 us -> 2.19 us  [swap(): lax.ppermute(a, AXES, permutation(lambda x, c, z, y: (x, 1 - c, z, y)))]
    pallas_call x23 -> x20, Pallas kernels: 15.5 us -> 15.5 us  [call(): pl.pallas_call(kernel, out_shape=outs, in_specs=[SMEM] * len(scalars) + (...]
  transfers between devices with their start and end apart: 24 -> 24, of which waited for: 13 -> 14; matrix products, arithmetic and copies ran while one was open for 0% -> 0% of each run, Pallas kernels for 12% -> 12%
where the time goes in v8:
time: 88.6 us; the launch traced here: 88.5 us
  waiting for transfers between devices  37.8 us (43%)
  starting transfers between devices  33.1 us (37%)
  Pallas kernels  15.5 us (17%)
  between operations  2.13 us (2%)
    ppermute x6, waiting for transfers between devices, second(): lax.ppermute(a, AXES, permutation(lambda x, c, z, y: (x + s, c, z, y) if...  16.5 us
    pallas_call x20, Pallas kernels, call(): pl.pallas_call(kernel, out_shape=outs, in_specs=[SMEM] * len(scalars) + (...  15.5 us
    ppermute x6, starting transfers between devices, ring(): lax.ppermute(a, AXES, permutation(lambda x, c, z, y: (x, c, z - s if c el...  11.4 us
    ppermute x6, waiting for transfers between devices, ring(): lax.ppermute(a, AXES, permutation(lambda x, c, z, y: (x, c, z - s if c el...  10.6 us
    ppermute x6, starting transfers between devices, swap(): lax.ppermute(a, AXES, permutation(lambda x, c, z, y: (x, 1 - c, z, y)))  8.51 us
    ppermute x6, waiting for transfers between devices, first(): lax.ppermute(a, AXES, permutation(lambda x, c, z, y: (x, c, z, y + s) if...  8.45 us
    ppermute x6, starting transfers between devices, second(): lax.ppermute(a, AXES, permutation(lambda x, c, z, y: (x + s, c, z, y) if...  7.9 us
    ppermute x6, starting transfers between devices, first(): lax.ppermute(a, AXES, permutation(lambda x, c, z, y: (x, c, z, y + s) if...  5.31 us
  transfers between devices with their start and end apart: 24, of which 14 were waited for; matrix products, arithmetic and copies ran while one was open for 0% of the time, Pallas kernels for 12%

profile of v8, /device:TPU:1, one launch (start us, length us, event | category | flops | bytes accessed | tf_op | source)
XLA Modules:
  0.0 88.5 jit_solution(10511559487442643769)
XLA Ops:
  0.6 1.2 %normalize.1 = (bf16[64,1152]{1,0:T(8,128)(2,1)S(1)}, bf16[64,1152]{1,0:T(8,128)(2,1)S(1)}, f32[64,1]{1,0:T(8,128)S(1)}, f32[64,1]{1,0:T(8,128)S(1)}) custom-call(bf16[64,1152]{1,0:T(8,128)(2,1)} %refs_5_.1, bf16[64,1152]{1,0:T(8,128)(2,1)} %refs_11_.1), custom_call_target="tpu_custom_call" | custom-call | flops 1 | bytes 1 | tf_op jit(solution)/shard_map/normalize/pallas_call | solution.py:65
  1.8 3.3 %collective-permute-start.3 = (bf16[64,1152]{1,0:T(8,128)(2,1)S(1)}, bf16[64,1152]{1,0:T(8,128)(2,1)S(1)}, u32[]{:S(2)}, u32[]{:S(2)}) collective-permute-start(bf16[64,1152]{1,0:T(8,128)(2,1)S(1)} %get-tuple-element.40.refs_0_), channel_id=1, source_target_pairs={{0,32},{1,33},{2,34},{3,35},{4,36},{5,37},{6,38},{7,39},{8,40},{9,... | collective-permute-start | bytes 442376 | tf_op jit(solution)/shard_map/ppermute | solution.py:55
  5.1 1.0 %collective-permute-done.3.refs_1_ = bf16[64,1152]{1,0:T(8,128)(2,1)S(1)} collective-permute-done((bf16[64,1152]{1,0:T(8,128)(2,1)S(1)}, bf16[64,1152]{1,0:T(8,128)(2,1)S(1)}, u32[]{:S(2)}, u32[]{:S(2)}) %collective-permute-start.3) | collective-permute-done | bytes 147488 | tf_op jit(solution)/shard_map/ppermute | solution.py:55
  6.2 4.4 %collective-permute-start.5 = (bf16[128,1152]{1,0:T(8,128)(2,1)S(1)}, bf16[128,1152]{1,0:T(8,128)(2,1)S(1)}, u32[]{:S(2)}, u32[]{:S(2)}) collective-permute-start(bf16[128,1152]{1,0:T(8,128)(2,1)S(1)} %pair.1.refs_1_), channel_id=1, source_target_pairs={{0,8},{1,9},{2,10},{3,11},{4,12},{5,13},{6,14},{7,15},{8,16},{9,17... | collective-permute-start | bytes 884744 | tf_op jit(solution)/shard_map/ppermute | solution.py:51
  11.3 2.7 %collective-permute-start.2 = (bf16[64,1152]{1,0:T(8,128)(2,1)S(1)}, bf16[64,1152]{1,0:T(8,128)(2,1)S(1)}, u32[]{:S(2)}, u32[]{:S(2)}) collective-permute-start(bf16[64,1152]{1,0:T(8,128)(2,1)S(1)} %get-tuple-element.39.refs_0_), channel_id=1, source_target_pairs={{0,192},{1,193},{2,194},{3,195},{4,196},{5,197},{6,198},{7,199},{8... | collective-permute-start | bytes 442376 | tf_op jit(solution)/shard_map/ppermute | solution.py:39
  15.0 2.6 %collective-permute-done.2.refs_3_ = bf16[64,1152]{1,0:T(8,128)(2,1)S(1)} collective-permute-done((bf16[64,1152]{1,0:T(8,128)(2,1)S(1)}, bf16[64,1152]{1,0:T(8,128)(2,1)S(1)}, u32[]{:S(2)}, u32[]{:S(2)}) %collective-permute-start.2) | collective-permute-done | bytes 147488 | tf_op jit(solution)/shard_map/ppermute | solution.py:39
  17.7 1.9 %collective-permute-done.1.refs_2_ = bf16[64,1152]{1,0:T(8,128)(2,1)S(1)} collective-permute-done((bf16[64,1152]{1,0:T(8,128)(2,1)S(1)}, bf16[64,1152]{1,0:T(8,128)(2,1)S(1)}, u32[]{:S(2)}, u32[]{:S(2)}) %collective-permute-start.1) | collective-permute-done | bytes 147488 | tf_op jit(solution)/shard_map/ppermute | solution.py:39
  19.6 1.8 %collective-permute-done.refs_1_ = bf16[64,1152]{1,0:T(8,128)(2,1)S(1)} collective-permute-done((bf16[64,1152]{1,0:T(8,128)(2,1)S(1)}, bf16[64,1152]{1,0:T(8,128)(2,1)S(1)}, u32[]{:S(2)}, u32[]{:S(2)}) %collective-permute-start) | collective-permute-done | bytes 147488 | tf_op jit(solution)/shard_map/ppermute | solution.py:39
  21.9 2.6 %collective-permute-start.9 = (bf16[192,1152]{1,0:T(8,128)(2,1)S(1)}, bf16[192,1152]{1,0:T(8,128)(2,1)S(1)}, u32[]{:S(2)}, u32[]{:S(2)}) collective-permute-start(bf16[192,1152]{1,0:T(8,128)(2,1)S(1)} %get-tuple-element.43), channel_id=1, source_target_pairs={{0,8},{1,9},{2,10},{3,11},{4,12},{5,13},{6,14},{7,15},{8,16},{9,17... | collective-permute-start | bytes 1327112 | tf_op jit(solution)/shard_map/ppermute | solution.py:51
  24.6 2.5 %collective-permute-start.8 = (bf16[264,1152]{1,0:T(8,128)(2,1)S(1)}, bf16[264,1152]{1,0:T(8,128)(2,1)S(1)}, u32[]{:S(2)}, u32[]{:S(2)}) collective-permute-start(bf16[264,1152]{1,0:T(8,128)(2,1)S(1)} %group.1.refs_2_), channel_id=1, source_target_pairs={{0,3},{1,0},{2,1},{3,2},{4,7},{5,4},{6,5},{7,6},{8,11},{9,8},{10,9... | collective-permute-start | bytes 1824776 | tf_op jit(solution)/shard_map/ppermute | solution.py:45
  27.0 1.7 %collective-permute-start.11 = (bf16[264,1152]{1,0:T(8,128)(2,1)S(1)}, bf16[264,1152]{1,0:T(8,128)(2,1)S(1)}, u32[]{:S(2)}, u32[]{:S(2)}) collective-permute-start(bf16[264,1152]{1,0:T(8,128)(2,1)S(1)} %group.1.refs_2_), channel_id=1, source_target_pairs={{0,2},{1,3},{2,0},{3,1},{4,6},{5,7},{6,4},{7,5},{8,10},{9,11},{10,... | collective-permute-start | bytes 1824776 | tf_op jit(solution)/shard_map/ppermute | solution.py:45
  30.2 2.1 %own_near.1 = (bf16[256,640]{1,0:T(8,128)(2,1)}, f32[256,128]{1,0:T(8,128)S(1)}, f32[640,1152]{1,0:T(8,128)S(1)}, f32[256,1152]{1,0:T(8,128)S(1)}) custom-call(f32[1]{0:T(128)S(6)} %copy.7.refs_0_, f32[1]{0:T(128)S(6)} %copy.8.refs_1_, bf16[264,1152]{1,0:T(8,128)(2,1)S(1)} %group.1.refs_2_, ...), custom_call_target="tpu_custom_call" | custom-call | flops 1 | bytes 1 | tf_op jit(solution)/shard_map/own_near/pallas_call | solution.py:65
  32.3 3.1 %collective-permute-done.9.refs_0_ = bf16[192,1152]{1,0:T(8,128)(2,1)S(1)} collective-permute-done((bf16[192,1152]{1,0:T(8,128)(2,1)S(1)}, bf16[192,1152]{1,0:T(8,128)(2,1)S(1)}, u32[]{:S(2)}, u32[]{:S(2)}) %collective-permute-start.9) | collective-permute-done | bytes 442400 | tf_op jit(solution)/shard_map/ppermute | solution.py:51
  35.7 4.9 %collective-permute-done.8.refs_3_.refs_4_.refs_5_ = bf16[264,1152]{1,0:T(8,128)(2,1)S(1)} collective-permute-done((bf16[264,1152]{1,0:T(8,128)(2,1)S(1)}, bf16[264,1152]{1,0:T(8,128)(2,1)S(1)}, u32[]{:S(2)}, u32[]{:S(2)}) %collective-permute-start.8) | collective-permute-done | bytes 608288 | tf_op jit(solution)/shard_map/ppermute | solution.py:45
  40.6 3.4 %collective-permute-done.7.refs_2_.refs_3_ = bf16[264,1152]{1,0:T(8,128)(2,1)S(1)} collective-permute-done((bf16[264,1152]{1,0:T(8,128)(2,1)S(1)}, bf16[264,1152]{1,0:T(8,128)(2,1)S(1)}, u32[]{:S(2)}, u32[]{:S(2)}) %collective-permute-start.7) | collective-permute-done | bytes 608288 | tf_op jit(solution)/shard_map/ppermute | solution.py:45
  44.0 2.5 %near_pair.1 = (bf16[256,640]{1,0:T(8,128)(2,1)S(1)}, bf16[256,640]{1,0:T(8,128)(2,1)S(1)}, f32[256,128]{1,0:T(8,128)S(1)}, f32[256,128]{1,0:T(8,128)S(1)}, f32[640,1152]{1,0:T(8,128)S(1)}) custom-call(f32[1]{0:T(128)S(6)} %copy.7.refs_0_, f32[1]{0:T(128)S(6)} %copy.8.refs_1_, bf16[264,1152]{1,0:T(8,128)(2,1)S(1)} %collective-permute-done.7.refs_2_.refs_3_, ...), custom_call_target="tpu_custom_call" | custom-call | flops 1 | bytes 1 | tf_op jit(solution)/shard_map/near_pair/pallas_call | solution.py:65
  46.6 1.6 %far.1 = (bf16[256,384]{1,0:T(8,128)(2,1)S(1)}, bf16[256,384]{1,0:T(8,128)(2,1)S(1)}, bf16[256,384]{1,0:T(8,128)(2,1)S(1)}, f32[8,768]{1,0:T(8,128)S(1)}) custom-call(f32[1]{0:T(128)S(6)} %copy.7.refs_0_, f32[1]{0:T(128)S(6)} %copy.8.refs_1_, bf16[264,1152]{1,0:T(8,128)(2,1)S(1)} %group.1.refs_2_, ...), custom_call_target="tpu_custom_call" | custom-call | flops 1 | bytes 1 | tf_op jit(solution)/shard_map/far/pallas_call | solution.py:65
  48.2 2.7 %last.1 = (bf16[256,640]{1,0:T(8,128)(2,1)S(1)}, bf16[256,384]{1,0:T(8,128)(2,1)S(1)}, f32[8,256]{1,0:T(8,128)S(1)}, f32[192,1152]{1,0:T(8,128)S(1)}, bf16[192,1...) custom-call(f32[1]{0:T(128)S(6)} %copy.7.refs_0_, ...), custom_call_target="tpu_custom_call" | custom-call | flops 1 | bytes 1 | tf_op jit(solution)/shard_map/last/pallas_call | solution.py:65
  50.9 1.9 %collective-permute-start.13 = (bf16[256,1152]{1,0:T(8,128)(2,1)S(1)}, bf16[256,1152]{1,0:T(8,128)(2,1)S(1)}, u32[]{:S(2)}, u32[]{:S(2)}) collective-permute-start(bf16[256,1152]{1,0:T(8,128)(2,1)S(1)} %get-tuple-element.60), channel_id=1, source_target_pairs={{0,32},{1,33},{2,34},{3,35},{4,36},{5,37},{6,38},{7,39},{8,40},{9,... | collective-permute-start | bytes 1769480 | tf_op jit(solution)/shard_map/ppermute | solution.py:55
  53.9 1.2 %collective-permute-done.12.refs_1_ = bf16[192,1152]{1,0:T(8,128)(2,1)S(1)} collective-permute-done((bf16[192,1152]{1,0:T(8,128)(2,1)S(1)}, bf16[192,1152]{1,0:T(8,128)(2,1)S(1)}, u32[]{:S(2)}, u32[]{:S(2)}) %collective-permute-start.12) | collective-permute-done | bytes 442400 | tf_op jit(solution)/shard_map/ppermute | solution.py:55
  55.1 2.4 %collective-permute-start.17 = (bf16[192,1152]{1,0:T(8,128)(2,1)S(1)}, bf16[192,1152]{1,0:T(8,128)(2,1)S(1)}, u32[]{:S(2)}, u32[]{:S(2)}) collective-permute-start(bf16[192,1152]{1,0:T(8,128)(2,1)S(1)} %step1.1.refs_6_), channel_id=1, source_target_pairs={{0,24},{1,25},{2,26},{3,27},{4,28},{5,29},{6,30},{7,31},{8,0},{9,1... | collective-permute-start | bytes 1327112 | tf_op jit(solution)/shard_map/ppermute | solution.py:51
  57.6 2.5 %collective-permute-start.14 = (bf16[264,1152]{1,0:T(8,128)(2,1)S(1)}, bf16[264,1152]{1,0:T(8,128)(2,1)S(1)}, u32[]{:S(2)}, u32[]{:S(2)}) collective-permute-start(bf16[264,1152]{1,0:T(8,128)(2,1)S(1)} %image1.1.refs_2_), channel_id=1, source_target_pairs={{0,3},{1,0},{2,1},{3,2},{4,7},{5,4},{6,5},{7,6},{8,11},{9,8},{10,9... | collective-permute-start | bytes 1824776 | tf_op jit(solution)/shard_map/ppermute | solution.py:45
  60.0 1.0 %image3.1.refs_6_ = bf16[264,1152]{1,0:T(8,128)(2,1)S(1)} custom-call(bf16[256,640]{1,0:T(8,128)(2,1)S(1)} %get-tuple-element.55.refs_0_, bf16[256,384]{1,0:T(8,128)(2,1)S(1)} %get-tuple-element.50.refs_11_.refs_1_, bf16[256,1152]{1,0:T(8,128)(2,1)S(1)} %get-tuple-element.41.refs_3_.refs_4_.refs_6_.refs_2_, ...), custom_call_target="tpu_custom_call" | custom-call | flops 1 | bytes 1 | tf_op jit(solution)/shard_map/image3/pallas_call | solution.py:65
  63.7 5.8 %collective-permute-done.17.refs_2_ = bf16[192,1152]{1,0:T(8,128)(2,1)S(1)} collective-permute-done((bf16[192,1152]{1,0:T(8,128)(2,1)S(1)}, bf16[192,1152]{1,0:T(8,128)(2,1)S(1)}, u32[]{:S(2)}, u32[]{:S(2)}) %collective-permute-start.17) | collective-permute-done | bytes 442400 | tf_op jit(solution)/shard_map/ppermute | solution.py:51
  69.7 1.3 %collective-permute-start.22 = (bf16[128,1152]{1,0:T(8,128)(2,1)S(1)}, bf16[128,1152]{1,0:T(8,128)(2,1)S(1)}, u32[]{:S(2)}, u32[]{:S(2)}) collective-permute-start(bf16[128,1152]{1,0:T(8,128)(2,1)S(1)} %get-tuple-element.70), channel_id=1, source_target_pairs={{0,24},{1,25},{2,26},{3,27},{4,28},{5,29},{6,30},{7,31},{8,0},{9,1... | collective-permute-start | bytes 884744 | tf_op jit(solution)/shard_map/ppermute | solution.py:51
  71.0 2.6 %collective-permute-done.14.refs_2_ = bf16[264,1152]{1,0:T(8,128)(2,1)S(1)} collective-permute-done((bf16[264,1152]{1,0:T(8,128)(2,1)S(1)}, bf16[264,1152]{1,0:T(8,128)(2,1)S(1)}, u32[]{:S(2)}, u32[]{:S(2)}) %collective-permute-start.14) | collective-permute-done | bytes 608288 | tf_op jit(solution)/shard_map/ppermute | solution.py:45
  73.6 5.6 %collective-permute-done.16.refs_4_ = bf16[264,1152]{1,0:T(8,128)(2,1)S(1)} collective-permute-done((bf16[264,1152]{1,0:T(8,128)(2,1)S(1)}, bf16[264,1152]{1,0:T(8,128)(2,1)S(1)}, u32[]{:S(2)}, u32[]{:S(2)}) %collective-permute-start.16) | collective-permute-done | bytes 608288 | tf_op jit(solution)/shard_map/ppermute | solution.py:45
  79.7 1.4 %collective-permute-start.20 = (bf16[72,1152]{1,0:T(8,128)(2,1)S(1)}, bf16[72,1152]{1,0:T(8,128)(2,1)S(1)}, u32[]{:S(2)}, u32[]{:S(2)}) collective-permute-start(bf16[72,1152]{1,0:T(8,128)(2,1)S(1)} %get-tuple-element.67.refs_3_), channel_id=1, source_target_pairs={{0,64},{1,65},{2,66},{3,67},{4,68},{5,69},{6,70},{7,71},{8,72},{9,... | collective-permute-start | bytes 497672 | tf_op jit(solution)/shard_map/ppermute | solution.py:39
  81.1 1.7 %collective-permute-done.21.refs_1_.refs_8_ = bf16[128,1152]{1,0:T(8,128)(2,1)S(1)} collective-permute-done((bf16[128,1152]{1,0:T(8,128)(2,1)S(1)}, bf16[128,1152]{1,0:T(8,128)(2,1)S(1)}, u32[]{:S(2)}, u32[]{:S(2)}) %collective-permute-start.21) | collective-permute-done | bytes 294944 | tf_op jit(solution)/shard_map/ppermute | solution.py:51
  82.8 2.5 %collective-permute-start.23 = (bf16[64,1152]{1,0:T(8,128)(2,1)S(1)}, bf16[64,1152]{1,0:T(8,128)(2,1)S(1)}, u32[]{:S(2)}, u32[]{:S(2)}) collective-permute-start(bf16[64,1152]{1,0:T(8,128)(2,1)S(1)} %step3.1), channel_id=1, source_target_pairs={{0,32},{1,33},{2,34},{3,35},{4,36},{5,37},{6,38},{7,39},{8,40},{9,... | collective-permute-start | bytes 442376 | tf_op jit(solution)/shard_map/ppermute | solution.py:55
  85.7 1.8 %collective-permute-done.20.refs_4_ = bf16[72,1152]{1,0:T(8,128)(2,1)S(1)} collective-permute-done((bf16[72,1152]{1,0:T(8,128)(2,1)S(1)}, bf16[72,1152]{1,0:T(8,128)(2,1)S(1)}, u32[]{:S(2)}, u32[]{:S(2)}) %collective-permute-start.20) | collective-permute-done | bytes 165920 | tf_op jit(solution)/shard_map/ppermute | solution.py:39
  87.5 1.1 %finish.1 = (f32[64,1152]{1,0:T(8,128)}, f32[64,1152]{1,0:T(8,128)}, f32[1,64]{1,0:T(1,128)}) custom-call(f32[64,1152]{1,0:T(8,128)S(1)} %get-tuple-element.63.refs_0_, f32[8,256]{1,0:T(8,128)S(1)} %get-tuple-element.64.refs_1_, bf16[72,1152]{1,0:T(8,128)(2,1)S(1)} %collective-permute-done.18.refs_2_, bf16[72,1152]{1,0:T(8,128)(2,1)S(1)} %collective-permute-done.19.refs_3_, ...), custom_call_target="tpu_custom_call" | custom-call | flops 1 | bytes 1 | tf_op jit(solution)/shard_map/finish/pallas_call | solution.py:65
  (40 shorter events, 7.7 us)
Async XLA Ops:
  1.8 4.3 %collective-permute-start.3 = (bf16[64,1152]{1,0:T(8,128)(2,1)S(1)}, bf16[64,1152]{1,0:T(8,128)(2,1)S(1)}, u32[]{:S(2)}, u32[]{:S(2)}) collective-permute-start(bf16[64,1152]{1,0:T(8,128)(2,1)S(1)} %get-tuple-element.40.refs_0_), channel_id=1, source_target_pairs={{0,32},{1,33},{2,34},{3,35},{4,36},{5,37},{6,38},{7,39},{8,40},{9,... | collective-permute-start | bytes 442376 | tf_op jit(solution)/shard_map/ppermute | solution.py:55
  6.2 15.2 %collective-permute-start.5 = (bf16[128,1152]{1,0:T(8,128)(2,1)S(1)}, bf16[128,1152]{1,0:T(8,128)(2,1)S(1)}, u32[]{:S(2)}, u32[]{:S(2)}) collective-permute-start(bf16[128,1152]{1,0:T(8,128)(2,1)S(1)} %pair.1.refs_1_), channel_id=1, source_target_pairs={{0,8},{1,9},{2,10},{3,11},{4,12},{5,13},{6,14},{7,15},{8,16},{9,17... | collective-permute-start | bytes 884744 | tf_op jit(solution)/shard_map/ppermute | solution.py:51
  10.5 10.9 %collective-permute-start.4 = (bf16[128,1152]{1,0:T(8,128)(2,1)S(1)}, bf16[128,1152]{1,0:T(8,128)(2,1)S(1)}, u32[]{:S(2)}, u32[]{:S(2)}) collective-permute-start(bf16[128,1152]{1,0:T(8,128)(2,1)S(1)} %pair.1.refs_1_), channel_id=1, source_target_pairs={{0,4},{1,5},{2,6},{3,7},{4,8},{5,9},{6,10},{7,11},{8,12},{9,13},{1... | collective-permute-start | bytes 884744 | tf_op jit(solution)/shard_map/ppermute | solution.py:51
  11.3 6.4 %collective-permute-start.2 = (bf16[64,1152]{1,0:T(8,128)(2,1)S(1)}, bf16[64,1152]{1,0:T(8,128)(2,1)S(1)}, u32[]{:S(2)}, u32[]{:S(2)}) collective-permute-start(bf16[64,1152]{1,0:T(8,128)(2,1)S(1)} %get-tuple-element.39.refs_0_), channel_id=1, source_target_pairs={{0,192},{1,193},{2,194},{3,195},{4,196},{5,197},{6,198},{7,199},{8... | collective-permute-start | bytes 442376 | tf_op jit(solution)/shard_map/ppermute | solution.py:39
  14.0 5.6 %collective-permute-start.1 = (bf16[64,1152]{1,0:T(8,128)(2,1)S(1)}, bf16[64,1152]{1,0:T(8,128)(2,1)S(1)}, u32[]{:S(2)}, u32[]{:S(2)}) collective-permute-start(bf16[64,1152]{1,0:T(8,128)(2,1)S(1)} %get-tuple-element.39.refs_0_), channel_id=1, source_target_pairs={{0,128},{1,129},{2,130},{3,131},{4,132},{5,133},{6,134},{7,135},{8... | collective-permute-start | bytes 442376 | tf_op jit(solution)/shard_map/ppermute | solution.py:39
  14.3 7.0 %collective-permute-start = (bf16[64,1152]{1,0:T(8,128)(2,1)S(1)}, bf16[64,1152]{1,0:T(8,128)(2,1)S(1)}, u32[]{:S(2)}, u32[]{:S(2)}) collective-permute-start(bf16[64,1152]{1,0:T(8,128)(2,1)S(1)} %get-tuple-element.39.refs_0_), channel_id=1, source_target_pairs={{0,64},{1,65},{2,66},{3,67},{4,68},{5,69},{6,70},{7,71},{8,72},{9,... | collective-permute-start | bytes 442376 | tf_op jit(solution)/shard_map/ppermute | solution.py:39
  21.5 8.6 %collective-permute-start.6 = (bf16[256,1152]{1,0:T(8,128)(2,1)S(1)}, bf16[256,1152]{1,0:T(8,128)(2,1)S(1)}, u32[]{:S(2)}, u32[]{:S(2)}) collective-permute-start(bf16[256,1152]{1,0:T(8,128)(2,1)S(1)} %get-tuple-element.41.refs_3_.refs_4_.refs_6_.refs_2_), channel_id=1, source_target_pairs={{0,32},{1,33},{2,34},{3,35},{4,36},{5,37},{6,38},{7,39},{8,40},{9,... | collective-permute-start | bytes 1769480 | tf_op jit(solution)/shard_map/ppermute | solution.py:55
  21.9 13.4 %collective-permute-start.9 = (bf16[192,1152]{1,0:T(8,128)(2,1)S(1)}, bf16[192,1152]{1,0:T(8,128)(2,1)S(1)}, u32[]{:S(2)}, u32[]{:S(2)}) collective-permute-start(bf16[192,1152]{1,0:T(8,128)(2,1)S(1)} %get-tuple-element.43), channel_id=1, source_target_pairs={{0,8},{1,9},{2,10},{3,11},{4,12},{5,13},{6,14},{7,15},{8,16},{9,17... | collective-permute-start | bytes 1327112 | tf_op jit(solution)/shard_map/ppermute | solution.py:51
  24.6 16.0 %collective-permute-start.8 = (bf16[264,1152]{1,0:T(8,128)(2,1)S(1)}, bf16[264,1152]{1,0:T(8,128)(2,1)S(1)}, u32[]{:S(2)}, u32[]{:S(2)}) collective-permute-start(bf16[264,1152]{1,0:T(8,128)(2,1)S(1)} %group.1.refs_2_), channel_id=1, source_target_pairs={{0,3},{1,0},{2,1},{3,2},{4,7},{5,4},{6,5},{7,6},{8,11},{9,8},{10,9... | collective-permute-start | bytes 1824776 | tf_op jit(solution)/shard_map/ppermute | solution.py:45
  27.0 17.0 %collective-permute-start.7 = (bf16[264,1152]{1,0:T(8,128)(2,1)S(1)}, bf16[264,1152]{1,0:T(8,128)(2,1)S(1)}, u32[]{:S(2)}, u32[]{:S(2)}) collective-permute-start(bf16[264,1152]{1,0:T(8,128)(2,1)S(1)} %group.1.refs_2_), channel_id=1, source_target_pairs={{0,1},{1,2},{2,3},{3,0},{4,5},{5,6},{6,7},{7,4},{8,9},{9,10},{10,1... | collective-permute-start | bytes 1824776 | tf_op jit(solution)/shard_map/ppermute | solution.py:45
  27.0 21.1 %collective-permute-start.11 = (bf16[264,1152]{1,0:T(8,128)(2,1)S(1)}, bf16[264,1152]{1,0:T(8,128)(2,1)S(1)}, u32[]{:S(2)}, u32[]{:S(2)}) collective-permute-start(bf16[264,1152]{1,0:T(8,128)(2,1)S(1)} %group.1.refs_2_), channel_id=1, source_target_pairs={{0,2},{1,3},{2,0},{3,1},{4,6},{5,7},{6,4},{7,5},{8,10},{9,11},{10,... | collective-permute-start | bytes 1824776 | tf_op jit(solution)/shard_map/ppermute | solution.py:45
  35.4 11.1 %collective-permute-start.10 = (bf16[192,1152]{1,0:T(8,128)(2,1)S(1)}, bf16[192,1152]{1,0:T(8,128)(2,1)S(1)}, u32[]{:S(2)}, u32[]{:S(2)}) collective-permute-start(bf16[192,1152]{1,0:T(8,128)(2,1)S(1)} %far_mine.1.refs_7_.refs_0_), channel_id=1, source_target_pairs={{0,32},{1,33},{2,34},{3,35},{4,36},{5,37},{6,38},{7,39},{8,40},{9,... | collective-permute-start | bytes 1327112 | tf_op jit(solution)/shard_map/ppermute | solution.py:55
  50.9 4.1 %collective-permute-start.13 = (bf16[256,1152]{1,0:T(8,128)(2,1)S(1)}, bf16[256,1152]{1,0:T(8,128)(2,1)S(1)}, u32[]{:S(2)}, u32[]{:S(2)}) collective-permute-start(bf16[256,1152]{1,0:T(8,128)(2,1)S(1)} %get-tuple-element.60), channel_id=1, source_target_pairs={{0,32},{1,33},{2,34},{3,35},{4,36},{5,37},{6,38},{7,39},{8,40},{9,... | collective-permute-start | bytes 1769480 | tf_op jit(solution)/shard_map/ppermute | solution.py:55
  52.8 2.3 %collective-permute-start.12 = (bf16[192,1152]{1,0:T(8,128)(2,1)S(1)}, bf16[192,1152]{1,0:T(8,128)(2,1)S(1)}, u32[]{:S(2)}, u32[]{:S(2)}) collective-permute-start(bf16[192,1152]{1,0:T(8,128)(2,1)S(1)} %get-tuple-element.58.refs_6_), channel_id=1, source_target_pairs={{0,32},{1,33},{2,34},{3,35},{4,36},{5,37},{6,38},{7,39},{8,40},{9,... | collective-permute-start | bytes 1327112 | tf_op jit(solution)/shard_map/ppermute | solution.py:55
  55.1 14.4 %collective-permute-start.17 = (bf16[192,1152]{1,0:T(8,128)(2,1)S(1)}, bf16[192,1152]{1,0:T(8,128)(2,1)S(1)}, u32[]{:S(2)}, u32[]{:S(2)}) collective-permute-start(bf16[192,1152]{1,0:T(8,128)(2,1)S(1)} %step1.1.refs_6_), channel_id=1, source_target_pairs={{0,24},{1,25},{2,26},{3,27},{4,28},{5,29},{6,30},{7,31},{8,0},{9,1... | collective-permute-start | bytes 1327112 | tf_op jit(solution)/shard_map/ppermute | solution.py:51
  57.6 16.0 %collective-permute-start.14 = (bf16[264,1152]{1,0:T(8,128)(2,1)S(1)}, bf16[264,1152]{1,0:T(8,128)(2,1)S(1)}, u32[]{:S(2)}, u32[]{:S(2)}) collective-permute-start(bf16[264,1152]{1,0:T(8,128)(2,1)S(1)} %image1.1.refs_2_), channel_id=1, source_target_pairs={{0,3},{1,0},{2,1},{3,2},{4,7},{5,4},{6,5},{7,6},{8,11},{9,8},{10,9... | collective-permute-start | bytes 1824776 | tf_op jit(solution)/shard_map/ppermute | solution.py:45
  62.0 11.6 %collective-permute-start.15 = (bf16[264,1152]{1,0:T(8,128)(2,1)S(1)}, bf16[264,1152]{1,0:T(8,128)(2,1)S(1)}, u32[]{:S(2)}, u32[]{:S(2)}) collective-permute-start(bf16[264,1152]{1,0:T(8,128)(2,1)S(1)} %image2.1.refs_3_), channel_id=1, source_target_pairs={{0,2},{1,3},{2,0},{3,1},{4,6},{5,7},{6,4},{7,5},{8,10},{9,11},{10,... | collective-permute-start | bytes 1824776 | tf_op jit(solution)/shard_map/ppermute | solution.py:45
  62.6 16.6 %collective-permute-start.16 = (bf16[264,1152]{1,0:T(8,128)(2,1)S(1)}, bf16[264,1152]{1,0:T(8,128)(2,1)S(1)}, u32[]{:S(2)}, u32[]{:S(2)}) collective-permute-start(bf16[264,1152]{1,0:T(8,128)(2,1)S(1)} %image3.1.refs_6_), channel_id=1, source_target_pairs={{0,1},{1,2},{2,3},{3,0},{4,5},{5,6},{6,7},{7,4},{8,9},{9,10},{10,1... | collective-permute-start | bytes 1824776 | tf_op jit(solution)/shard_map/ppermute | solution.py:45
  69.7 11.4 %collective-permute-start.22 = (bf16[128,1152]{1,0:T(8,128)(2,1)S(1)}, bf16[128,1152]{1,0:T(8,128)(2,1)S(1)}, u32[]{:S(2)}, u32[]{:S(2)}) collective-permute-start(bf16[128,1152]{1,0:T(8,128)(2,1)S(1)} %get-tuple-element.70), channel_id=1, source_target_pairs={{0,24},{1,25},{2,26},{3,27},{4,28},{5,29},{6,30},{7,31},{8,0},{9,1... | collective-permute-start | bytes 884744 | tf_op jit(solution)/shard_map/ppermute | solution.py:51
  71.0 11.8 %collective-permute-start.21 = (bf16[128,1152]{1,0:T(8,128)(2,1)S(1)}, bf16[128,1152]{1,0:T(8,128)(2,1)S(1)}, u32[]{:S(2)}, u32[]{:S(2)}) collective-permute-start(bf16[128,1152]{1,0:T(8,128)(2,1)S(1)} %get-tuple-element.62.refs_5_), channel_id=1, source_target_pairs={{0,28},{1,29},{2,30},{3,31},{4,0},{5,1},{6,2},{7,3},{8,4},{9,5},{1... | collective-permute-start | bytes 884744 | tf_op jit(solution)/shard_map/ppermute | solution.py:51
  79.5 8.0 %copy-start = (bf16[64,1152]{1,0:T(8,128)(2,1)S(1)}, bf16[64,1152]{1,0:T(8,128)(2,1)}, u32[]{:S(2)}) copy-start(bf16[64,1152]{1,0:T(8,128)(2,1)} %refs_5_.1) | copy-start | bytes 442372
  79.5 8.0 %copy-start.1 = (bf16[64,1152]{1,0:T(8,128)(2,1)S(1)}, bf16[64,1152]{1,0:T(8,128)(2,1)}, u32[]{:S(2)}) copy-start(bf16[64,1152]{1,0:T(8,128)(2,1)} %refs_11_.1) | copy-start | bytes 442372
  79.5 5.8 %collective-permute-start.18 = (bf16[72,1152]{1,0:T(8,128)(2,1)S(1)}, bf16[72,1152]{1,0:T(8,128)(2,1)S(1)}, u32[]{:S(2)}, u32[]{:S(2)}) collective-permute-start(bf16[72,1152]{1,0:T(8,128)(2,1)S(1)} %get-tuple-element.65), channel_id=1, source_target_pairs={{0,192},{1,193},{2,194},{3,195},{4,196},{5,197},{6,198},{7,199},{8... | collective-permute-start | bytes 497672 | tf_op jit(solution)/shard_map/ppermute | solution.py:39
  79.6 6.1 %collective-permute-start.19 = (bf16[72,1152]{1,0:T(8,128)(2,1)S(1)}, bf16[72,1152]{1,0:T(8,128)(2,1)S(1)}, u32[]{:S(2)}, u32[]{:S(2)}) collective-permute-start(bf16[72,1152]{1,0:T(8,128)(2,1)S(1)} %get-tuple-element.66), channel_id=1, source_target_pairs={{0,128},{1,129},{2,130},{3,131},{4,132},{5,133},{6,134},{7,135},{8... | collective-permute-start | bytes 497672 | tf_op jit(solution)/shard_map/ppermute | solution.py:39
  79.7 7.8 %collective-permute-start.20 = (bf16[72,1152]{1,0:T(8,128)(2,1)S(1)}, bf16[72,1152]{1,0:T(8,128)(2,1)S(1)}, u32[]{:S(2)}, u32[]{:S(2)}) collective-permute-start(bf16[72,1152]{1,0:T(8,128)(2,1)S(1)} %get-tuple-element.67.refs_3_), channel_id=1, source_target_pairs={{0,64},{1,65},{2,66},{3,67},{4,68},{5,69},{6,70},{7,71},{8,72},{9,... | collective-permute-start | bytes 497672 | tf_op jit(solution)/shard_map/ppermute | solution.py:39
  82.8 4.7 %collective-permute-start.23 = (bf16[64,1152]{1,0:T(8,128)(2,1)S(1)}, bf16[64,1152]{1,0:T(8,128)(2,1)S(1)}, u32[]{:S(2)}, u32[]{:S(2)}) collective-permute-start(bf16[64,1152]{1,0:T(8,128)(2,1)S(1)} %step3.1), channel_id=1, source_target_pairs={{0,32},{1,33},{2,34},{3,35},{4,36},{5,37},{6,38},{7,39},{8,40},{9,... | collective-permute-start | bytes 442376 | tf_op jit(solution)/shard_map/ppermute | solution.py:55

commit v9 on v8

--- a/solution.py
+++ b/solution.py
@@ -179,18 +179,23 @@
     return jnp.dot(cf[...], far[...], preferred_element_type=F32)
 
 
-def own_near_body(scale_ref, bias_ref, img, mine, other, cn, loss, part, g):
-    zero = jnp.zeros((256, 128), F32)
-    loss[...] = near_tile(img, mine, other, cn, zero, scale_ref[0], bias_ref[0], True)
-    part[...] = texts((cn,), (img,), 0, 640)
-    g[...] = near_image(cn, mine, other)
-
-
-def near_pair_body(scale_ref, bias_ref, i1, i3, mine, other, part0, n1, n3, l1, l3, part):
-    zero = jnp.zeros((256, 128), F32)
-    for i, n, l in ((i1, n1, l1), (i3, n3, l3)):
-        l[...] = near_tile(i, mine, other, n, zero, scale_ref[0], bias_ref[0])
-    part[...] = part0[...] + texts((n1, n3), (i1, i3), 0, 640)
+def mine_body(scale_ref, bias_ref, img_ref, txt_ref, coeff_ref, loss_ref):
+    weight, softplus = entry(img_ref[:256, :], txt_ref[...], scale_ref[0], bias_ref[0])
+    coeff_ref[...] = weight
+    loss_ref[...] = fold(softplus)
+
+
+def other_body(scale_ref, bias_ref, i0, i1, i3, m0, m1, m3, l0, l1, l3, txt_ref, n0, n1, n3, t0, t1, t3, part):
+    groups = ((i0, m0, l0, n0, t0), (i1, m1, l1, n1, t1), (i3, m3, l3, n3, t3))
+    for k, (i, m, l, n, t) in enumerate(groups):
+        n[:, :256] = m[...]
+        t[...] = tile(i, txt_ref, n.at[:, 256:], l[...], scale_ref[0], bias_ref[0], k == 0)
+    part[...] = texts((n0, n1, n3), (i0, i1, i3), 0, 640)
+
+
+def near_images_body(n0, n1, n3, mine, other, g0, g1, g3):
+    for n, g in ((n0, g0), (n1, g1), (n3, g3)):
+        g[...] = near_image(n, mine, other)
 
 
 def far_body(scale_ref, bias_ref, i0, i1, i3, far, l0, l1, l3, c0, c1, c3, rows):
@@ -212,11 +217,18 @@
     pair[...] = g[512:, :]
 
 
-def image_body(at, cn, cf, mine, other, far, row, out):
-    g = near_image(cn, mine, other) + far_image(cf, far)
+def send_image(out, g, row):
     out[:256, :] = g.astype(BF16)
     out[256:, :] = jnp.zeros((8, g.shape[1]), BF16)
-    out[256:, :256] = loss_rows(row[:, 256 * at : 256 * (at + 1)])
+    out[256:, :256] = loss_rows(row)
+
+
+def image_body(at, near, cf, far, row, out):
+    send_image(out, near[...] + far_image(cf, far), row[:, 256 * at : 256 * (at + 1)])
+
+
+def last_image_body(cn, cf, mine, other, far, row, out):
+    send_image(out, near_image(cn, mine, other) + far_image(cf, far), row[...])
 
 
 def own_image_body(near, cf, far, out):
@@ -248,9 +260,8 @@
         out[at:, :] = jnp.zeros((out.shape[0] - at, out.shape[1]), out.dtype)
 
 
-def split_body(b1, b2, far, near):
-    far[:U, :] = b2[:U, :]
-    far[U:, :] = b1[...]
+def split_body(b1, b2, half, near):
+    half[...] = b2[:U, :]
     near[:128, :] = b2[...]
     near[128:, :] = b1[...]
 
@@ -303,29 +314,36 @@
     group = pack("group", 264, (img, f1, f2, f3))
     g1, g3, g2 = second(group, 1), second(group, 3), second(group, 2)
     groups = (group, g1, g2, g3)
-    far_pack, near_mine = call(
-        "pack", split_body, [shape(192, d), shape(256, d)], (b1, b2), (), (group,)
-    )
-    far_got = ring(far_pack, 2)
+    half, near_mine = call(
+        "pack", split_body, [shape(64, d), shape(256, d)], (b1, b2), (), (group,)
+    )
     near_other = swap(near_mine)
+    b3, b4 = ring(b2, 1), ring(half, 2)
 
     sc = (scale, bias)
-    other = pack("other_texts", 384, (near_other, pair))
-    own_c, own_l, part0, own_near = call(
-        "own_near", own_near_body,
-        [shape(256, 640), shape(256, 128, dtype=F32), shape(640, d, dtype=F32), shape(256, d, dtype=F32)],
-        (group, near_mine, other), sc,
-    )
-    far_mine = pack("far_mine", 192, (far_got,), (own_l,))
-    n1, n3, l1, l3, part = call(
-        "near_pair", near_pair_body,
-        [shape(256, 640)] * 2 + [shape(256, 128, dtype=F32)] * 2 + [shape(640, d, dtype=F32)],
-        (g1, g3, near_mine, other, part0), sc, (far_mine,),
-    )
-    far = pack("far_texts", 384, (far_mine, swap(far_mine)), (l1,))
+    mine_c, mine_l, last = {}, {}, ()
+    for k in (0, 1, 3):
+        mine_c[k], mine_l[k] = call(
+            f"mine{k}", mine_body, [shape(256, 256), shape(256, 128, dtype=F32)],
+            (groups[k], near_mine), sc, last,
+        )
+        last = (mine_l[k],)
+    other = pack("other_texts", 384, (near_other, pair), last)
+    n0, n1, n3, l0, l1, l3, part = call(
+        "other", other_body,
+        [shape(256, 640)] * 3 + [shape(256, 128, dtype=F32)] * 3 + [shape(640, d, dtype=F32)],
+        (group, g1, g3, *mine_c.values(), *mine_l.values(), other), sc,
+    )
+    far_mine = pack("far_mine", 192, (b4, b3), (l0,))
+    far_other = swap(far_mine)
+    t0, t1, t3 = call(
+        "near_images", near_images_body, [shape(256, d, dtype=F32)] * 3,
+        (n0, n1, n3, near_mine, other), (), (far_mine,),
+    )
+    far = pack("far_texts", 384, (far_mine, far_other), (t0,))
     c0, c1, c3, rows013 = call(
         "far", far_body, [shape(256, 384)] * 3 + [shape(8, 768, dtype=F32)],
-        (group, g1, g3, far, own_l, l1, l3), sc,
+        (group, g1, g3, far, l0, l1, l3), sc,
     )
     n2, c2, row2, keep_a, send_a, keep_b, send_b, own_pair = call(
         "last", last_body,
@@ -335,20 +353,22 @@
     )
     got_a, got_b = swap(send_a), swap(send_b)
 
-    def sent(name, at, cn, cf, row, after):
+    def sent(name, at, near, cf, after):
         return call(
             name, functools.partial(image_body, at), [shape(264, d)],
-            (cn, cf, near_mine, other, far, row), (), after,
+            (near, cf, far, rows013), (), after,
         )[0]
 
-    p1 = sent("image1", 1, n1, c1, rows013, (send_a,))
+    p1 = sent("image1", 1, t1, c1, (send_a,))
     z1 = call("step1", step1_body, [shape(192, d)], (keep_a, got_a), (), (p1, got_b))[0]
     w = ring(z1, -2)
-    p3 = sent("image3", 2, n3, c3, rows013, (z1,))
-    p2 = sent("image2", 0, n2, c2, row2, (p3,))
+    p3 = sent("image3", 2, t3, c3, (z1,))
+    p2 = call(
+        "image2", last_image_body, [shape(264, d)], (n2, c2, near_mine, other, far, row2), (), (p3,)
+    )[0]
     r1, r3, r2 = second(p1, -1), second(p3, -3), second(p2, -2)
     p0 = call(
-        "own_image", own_image_body, [shape(256, d, dtype=F32)], (own_near, c0, far), (), (p2,)
+        "own_image", own_image_body, [shape(256, d, dtype=F32)], (t0, c0, far), (), (p2,)
     )[0]
     two, one = call("step2", step2_body, [shape(128, d)] * 2, (keep_b, got_b, w), (), (p0,))
     v2, v1 = ring(two, -2), ring(one, -1)

time: 88.6 us -> 81 us (0.914); the launches traced: 88.5 us -> 79.8 us
  waiting for transfers between devices: 37.8 us -> 27.9 us
  starting transfers between devices: 33.1 us -> 34.3 us
    ppermute x6, waiting for transfers between devices: 16.5 us -> 6.46 us  [second(): lax.ppermute(a, AXES, permutation(lambda x, c, z, y: (x + s, c, z, y) if...]
    ppermute x6 -> x7, waiting for transfers between devices: 10.6 us -> 16.9 us  [ring(): lax.ppermute(a, AXES, permutation(lambda x, c, z, y: (x, c, z - s if c el...]
    ppermute x6, waiting for transfers between devices: 8.45 us -> 2.86 us  [first(): lax.ppermute(a, AXES, permutation(lambda x, c, z, y: (x, c, z, y + s) if...]
    ppermute x6, starting transfers between devices: 5.31 us -> 3.61 us  [first(): lax.ppermute(a, AXES, permutation(lambda x, c, z, y: (x, c, z, y + s) if...]
    ppermute x6 -> x7, starting transfers between devices: 11.4 us -> 13 us  [ring(): lax.ppermute(a, AXES, permutation(lambda x, c, z, y: (x, c, z - s if c el...]
    ppermute x6, starting transfers between devices: 7.9 us -> 8.91 us  [second(): lax.ppermute(a, AXES, permutation(lambda x, c, z, y: (x + s, c, z, y) if...]
    pallas_call x20 -> x23, Pallas kernels: 15.5 us -> 15.5 us  [call(): pl.pallas_call(kernel, out_shape=outs, in_specs=[SMEM] * len(scalars) + (...]
  transfers between devices with their start and end apart: 24 -> 25, of which waited for: 14 -> 11; matrix products, arithmetic and copies ran while one was open for 0% -> 0% of each run, Pallas kernels for 12% -> 13%
where the time goes in v9:
time: 81 us; the launch traced here: 79.8 us
  starting transfers between devices  34.3 us (42%)
  waiting for transfers between devices  27.9 us (34%)
  Pallas kernels  15.5 us (19%)
  between operations  2.13 us (3%)
    ppermute x7, waiting for transfers between devices, ring(): lax.ppermute(a, AXES, permutation(lambda x, c, z, y: (x, c, z - s if c el...  16.9 us
    pallas_call x23, Pallas kernels, call(): pl.pallas_call(kernel, out_shape=outs, in_specs=[SMEM] * len(scalars) + (...  15.5 us
    ppermute x7, starting transfers between devices, ring(): lax.ppermute(a, AXES, permutation(lambda x, c, z, y: (x, c, z - s if c el...  13 us
    ppermute x6, starting transfers between devices, second(): lax.ppermute(a, AXES, permutation(lambda x, c, z, y: (x + s, c, z, y) if...  8.91 us
    ppermute x6, starting transfers between devices, swap(): lax.ppermute(a, AXES, permutation(lambda x, c, z, y: (x, 1 - c, z, y)))  8.78 us
    ppermute x6, waiting for transfers between devices, second(): lax.ppermute(a, AXES, permutation(lambda x, c, z, y: (x + s, c, z, y) if...  6.46 us
    ppermute x6, starting transfers between devices, first(): lax.ppermute(a, AXES, permutation(lambda x, c, z, y: (x, c, z, y + s) if...  3.61 us
    ppermute x6, waiting for transfers between devices, first(): lax.ppermute(a, AXES, permutation(lambda x, c, z, y: (x, c, z, y + s) if...  2.86 us
  transfers between devices with their start and end apart: 25, of which 11 were waited for; matrix products, arithmetic and copies ran while one was open for 0% of the time, Pallas kernels for 13%

profile of v9, /device:TPU:1, one launch (start us, length us, event | category | flops | bytes accessed | tf_op | source)
XLA Modules:
  0.0 79.8 jit_solution(9876409864993994017)
XLA Ops:
  0.6 1.2 %normalize.1 = (bf16[64,1152]{1,0:T(8,128)(2,1)S(1)}, bf16[64,1152]{1,0:T(8,128)(2,1)S(1)}, f32[64,1]{1,0:T(8,128)S(1)}, f32[64,1]{1,0:T(8,128)S(1)}) custom-call(bf16[64,1152]{1,0:T(8,128)(2,1)} %refs_5_.1, bf16[64,1152]{1,0:T(8,128)(2,1)} %refs_11_.1), custom_call_target="tpu_custom_call" | custom-call | flops 1 | bytes 1 | tf_op jit(solution)/shard_map/normalize/pallas_call | solution.py:65
  1.8 3.3 %collective-permute-start.5 = (bf16[64,1152]{1,0:T(8,128)(2,1)S(1)}, bf16[64,1152]{1,0:T(8,128)(2,1)S(1)}, u32[]{:S(2)}, u32[]{:S(2)}) collective-permute-start(bf16[64,1152]{1,0:T(8,128)(2,1)S(1)} %get-tuple-element.48.refs_0_), channel_id=1, source_target_pairs={{0,32},{1,33},{2,34},{3,35},{4,36},{5,37},{6,38},{7,39},{8,40},{9,... | collective-permute-start | bytes 442376 | tf_op jit(solution)/shard_map/ppermute | solution.py:55
  5.1 1.0 %collective-permute-start.2 = (bf16[64,1152]{1,0:T(8,128)(2,1)S(1)}, bf16[64,1152]{1,0:T(8,128)(2,1)S(1)}, u32[]{:S(2)}, u32[]{:S(2)}) collective-permute-start(bf16[64,1152]{1,0:T(8,128)(2,1)S(1)} %get-tuple-element.47.refs_0_), channel_id=1, source_target_pairs={{0,192},{1,193},{2,194},{3,195},{4,196},{5,197},{6,198},{7,199},{8... | collective-permute-start | bytes 442376 | tf_op jit(solution)/shard_map/ppermute | solution.py:39
  7.2 6.1 %collective-permute-start.7 = (bf16[128,1152]{1,0:T(8,128)(2,1)S(1)}, bf16[128,1152]{1,0:T(8,128)(2,1)S(1)}, u32[]{:S(2)}, u32[]{:S(2)}) collective-permute-start(bf16[128,1152]{1,0:T(8,128)(2,1)S(1)} %pair.1.refs_1_), channel_id=1, source_target_pairs={{0,8},{1,9},{2,10},{3,11},{4,12},{5,13},{6,14},{7,15},{8,16},{9,17... | collective-permute-start | bytes 884744 | tf_op jit(solution)/shard_map/ppermute | solution.py:51
  14.1 1.3 %collective-permute-start.3 = (bf16[264,1152]{1,0:T(8,128)(2,1)S(1)}, bf16[264,1152]{1,0:T(8,128)(2,1)S(1)}, u32[]{:S(2)}, u32[]{:S(2)}) collective-permute-start(bf16[264,1152]{1,0:T(8,128)(2,1)S(1)} %group.1.refs_2_), channel_id=1, source_target_pairs={{0,1},{1,2},{2,3},{3,0},{4,5},{5,6},{6,7},{7,4},{8,9},{9,10},{10,1... | collective-permute-start | bytes 1824776 | tf_op jit(solution)/shard_map/ppermute | solution.py:45
  15.4 1.5 %collective-permute-start.4 = (bf16[264,1152]{1,0:T(8,128)(2,1)S(1)}, bf16[264,1152]{1,0:T(8,128)(2,1)S(1)}, u32[]{:S(2)}, u32[]{:S(2)}) collective-permute-start(bf16[264,1152]{1,0:T(8,128)(2,1)S(1)} %group.1.refs_2_), channel_id=1, source_target_pairs={{0,3},{1,0},{2,1},{3,2},{4,7},{5,4},{6,5},{7,6},{8,11},{9,8},{10,9... | collective-permute-start | bytes 1824776 | tf_op jit(solution)/shard_map/ppermute | solution.py:45
  16.9 3.3 %collective-permute-done.7.refs_1_ = bf16[128,1152]{1,0:T(8,128)(2,1)S(1)} collective-permute-done((bf16[128,1152]{1,0:T(8,128)(2,1)S(1)}, bf16[128,1152]{1,0:T(8,128)(2,1)S(1)}, u32[]{:S(2)}, u32[]{:S(2)}) %collective-permute-start.7) | collective-permute-done | bytes 294944 | tf_op jit(solution)/shard_map/ppermute | solution.py:51
  20.1 3.2 %collective-permute-done.6.refs_0_ = bf16[128,1152]{1,0:T(8,128)(2,1)S(1)} collective-permute-done((bf16[128,1152]{1,0:T(8,128)(2,1)S(1)}, bf16[128,1152]{1,0:T(8,128)(2,1)S(1)}, u32[]{:S(2)}, u32[]{:S(2)}) %collective-permute-start.6) | collective-permute-done | bytes 294944 | tf_op jit(solution)/shard_map/ppermute | solution.py:51
  23.4 1.7 %collective-permute-start.8 = (bf16[256,1152]{1,0:T(8,128)(2,1)S(1)}, bf16[256,1152]{1,0:T(8,128)(2,1)S(1)}, u32[]{:S(2)}, u32[]{:S(2)}) collective-permute-start(bf16[256,1152]{1,0:T(8,128)(2,1)S(1)} %get-tuple-element.49.refs_3_.refs_6_.refs_2_), channel_id=1, source_target_pairs={{0,32},{1,33},{2,34},{3,35},{4,36},{5,37},{6,38},{7,39},{8,40},{9,... | collective-permute-start | bytes 1769480 | tf_op jit(solution)/shard_map/ppermute | solution.py:55
  25.1 1.9 %collective-permute-start.10 = (bf16[128,1152]{1,0:T(8,128)(2,1)S(1)}, bf16[128,1152]{1,0:T(8,128)(2,1)S(1)}, u32[]{:S(2)}, u32[]{:S(2)}) collective-permute-start(bf16[128,1152]{1,0:T(8,128)(2,1)S(1)} %collective-permute-done.7.refs_1_), channel_id=1, source_target_pairs={{0,4},{1,5},{2,6},{3,7},{4,8},{5,9},{6,10},{7,11},{8,12},{9,13},{1... | collective-permute-start | bytes 884744 | tf_op jit(solution)/shard_map/ppermute | solution.py:51
  26.9 2.7 %collective-permute-start.12 = (bf16[264,1152]{1,0:T(8,128)(2,1)S(1)}, bf16[264,1152]{1,0:T(8,128)(2,1)S(1)}, u32[]{:S(2)}, u32[]{:S(2)}) collective-permute-start(bf16[264,1152]{1,0:T(8,128)(2,1)S(1)} %group.1.refs_2_), channel_id=1, source_target_pairs={{0,2},{1,3},{2,0},{3,1},{4,6},{5,7},{6,4},{7,5},{8,10},{9,11},{10,... | collective-permute-start | bytes 1824776 | tf_op jit(solution)/shard_map/ppermute | solution.py:45
  32.9 2.7 %other.1 = (bf16[256,640]{1,0:T(8,128)(2,1)S(1)}, bf16[256,640]{1,0:T(8,128)(2,1)S(1)}, bf16[256,640]{1,0:T(8,128)(2,1)S(1)}, f32[256,128]{1,0:T(8,128)S(1)}, f3...) custom-call(f32[1]{0:T(128)S(6)} %copy.7.refs_0_, f32[1]{0:T(128)S(6)} %copy.8.refs_1_, ...), custom_call_target="tpu_custom_call" | custom-call | flops 1 | bytes 1 | tf_op jit(solution)/shard_map/other/pallas_call | solution.py:65
  35.7 2.3 %collective-permute-start.11 = (bf16[192,1152]{1,0:T(8,128)(2,1)S(1)}, bf16[192,1152]{1,0:T(8,128)(2,1)S(1)}, u32[]{:S(2)}, u32[]{:S(2)}) collective-permute-start(bf16[192,1152]{1,0:T(8,128)(2,1)S(1)} %far_mine.1.refs_5_.refs_0_), channel_id=1, source_target_pairs={{0,32},{1,33},{2,34},{3,35},{4,36},{5,37},{6,38},{7,39},{8,40},{9,... | collective-permute-start | bytes 1327112 | tf_op jit(solution)/shard_map/ppermute | solution.py:55
  38.0 1.6 %near_images.1 = (f32[256,1152]{1,0:T(8,128)S(1)}, f32[256,1152]{1,0:T(8,128)S(1)}, f32[256,1152]{1,0:T(8,128)S(1)}) custom-call(bf16[256,640]{1,0:T(8,128)(2,1)S(1)} %get-tuple-element.56.refs_0_, bf16[256,640]{1,0:T(8,128)(2,1)S(1)} %get-tuple-element.57.refs_1_, bf16[256,640]{1,0:T(8,128)(2,1)S(1)} %get-tuple-element.58.refs_2_, ...), custom_call_target="tpu_custom_call" | custom-call | flops 1 | bytes 1 | tf_op jit(solution)/shard_map/near_images/pallas_call | solution.py:65
  39.7 1.5 %far.1 = (bf16[256,384]{1,0:T(8,128)(2,1)S(1)}, bf16[256,384]{1,0:T(8,128)(2,1)S(1)}, bf16[256,384]{1,0:T(8,128)(2,1)S(1)}, f32[8,768]{1,0:T(8,128)S(1)}) custom-call(f32[1]{0:T(128)S(6)} %copy.7.refs_0_, f32[1]{0:T(128)S(6)} %copy.8.refs_1_, bf16[264,1152]{1,0:T(8,128)(2,1)S(1)} %group.1.refs_2_, ...), custom_call_target="tpu_custom_call" | custom-call | flops 1 | bytes 1 | tf_op jit(solution)/shard_map/far/pallas_call | solution.py:65
  41.3 2.7 %last.1 = (bf16[256,640]{1,0:T(8,128)(2,1)S(1)}, bf16[256,384]{1,0:T(8,128)(2,1)S(1)}, f32[8,256]{1,0:T(8,128)S(1)}, f32[192,1152]{1,0:T(8,128)S(1)}, bf16[192,1...) custom-call(f32[1]{0:T(128)S(6)} %copy.7.refs_0_, ...), custom_call_target="tpu_custom_call" | custom-call | flops 1 | bytes 1 | tf_op jit(solution)/shard_map/last/pallas_call | solution.py:65
  45.1 1.6 %collective-permute-done.13.refs_1_ = bf16[192,1152]{1,0:T(8,128)(2,1)S(1)} collective-permute-done((bf16[192,1152]{1,0:T(8,128)(2,1)S(1)}, bf16[192,1152]{1,0:T(8,128)(2,1)S(1)}, u32[]{:S(2)}, u32[]{:S(2)}) %collective-permute-start.13) | collective-permute-done | bytes 442400 | tf_op jit(solution)/shard_map/ppermute | solution.py:55
  46.8 2.0 %collective-permute-start.18 = (bf16[192,1152]{1,0:T(8,128)(2,1)S(1)}, bf16[192,1152]{1,0:T(8,128)(2,1)S(1)}, u32[]{:S(2)}, u32[]{:S(2)}) collective-permute-start(bf16[192,1152]{1,0:T(8,128)(2,1)S(1)} %step1.1.refs_4_), channel_id=1, source_target_pairs={{0,24},{1,25},{2,26},{3,27},{4,28},{5,29},{6,30},{7,31},{8,0},{9,1... | collective-permute-start | bytes 1327112 | tf_op jit(solution)/shard_map/ppermute | solution.py:51
  48.8 2.1 %collective-permute-start.15 = (bf16[264,1152]{1,0:T(8,128)(2,1)S(1)}, bf16[264,1152]{1,0:T(8,128)(2,1)S(1)}, u32[]{:S(2)}, u32[]{:S(2)}) collective-permute-start(bf16[264,1152]{1,0:T(8,128)(2,1)S(1)} %image1.1.refs_2_), channel_id=1, source_target_pairs={{0,3},{1,0},{2,1},{3,2},{4,7},{5,4},{6,5},{7,6},{8,11},{9,8},{10,9... | collective-permute-start | bytes 1824776 | tf_op jit(solution)/shard_map/ppermute | solution.py:45
  51.4 1.0 %image2.1.refs_3_ = bf16[264,1152]{1,0:T(8,128)(2,1)S(1)} custom-call(bf16[256,640]{1,0:T(8,128)(2,1)S(1)} %get-tuple-element.68.refs_0_, bf16[256,384]{1,0:T(8,128)(2,1)S(1)} %get-tuple-element.69.refs_1_, bf16[256,1152]{1,0:T(8,128)(2,1)S(1)} %get-tuple-element.49.refs_3_.refs_6_.refs_2_, ...), custom_call_target="tpu_custom_call" | custom-call | flops 1 | bytes 1 | tf_op jit(solution)/shard_map/image2/pallas_call | solution.py:65
  52.4 1.3 %collective-permute-start.16 = (bf16[264,1152]{1,0:T(8,128)(2,1)S(1)}, bf16[264,1152]{1,0:T(8,128)(2,1)S(1)}, u32[]{:S(2)}, u32[]{:S(2)}) collective-permute-start(bf16[264,1152]{1,0:T(8,128)(2,1)S(1)} %image2.1.refs_3_), channel_id=1, source_target_pairs={{0,2},{1,3},{2,0},{3,1},{4,6},{5,7},{6,4},{7,5},{8,10},{9,11},{10,... | collective-permute-start | bytes 1824776 | tf_op jit(solution)/shard_map/ppermute | solution.py:45
  54.2 7.0 %collective-permute-done.18.refs_2_ = bf16[192,1152]{1,0:T(8,128)(2,1)S(1)} collective-permute-done((bf16[192,1152]{1,0:T(8,128)(2,1)S(1)}, bf16[192,1152]{1,0:T(8,128)(2,1)S(1)}, u32[]{:S(2)}, u32[]{:S(2)}) %collective-permute-start.18) | collective-permute-done | bytes 442400 | tf_op jit(solution)/shard_map/ppermute | solution.py:51
  61.5 1.8 %collective-permute-start.22 = (bf16[128,1152]{1,0:T(8,128)(2,1)S(1)}, bf16[128,1152]{1,0:T(8,128)(2,1)S(1)}, u32[]{:S(2)}, u32[]{:S(2)}) collective-permute-start(bf16[128,1152]{1,0:T(8,128)(2,1)S(1)} %get-tuple-element.78.refs_5_), channel_id=1, source_target_pairs={{0,28},{1,29},{2,30},{3,31},{4,0},{5,1},{6,2},{7,3},{8,4},{9,5},{1... | collective-permute-start | bytes 884744 | tf_op jit(solution)/shard_map/ppermute | solution.py:51
  63.3 1.2 %collective-permute-done.15.refs_2_ = bf16[264,1152]{1,0:T(8,128)(2,1)S(1)} collective-permute-done((bf16[264,1152]{1,0:T(8,128)(2,1)S(1)}, bf16[264,1152]{1,0:T(8,128)(2,1)S(1)}, u32[]{:S(2)}, u32[]{:S(2)}) %collective-permute-start.15) | collective-permute-done | bytes 608288 | tf_op jit(solution)/shard_map/ppermute | solution.py:45
  64.5 5.3 %collective-permute-done.17.refs_4_ = bf16[264,1152]{1,0:T(8,128)(2,1)S(1)} collective-permute-done((bf16[264,1152]{1,0:T(8,128)(2,1)S(1)}, bf16[264,1152]{1,0:T(8,128)(2,1)S(1)}, u32[]{:S(2)}, u32[]{:S(2)}) %collective-permute-start.17) | collective-permute-done | bytes 608288 | tf_op jit(solution)/shard_map/ppermute | solution.py:45
  70.1 0.9 %collective-permute-start.19 = (bf16[72,1152]{1,0:T(8,128)(2,1)S(1)}, bf16[72,1152]{1,0:T(8,128)(2,1)S(1)}, u32[]{:S(2)}, u32[]{:S(2)}) collective-permute-start(bf16[72,1152]{1,0:T(8,128)(2,1)S(1)} %get-tuple-element.81), channel_id=1, source_target_pairs={{0,192},{1,193},{2,194},{3,195},{4,196},{5,197},{6,198},{7,199},{8... | collective-permute-start | bytes 497672 | tf_op jit(solution)/shard_map/ppermute | solution.py:39
  71.6 0.7 collective-permute-done.23.refs_2_.refs_9_
  72.4 2.6 %collective-permute-done.22.refs_1_.refs_8_ = bf16[128,1152]{1,0:T(8,128)(2,1)S(1)} collective-permute-done((bf16[128,1152]{1,0:T(8,128)(2,1)S(1)}, bf16[128,1152]{1,0:T(8,128)(2,1)S(1)}, u32[]{:S(2)}, u32[]{:S(2)}) %collective-permute-start.22) | collective-permute-done | bytes 294944 | tf_op jit(solution)/shard_map/ppermute | solution.py:51
  75.0 0.8 %collective-permute-start.24 = (bf16[64,1152]{1,0:T(8,128)(2,1)S(1)}, bf16[64,1152]{1,0:T(8,128)(2,1)S(1)}, u32[]{:S(2)}, u32[]{:S(2)}) collective-permute-start(bf16[64,1152]{1,0:T(8,128)(2,1)S(1)} %step3.1), channel_id=1, source_target_pairs={{0,32},{1,33},{2,34},{3,35},{4,36},{5,37},{6,38},{7,39},{8,40},{9,... | collective-permute-start | bytes 442376 | tf_op jit(solution)/shard_map/ppermute | solution.py:55
  75.9 0.9 %collective-permute-done.20.refs_3_ = bf16[72,1152]{1,0:T(8,128)(2,1)S(1)} collective-permute-done((bf16[72,1152]{1,0:T(8,128)(2,1)S(1)}, bf16[72,1152]{1,0:T(8,128)(2,1)S(1)}, u32[]{:S(2)}, u32[]{:S(2)}) %collective-permute-start.20) | collective-permute-done | bytes 165920 | tf_op jit(solution)/shard_map/ppermute | solution.py:39
  76.8 2.0 %collective-permute-done.21.refs_4_ = bf16[72,1152]{1,0:T(8,128)(2,1)S(1)} collective-permute-done((bf16[72,1152]{1,0:T(8,128)(2,1)S(1)}, bf16[72,1152]{1,0:T(8,128)(2,1)S(1)}, u32[]{:S(2)}, u32[]{:S(2)}) %collective-permute-start.21) | collective-permute-done | bytes 165920 | tf_op jit(solution)/shard_map/ppermute | solution.py:39
  78.7 1.1 %finish.1 = (f32[64,1152]{1,0:T(8,128)}, f32[64,1152]{1,0:T(8,128)}, f32[1,64]{1,0:T(1,128)}) custom-call(f32[64,1152]{1,0:T(8,128)S(1)} %get-tuple-element.79.refs_0_, f32[8,256]{1,0:T(8,128)S(1)} %get-tuple-element.80.refs_1_, bf16[72,1152]{1,0:T(8,128)(2,1)S(1)} %collective-permute-done.19.refs_2_, bf16[72,1152]{1,0:T(8,128)(2,1)S(1)} %collective-permute-done.20.refs_3_, ...), custom_call_target="tpu_custom_call" | custom-call | flops 1 | bytes 1 | tf_op jit(solution)/shard_map/finish/pallas_call | solution.py:65
  (45 shorter events, 7.4 us)
Async XLA Ops:
  1.8 5.4 %collective-permute-start.5 = (bf16[64,1152]{1,0:T(8,128)(2,1)S(1)}, bf16[64,1152]{1,0:T(8,128)(2,1)S(1)}, u32[]{:S(2)}, u32[]{:S(2)}) collective-permute-start(bf16[64,1152]{1,0:T(8,128)(2,1)S(1)} %get-tuple-element.48.refs_0_), channel_id=1, source_target_pairs={{0,32},{1,33},{2,34},{3,35},{4,36},{5,37},{6,38},{7,39},{8,40},{9,... | collective-permute-start | bytes 442376 | tf_op jit(solution)/shard_map/ppermute | solution.py:55
  5.1 8.9 %collective-permute-start.2 = (bf16[64,1152]{1,0:T(8,128)(2,1)S(1)}, bf16[64,1152]{1,0:T(8,128)(2,1)S(1)}, u32[]{:S(2)}, u32[]{:S(2)}) collective-permute-start(bf16[64,1152]{1,0:T(8,128)(2,1)S(1)} %get-tuple-element.47.refs_0_), channel_id=1, source_target_pairs={{0,192},{1,193},{2,194},{3,195},{4,196},{5,197},{6,198},{7,199},{8... | collective-permute-start | bytes 442376 | tf_op jit(solution)/shard_map/ppermute | solution.py:39
  6.1 7.9 %collective-permute-start.1 = (bf16[64,1152]{1,0:T(8,128)(2,1)S(1)}, bf16[64,1152]{1,0:T(8,128)(2,1)S(1)}, u32[]{:S(2)}, u32[]{:S(2)}) collective-permute-start(bf16[64,1152]{1,0:T(8,128)(2,1)S(1)} %get-tuple-element.47.refs_0_), channel_id=1, source_target_pairs={{0,128},{1,129},{2,130},{3,131},{4,132},{5,133},{6,134},{7,135},{8... | collective-permute-start | bytes 442376 | tf_op jit(solution)/shard_map/ppermute | solution.py:39
  6.5 7.6 %collective-permute-start = (bf16[64,1152]{1,0:T(8,128)(2,1)S(1)}, bf16[64,1152]{1,0:T(8,128)(2,1)S(1)}, u32[]{:S(2)}, u32[]{:S(2)}) collective-permute-start(bf16[64,1152]{1,0:T(8,128)(2,1)S(1)} %get-tuple-element.47.refs_0_), channel_id=1, source_target_pairs={{0,64},{1,65},{2,66},{3,67},{4,68},{5,69},{6,70},{7,71},{8,72},{9,... | collective-permute-start | bytes 442376 | tf_op jit(solution)/shard_map/ppermute | solution.py:39
  7.2 12.9 %collective-permute-start.7 = (bf16[128,1152]{1,0:T(8,128)(2,1)S(1)}, bf16[128,1152]{1,0:T(8,128)(2,1)S(1)}, u32[]{:S(2)}, u32[]{:S(2)}) collective-permute-start(bf16[128,1152]{1,0:T(8,128)(2,1)S(1)} %pair.1.refs_1_), channel_id=1, source_target_pairs={{0,8},{1,9},{2,10},{3,11},{4,12},{5,13},{6,14},{7,15},{8,16},{9,17... | collective-permute-start | bytes 884744 | tf_op jit(solution)/shard_map/ppermute | solution.py:51
  13.3 10.0 %collective-permute-start.6 = (bf16[128,1152]{1,0:T(8,128)(2,1)S(1)}, bf16[128,1152]{1,0:T(8,128)(2,1)S(1)}, u32[]{:S(2)}, u32[]{:S(2)}) collective-permute-start(bf16[128,1152]{1,0:T(8,128)(2,1)S(1)} %pair.1.refs_1_), channel_id=1, source_target_pairs={{0,4},{1,5},{2,6},{3,7},{4,8},{5,9},{6,10},{7,11},{8,12},{9,13},{1... | collective-permute-start | bytes 884744 | tf_op jit(solution)/shard_map/ppermute | solution.py:51
  14.1 15.6 %collective-permute-start.3 = (bf16[264,1152]{1,0:T(8,128)(2,1)S(1)}, bf16[264,1152]{1,0:T(8,128)(2,1)S(1)}, u32[]{:S(2)}, u32[]{:S(2)}) collective-permute-start(bf16[264,1152]{1,0:T(8,128)(2,1)S(1)} %group.1.refs_2_), channel_id=1, source_target_pairs={{0,1},{1,2},{2,3},{3,0},{4,5},{5,6},{6,7},{7,4},{8,9},{9,10},{10,1... | collective-permute-start | bytes 1824776 | tf_op jit(solution)/shard_map/ppermute | solution.py:45
  15.4 16.9 %collective-permute-start.4 = (bf16[264,1152]{1,0:T(8,128)(2,1)S(1)}, bf16[264,1152]{1,0:T(8,128)(2,1)S(1)}, u32[]{:S(2)}, u32[]{:S(2)}) collective-permute-start(bf16[264,1152]{1,0:T(8,128)(2,1)S(1)} %group.1.refs_2_), channel_id=1, source_target_pairs={{0,3},{1,0},{2,1},{3,2},{4,7},{5,4},{6,5},{7,6},{8,11},{9,8},{10,9... | collective-permute-start | bytes 1824776 | tf_op jit(solution)/shard_map/ppermute | solution.py:45
  23.4 9.4 %collective-permute-start.8 = (bf16[256,1152]{1,0:T(8,128)(2,1)S(1)}, bf16[256,1152]{1,0:T(8,128)(2,1)S(1)}, u32[]{:S(2)}, u32[]{:S(2)}) collective-permute-start(bf16[256,1152]{1,0:T(8,128)(2,1)S(1)} %get-tuple-element.49.refs_3_.refs_6_.refs_2_), channel_id=1, source_target_pairs={{0,32},{1,33},{2,34},{3,35},{4,36},{5,37},{6,38},{7,39},{8,40},{9,... | collective-permute-start | bytes 1769480 | tf_op jit(solution)/shard_map/ppermute | solution.py:55
  25.1 10.6 %collective-permute-start.10 = (bf16[128,1152]{1,0:T(8,128)(2,1)S(1)}, bf16[128,1152]{1,0:T(8,128)(2,1)S(1)}, u32[]{:S(2)}, u32[]{:S(2)}) collective-permute-start(bf16[128,1152]{1,0:T(8,128)(2,1)S(1)} %collective-permute-done.7.refs_1_), channel_id=1, source_target_pairs={{0,4},{1,5},{2,6},{3,7},{4,8},{5,9},{6,10},{7,11},{8,12},{9,13},{1... | collective-permute-start | bytes 884744 | tf_op jit(solution)/shard_map/ppermute | solution.py:51
  26.9 14.3 %collective-permute-start.12 = (bf16[264,1152]{1,0:T(8,128)(2,1)S(1)}, bf16[264,1152]{1,0:T(8,128)(2,1)S(1)}, u32[]{:S(2)}, u32[]{:S(2)}) collective-permute-start(bf16[264,1152]{1,0:T(8,128)(2,1)S(1)} %group.1.refs_2_), channel_id=1, source_target_pairs={{0,2},{1,3},{2,0},{3,1},{4,6},{5,7},{6,4},{7,5},{8,10},{9,11},{10,... | collective-permute-start | bytes 1824776 | tf_op jit(solution)/shard_map/ppermute | solution.py:45
  29.7 6.0 %collective-permute-start.9 = (bf16[64,1152]{1,0:T(8,128)(2,1)S(1)}, bf16[64,1152]{1,0:T(8,128)(2,1)S(1)}, u32[]{:S(2)}, u32[]{:S(2)}) collective-permute-start(bf16[64,1152]{1,0:T(8,128)(2,1)S(1)} %get-tuple-element.59), channel_id=1, source_target_pairs={{0,8},{1,9},{2,10},{3,11},{4,12},{5,13},{6,14},{7,15},{8,16},{9,17... | collective-permute-start | bytes 442376 | tf_op jit(solution)/shard_map/ppermute | solution.py:51
  35.7 4.0 %collective-permute-start.11 = (bf16[192,1152]{1,0:T(8,128)(2,1)S(1)}, bf16[192,1152]{1,0:T(8,128)(2,1)S(1)}, u32[]{:S(2)}, u32[]{:S(2)}) collective-permute-start(bf16[192,1152]{1,0:T(8,128)(2,1)S(1)} %far_mine.1.refs_5_.refs_0_), channel_id=1, source_target_pairs={{0,32},{1,33},{2,34},{3,35},{4,36},{5,37},{6,38},{7,39},{8,40},{9,... | collective-permute-start | bytes 1327112 | tf_op jit(solution)/shard_map/ppermute | solution.py:55
  44.0 2.7 %collective-permute-start.14 = (bf16[256,1152]{1,0:T(8,128)(2,1)S(1)}, bf16[256,1152]{1,0:T(8,128)(2,1)S(1)}, u32[]{:S(2)}, u32[]{:S(2)}) collective-permute-start(bf16[256,1152]{1,0:T(8,128)(2,1)S(1)} %get-tuple-element.76), channel_id=1, source_target_pairs={{0,32},{1,33},{2,34},{3,35},{4,36},{5,37},{6,38},{7,39},{8,40},{9,... | collective-permute-start | bytes 1769480 | tf_op jit(solution)/shard_map/ppermute | solution.py:55
  44.2 2.5 %collective-permute-start.13 = (bf16[192,1152]{1,0:T(8,128)(2,1)S(1)}, bf16[192,1152]{1,0:T(8,128)(2,1)S(1)}, u32[]{:S(2)}, u32[]{:S(2)}) collective-permute-start(bf16[192,1152]{1,0:T(8,128)(2,1)S(1)} %get-tuple-element.74.refs_4_), channel_id=1, source_target_pairs={{0,32},{1,33},{2,34},{3,35},{4,36},{5,37},{6,38},{7,39},{8,40},{9,... | collective-permute-start | bytes 1327112 | tf_op jit(solution)/shard_map/ppermute | solution.py:55
  46.8 14.4 %collective-permute-start.18 = (bf16[192,1152]{1,0:T(8,128)(2,1)S(1)}, bf16[192,1152]{1,0:T(8,128)(2,1)S(1)}, u32[]{:S(2)}, u32[]{:S(2)}) collective-permute-start(bf16[192,1152]{1,0:T(8,128)(2,1)S(1)} %step1.1.refs_4_), channel_id=1, source_target_pairs={{0,24},{1,25},{2,26},{3,27},{4,28},{5,29},{6,30},{7,31},{8,0},{9,1... | collective-permute-start | bytes 1327112 | tf_op jit(solution)/shard_map/ppermute | solution.py:51
  48.8 15.6 %collective-permute-start.15 = (bf16[264,1152]{1,0:T(8,128)(2,1)S(1)}, bf16[264,1152]{1,0:T(8,128)(2,1)S(1)}, u32[]{:S(2)}, u32[]{:S(2)}) collective-permute-start(bf16[264,1152]{1,0:T(8,128)(2,1)S(1)} %image1.1.refs_2_), channel_id=1, source_target_pairs={{0,3},{1,0},{2,1},{3,2},{4,7},{5,4},{6,5},{7,6},{8,11},{9,8},{10,9... | collective-permute-start | bytes 1824776 | tf_op jit(solution)/shard_map/ppermute | solution.py:45
  52.4 12.1 %collective-permute-start.16 = (bf16[264,1152]{1,0:T(8,128)(2,1)S(1)}, bf16[264,1152]{1,0:T(8,128)(2,1)S(1)}, u32[]{:S(2)}, u32[]{:S(2)}) collective-permute-start(bf16[264,1152]{1,0:T(8,128)(2,1)S(1)} %image2.1.refs_3_), channel_id=1, source_target_pairs={{0,2},{1,3},{2,0},{3,1},{4,6},{5,7},{6,4},{7,5},{8,10},{9,11},{10,... | collective-permute-start | bytes 1824776 | tf_op jit(solution)/shard_map/ppermute | solution.py:45
  53.7 16.0 %collective-permute-start.17 = (bf16[264,1152]{1,0:T(8,128)(2,1)S(1)}, bf16[264,1152]{1,0:T(8,128)(2,1)S(1)}, u32[]{:S(2)}, u32[]{:S(2)}) collective-permute-start(bf16[264,1152]{1,0:T(8,128)(2,1)S(1)} %image3.1.refs_6_), channel_id=1, source_target_pairs={{0,1},{1,2},{2,3},{3,0},{4,5},{5,6},{6,7},{7,4},{8,9},{9,10},{10,1... | collective-permute-start | bytes 1824776 | tf_op jit(solution)/shard_map/ppermute | solution.py:45
  61.4 11.0 %collective-permute-start.23 = (bf16[128,1152]{1,0:T(8,128)(2,1)S(1)}, bf16[128,1152]{1,0:T(8,128)(2,1)S(1)}, u32[]{:S(2)}, u32[]{:S(2)}) collective-permute-start(bf16[128,1152]{1,0:T(8,128)(2,1)S(1)} %get-tuple-element.86), channel_id=1, source_target_pairs={{0,24},{1,25},{2,26},{3,27},{4,28},{5,29},{6,30},{7,31},{8,0},{9,1... | collective-permute-start | bytes 884744 | tf_op jit(solution)/shard_map/ppermute | solution.py:51
  61.5 13.5 %collective-permute-start.22 = (bf16[128,1152]{1,0:T(8,128)(2,1)S(1)}, bf16[128,1152]{1,0:T(8,128)(2,1)S(1)}, u32[]{:S(2)}, u32[]{:S(2)}) collective-permute-start(bf16[128,1152]{1,0:T(8,128)(2,1)S(1)} %get-tuple-element.78.refs_5_), channel_id=1, source_target_pairs={{0,28},{1,29},{2,30},{3,31},{4,0},{5,1},{6,2},{7,3},{8,4},{9,5},{1... | collective-permute-start | bytes 884744 | tf_op jit(solution)/shard_map/ppermute | solution.py:51
  70.0 8.7 %copy-start = (bf16[64,1152]{1,0:T(8,128)(2,1)S(1)}, bf16[64,1152]{1,0:T(8,128)(2,1)}, u32[]{:S(2)}) copy-start(bf16[64,1152]{1,0:T(8,128)(2,1)} %refs_5_.1) | copy-start | bytes 442372
  70.0 8.7 %copy-start.1 = (bf16[64,1152]{1,0:T(8,128)(2,1)S(1)}, bf16[64,1152]{1,0:T(8,128)(2,1)}, u32[]{:S(2)}) copy-start(bf16[64,1152]{1,0:T(8,128)(2,1)} %refs_11_.1) | copy-start | bytes 442372
  70.1 5.8 %collective-permute-start.19 = (bf16[72,1152]{1,0:T(8,128)(2,1)S(1)}, bf16[72,1152]{1,0:T(8,128)(2,1)S(1)}, u32[]{:S(2)}, u32[]{:S(2)}) collective-permute-start(bf16[72,1152]{1,0:T(8,128)(2,1)S(1)} %get-tuple-element.81), channel_id=1, source_target_pairs={{0,192},{1,193},{2,194},{3,195},{4,196},{5,197},{6,198},{7,199},{8... | collective-permute-start | bytes 497672 | tf_op jit(solution)/shard_map/ppermute | solution.py:39
  71.0 5.8 %collective-permute-start.20 = (bf16[72,1152]{1,0:T(8,128)(2,1)S(1)}, bf16[72,1152]{1,0:T(8,128)(2,1)S(1)}, u32[]{:S(2)}, u32[]{:S(2)}) collective-permute-start(bf16[72,1152]{1,0:T(8,128)(2,1)S(1)} %get-tuple-element.82), channel_id=1, source_target_pairs={{0,128},{1,129},{2,130},{3,131},{4,132},{5,133},{6,134},{7,135},{8... | collective-permute-start | bytes 497672 | tf_op jit(solution)/shard_map/ppermute | solution.py:39
  71.6 7.1 %collective-permute-start.21 = (bf16[72,1152]{1,0:T(8,128)(2,1)S(1)}, bf16[72,1152]{1,0:T(8,128)(2,1)S(1)}, u32[]{:S(2)}, u32[]{:S(2)}) collective-permute-start(bf16[72,1152]{1,0:T(8,128)(2,1)S(1)} %get-tuple-element.83.refs_3_), channel_id=1, source_target_pairs={{0,64},{1,65},{2,66},{3,67},{4,68},{5,69},{6,70},{7,71},{8,72},{9,... | collective-permute-start | bytes 497672 | tf_op jit(solution)/shard_map/ppermute | solution.py:39
  75.0 3.7 %collective-permute-start.24 = (bf16[64,1152]{1,0:T(8,128)(2,1)S(1)}, bf16[64,1152]{1,0:T(8,128)(2,1)S(1)}, u32[]{:S(2)}, u32[]{:S(2)}) collective-permute-start(bf16[64,1152]{1,0:T(8,128)(2,1)S(1)} %step3.1), channel_id=1, source_target_pairs={{0,32},{1,33},{2,34},{3,35},{4,36},{5,37},{6,38},{7,39},{8,40},{9,... | collective-permute-start | bytes 442376 | tf_op jit(solution)/shard_map/ppermute | solution.py:55

commit v10 on v9

--- a/solution.py
+++ b/solution.py
@@ -360,15 +360,15 @@
         )[0]
 
     p1 = sent("image1", 1, t1, c1, (send_a,))
-    z1 = call("step1", step1_body, [shape(192, d)], (keep_a, got_a), (), (p1, got_b))[0]
-    w = ring(z1, -2)
-    p3 = sent("image3", 2, t3, c3, (z1,))
+    p3 = sent("image3", 2, t3, c3, (p1,))
     p2 = call(
         "image2", last_image_body, [shape(264, d)], (n2, c2, near_mine, other, far, row2), (), (p3,)
     )[0]
+    z1 = call("step1", step1_body, [shape(192, d)], (keep_a, got_a), (), (p2, got_b))[0]
+    w = ring(z1, -2)
     r1, r3, r2 = second(p1, -1), second(p3, -3), second(p2, -2)
     p0 = call(
-        "own_image", own_image_body, [shape(256, d, dtype=F32)], (t0, c0, far), (), (p2,)
+        "own_image", own_image_body, [shape(256, d, dtype=F32)], (t0, c0, far), (), (z1,)
     )[0]
     two, one = call("step2", step2_body, [shape(128, d)] * 2, (keep_b, got_b, w), (), (p0,))
     v2, v1 = ring(two, -2), ring(one, -1)

time: 81 us -> 78.1 us (0.964); the launches traced: 79.8 us -> 78 us
  waiting for transfers between devices: 27.9 us -> 24.3 us
  starting transfers between devices: 34.3 us -> 36 us
    ppermute x6, waiting for transfers between devices: 6.46 us -> 2.67 us  [second(): lax.ppermute(a, AXES, permutation(lambda x, c, z, y: (x + s, c, z, y) if...]
    ppermute x7, waiting for transfers between devices: 16.9 us -> 20.4 us  [ring(): lax.ppermute(a, AXES, permutation(lambda x, c, z, y: (x, c, z - s if c el...]
    ppermute x6, waiting for transfers between devices: 2.86 us -> 0.02 us  [first(): lax.ppermute(a, AXES, permutation(lambda x, c, z, y: (x, c, z, y + s) if...]
    ppermute x6, starting transfers between devices: 3.61 us -> 4.52 us  [first(): lax.ppermute(a, AXES, permutation(lambda x, c, z, y: (x, c, z, y + s) if...]
  transfers between devices with their start and end apart: 25 -> 25, of which waited for: 11 -> 9; matrix products, arithmetic and copies ran while one was open for 0% -> 0% of each run, Pallas kernels for 13% -> 13%
where the time goes in v10:
time: 78.1 us; the launch traced here: 78 us
  starting transfers between devices  36 us (46%)
  waiting for transfers between devices  24.3 us (31%)
  Pallas kernels  15.5 us (20%)
  between operations  2.13 us (3%)
    ppermute x7, waiting for transfers between devices, ring(): lax.ppermute(a, AXES, permutation(lambda x, c, z, y: (x, c, z - s if c el...  20.4 us
    pallas_call x23, Pallas kernels, call(): pl.pallas_call(kernel, out_shape=outs, in_specs=[SMEM] * len(scalars) + (...  15.5 us
    ppermute x7, starting transfers between devices, ring(): lax.ppermute(a, AXES, permutation(lambda x, c, z, y: (x, c, z - s if c el...  13.2 us
    ppermute x6, starting transfers between devices, second(): lax.ppermute(a, AXES, permutation(lambda x, c, z, y: (x + s, c, z, y) if...  9.41 us
    ppermute x6, starting transfers between devices, swap(): lax.ppermute(a, AXES, permutation(lambda x, c, z, y: (x, 1 - c, z, y)))  8.89 us
    ppermute x6, starting transfers between devices, first(): lax.ppermute(a, AXES, permutation(lambda x, c, z, y: (x, c, z, y + s) if...  4.52 us
    ppermute x6, waiting for transfers between devices, second(): lax.ppermute(a, AXES, permutation(lambda x, c, z, y: (x + s, c, z, y) if...  2.67 us
  transfers between devices with their start and end apart: 25, of which 9 were waited for; matrix products, arithmetic and copies ran while one was open for 0% of the time, Pallas kernels for 13%

profile of v10, /device:TPU:1, one launch (start us, length us, event | category | flops | bytes accessed | tf_op | source)
XLA Modules:
  0.0 78.0 jit_solution(13099599862692773188)
XLA Ops:
  0.6 1.2 %normalize.1 = (bf16[64,1152]{1,0:T(8,128)(2,1)S(1)}, bf16[64,1152]{1,0:T(8,128)(2,1)S(1)}, f32[64,1]{1,0:T(8,128)S(1)}, f32[64,1]{1,0:T(8,128)S(1)}) custom-call(bf16[64,1152]{1,0:T(8,128)(2,1)} %refs_5_.1, bf16[64,1152]{1,0:T(8,128)(2,1)} %refs_11_.1), custom_call_target="tpu_custom_call" | custom-call | flops 1 | bytes 1 | tf_op jit(solution)/shard_map/normalize/pallas_call | solution.py:65
  1.8 3.3 %collective-permute-start.5 = (bf16[64,1152]{1,0:T(8,128)(2,1)S(1)}, bf16[64,1152]{1,0:T(8,128)(2,1)S(1)}, u32[]{:S(2)}, u32[]{:S(2)}) collective-permute-start(bf16[64,1152]{1,0:T(8,128)(2,1)S(1)} %get-tuple-element.48.refs_0_), channel_id=1, source_target_pairs={{0,32},{1,33},{2,34},{3,35},{4,36},{5,37},{6,38},{7,39},{8,40},{9,... | collective-permute-start | bytes 442376 | tf_op jit(solution)/shard_map/ppermute | solution.py:55
  5.1 1.0 %collective-permute-start.2 = (bf16[64,1152]{1,0:T(8,128)(2,1)S(1)}, bf16[64,1152]{1,0:T(8,128)(2,1)S(1)}, u32[]{:S(2)}, u32[]{:S(2)}) collective-permute-start(bf16[64,1152]{1,0:T(8,128)(2,1)S(1)} %get-tuple-element.47.refs_0_), channel_id=1, source_target_pairs={{0,192},{1,193},{2,194},{3,195},{4,196},{5,197},{6,198},{7,199},{8... | collective-permute-start | bytes 442376 | tf_op jit(solution)/shard_map/ppermute | solution.py:39
  6.5 0.7 collective-permute-start
  7.2 6.1 %collective-permute-start.7 = (bf16[128,1152]{1,0:T(8,128)(2,1)S(1)}, bf16[128,1152]{1,0:T(8,128)(2,1)S(1)}, u32[]{:S(2)}, u32[]{:S(2)}) collective-permute-start(bf16[128,1152]{1,0:T(8,128)(2,1)S(1)} %pair.1.refs_1_), channel_id=1, source_target_pairs={{0,8},{1,9},{2,10},{3,11},{4,12},{5,13},{6,14},{7,15},{8,16},{9,17... | collective-permute-start | bytes 884744 | tf_op jit(solution)/shard_map/ppermute | solution.py:51
  13.3 0.7 collective-permute-start.6
  14.1 1.3 %collective-permute-start.3 = (bf16[264,1152]{1,0:T(8,128)(2,1)S(1)}, bf16[264,1152]{1,0:T(8,128)(2,1)S(1)}, u32[]{:S(2)}, u32[]{:S(2)}) collective-permute-start(bf16[264,1152]{1,0:T(8,128)(2,1)S(1)} %group.1.refs_2_), channel_id=1, source_target_pairs={{0,1},{1,2},{2,3},{3,0},{4,5},{5,6},{6,7},{7,4},{8,9},{9,10},{10,1... | collective-permute-start | bytes 1824776 | tf_op jit(solution)/shard_map/ppermute | solution.py:45
  15.4 1.5 %collective-permute-start.4 = (bf16[264,1152]{1,0:T(8,128)(2,1)S(1)}, bf16[264,1152]{1,0:T(8,128)(2,1)S(1)}, u32[]{:S(2)}, u32[]{:S(2)}) collective-permute-start(bf16[264,1152]{1,0:T(8,128)(2,1)S(1)} %group.1.refs_2_), channel_id=1, source_target_pairs={{0,3},{1,0},{2,1},{3,2},{4,7},{5,4},{6,5},{7,6},{8,11},{9,8},{10,9... | collective-permute-start | bytes 1824776 | tf_op jit(solution)/shard_map/ppermute | solution.py:45
  16.9 3.3 %collective-permute-done.7.refs_1_ = bf16[128,1152]{1,0:T(8,128)(2,1)S(1)} collective-permute-done((bf16[128,1152]{1,0:T(8,128)(2,1)S(1)}, bf16[128,1152]{1,0:T(8,128)(2,1)S(1)}, u32[]{:S(2)}, u32[]{:S(2)}) %collective-permute-start.7) | collective-permute-done | bytes 294944 | tf_op jit(solution)/shard_map/ppermute | solution.py:51
  20.1 3.2 %collective-permute-done.6.refs_0_ = bf16[128,1152]{1,0:T(8,128)(2,1)S(1)} collective-permute-done((bf16[128,1152]{1,0:T(8,128)(2,1)S(1)}, bf16[128,1152]{1,0:T(8,128)(2,1)S(1)}, u32[]{:S(2)}, u32[]{:S(2)}) %collective-permute-start.6) | collective-permute-done | bytes 294944 | tf_op jit(solution)/shard_map/ppermute | solution.py:51
  23.4 1.7 %collective-permute-start.8 = (bf16[256,1152]{1,0:T(8,128)(2,1)S(1)}, bf16[256,1152]{1,0:T(8,128)(2,1)S(1)}, u32[]{:S(2)}, u32[]{:S(2)}) collective-permute-start(bf16[256,1152]{1,0:T(8,128)(2,1)S(1)} %get-tuple-element.49.refs_3_.refs_6_.refs_2_), channel_id=1, source_target_pairs={{0,32},{1,33},{2,34},{3,35},{4,36},{5,37},{6,38},{7,39},{8,40},{9,... | collective-permute-start | bytes 1769480 | tf_op jit(solution)/shard_map/ppermute | solution.py:55
  25.1 1.9 %collective-permute-start.10 = (bf16[128,1152]{1,0:T(8,128)(2,1)S(1)}, bf16[128,1152]{1,0:T(8,128)(2,1)S(1)}, u32[]{:S(2)}, u32[]{:S(2)}) collective-permute-start(bf16[128,1152]{1,0:T(8,128)(2,1)S(1)} %collective-permute-done.7.refs_1_), channel_id=1, source_target_pairs={{0,4},{1,5},{2,6},{3,7},{4,8},{5,9},{6,10},{7,11},{8,12},{9,13},{1... | collective-permute-start | bytes 884744 | tf_op jit(solution)/shard_map/ppermute | solution.py:51
  26.9 2.7 %collective-permute-start.12 = (bf16[264,1152]{1,0:T(8,128)(2,1)S(1)}, bf16[264,1152]{1,0:T(8,128)(2,1)S(1)}, u32[]{:S(2)}, u32[]{:S(2)}) collective-permute-start(bf16[264,1152]{1,0:T(8,128)(2,1)S(1)} %group.1.refs_2_), channel_id=1, source_target_pairs={{0,2},{1,3},{2,0},{3,1},{4,6},{5,7},{6,4},{7,5},{8,10},{9,11},{10,... | collective-permute-start | bytes 1824776 | tf_op jit(solution)/shard_map/ppermute | solution.py:45
  32.9 2.7 %other.1 = (bf16[256,640]{1,0:T(8,128)(2,1)S(1)}, bf16[256,640]{1,0:T(8,128)(2,1)S(1)}, bf16[256,640]{1,0:T(8,128)(2,1)S(1)}, f32[256,128]{1,0:T(8,128)S(1)}, f3...) custom-call(f32[1]{0:T(128)S(6)} %copy.7.refs_0_, f32[1]{0:T(128)S(6)} %copy.8.refs_1_, ...), custom_call_target="tpu_custom_call" | custom-call | flops 1 | bytes 1 | tf_op jit(solution)/shard_map/other/pallas_call | solution.py:65
  35.7 2.3 %collective-permute-start.11 = (bf16[192,1152]{1,0:T(8,128)(2,1)S(1)}, bf16[192,1152]{1,0:T(8,128)(2,1)S(1)}, u32[]{:S(2)}, u32[]{:S(2)}) collective-permute-start(bf16[192,1152]{1,0:T(8,128)(2,1)S(1)} %far_mine.1.refs_5_.refs_0_), channel_id=1, source_target_pairs={{0,32},{1,33},{2,34},{3,35},{4,36},{5,37},{6,38},{7,39},{8,40},{9,... | collective-permute-start | bytes 1327112 | tf_op jit(solution)/shard_map/ppermute | solution.py:55
  38.0 1.6 %near_images.1 = (f32[256,1152]{1,0:T(8,128)S(1)}, f32[256,1152]{1,0:T(8,128)S(1)}, f32[256,1152]{1,0:T(8,128)S(1)}) custom-call(bf16[256,640]{1,0:T(8,128)(2,1)S(1)} %get-tuple-element.56.refs_0_, bf16[256,640]{1,0:T(8,128)(2,1)S(1)} %get-tuple-element.57.refs_1_, bf16[256,640]{1,0:T(8,128)(2,1)S(1)} %get-tuple-element.58.refs_2_, ...), custom_call_target="tpu_custom_call" | custom-call | flops 1 | bytes 1 | tf_op jit(solution)/shard_map/near_images/pallas_call | solution.py:65
  39.7 1.5 %far.1 = (bf16[256,384]{1,0:T(8,128)(2,1)S(1)}, bf16[256,384]{1,0:T(8,128)(2,1)S(1)}, bf16[256,384]{1,0:T(8,128)(2,1)S(1)}, f32[8,768]{1,0:T(8,128)S(1)}) custom-call(f32[1]{0:T(128)S(6)} %copy.7.refs_0_, f32[1]{0:T(128)S(6)} %copy.8.refs_1_, bf16[264,1152]{1,0:T(8,128)(2,1)S(1)} %group.1.refs_2_, ...), custom_call_target="tpu_custom_call" | custom-call | flops 1 | bytes 1 | tf_op jit(solution)/shard_map/far/pallas_call | solution.py:65
  41.3 2.7 %last.1 = (bf16[256,640]{1,0:T(8,128)(2,1)S(1)}, bf16[256,384]{1,0:T(8,128)(2,1)S(1)}, f32[8,256]{1,0:T(8,128)S(1)}, f32[192,1152]{1,0:T(8,128)S(1)}, bf16[192,1...) custom-call(f32[1]{0:T(128)S(6)} %copy.7.refs_0_, ...), custom_call_target="tpu_custom_call" | custom-call | flops 1 | bytes 1 | tf_op jit(solution)/shard_map/last/pallas_call | solution.py:65
  45.6 1.0 %image2.1.refs_2_ = bf16[264,1152]{1,0:T(8,128)(2,1)S(1)} custom-call(bf16[256,640]{1,0:T(8,128)(2,1)S(1)} %get-tuple-element.70.refs_0_, bf16[256,384]{1,0:T(8,128)(2,1)S(1)} %get-tuple-element.71.refs_1_, bf16[256,1152]{1,0:T(8,128)(2,1)S(1)} %get-tuple-element.49.refs_3_.refs_6_.refs_2_, ...), custom_call_target="tpu_custom_call" | custom-call | flops 1 | bytes 1 | tf_op jit(solution)/shard_map/image2/pallas_call | solution.py:65
  46.9 2.0 %collective-permute-start.18 = (bf16[192,1152]{1,0:T(8,128)(2,1)S(1)}, bf16[192,1152]{1,0:T(8,128)(2,1)S(1)}, u32[]{:S(2)}, u32[]{:S(2)}) collective-permute-start(bf16[192,1152]{1,0:T(8,128)(2,1)S(1)} %step1.1.refs_3_), channel_id=1, source_target_pairs={{0,24},{1,25},{2,26},{3,27},{4,28},{5,29},{6,30},{7,31},{8,0},{9,1... | collective-permute-start | bytes 1327112 | tf_op jit(solution)/shard_map/ppermute | solution.py:51
  48.9 1.2 %collective-permute-start.16 = (bf16[264,1152]{1,0:T(8,128)(2,1)S(1)}, bf16[264,1152]{1,0:T(8,128)(2,1)S(1)}, u32[]{:S(2)}, u32[]{:S(2)}) collective-permute-start(bf16[264,1152]{1,0:T(8,128)(2,1)S(1)} %image2.1.refs_2_), channel_id=1, source_target_pairs={{0,2},{1,3},{2,0},{3,1},{4,6},{5,7},{6,4},{7,5},{8,10},{9,11},{10,... | collective-permute-start | bytes 1824776 | tf_op jit(solution)/shard_map/ppermute | solution.py:45
  50.1 1.4 %collective-permute-start.17 = (bf16[264,1152]{1,0:T(8,128)(2,1)S(1)}, bf16[264,1152]{1,0:T(8,128)(2,1)S(1)}, u32[]{:S(2)}, u32[]{:S(2)}) collective-permute-start(bf16[264,1152]{1,0:T(8,128)(2,1)S(1)} %image3.1.refs_6_), channel_id=1, source_target_pairs={{0,1},{1,2},{2,3},{3,0},{4,5},{5,6},{6,7},{7,4},{8,9},{9,10},{10,1... | collective-permute-start | bytes 1824776 | tf_op jit(solution)/shard_map/ppermute | solution.py:45
  51.5 1.3 %collective-permute-start.15 = (bf16[264,1152]{1,0:T(8,128)(2,1)S(1)}, bf16[264,1152]{1,0:T(8,128)(2,1)S(1)}, u32[]{:S(2)}, u32[]{:S(2)}) collective-permute-start(bf16[264,1152]{1,0:T(8,128)(2,1)S(1)} %image1.1.refs_4_), channel_id=1, source_target_pairs={{0,3},{1,0},{2,1},{3,2},{4,7},{5,4},{6,5},{7,6},{8,11},{9,8},{10,9... | collective-permute-start | bytes 1824776 | tf_op jit(solution)/shard_map/ppermute | solution.py:45
  53.3 7.7 %collective-permute-done.18.refs_2_ = bf16[192,1152]{1,0:T(8,128)(2,1)S(1)} collective-permute-done((bf16[192,1152]{1,0:T(8,128)(2,1)S(1)}, bf16[192,1152]{1,0:T(8,128)(2,1)S(1)}, u32[]{:S(2)}, u32[]{:S(2)}) %collective-permute-start.18) | collective-permute-done | bytes 442400 | tf_op jit(solution)/shard_map/ppermute | solution.py:51
  61.3 2.0 %collective-permute-start.22 = (bf16[128,1152]{1,0:T(8,128)(2,1)S(1)}, bf16[128,1152]{1,0:T(8,128)(2,1)S(1)}, u32[]{:S(2)}, u32[]{:S(2)}) collective-permute-start(bf16[128,1152]{1,0:T(8,128)(2,1)S(1)} %get-tuple-element.78.refs_5_), channel_id=1, source_target_pairs={{0,28},{1,29},{2,30},{3,31},{4,0},{5,1},{6,2},{7,3},{8,4},{9,5},{1... | collective-permute-start | bytes 884744 | tf_op jit(solution)/shard_map/ppermute | solution.py:51
  63.3 2.7 %collective-permute-done.17.refs_4_ = bf16[264,1152]{1,0:T(8,128)(2,1)S(1)} collective-permute-done((bf16[264,1152]{1,0:T(8,128)(2,1)S(1)}, bf16[264,1152]{1,0:T(8,128)(2,1)S(1)}, u32[]{:S(2)}, u32[]{:S(2)}) %collective-permute-start.17) | collective-permute-done | bytes 608288 | tf_op jit(solution)/shard_map/ppermute | solution.py:45
  66.3 1.8 %collective-permute-start.19 = (bf16[72,1152]{1,0:T(8,128)(2,1)S(1)}, bf16[72,1152]{1,0:T(8,128)(2,1)S(1)}, u32[]{:S(2)}, u32[]{:S(2)}) collective-permute-start(bf16[72,1152]{1,0:T(8,128)(2,1)S(1)} %get-tuple-element.81), channel_id=1, source_target_pairs={{0,192},{1,193},{2,194},{3,195},{4,196},{5,197},{6,198},{7,199},{8... | collective-permute-start | bytes 497672 | tf_op jit(solution)/shard_map/ppermute | solution.py:39
  68.8 3.4 %collective-permute-done.23.refs_2_.refs_9_ = bf16[128,1152]{1,0:T(8,128)(2,1)S(1)} collective-permute-done((bf16[128,1152]{1,0:T(8,128)(2,1)S(1)}, bf16[128,1152]{1,0:T(8,128)(2,1)S(1)}, u32[]{:S(2)}, u32[]{:S(2)}) %collective-permute-start.23) | collective-permute-done | bytes 294944 | tf_op jit(solution)/shard_map/ppermute | solution.py:51
  72.2 2.7 %collective-permute-done.22.refs_1_.refs_8_ = bf16[128,1152]{1,0:T(8,128)(2,1)S(1)} collective-permute-done((bf16[128,1152]{1,0:T(8,128)(2,1)S(1)}, bf16[128,1152]{1,0:T(8,128)(2,1)S(1)}, u32[]{:S(2)}, u32[]{:S(2)}) %collective-permute-start.22) | collective-permute-done | bytes 294944 | tf_op jit(solution)/shard_map/ppermute | solution.py:51
  74.9 1.0 %collective-permute-start.24 = (bf16[64,1152]{1,0:T(8,128)(2,1)S(1)}, bf16[64,1152]{1,0:T(8,128)(2,1)S(1)}, u32[]{:S(2)}, u32[]{:S(2)}) collective-permute-start(bf16[64,1152]{1,0:T(8,128)(2,1)S(1)} %step3.1), channel_id=1, source_target_pairs={{0,32},{1,33},{2,34},{3,35},{4,36},{5,37},{6,38},{7,39},{8,40},{9,... | collective-permute-start | bytes 442376 | tf_op jit(solution)/shard_map/ppermute | solution.py:55
  75.9 1.0 %collective-permute-done.24.refs_10_ = bf16[64,1152]{1,0:T(8,128)(2,1)S(1)} collective-permute-done((bf16[64,1152]{1,0:T(8,128)(2,1)S(1)}, bf16[64,1152]{1,0:T(8,128)(2,1)S(1)}, u32[]{:S(2)}, u32[]{:S(2)}) %collective-permute-start.24) | collective-permute-done | bytes 147488 | tf_op jit(solution)/shard_map/ppermute | solution.py:55
  76.9 1.1 %finish.1 = (f32[64,1152]{1,0:T(8,128)}, f32[64,1152]{1,0:T(8,128)}, f32[1,64]{1,0:T(1,128)}) custom-call(f32[64,1152]{1,0:T(8,128)S(1)} %get-tuple-element.79.refs_0_, f32[8,256]{1,0:T(8,128)S(1)} %get-tuple-element.80.refs_1_, bf16[72,1152]{1,0:T(8,128)(2,1)S(1)} %collective-permute-done.19.refs_2_, bf16[72,1152]{1,0:T(8,128)(2,1)S(1)} %collective-permute-done.20.refs_3_, ...), custom_call_target="tpu_custom_call" | custom-call | flops 1 | bytes 1 | tf_op jit(solution)/shard_map/finish/pallas_call | solution.py:65
  (45 shorter events, 6.1 us)
Async XLA Ops:
  1.8 5.4 %collective-permute-start.5 = (bf16[64,1152]{1,0:T(8,128)(2,1)S(1)}, bf16[64,1152]{1,0:T(8,128)(2,1)S(1)}, u32[]{:S(2)}, u32[]{:S(2)}) collective-permute-start(bf16[64,1152]{1,0:T(8,128)(2,1)S(1)} %get-tuple-element.48.refs_0_), channel_id=1, source_target_pairs={{0,32},{1,33},{2,34},{3,35},{4,36},{5,37},{6,38},{7,39},{8,40},{9,... | collective-permute-start | bytes 442376 | tf_op jit(solution)/shard_map/ppermute | solution.py:55
  5.1 8.9 %collective-permute-start.2 = (bf16[64,1152]{1,0:T(8,128)(2,1)S(1)}, bf16[64,1152]{1,0:T(8,128)(2,1)S(1)}, u32[]{:S(2)}, u32[]{:S(2)}) collective-permute-start(bf16[64,1152]{1,0:T(8,128)(2,1)S(1)} %get-tuple-element.47.refs_0_), channel_id=1, source_target_pairs={{0,192},{1,193},{2,194},{3,195},{4,196},{5,197},{6,198},{7,199},{8... | collective-permute-start | bytes 442376 | tf_op jit(solution)/shard_map/ppermute | solution.py:39
  6.1 7.9 %collective-permute-start.1 = (bf16[64,1152]{1,0:T(8,128)(2,1)S(1)}, bf16[64,1152]{1,0:T(8,128)(2,1)S(1)}, u32[]{:S(2)}, u32[]{:S(2)}) collective-permute-start(bf16[64,1152]{1,0:T(8,128)(2,1)S(1)} %get-tuple-element.47.refs_0_), channel_id=1, source_target_pairs={{0,128},{1,129},{2,130},{3,131},{4,132},{5,133},{6,134},{7,135},{8... | collective-permute-start | bytes 442376 | tf_op jit(solution)/shard_map/ppermute | solution.py:39
  6.5 7.6 %collective-permute-start = (bf16[64,1152]{1,0:T(8,128)(2,1)S(1)}, bf16[64,1152]{1,0:T(8,128)(2,1)S(1)}, u32[]{:S(2)}, u32[]{:S(2)}) collective-permute-start(bf16[64,1152]{1,0:T(8,128)(2,1)S(1)} %get-tuple-element.47.refs_0_), channel_id=1, source_target_pairs={{0,64},{1,65},{2,66},{3,67},{4,68},{5,69},{6,70},{7,71},{8,72},{9,... | collective-permute-start | bytes 442376 | tf_op jit(solution)/shard_map/ppermute | solution.py:39
  7.2 12.9 %collective-permute-start.7 = (bf16[128,1152]{1,0:T(8,128)(2,1)S(1)}, bf16[128,1152]{1,0:T(8,128)(2,1)S(1)}, u32[]{:S(2)}, u32[]{:S(2)}) collective-permute-start(bf16[128,1152]{1,0:T(8,128)(2,1)S(1)} %pair.1.refs_1_), channel_id=1, source_target_pairs={{0,8},{1,9},{2,10},{3,11},{4,12},{5,13},{6,14},{7,15},{8,16},{9,17... | collective-permute-start | bytes 884744 | tf_op jit(solution)/shard_map/ppermute | solution.py:51
  13.3 10.0 %collective-permute-start.6 = (bf16[128,1152]{1,0:T(8,128)(2,1)S(1)}, bf16[128,1152]{1,0:T(8,128)(2,1)S(1)}, u32[]{:S(2)}, u32[]{:S(2)}) collective-permute-start(bf16[128,1152]{1,0:T(8,128)(2,1)S(1)} %pair.1.refs_1_), channel_id=1, source_target_pairs={{0,4},{1,5},{2,6},{3,7},{4,8},{5,9},{6,10},{7,11},{8,12},{9,13},{1... | collective-permute-start | bytes 884744 | tf_op jit(solution)/shard_map/ppermute | solution.py:51
  14.1 15.6 %collective-permute-start.3 = (bf16[264,1152]{1,0:T(8,128)(2,1)S(1)}, bf16[264,1152]{1,0:T(8,128)(2,1)S(1)}, u32[]{:S(2)}, u32[]{:S(2)}) collective-permute-start(bf16[264,1152]{1,0:T(8,128)(2,1)S(1)} %group.1.refs_2_), channel_id=1, source_target_pairs={{0,1},{1,2},{2,3},{3,0},{4,5},{5,6},{6,7},{7,4},{8,9},{9,10},{10,1... | collective-permute-start | bytes 1824776 | tf_op jit(solution)/shard_map/ppermute | solution.py:45
  15.4 16.9 %collective-permute-start.4 = (bf16[264,1152]{1,0:T(8,128)(2,1)S(1)}, bf16[264,1152]{1,0:T(8,128)(2,1)S(1)}, u32[]{:S(2)}, u32[]{:S(2)}) collective-permute-start(bf16[264,1152]{1,0:T(8,128)(2,1)S(1)} %group.1.refs_2_), channel_id=1, source_target_pairs={{0,3},{1,0},{2,1},{3,2},{4,7},{5,4},{6,5},{7,6},{8,11},{9,8},{10,9... | collective-permute-start | bytes 1824776 | tf_op jit(solution)/shard_map/ppermute | solution.py:45
  23.4 9.4 %collective-permute-start.8 = (bf16[256,1152]{1,0:T(8,128)(2,1)S(1)}, bf16[256,1152]{1,0:T(8,128)(2,1)S(1)}, u32[]{:S(2)}, u32[]{:S(2)}) collective-permute-start(bf16[256,1152]{1,0:T(8,128)(2,1)S(1)} %get-tuple-element.49.refs_3_.refs_6_.refs_2_), channel_id=1, source_target_pairs={{0,32},{1,33},{2,34},{3,35},{4,36},{5,37},{6,38},{7,39},{8,40},{9,... | collective-permute-start | bytes 1769480 | tf_op jit(solution)/shard_map/ppermute | solution.py:55
  25.1 10.6 %collective-permute-start.10 = (bf16[128,1152]{1,0:T(8,128)(2,1)S(1)}, bf16[128,1152]{1,0:T(8,128)(2,1)S(1)}, u32[]{:S(2)}, u32[]{:S(2)}) collective-permute-start(bf16[128,1152]{1,0:T(8,128)(2,1)S(1)} %collective-permute-done.7.refs_1_), channel_id=1, source_target_pairs={{0,4},{1,5},{2,6},{3,7},{4,8},{5,9},{6,10},{7,11},{8,12},{9,13},{1... | collective-permute-start | bytes 884744 | tf_op jit(solution)/shard_map/ppermute | solution.py:51
  26.9 14.4 %collective-permute-start.12 = (bf16[264,1152]{1,0:T(8,128)(2,1)S(1)}, bf16[264,1152]{1,0:T(8,128)(2,1)S(1)}, u32[]{:S(2)}, u32[]{:S(2)}) collective-permute-start(bf16[264,1152]{1,0:T(8,128)(2,1)S(1)} %group.1.refs_2_), channel_id=1, source_target_pairs={{0,2},{1,3},{2,0},{3,1},{4,6},{5,7},{6,4},{7,5},{8,10},{9,11},{10,... | collective-permute-start | bytes 1824776 | tf_op jit(solution)/shard_map/ppermute | solution.py:45
  29.7 6.0 %collective-permute-start.9 = (bf16[64,1152]{1,0:T(8,128)(2,1)S(1)}, bf16[64,1152]{1,0:T(8,128)(2,1)S(1)}, u32[]{:S(2)}, u32[]{:S(2)}) collective-permute-start(bf16[64,1152]{1,0:T(8,128)(2,1)S(1)} %get-tuple-element.59), channel_id=1, source_target_pairs={{0,8},{1,9},{2,10},{3,11},{4,12},{5,13},{6,14},{7,15},{8,16},{9,17... | collective-permute-start | bytes 442376 | tf_op jit(solution)/shard_map/ppermute | solution.py:51
  35.7 4.0 %collective-permute-start.11 = (bf16[192,1152]{1,0:T(8,128)(2,1)S(1)}, bf16[192,1152]{1,0:T(8,128)(2,1)S(1)}, u32[]{:S(2)}, u32[]{:S(2)}) collective-permute-start(bf16[192,1152]{1,0:T(8,128)(2,1)S(1)} %far_mine.1.refs_5_.refs_0_), channel_id=1, source_target_pairs={{0,32},{1,33},{2,34},{3,35},{4,36},{5,37},{6,38},{7,39},{8,40},{9,... | collective-permute-start | bytes 1327112 | tf_op jit(solution)/shard_map/ppermute | solution.py:55
  44.0 2.7 %collective-permute-start.14 = (bf16[256,1152]{1,0:T(8,128)(2,1)S(1)}, bf16[256,1152]{1,0:T(8,128)(2,1)S(1)}, u32[]{:S(2)}, u32[]{:S(2)}) collective-permute-start(bf16[256,1152]{1,0:T(8,128)(2,1)S(1)} %get-tuple-element.76), channel_id=1, source_target_pairs={{0,32},{1,33},{2,34},{3,35},{4,36},{5,37},{6,38},{7,39},{8,40},{9,... | collective-permute-start | bytes 1769480 | tf_op jit(solution)/shard_map/ppermute | solution.py:55
  44.3 2.5 %collective-permute-start.13 = (bf16[192,1152]{1,0:T(8,128)(2,1)S(1)}, bf16[192,1152]{1,0:T(8,128)(2,1)S(1)}, u32[]{:S(2)}, u32[]{:S(2)}) collective-permute-start(bf16[192,1152]{1,0:T(8,128)(2,1)S(1)} %get-tuple-element.69.refs_4_), channel_id=1, source_target_pairs={{0,32},{1,33},{2,34},{3,35},{4,36},{5,37},{6,38},{7,39},{8,40},{9,... | collective-permute-start | bytes 1327112 | tf_op jit(solution)/shard_map/ppermute | solution.py:55
  46.9 14.2 %collective-permute-start.18 = (bf16[192,1152]{1,0:T(8,128)(2,1)S(1)}, bf16[192,1152]{1,0:T(8,128)(2,1)S(1)}, u32[]{:S(2)}, u32[]{:S(2)}) collective-permute-start(bf16[192,1152]{1,0:T(8,128)(2,1)S(1)} %step1.1.refs_3_), channel_id=1, source_target_pairs={{0,24},{1,25},{2,26},{3,27},{4,28},{5,29},{6,30},{7,31},{8,0},{9,1... | collective-permute-start | bytes 1327112 | tf_op jit(solution)/shard_map/ppermute | solution.py:51
  48.9 14.4 %collective-permute-start.16 = (bf16[264,1152]{1,0:T(8,128)(2,1)S(1)}, bf16[264,1152]{1,0:T(8,128)(2,1)S(1)}, u32[]{:S(2)}, u32[]{:S(2)}) collective-permute-start(bf16[264,1152]{1,0:T(8,128)(2,1)S(1)} %image2.1.refs_2_), channel_id=1, source_target_pairs={{0,2},{1,3},{2,0},{3,1},{4,6},{5,7},{6,4},{7,5},{8,10},{9,11},{10,... | collective-permute-start | bytes 1824776 | tf_op jit(solution)/shard_map/ppermute | solution.py:45
  50.1 15.9 %collective-permute-start.17 = (bf16[264,1152]{1,0:T(8,128)(2,1)S(1)}, bf16[264,1152]{1,0:T(8,128)(2,1)S(1)}, u32[]{:S(2)}, u32[]{:S(2)}) collective-permute-start(bf16[264,1152]{1,0:T(8,128)(2,1)S(1)} %image3.1.refs_6_), channel_id=1, source_target_pairs={{0,1},{1,2},{2,3},{3,0},{4,5},{5,6},{6,7},{7,4},{8,9},{9,10},{10,1... | collective-permute-start | bytes 1824776 | tf_op jit(solution)/shard_map/ppermute | solution.py:45
  51.5 14.4 %collective-permute-start.15 = (bf16[264,1152]{1,0:T(8,128)(2,1)S(1)}, bf16[264,1152]{1,0:T(8,128)(2,1)S(1)}, u32[]{:S(2)}, u32[]{:S(2)}) collective-permute-start(bf16[264,1152]{1,0:T(8,128)(2,1)S(1)} %image1.1.refs_4_), channel_id=1, source_target_pairs={{0,3},{1,0},{2,1},{3,2},{4,7},{5,4},{6,5},{7,6},{8,11},{9,8},{10,9... | collective-permute-start | bytes 1824776 | tf_op jit(solution)/shard_map/ppermute | solution.py:45
  61.2 11.0 %collective-permute-start.23 = (bf16[128,1152]{1,0:T(8,128)(2,1)S(1)}, bf16[128,1152]{1,0:T(8,128)(2,1)S(1)}, u32[]{:S(2)}, u32[]{:S(2)}) collective-permute-start(bf16[128,1152]{1,0:T(8,128)(2,1)S(1)} %get-tuple-element.86), channel_id=1, source_target_pairs={{0,24},{1,25},{2,26},{3,27},{4,28},{5,29},{6,30},{7,31},{8,0},{9,1... | collective-permute-start | bytes 884744 | tf_op jit(solution)/shard_map/ppermute | solution.py:51
  61.3 13.6 %collective-permute-start.22 = (bf16[128,1152]{1,0:T(8,128)(2,1)S(1)}, bf16[128,1152]{1,0:T(8,128)(2,1)S(1)}, u32[]{:S(2)}, u32[]{:S(2)}) collective-permute-start(bf16[128,1152]{1,0:T(8,128)(2,1)S(1)} %get-tuple-element.78.refs_5_), channel_id=1, source_target_pairs={{0,28},{1,29},{2,30},{3,31},{4,0},{5,1},{6,2},{7,3},{8,4},{9,5},{1... | collective-permute-start | bytes 884744 | tf_op jit(solution)/shard_map/ppermute | solution.py:51
  66.2 10.6 %copy-start = (bf16[64,1152]{1,0:T(8,128)(2,1)S(1)}, bf16[64,1152]{1,0:T(8,128)(2,1)}, u32[]{:S(2)}) copy-start(bf16[64,1152]{1,0:T(8,128)(2,1)} %refs_5_.1) | copy-start | bytes 442372
  66.3 10.6 %copy-start.1 = (bf16[64,1152]{1,0:T(8,128)(2,1)S(1)}, bf16[64,1152]{1,0:T(8,128)(2,1)}, u32[]{:S(2)}) copy-start(bf16[64,1152]{1,0:T(8,128)(2,1)} %refs_11_.1) | copy-start | bytes 442372
  66.3 9.6 %collective-permute-start.19 = (bf16[72,1152]{1,0:T(8,128)(2,1)S(1)}, bf16[72,1152]{1,0:T(8,128)(2,1)S(1)}, u32[]{:S(2)}, u32[]{:S(2)}) collective-permute-start(bf16[72,1152]{1,0:T(8,128)(2,1)S(1)} %get-tuple-element.81), channel_id=1, source_target_pairs={{0,192},{1,193},{2,194},{3,195},{4,196},{5,197},{6,198},{7,199},{8... | collective-permute-start | bytes 497672 | tf_op jit(solution)/shard_map/ppermute | solution.py:39
  68.1 7.8 %collective-permute-start.20 = (bf16[72,1152]{1,0:T(8,128)(2,1)S(1)}, bf16[72,1152]{1,0:T(8,128)(2,1)S(1)}, u32[]{:S(2)}, u32[]{:S(2)}) collective-permute-start(bf16[72,1152]{1,0:T(8,128)(2,1)S(1)} %get-tuple-element.82), channel_id=1, source_target_pairs={{0,128},{1,129},{2,130},{3,131},{4,132},{5,133},{6,134},{7,135},{8... | collective-permute-start | bytes 497672 | tf_op jit(solution)/shard_map/ppermute | solution.py:39
  68.1 7.8 %collective-permute-start.21 = (bf16[72,1152]{1,0:T(8,128)(2,1)S(1)}, bf16[72,1152]{1,0:T(8,128)(2,1)S(1)}, u32[]{:S(2)}, u32[]{:S(2)}) collective-permute-start(bf16[72,1152]{1,0:T(8,128)(2,1)S(1)} %get-tuple-element.83.refs_3_), channel_id=1, source_target_pairs={{0,64},{1,65},{2,66},{3,67},{4,68},{5,69},{6,70},{7,71},{8,72},{9,... | collective-permute-start | bytes 497672 | tf_op jit(solution)/shard_map/ppermute | solution.py:39
  74.9 2.0 %collective-permute-start.24 = (bf16[64,1152]{1,0:T(8,128)(2,1)S(1)}, bf16[64,1152]{1,0:T(8,128)(2,1)S(1)}, u32[]{:S(2)}, u32[]{:S(2)}) collective-permute-start(bf16[64,1152]{1,0:T(8,128)(2,1)S(1)} %step3.1), channel_id=1, source_target_pairs={{0,32},{1,33},{2,34},{3,35},{4,36},{5,37},{6,38},{7,39},{8,40},{9,... | collective-permute-start | bytes 442376 | tf_op jit(solution)/shard_map/ppermute | solution.py:55

commit v11 on v10

--- a/solution.py
+++ b/solution.py
@@ -185,16 +185,17 @@
     loss_ref[...] = fold(softplus)
 
 
-def other_body(scale_ref, bias_ref, i0, i1, i3, m0, m1, m3, l0, l1, l3, txt_ref, n0, n1, n3, t0, t1, t3, part):
+def other_body(scale_ref, bias_ref, i0, i1, i3, m0, m1, m3, l0, l1, l3, mine, txt_ref, n1, n3, t0, t1, t3, part, g0, n0):
     groups = ((i0, m0, l0, n0, t0), (i1, m1, l1, n1, t1), (i3, m3, l3, n3, t3))
     for k, (i, m, l, n, t) in enumerate(groups):
         n[:, :256] = m[...]
         t[...] = tile(i, txt_ref, n.at[:, 256:], l[...], scale_ref[0], bias_ref[0], k == 0)
     part[...] = texts((n0, n1, n3), (i0, i1, i3), 0, 640)
-
-
-def near_images_body(n0, n1, n3, mine, other, g0, g1, g3):
-    for n, g in ((n0, g0), (n1, g1), (n3, g3)):
+    g0[...] = near_image(n0, mine, txt_ref)
+
+
+def near_images_body(n1, n3, mine, other, g1, g3):
+    for n, g in ((n1, g1), (n3, g3)):
         g[...] = near_image(n, mine, other)
 
 
@@ -309,8 +310,8 @@
         return call(name, pack_body, [shape(n, d)], parts, (), after)[0]
 
     pair = pack("pair", 128, (txt, swap(txt)))
-    b2, b1 = ring(pair, 2), ring(pair, 1)
-    f2, f1, f3 = first(img, 2), first(img, 1), first(img, 3)
+    b1, b2 = ring(pair, 1), ring(pair, 2)
+    f1, f3, f2 = first(img, 1), first(img, 3), first(img, 2)
     group = pack("group", 264, (img, f1, f2, f3))
     g1, g3, g2 = second(group, 1), second(group, 3), second(group, 2)
     groups = (group, g1, g2, g3)
@@ -329,18 +330,20 @@
         )
         last = (mine_l[k],)
     other = pack("other_texts", 384, (near_other, pair), last)
-    n0, n1, n3, l0, l1, l3, part = call(
+    n1, n3, l0, l1, l3, part, t0 = call(
         "other", other_body,
-        [shape(256, 640)] * 3 + [shape(256, 128, dtype=F32)] * 3 + [shape(640, d, dtype=F32)],
-        (group, g1, g3, *mine_c.values(), *mine_l.values(), other), sc,
+        [shape(256, 640)] * 2 + [shape(256, 128, dtype=F32)] * 3
+        + [shape(640, d, dtype=F32), shape(256, d, dtype=F32)],
+        (group, g1, g3, *mine_c.values(), *mine_l.values(), near_mine, other), sc,
+        scratch=[pltpu.VMEM((256, 640), BF16)],
     )
     far_mine = pack("far_mine", 192, (b4, b3), (l0,))
     far_other = swap(far_mine)
-    t0, t1, t3 = call(
-        "near_images", near_images_body, [shape(256, d, dtype=F32)] * 3,
-        (n0, n1, n3, near_mine, other), (), (far_mine,),
-    )
-    far = pack("far_texts", 384, (far_mine, far_other), (t0,))
+    t1, t3 = call(
+        "near_images", near_images_body, [shape(256, d, dtype=F32)] * 2,
+        (n1, n3, near_mine, other), (), (far_mine,),
+    )
+    far = pack("far_texts", 384, (far_mine, far_other), (t1,))
     c0, c1, c3, rows013 = call(
         "far", far_body, [shape(256, 384)] * 3 + [shape(8, 768, dtype=F32)],
         (group, g1, g3, far, l0, l1, l3), sc,

time: 78.1 us -> 78.3 us (level)
  transfers between devices with their start and end apart: 25 -> 25, of which waited for: 9 -> 9; matrix products, arithmetic and copies ran while one was open for 0% -> 0% of each run, Pallas kernels for 13% -> 14%
where the time goes in v11:
time: 78.3 us; the launch traced here: 78.2 us
  starting transfers between devices  35.7 us (46%)
  waiting for transfers between devices  24.7 us (32%)
  Pallas kernels  15.6 us (20%)
  between operations  2.14 us (3%)
    ppermute x7, waiting for transfers between devices, ring(): lax.ppermute(a, AXES, permutation(lambda x, c, z, y: (x, c, z - s if c el...  20.5 us
    pallas_call x23, Pallas kernels, call(): pl.pallas_call(kernel, out_shape=outs, in_specs=[SMEM] * len(scalars) + (...  15.6 us
    ppermute x7, starting transfers between devices, ring(): lax.ppermute(a, AXES, permutation(lambda x, c, z, y: (x, c, z - s if c el...  12.5 us
    ppermute x6, starting transfers between devices, second(): lax.ppermute(a, AXES, permutation(lambda x, c, z, y: (x + s, c, z, y) if...  9.74 us
    ppermute x6, starting transfers between devices, swap(): lax.ppermute(a, AXES, permutation(lambda x, c, z, y: (x, 1 - c, z, y)))  8.88 us
    ppermute x6, starting transfers between devices, first(): lax.ppermute(a, AXES, permutation(lambda x, c, z, y: (x, c, z, y + s) if...  4.58 us
    ppermute x6, waiting for transfers between devices, second(): lax.ppermute(a, AXES, permutation(lambda x, c, z, y: (x + s, c, z, y) if...  2.84 us
  transfers between devices with their start and end apart: 25, of which 9 were waited for; matrix products, arithmetic and copies ran while one was open for 0% of the time, Pallas kernels for 14%

profile of v11, /device:TPU:1, one launch (start us, length us, event | category | flops | bytes accessed | tf_op | source)
XLA Modules:
  0.0 78.2 jit_solution(17687420047383657821)
XLA Ops:
  0.6 1.2 %normalize.1 = (bf16[64,1152]{1,0:T(8,128)(2,1)S(1)}, bf16[64,1152]{1,0:T(8,128)(2,1)S(1)}, f32[64,1]{1,0:T(8,128)S(1)}, f32[64,1]{1,0:T(8,128)S(1)}) custom-call(bf16[64,1152]{1,0:T(8,128)(2,1)} %refs_5_.1, bf16[64,1152]{1,0:T(8,128)(2,1)} %refs_11_.1), custom_call_target="tpu_custom_call" | custom-call | flops 1 | bytes 1 | tf_op jit(solution)/shard_map/normalize/pallas_call | solution.py:65
  1.8 3.3 %collective-permute-start.5 = (bf16[64,1152]{1,0:T(8,128)(2,1)S(1)}, bf16[64,1152]{1,0:T(8,128)(2,1)S(1)}, u32[]{:S(2)}, u32[]{:S(2)}) collective-permute-start(bf16[64,1152]{1,0:T(8,128)(2,1)S(1)} %get-tuple-element.47.refs_0_), channel_id=1, source_target_pairs={{0,32},{1,33},{2,34},{3,35},{4,36},{5,37},{6,38},{7,39},{8,40},{9,... | collective-permute-start | bytes 442376 | tf_op jit(solution)/shard_map/ppermute | solution.py:55
  5.1 1.0 %collective-permute-start.2 = (bf16[64,1152]{1,0:T(8,128)(2,1)S(1)}, bf16[64,1152]{1,0:T(8,128)(2,1)S(1)}, u32[]{:S(2)}, u32[]{:S(2)}) collective-permute-start(bf16[64,1152]{1,0:T(8,128)(2,1)S(1)} %get-tuple-element.46.refs_0_), channel_id=1, source_target_pairs={{0,192},{1,193},{2,194},{3,195},{4,196},{5,197},{6,198},{7,199},{8... | collective-permute-start | bytes 442376 | tf_op jit(solution)/shard_map/ppermute | solution.py:39
  6.5 0.7 collective-permute-start
  7.2 6.1 %collective-permute-start.7 = (bf16[128,1152]{1,0:T(8,128)(2,1)S(1)}, bf16[128,1152]{1,0:T(8,128)(2,1)S(1)}, u32[]{:S(2)}, u32[]{:S(2)}) collective-permute-start(bf16[128,1152]{1,0:T(8,128)(2,1)S(1)} %pair.1.refs_1_), channel_id=1, source_target_pairs={{0,8},{1,9},{2,10},{3,11},{4,12},{5,13},{6,14},{7,15},{8,16},{9,17... | collective-permute-start | bytes 884744 | tf_op jit(solution)/shard_map/ppermute | solution.py:51
  13.3 0.7 collective-permute-start.6
  14.1 1.3 %collective-permute-start.3 = (bf16[264,1152]{1,0:T(8,128)(2,1)S(1)}, bf16[264,1152]{1,0:T(8,128)(2,1)S(1)}, u32[]{:S(2)}, u32[]{:S(2)}) collective-permute-start(bf16[264,1152]{1,0:T(8,128)(2,1)S(1)} %group.1.refs_2_), channel_id=1, source_target_pairs={{0,1},{1,2},{2,3},{3,0},{4,5},{5,6},{6,7},{7,4},{8,9},{9,10},{10,1... | collective-permute-start | bytes 1824776 | tf_op jit(solution)/shard_map/ppermute | solution.py:45
  15.4 1.5 %collective-permute-start.4 = (bf16[264,1152]{1,0:T(8,128)(2,1)S(1)}, bf16[264,1152]{1,0:T(8,128)(2,1)S(1)}, u32[]{:S(2)}, u32[]{:S(2)}) collective-permute-start(bf16[264,1152]{1,0:T(8,128)(2,1)S(1)} %group.1.refs_2_), channel_id=1, source_target_pairs={{0,3},{1,0},{2,1},{3,2},{4,7},{5,4},{6,5},{7,6},{8,11},{9,8},{10,9... | collective-permute-start | bytes 1824776 | tf_op jit(solution)/shard_map/ppermute | solution.py:45
  16.9 3.3 %collective-permute-done.7.refs_1_ = bf16[128,1152]{1,0:T(8,128)(2,1)S(1)} collective-permute-done((bf16[128,1152]{1,0:T(8,128)(2,1)S(1)}, bf16[128,1152]{1,0:T(8,128)(2,1)S(1)}, u32[]{:S(2)}, u32[]{:S(2)}) %collective-permute-start.7) | collective-permute-done | bytes 294944 | tf_op jit(solution)/shard_map/ppermute | solution.py:51
  20.1 3.2 %collective-permute-done.6.refs_0_ = bf16[128,1152]{1,0:T(8,128)(2,1)S(1)} collective-permute-done((bf16[128,1152]{1,0:T(8,128)(2,1)S(1)}, bf16[128,1152]{1,0:T(8,128)(2,1)S(1)}, u32[]{:S(2)}, u32[]{:S(2)}) %collective-permute-start.6) | collective-permute-done | bytes 294944 | tf_op jit(solution)/shard_map/ppermute | solution.py:51
  23.4 1.7 %collective-permute-start.8 = (bf16[256,1152]{1,0:T(8,128)(2,1)S(1)}, bf16[256,1152]{1,0:T(8,128)(2,1)S(1)}, u32[]{:S(2)}, u32[]{:S(2)}) collective-permute-start(bf16[256,1152]{1,0:T(8,128)(2,1)S(1)} %get-tuple-element.48.refs_3_.refs_11_.refs_2_.refs_6_), channel_id=1, source_target_pairs={{0,32},{1,33},{2,34},{3,35},{4,36},{5,37},{6,38},{7,39},{8,40},{9,... | collective-permute-start | bytes 1769480 | tf_op jit(solution)/shard_map/ppermute | solution.py:55
  25.1 1.9 %collective-permute-start.10 = (bf16[128,1152]{1,0:T(8,128)(2,1)S(1)}, bf16[128,1152]{1,0:T(8,128)(2,1)S(1)}, u32[]{:S(2)}, u32[]{:S(2)}) collective-permute-start(bf16[128,1152]{1,0:T(8,128)(2,1)S(1)} %collective-permute-done.7.refs_1_), channel_id=1, source_target_pairs={{0,4},{1,5},{2,6},{3,7},{4,8},{5,9},{6,10},{7,11},{8,12},{9,13},{1... | collective-permute-start | bytes 884744 | tf_op jit(solution)/shard_map/ppermute | solution.py:51
  26.9 2.7 %collective-permute-start.12 = (bf16[264,1152]{1,0:T(8,128)(2,1)S(1)}, bf16[264,1152]{1,0:T(8,128)(2,1)S(1)}, u32[]{:S(2)}, u32[]{:S(2)}) collective-permute-start(bf16[264,1152]{1,0:T(8,128)(2,1)S(1)} %group.1.refs_2_), channel_id=1, source_target_pairs={{0,2},{1,3},{2,0},{3,1},{4,6},{5,7},{6,4},{7,5},{8,10},{9,11},{10,... | collective-permute-start | bytes 1824776 | tf_op jit(solution)/shard_map/ppermute | solution.py:45
  32.9 3.2 %other.1 = (bf16[256,640]{1,0:T(8,128)(2,1)S(1)}, bf16[256,640]{1,0:T(8,128)(2,1)S(1)}, f32[256,128]{1,0:T(8,128)S(1)}, f32[256,128]{1,0:T(8,128)S(1)}, f32[256,...) custom-call(f32[1]{0:T(128)S(6)} %copy.7.refs_0_, f32[1]{0:T(128)S(6)} %copy.8.refs_1_, ...), custom_call_target="tpu_custom_call" | custom-call | flops 1 | bytes 1 | tf_op jit(solution)/shard_map/other/pallas_call | solution.py:65
  36.2 2.2 %collective-permute-start.11 = (bf16[192,1152]{1,0:T(8,128)(2,1)S(1)}, bf16[192,1152]{1,0:T(8,128)(2,1)S(1)}, u32[]{:S(2)}, u32[]{:S(2)}) collective-permute-start(bf16[192,1152]{1,0:T(8,128)(2,1)S(1)} %far_mine.1.refs_4_.refs_0_), channel_id=1, source_target_pairs={{0,32},{1,33},{2,34},{3,35},{4,36},{5,37},{6,38},{7,39},{8,40},{9,... | collective-permute-start | bytes 1327112 | tf_op jit(solution)/shard_map/ppermute | solution.py:55
  38.4 1.2 %near_images.1 = (f32[256,1152]{1,0:T(8,128)S(1)}, f32[256,1152]{1,0:T(8,128)S(1)}) custom-call(bf16[256,640]{1,0:T(8,128)(2,1)S(1)} %get-tuple-element.58.refs_0_, bf16[256,640]{1,0:T(8,128)(2,1)S(1)} %get-tuple-element.59.refs_1_, bf16[256,1152]{1,0:T(8,128)(2,1)S(1)} %get-tuple-element.48.refs_3_.refs_11_.refs_2_.refs_6_, ...), custom_call_target="tpu_custom_call" | custom-call | flops 1 | bytes 1 | tf_op jit(solution)/shard_map/near_images/pallas_call | solution.py:65
  39.9 1.5 %far.1 = (bf16[256,384]{1,0:T(8,128)(2,1)S(1)}, bf16[256,384]{1,0:T(8,128)(2,1)S(1)}, bf16[256,384]{1,0:T(8,128)(2,1)S(1)}, f32[8,768]{1,0:T(8,128)S(1)}) custom-call(f32[1]{0:T(128)S(6)} %copy.7.refs_0_, f32[1]{0:T(128)S(6)} %copy.8.refs_1_, bf16[264,1152]{1,0:T(8,128)(2,1)S(1)} %group.1.refs_2_, ...), custom_call_target="tpu_custom_call" | custom-call | flops 1 | bytes 1 | tf_op jit(solution)/shard_map/far/pallas_call | solution.py:65
  41.5 2.7 %last.1 = (bf16[256,640]{1,0:T(8,128)(2,1)S(1)}, bf16[256,384]{1,0:T(8,128)(2,1)S(1)}, f32[8,256]{1,0:T(8,128)S(1)}, f32[192,1152]{1,0:T(8,128)S(1)}, bf16[192,1...) custom-call(f32[1]{0:T(128)S(6)} %copy.7.refs_0_, ...), custom_call_target="tpu_custom_call" | custom-call | flops 1 | bytes 1 | tf_op jit(solution)/shard_map/last/pallas_call | solution.py:65
  45.8 1.0 %image2.1.refs_2_ = bf16[264,1152]{1,0:T(8,128)(2,1)S(1)} custom-call(bf16[256,640]{1,0:T(8,128)(2,1)S(1)} %get-tuple-element.69.refs_0_, bf16[256,384]{1,0:T(8,128)(2,1)S(1)} %get-tuple-element.70.refs_1_, bf16[256,1152]{1,0:T(8,128)(2,1)S(1)} %get-tuple-element.48.refs_3_.refs_11_.refs_2_.refs_6_, ...), custom_call_target="tpu_custom_call" | custom-call | flops 1 | bytes 1 | tf_op jit(solution)/shard_map/image2/pallas_call | solution.py:65
  47.0 1.8 %collective-permute-start.18 = (bf16[192,1152]{1,0:T(8,128)(2,1)S(1)}, bf16[192,1152]{1,0:T(8,128)(2,1)S(1)}, u32[]{:S(2)}, u32[]{:S(2)}) collective-permute-start(bf16[192,1152]{1,0:T(8,128)(2,1)S(1)} %step1.1.refs_3_), channel_id=1, source_target_pairs={{0,24},{1,25},{2,26},{3,27},{4,28},{5,29},{6,30},{7,31},{8,0},{9,1... | collective-permute-start | bytes 1327112 | tf_op jit(solution)/shard_map/ppermute | solution.py:51
  48.8 1.6 %collective-permute-start.16 = (bf16[264,1152]{1,0:T(8,128)(2,1)S(1)}, bf16[264,1152]{1,0:T(8,128)(2,1)S(1)}, u32[]{:S(2)}, u32[]{:S(2)}) collective-permute-start(bf16[264,1152]{1,0:T(8,128)(2,1)S(1)} %image2.1.refs_2_), channel_id=1, source_target_pairs={{0,2},{1,3},{2,0},{3,1},{4,6},{5,7},{6,4},{7,5},{8,10},{9,11},{10,... | collective-permute-start | bytes 1824776 | tf_op jit(solution)/shard_map/ppermute | solution.py:45
  50.4 1.1 %collective-permute-start.17 = (bf16[264,1152]{1,0:T(8,128)(2,1)S(1)}, bf16[264,1152]{1,0:T(8,128)(2,1)S(1)}, u32[]{:S(2)}, u32[]{:S(2)}) collective-permute-start(bf16[264,1152]{1,0:T(8,128)(2,1)S(1)} %image3.1.refs_6_), channel_id=1, source_target_pairs={{0,1},{1,2},{2,3},{3,0},{4,5},{5,6},{6,7},{7,4},{8,9},{9,10},{10,1... | collective-permute-start | bytes 1824776 | tf_op jit(solution)/shard_map/ppermute | solution.py:45
  51.5 1.6 %collective-permute-start.15 = (bf16[264,1152]{1,0:T(8,128)(2,1)S(1)}, bf16[264,1152]{1,0:T(8,128)(2,1)S(1)}, u32[]{:S(2)}, u32[]{:S(2)}) collective-permute-start(bf16[264,1152]{1,0:T(8,128)(2,1)S(1)} %image1.1.refs_4_), channel_id=1, source_target_pairs={{0,3},{1,0},{2,1},{3,2},{4,7},{5,4},{6,5},{7,6},{8,11},{9,8},{10,9... | collective-permute-start | bytes 1824776 | tf_op jit(solution)/shard_map/ppermute | solution.py:45
  53.6 7.8 %collective-permute-done.18.refs_2_ = bf16[192,1152]{1,0:T(8,128)(2,1)S(1)} collective-permute-done((bf16[192,1152]{1,0:T(8,128)(2,1)S(1)}, bf16[192,1152]{1,0:T(8,128)(2,1)S(1)}, u32[]{:S(2)}, u32[]{:S(2)}) %collective-permute-start.18) | collective-permute-done | bytes 442400 | tf_op jit(solution)/shard_map/ppermute | solution.py:51
  61.6 1.5 %collective-permute-start.22 = (bf16[128,1152]{1,0:T(8,128)(2,1)S(1)}, bf16[128,1152]{1,0:T(8,128)(2,1)S(1)}, u32[]{:S(2)}, u32[]{:S(2)}) collective-permute-start(bf16[128,1152]{1,0:T(8,128)(2,1)S(1)} %get-tuple-element.76.refs_5_), channel_id=1, source_target_pairs={{0,28},{1,29},{2,30},{3,31},{4,0},{5,1},{6,2},{7,3},{8,4},{9,5},{1... | collective-permute-start | bytes 884744 | tf_op jit(solution)/shard_map/ppermute | solution.py:51
  63.1 2.8 %collective-permute-done.17.refs_4_ = bf16[264,1152]{1,0:T(8,128)(2,1)S(1)} collective-permute-done((bf16[264,1152]{1,0:T(8,128)(2,1)S(1)}, bf16[264,1152]{1,0:T(8,128)(2,1)S(1)}, u32[]{:S(2)}, u32[]{:S(2)}) %collective-permute-start.17) | collective-permute-done | bytes 608288 | tf_op jit(solution)/shard_map/ppermute | solution.py:45
  66.2 1.9 %collective-permute-start.19 = (bf16[72,1152]{1,0:T(8,128)(2,1)S(1)}, bf16[72,1152]{1,0:T(8,128)(2,1)S(1)}, u32[]{:S(2)}, u32[]{:S(2)}) collective-permute-start(bf16[72,1152]{1,0:T(8,128)(2,1)S(1)} %get-tuple-element.79), channel_id=1, source_target_pairs={{0,192},{1,193},{2,194},{3,195},{4,196},{5,197},{6,198},{7,199},{8... | collective-permute-start | bytes 497672 | tf_op jit(solution)/shard_map/ppermute | solution.py:39
  68.8 3.8 %collective-permute-done.23.refs_2_.refs_9_ = bf16[128,1152]{1,0:T(8,128)(2,1)S(1)} collective-permute-done((bf16[128,1152]{1,0:T(8,128)(2,1)S(1)}, bf16[128,1152]{1,0:T(8,128)(2,1)S(1)}, u32[]{:S(2)}, u32[]{:S(2)}) %collective-permute-start.23) | collective-permute-done | bytes 294944 | tf_op jit(solution)/shard_map/ppermute | solution.py:51
  72.5 2.5 %collective-permute-done.22.refs_1_.refs_8_ = bf16[128,1152]{1,0:T(8,128)(2,1)S(1)} collective-permute-done((bf16[128,1152]{1,0:T(8,128)(2,1)S(1)}, bf16[128,1152]{1,0:T(8,128)(2,1)S(1)}, u32[]{:S(2)}, u32[]{:S(2)}) %collective-permute-start.22) | collective-permute-done | bytes 294944 | tf_op jit(solution)/shard_map/ppermute | solution.py:51
  75.1 1.0 %collective-permute-start.24 = (bf16[64,1152]{1,0:T(8,128)(2,1)S(1)}, bf16[64,1152]{1,0:T(8,128)(2,1)S(1)}, u32[]{:S(2)}, u32[]{:S(2)}) collective-permute-start(bf16[64,1152]{1,0:T(8,128)(2,1)S(1)} %step3.1), channel_id=1, source_target_pairs={{0,32},{1,33},{2,34},{3,35},{4,36},{5,37},{6,38},{7,39},{8,40},{9,... | collective-permute-start | bytes 442376 | tf_op jit(solution)/shard_map/ppermute | solution.py:55
  76.1 1.0 %collective-permute-done.24.refs_10_ = bf16[64,1152]{1,0:T(8,128)(2,1)S(1)} collective-permute-done((bf16[64,1152]{1,0:T(8,128)(2,1)S(1)}, bf16[64,1152]{1,0:T(8,128)(2,1)S(1)}, u32[]{:S(2)}, u32[]{:S(2)}) %collective-permute-start.24) | collective-permute-done | bytes 147488 | tf_op jit(solution)/shard_map/ppermute | solution.py:55
  77.1 1.1 %finish.1 = (f32[64,1152]{1,0:T(8,128)}, f32[64,1152]{1,0:T(8,128)}, f32[1,64]{1,0:T(1,128)}) custom-call(f32[64,1152]{1,0:T(8,128)S(1)} %get-tuple-element.77.refs_0_, f32[8,256]{1,0:T(8,128)S(1)} %get-tuple-element.78.refs_1_, bf16[72,1152]{1,0:T(8,128)(2,1)S(1)} %collective-permute-done.19.refs_2_, bf16[72,1152]{1,0:T(8,128)(2,1)S(1)} %collective-permute-done.20.refs_3_, ...), custom_call_target="tpu_custom_call" | custom-call | flops 1 | bytes 1 | tf_op jit(solution)/shard_map/finish/pallas_call | solution.py:65
  (45 shorter events, 6.3 us)
Async XLA Ops:
  1.8 5.4 %collective-permute-start.5 = (bf16[64,1152]{1,0:T(8,128)(2,1)S(1)}, bf16[64,1152]{1,0:T(8,128)(2,1)S(1)}, u32[]{:S(2)}, u32[]{:S(2)}) collective-permute-start(bf16[64,1152]{1,0:T(8,128)(2,1)S(1)} %get-tuple-element.47.refs_0_), channel_id=1, source_target_pairs={{0,32},{1,33},{2,34},{3,35},{4,36},{5,37},{6,38},{7,39},{8,40},{9,... | collective-permute-start | bytes 442376 | tf_op jit(solution)/shard_map/ppermute | solution.py:55
  5.1 8.9 %collective-permute-start.2 = (bf16[64,1152]{1,0:T(8,128)(2,1)S(1)}, bf16[64,1152]{1,0:T(8,128)(2,1)S(1)}, u32[]{:S(2)}, u32[]{:S(2)}) collective-permute-start(bf16[64,1152]{1,0:T(8,128)(2,1)S(1)} %get-tuple-element.46.refs_0_), channel_id=1, source_target_pairs={{0,192},{1,193},{2,194},{3,195},{4,196},{5,197},{6,198},{7,199},{8... | collective-permute-start | bytes 442376 | tf_op jit(solution)/shard_map/ppermute | solution.py:39
  6.1 7.9 %collective-permute-start.1 = (bf16[64,1152]{1,0:T(8,128)(2,1)S(1)}, bf16[64,1152]{1,0:T(8,128)(2,1)S(1)}, u32[]{:S(2)}, u32[]{:S(2)}) collective-permute-start(bf16[64,1152]{1,0:T(8,128)(2,1)S(1)} %get-tuple-element.46.refs_0_), channel_id=1, source_target_pairs={{0,128},{1,129},{2,130},{3,131},{4,132},{5,133},{6,134},{7,135},{8... | collective-permute-start | bytes 442376 | tf_op jit(solution)/shard_map/ppermute | solution.py:39
  6.5 7.6 %collective-permute-start = (bf16[64,1152]{1,0:T(8,128)(2,1)S(1)}, bf16[64,1152]{1,0:T(8,128)(2,1)S(1)}, u32[]{:S(2)}, u32[]{:S(2)}) collective-permute-start(bf16[64,1152]{1,0:T(8,128)(2,1)S(1)} %get-tuple-element.46.refs_0_), channel_id=1, source_target_pairs={{0,64},{1,65},{2,66},{3,67},{4,68},{5,69},{6,70},{7,71},{8,72},{9,... | collective-permute-start | bytes 442376 | tf_op jit(solution)/shard_map/ppermute | solution.py:39
  7.2 12.9 %collective-permute-start.7 = (bf16[128,1152]{1,0:T(8,128)(2,1)S(1)}, bf16[128,1152]{1,0:T(8,128)(2,1)S(1)}, u32[]{:S(2)}, u32[]{:S(2)}) collective-permute-start(bf16[128,1152]{1,0:T(8,128)(2,1)S(1)} %pair.1.refs_1_), channel_id=1, source_target_pairs={{0,8},{1,9},{2,10},{3,11},{4,12},{5,13},{6,14},{7,15},{8,16},{9,17... | collective-permute-start | bytes 884744 | tf_op jit(solution)/shard_map/ppermute | solution.py:51
  13.3 10.0 %collective-permute-start.6 = (bf16[128,1152]{1,0:T(8,128)(2,1)S(1)}, bf16[128,1152]{1,0:T(8,128)(2,1)S(1)}, u32[]{:S(2)}, u32[]{:S(2)}) collective-permute-start(bf16[128,1152]{1,0:T(8,128)(2,1)S(1)} %pair.1.refs_1_), channel_id=1, source_target_pairs={{0,4},{1,5},{2,6},{3,7},{4,8},{5,9},{6,10},{7,11},{8,12},{9,13},{1... | collective-permute-start | bytes 884744 | tf_op jit(solution)/shard_map/ppermute | solution.py:51
  14.1 15.6 %collective-permute-start.3 = (bf16[264,1152]{1,0:T(8,128)(2,1)S(1)}, bf16[264,1152]{1,0:T(8,128)(2,1)S(1)}, u32[]{:S(2)}, u32[]{:S(2)}) collective-permute-start(bf16[264,1152]{1,0:T(8,128)(2,1)S(1)} %group.1.refs_2_), channel_id=1, source_target_pairs={{0,1},{1,2},{2,3},{3,0},{4,5},{5,6},{6,7},{7,4},{8,9},{9,10},{10,1... | collective-permute-start | bytes 1824776 | tf_op jit(solution)/shard_map/ppermute | solution.py:45
  15.4 16.9 %collective-permute-start.4 = (bf16[264,1152]{1,0:T(8,128)(2,1)S(1)}, bf16[264,1152]{1,0:T(8,128)(2,1)S(1)}, u32[]{:S(2)}, u32[]{:S(2)}) collective-permute-start(bf16[264,1152]{1,0:T(8,128)(2,1)S(1)} %group.1.refs_2_), channel_id=1, source_target_pairs={{0,3},{1,0},{2,1},{3,2},{4,7},{5,4},{6,5},{7,6},{8,11},{9,8},{10,9... | collective-permute-start | bytes 1824776 | tf_op jit(solution)/shard_map/ppermute | solution.py:45
  23.4 9.5 %collective-permute-start.8 = (bf16[256,1152]{1,0:T(8,128)(2,1)S(1)}, bf16[256,1152]{1,0:T(8,128)(2,1)S(1)}, u32[]{:S(2)}, u32[]{:S(2)}) collective-permute-start(bf16[256,1152]{1,0:T(8,128)(2,1)S(1)} %get-tuple-element.48.refs_3_.refs_11_.refs_2_.refs_6_), channel_id=1, source_target_pairs={{0,32},{1,33},{2,34},{3,35},{4,36},{5,37},{6,38},{7,39},{8,40},{9,... | collective-permute-start | bytes 1769480 | tf_op jit(solution)/shard_map/ppermute | solution.py:55
  25.1 11.1 %collective-permute-start.10 = (bf16[128,1152]{1,0:T(8,128)(2,1)S(1)}, bf16[128,1152]{1,0:T(8,128)(2,1)S(1)}, u32[]{:S(2)}, u32[]{:S(2)}) collective-permute-start(bf16[128,1152]{1,0:T(8,128)(2,1)S(1)} %collective-permute-done.7.refs_1_), channel_id=1, source_target_pairs={{0,4},{1,5},{2,6},{3,7},{4,8},{5,9},{6,10},{7,11},{8,12},{9,13},{1... | collective-permute-start | bytes 884744 | tf_op jit(solution)/shard_map/ppermute | solution.py:51
  26.9 14.5 %collective-permute-start.12 = (bf16[264,1152]{1,0:T(8,128)(2,1)S(1)}, bf16[264,1152]{1,0:T(8,128)(2,1)S(1)}, u32[]{:S(2)}, u32[]{:S(2)}) collective-permute-start(bf16[264,1152]{1,0:T(8,128)(2,1)S(1)} %group.1.refs_2_), channel_id=1, source_target_pairs={{0,2},{1,3},{2,0},{3,1},{4,6},{5,7},{6,4},{7,5},{8,10},{9,11},{10,... | collective-permute-start | bytes 1824776 | tf_op jit(solution)/shard_map/ppermute | solution.py:45
  29.7 6.5 %collective-permute-start.9 = (bf16[64,1152]{1,0:T(8,128)(2,1)S(1)}, bf16[64,1152]{1,0:T(8,128)(2,1)S(1)}, u32[]{:S(2)}, u32[]{:S(2)}) collective-permute-start(bf16[64,1152]{1,0:T(8,128)(2,1)S(1)} %get-tuple-element.56), channel_id=1, source_target_pairs={{0,8},{1,9},{2,10},{3,11},{4,12},{5,13},{6,14},{7,15},{8,16},{9,17... | collective-permute-start | bytes 442376 | tf_op jit(solution)/shard_map/ppermute | solution.py:51
  36.2 3.6 %collective-permute-start.11 = (bf16[192,1152]{1,0:T(8,128)(2,1)S(1)}, bf16[192,1152]{1,0:T(8,128)(2,1)S(1)}, u32[]{:S(2)}, u32[]{:S(2)}) collective-permute-start(bf16[192,1152]{1,0:T(8,128)(2,1)S(1)} %far_mine.1.refs_4_.refs_0_), channel_id=1, source_target_pairs={{0,32},{1,33},{2,34},{3,35},{4,36},{5,37},{6,38},{7,39},{8,40},{9,... | collective-permute-start | bytes 1327112 | tf_op jit(solution)/shard_map/ppermute | solution.py:55
  44.2 2.7 %collective-permute-start.14 = (bf16[256,1152]{1,0:T(8,128)(2,1)S(1)}, bf16[256,1152]{1,0:T(8,128)(2,1)S(1)}, u32[]{:S(2)}, u32[]{:S(2)}) collective-permute-start(bf16[256,1152]{1,0:T(8,128)(2,1)S(1)} %get-tuple-element.74), channel_id=1, source_target_pairs={{0,32},{1,33},{2,34},{3,35},{4,36},{5,37},{6,38},{7,39},{8,40},{9,... | collective-permute-start | bytes 1769480 | tf_op jit(solution)/shard_map/ppermute | solution.py:55
  44.7 2.3 %collective-permute-start.13 = (bf16[192,1152]{1,0:T(8,128)(2,1)S(1)}, bf16[192,1152]{1,0:T(8,128)(2,1)S(1)}, u32[]{:S(2)}, u32[]{:S(2)}) collective-permute-start(bf16[192,1152]{1,0:T(8,128)(2,1)S(1)} %get-tuple-element.68.refs_4_), channel_id=1, source_target_pairs={{0,32},{1,33},{2,34},{3,35},{4,36},{5,37},{6,38},{7,39},{8,40},{9,... | collective-permute-start | bytes 1327112 | tf_op jit(solution)/shard_map/ppermute | solution.py:55
  47.0 14.3 %collective-permute-start.18 = (bf16[192,1152]{1,0:T(8,128)(2,1)S(1)}, bf16[192,1152]{1,0:T(8,128)(2,1)S(1)}, u32[]{:S(2)}, u32[]{:S(2)}) collective-permute-start(bf16[192,1152]{1,0:T(8,128)(2,1)S(1)} %step1.1.refs_3_), channel_id=1, source_target_pairs={{0,24},{1,25},{2,26},{3,27},{4,28},{5,29},{6,30},{7,31},{8,0},{9,1... | collective-permute-start | bytes 1327112 | tf_op jit(solution)/shard_map/ppermute | solution.py:51
  48.8 14.2 %collective-permute-start.16 = (bf16[264,1152]{1,0:T(8,128)(2,1)S(1)}, bf16[264,1152]{1,0:T(8,128)(2,1)S(1)}, u32[]{:S(2)}, u32[]{:S(2)}) collective-permute-start(bf16[264,1152]{1,0:T(8,128)(2,1)S(1)} %image2.1.refs_2_), channel_id=1, source_target_pairs={{0,2},{1,3},{2,0},{3,1},{4,6},{5,7},{6,4},{7,5},{8,10},{9,11},{10,... | collective-permute-start | bytes 1824776 | tf_op jit(solution)/shard_map/ppermute | solution.py:45
  50.4 15.5 %collective-permute-start.17 = (bf16[264,1152]{1,0:T(8,128)(2,1)S(1)}, bf16[264,1152]{1,0:T(8,128)(2,1)S(1)}, u32[]{:S(2)}, u32[]{:S(2)}) collective-permute-start(bf16[264,1152]{1,0:T(8,128)(2,1)S(1)} %image3.1.refs_6_), channel_id=1, source_target_pairs={{0,1},{1,2},{2,3},{3,0},{4,5},{5,6},{6,7},{7,4},{8,9},{9,10},{10,1... | collective-permute-start | bytes 1824776 | tf_op jit(solution)/shard_map/ppermute | solution.py:45
  51.5 14.4 %collective-permute-start.15 = (bf16[264,1152]{1,0:T(8,128)(2,1)S(1)}, bf16[264,1152]{1,0:T(8,128)(2,1)S(1)}, u32[]{:S(2)}, u32[]{:S(2)}) collective-permute-start(bf16[264,1152]{1,0:T(8,128)(2,1)S(1)} %image1.1.refs_4_), channel_id=1, source_target_pairs={{0,3},{1,0},{2,1},{3,2},{4,7},{5,4},{6,5},{7,6},{8,11},{9,8},{10,9... | collective-permute-start | bytes 1824776 | tf_op jit(solution)/shard_map/ppermute | solution.py:45
  61.5 11.0 %collective-permute-start.23 = (bf16[128,1152]{1,0:T(8,128)(2,1)S(1)}, bf16[128,1152]{1,0:T(8,128)(2,1)S(1)}, u32[]{:S(2)}, u32[]{:S(2)}) collective-permute-start(bf16[128,1152]{1,0:T(8,128)(2,1)S(1)} %get-tuple-element.84), channel_id=1, source_target_pairs={{0,24},{1,25},{2,26},{3,27},{4,28},{5,29},{6,30},{7,31},{8,0},{9,1... | collective-permute-start | bytes 884744 | tf_op jit(solution)/shard_map/ppermute | solution.py:51
  61.6 13.4 %collective-permute-start.22 = (bf16[128,1152]{1,0:T(8,128)(2,1)S(1)}, bf16[128,1152]{1,0:T(8,128)(2,1)S(1)}, u32[]{:S(2)}, u32[]{:S(2)}) collective-permute-start(bf16[128,1152]{1,0:T(8,128)(2,1)S(1)} %get-tuple-element.76.refs_5_), channel_id=1, source_target_pairs={{0,28},{1,29},{2,30},{3,31},{4,0},{5,1},{6,2},{7,3},{8,4},{9,5},{1... | collective-permute-start | bytes 884744 | tf_op jit(solution)/shard_map/ppermute | solution.py:51
  66.2 10.9 %copy-start = (bf16[64,1152]{1,0:T(8,128)(2,1)S(1)}, bf16[64,1152]{1,0:T(8,128)(2,1)}, u32[]{:S(2)}) copy-start(bf16[64,1152]{1,0:T(8,128)(2,1)} %refs_5_.1) | copy-start | bytes 442372
  66.2 10.9 %copy-start.1 = (bf16[64,1152]{1,0:T(8,128)(2,1)S(1)}, bf16[64,1152]{1,0:T(8,128)(2,1)}, u32[]{:S(2)}) copy-start(bf16[64,1152]{1,0:T(8,128)(2,1)} %refs_11_.1) | copy-start | bytes 442372
  66.2 9.9 %collective-permute-start.19 = (bf16[72,1152]{1,0:T(8,128)(2,1)S(1)}, bf16[72,1152]{1,0:T(8,128)(2,1)S(1)}, u32[]{:S(2)}, u32[]{:S(2)}) collective-permute-start(bf16[72,1152]{1,0:T(8,128)(2,1)S(1)} %get-tuple-element.79), channel_id=1, source_target_pairs={{0,192},{1,193},{2,194},{3,195},{4,196},{5,197},{6,198},{7,199},{8... | collective-permute-start | bytes 497672 | tf_op jit(solution)/shard_map/ppermute | solution.py:39
  68.1 8.0 %collective-permute-start.20 = (bf16[72,1152]{1,0:T(8,128)(2,1)S(1)}, bf16[72,1152]{1,0:T(8,128)(2,1)S(1)}, u32[]{:S(2)}, u32[]{:S(2)}) collective-permute-start(bf16[72,1152]{1,0:T(8,128)(2,1)S(1)} %get-tuple-element.80), channel_id=1, source_target_pairs={{0,128},{1,129},{2,130},{3,131},{4,132},{5,133},{6,134},{7,135},{8... | collective-permute-start | bytes 497672 | tf_op jit(solution)/shard_map/ppermute | solution.py:39
  68.4 7.8 %collective-permute-start.21 = (bf16[72,1152]{1,0:T(8,128)(2,1)S(1)}, bf16[72,1152]{1,0:T(8,128)(2,1)S(1)}, u32[]{:S(2)}, u32[]{:S(2)}) collective-permute-start(bf16[72,1152]{1,0:T(8,128)(2,1)S(1)} %get-tuple-element.81.refs_3_), channel_id=1, source_target_pairs={{0,64},{1,65},{2,66},{3,67},{4,68},{5,69},{6,70},{7,71},{8,72},{9,... | collective-permute-start | bytes 497672 | tf_op jit(solution)/shard_map/ppermute | solution.py:39
  75.1 2.0 %collective-permute-start.24 = (bf16[64,1152]{1,0:T(8,128)(2,1)S(1)}, bf16[64,1152]{1,0:T(8,128)(2,1)S(1)}, u32[]{:S(2)}, u32[]{:S(2)}) collective-permute-start(bf16[64,1152]{1,0:T(8,128)(2,1)S(1)} %step3.1), channel_id=1, source_target_pairs={{0,32},{1,33},{2,34},{3,35},{4,36},{5,37},{6,38},{7,39},{8,40},{9,... | collective-permute-start | bytes 442376 | tf_op jit(solution)/shard_map/ppermute | solution.py:55

commit v12 on v11

--- a/solution.py
+++ b/solution.py
@@ -12,6 +12,7 @@
 NX, NC, NZ, NY = 4, 2, 8, 4
 U = 64
 EPS = 1e-06
+LOG2E = 1.4426950408889634
 F32 = jnp.float32
 BF16 = jnp.bfloat16
 MIB = 1 << 20
@@ -115,10 +116,10 @@
 
 def entry(img, txt, scale, bias, match=None):
     dots = lax.dot_general(img, txt, (((1,), (1,)), ((), ())), preferred_element_type=F32)
-    logits = dots * scale + bias
+    logits = dots * (scale * LOG2E) + bias * LOG2E
     if match is not None:
         logits = jnp.where(match, -logits, logits)
-    e = jnp.exp(logits)
+    e = jnp.exp2(logits)
     u = 1.0 + e
     inv = 1.0 / u
     softplus = jnp.log(u) + (e - (u - 1.0)) * inv

time: 78.3 us -> 78.2 us (level)
  transfers between devices with their start and end apart: 25 -> 25, of which waited for: 9 -> 9; matrix products, arithmetic and copies ran while one was open for 0% -> 0% of each run, Pallas kernels for 14% -> 13%
where the time goes in v12:
time: 78.2 us; the launch traced here: 78.1 us
  starting transfers between devices  35.8 us (46%)
  waiting for transfers between devices  24.6 us (31%)
  Pallas kernels  15.5 us (20%)
  between operations  2.14 us (3%)
    ppermute x7, waiting for transfers between devices, ring(): lax.ppermute(a, AXES, permutation(lambda x, c, z, y: (x, c, z - s if c el...  20.5 us
    pallas_call x23, Pallas kernels, call(): pl.pallas_call(kernel, out_shape=outs, in_specs=[SMEM] * len(scalars) + (...  15.5 us
    ppermute x7, starting transfers between devices, ring(): lax.ppermute(a, AXES, permutation(lambda x, c, z, y: (x, c, z - s if c el...  12.5 us
    ppermute x6, starting transfers between devices, second(): lax.ppermute(a, AXES, permutation(lambda x, c, z, y: (x + s, c, z, y) if...  9.74 us
    ppermute x6, starting transfers between devices, swap(): lax.ppermute(a, AXES, permutation(lambda x, c, z, y: (x, 1 - c, z, y)))  8.88 us
    ppermute x6, starting transfers between devices, first(): lax.ppermute(a, AXES, permutation(lambda x, c, z, y: (x, c, z, y + s) if...  4.63 us
    ppermute x6, waiting for transfers between devices, second(): lax.ppermute(a, AXES, permutation(lambda x, c, z, y: (x + s, c, z, y) if...  2.79 us
  transfers between devices with their start and end apart: 25, of which 9 were waited for; matrix products, arithmetic and copies ran while one was open for 0% of the time, Pallas kernels for 13%

profile of v12, /device:TPU:1, one launch (start us, length us, event | category | flops | bytes accessed | tf_op | source)
XLA Modules:
  0.0 78.1 jit_solution(14845565980202194263)
XLA Ops:
  0.6 1.2 %normalize.1 = (bf16[64,1152]{1,0:T(8,128)(2,1)S(1)}, bf16[64,1152]{1,0:T(8,128)(2,1)S(1)}, f32[64,1]{1,0:T(8,128)S(1)}, f32[64,1]{1,0:T(8,128)S(1)}) custom-call(bf16[64,1152]{1,0:T(8,128)(2,1)} %refs_5_.1, bf16[64,1152]{1,0:T(8,128)(2,1)} %refs_11_.1), custom_call_target="tpu_custom_call" | custom-call | flops 1 | bytes 1 | tf_op jit(solution)/shard_map/normalize/pallas_call | solution.py:66
  1.8 3.3 %collective-permute-start.5 = (bf16[64,1152]{1,0:T(8,128)(2,1)S(1)}, bf16[64,1152]{1,0:T(8,128)(2,1)S(1)}, u32[]{:S(2)}, u32[]{:S(2)}) collective-permute-start(bf16[64,1152]{1,0:T(8,128)(2,1)S(1)} %get-tuple-element.47.refs_0_), channel_id=1, source_target_pairs={{0,32},{1,33},{2,34},{3,35},{4,36},{5,37},{6,38},{7,39},{8,40},{9,... | collective-permute-start | bytes 442376 | tf_op jit(solution)/shard_map/ppermute | solution.py:56
  5.1 1.0 %collective-permute-start.2 = (bf16[64,1152]{1,0:T(8,128)(2,1)S(1)}, bf16[64,1152]{1,0:T(8,128)(2,1)S(1)}, u32[]{:S(2)}, u32[]{:S(2)}) collective-permute-start(bf16[64,1152]{1,0:T(8,128)(2,1)S(1)} %get-tuple-element.46.refs_0_), channel_id=1, source_target_pairs={{0,192},{1,193},{2,194},{3,195},{4,196},{5,197},{6,198},{7,199},{8... | collective-permute-start | bytes 442376 | tf_op jit(solution)/shard_map/ppermute | solution.py:40
  6.5 0.7 collective-permute-start
  7.2 6.1 %collective-permute-start.7 = (bf16[128,1152]{1,0:T(8,128)(2,1)S(1)}, bf16[128,1152]{1,0:T(8,128)(2,1)S(1)}, u32[]{:S(2)}, u32[]{:S(2)}) collective-permute-start(bf16[128,1152]{1,0:T(8,128)(2,1)S(1)} %pair.1.refs_1_), channel_id=1, source_target_pairs={{0,8},{1,9},{2,10},{3,11},{4,12},{5,13},{6,14},{7,15},{8,16},{9,17... | collective-permute-start | bytes 884744 | tf_op jit(solution)/shard_map/ppermute | solution.py:52
  13.3 0.7 collective-permute-start.6
  14.1 1.3 %collective-permute-start.3 = (bf16[264,1152]{1,0:T(8,128)(2,1)S(1)}, bf16[264,1152]{1,0:T(8,128)(2,1)S(1)}, u32[]{:S(2)}, u32[]{:S(2)}) collective-permute-start(bf16[264,1152]{1,0:T(8,128)(2,1)S(1)} %group.1.refs_2_), channel_id=1, source_target_pairs={{0,1},{1,2},{2,3},{3,0},{4,5},{5,6},{6,7},{7,4},{8,9},{9,10},{10,1... | collective-permute-start | bytes 1824776 | tf_op jit(solution)/shard_map/ppermute | solution.py:46
  15.4 1.5 %collective-permute-start.4 = (bf16[264,1152]{1,0:T(8,128)(2,1)S(1)}, bf16[264,1152]{1,0:T(8,128)(2,1)S(1)}, u32[]{:S(2)}, u32[]{:S(2)}) collective-permute-start(bf16[264,1152]{1,0:T(8,128)(2,1)S(1)} %group.1.refs_2_), channel_id=1, source_target_pairs={{0,3},{1,0},{2,1},{3,2},{4,7},{5,4},{6,5},{7,6},{8,11},{9,8},{10,9... | collective-permute-start | bytes 1824776 | tf_op jit(solution)/shard_map/ppermute | solution.py:46
  16.9 3.3 %collective-permute-done.7.refs_1_ = bf16[128,1152]{1,0:T(8,128)(2,1)S(1)} collective-permute-done((bf16[128,1152]{1,0:T(8,128)(2,1)S(1)}, bf16[128,1152]{1,0:T(8,128)(2,1)S(1)}, u32[]{:S(2)}, u32[]{:S(2)}) %collective-permute-start.7) | collective-permute-done | bytes 294944 | tf_op jit(solution)/shard_map/ppermute | solution.py:52
  20.1 3.2 %collective-permute-done.6.refs_0_ = bf16[128,1152]{1,0:T(8,128)(2,1)S(1)} collective-permute-done((bf16[128,1152]{1,0:T(8,128)(2,1)S(1)}, bf16[128,1152]{1,0:T(8,128)(2,1)S(1)}, u32[]{:S(2)}, u32[]{:S(2)}) %collective-permute-start.6) | collective-permute-done | bytes 294944 | tf_op jit(solution)/shard_map/ppermute | solution.py:52
  23.4 1.7 %collective-permute-start.8 = (bf16[256,1152]{1,0:T(8,128)(2,1)S(1)}, bf16[256,1152]{1,0:T(8,128)(2,1)S(1)}, u32[]{:S(2)}, u32[]{:S(2)}) collective-permute-start(bf16[256,1152]{1,0:T(8,128)(2,1)S(1)} %get-tuple-element.48.refs_3_.refs_11_.refs_2_.refs_6_), channel_id=1, source_target_pairs={{0,32},{1,33},{2,34},{3,35},{4,36},{5,37},{6,38},{7,39},{8,40},{9,... | collective-permute-start | bytes 1769480 | tf_op jit(solution)/shard_map/ppermute | solution.py:56
  25.1 1.9 %collective-permute-start.10 = (bf16[128,1152]{1,0:T(8,128)(2,1)S(1)}, bf16[128,1152]{1,0:T(8,128)(2,1)S(1)}, u32[]{:S(2)}, u32[]{:S(2)}) collective-permute-start(bf16[128,1152]{1,0:T(8,128)(2,1)S(1)} %collective-permute-done.7.refs_1_), channel_id=1, source_target_pairs={{0,4},{1,5},{2,6},{3,7},{4,8},{5,9},{6,10},{7,11},{8,12},{9,13},{1... | collective-permute-start | bytes 884744 | tf_op jit(solution)/shard_map/ppermute | solution.py:52
  26.9 2.7 %collective-permute-start.12 = (bf16[264,1152]{1,0:T(8,128)(2,1)S(1)}, bf16[264,1152]{1,0:T(8,128)(2,1)S(1)}, u32[]{:S(2)}, u32[]{:S(2)}) collective-permute-start(bf16[264,1152]{1,0:T(8,128)(2,1)S(1)} %group.1.refs_2_), channel_id=1, source_target_pairs={{0,2},{1,3},{2,0},{3,1},{4,6},{5,7},{6,4},{7,5},{8,10},{9,11},{10,... | collective-permute-start | bytes 1824776 | tf_op jit(solution)/shard_map/ppermute | solution.py:46
  32.9 3.2 %other.1 = (bf16[256,640]{1,0:T(8,128)(2,1)S(1)}, bf16[256,640]{1,0:T(8,128)(2,1)S(1)}, f32[256,128]{1,0:T(8,128)S(1)}, f32[256,128]{1,0:T(8,128)S(1)}, f32[256,...) custom-call(f32[1]{0:T(128)S(6)} %copy.7.refs_0_, f32[1]{0:T(128)S(6)} %copy.8.refs_1_, ...), custom_call_target="tpu_custom_call" | custom-call | flops 1 | bytes 1 | tf_op jit(solution)/shard_map/other/pallas_call | solution.py:66
  36.1 2.2 %collective-permute-start.11 = (bf16[192,1152]{1,0:T(8,128)(2,1)S(1)}, bf16[192,1152]{1,0:T(8,128)(2,1)S(1)}, u32[]{:S(2)}, u32[]{:S(2)}) collective-permute-start(bf16[192,1152]{1,0:T(8,128)(2,1)S(1)} %far_mine.1.refs_4_.refs_0_), channel_id=1, source_target_pairs={{0,32},{1,33},{2,34},{3,35},{4,36},{5,37},{6,38},{7,39},{8,40},{9,... | collective-permute-start | bytes 1327112 | tf_op jit(solution)/shard_map/ppermute | solution.py:56
  38.4 1.2 %near_images.1 = (f32[256,1152]{1,0:T(8,128)S(1)}, f32[256,1152]{1,0:T(8,128)S(1)}) custom-call(bf16[256,640]{1,0:T(8,128)(2,1)S(1)} %get-tuple-element.58.refs_0_, bf16[256,640]{1,0:T(8,128)(2,1)S(1)} %get-tuple-element.59.refs_1_, bf16[256,1152]{1,0:T(8,128)(2,1)S(1)} %get-tuple-element.48.refs_3_.refs_11_.refs_2_.refs_6_, ...), custom_call_target="tpu_custom_call" | custom-call | flops 1 | bytes 1 | tf_op jit(solution)/shard_map/near_images/pallas_call | solution.py:66
  39.9 1.5 %far.1 = (bf16[256,384]{1,0:T(8,128)(2,1)S(1)}, bf16[256,384]{1,0:T(8,128)(2,1)S(1)}, bf16[256,384]{1,0:T(8,128)(2,1)S(1)}, f32[8,768]{1,0:T(8,128)S(1)}) custom-call(f32[1]{0:T(128)S(6)} %copy.7.refs_0_, f32[1]{0:T(128)S(6)} %copy.8.refs_1_, bf16[264,1152]{1,0:T(8,128)(2,1)S(1)} %group.1.refs_2_, ...), custom_call_target="tpu_custom_call" | custom-call | flops 1 | bytes 1 | tf_op jit(solution)/shard_map/far/pallas_call | solution.py:66
  41.4 2.7 %last.1 = (bf16[256,640]{1,0:T(8,128)(2,1)S(1)}, bf16[256,384]{1,0:T(8,128)(2,1)S(1)}, f32[8,256]{1,0:T(8,128)S(1)}, f32[192,1152]{1,0:T(8,128)S(1)}, bf16[192,1...) custom-call(f32[1]{0:T(128)S(6)} %copy.7.refs_0_, ...), custom_call_target="tpu_custom_call" | custom-call | flops 1 | bytes 1 | tf_op jit(solution)/shard_map/last/pallas_call | solution.py:66
  45.7 1.0 %image2.1.refs_2_ = bf16[264,1152]{1,0:T(8,128)(2,1)S(1)} custom-call(bf16[256,640]{1,0:T(8,128)(2,1)S(1)} %get-tuple-element.69.refs_0_, bf16[256,384]{1,0:T(8,128)(2,1)S(1)} %get-tuple-element.70.refs_1_, bf16[256,1152]{1,0:T(8,128)(2,1)S(1)} %get-tuple-element.48.refs_3_.refs_11_.refs_2_.refs_6_, ...), custom_call_target="tpu_custom_call" | custom-call | flops 1 | bytes 1 | tf_op jit(solution)/shard_map/image2/pallas_call | solution.py:66
  46.9 1.8 %collective-permute-start.18 = (bf16[192,1152]{1,0:T(8,128)(2,1)S(1)}, bf16[192,1152]{1,0:T(8,128)(2,1)S(1)}, u32[]{:S(2)}, u32[]{:S(2)}) collective-permute-start(bf16[192,1152]{1,0:T(8,128)(2,1)S(1)} %step1.1.refs_3_), channel_id=1, source_target_pairs={{0,24},{1,25},{2,26},{3,27},{4,28},{5,29},{6,30},{7,31},{8,0},{9,1... | collective-permute-start | bytes 1327112 | tf_op jit(solution)/shard_map/ppermute | solution.py:52
  48.7 1.6 %collective-permute-start.16 = (bf16[264,1152]{1,0:T(8,128)(2,1)S(1)}, bf16[264,1152]{1,0:T(8,128)(2,1)S(1)}, u32[]{:S(2)}, u32[]{:S(2)}) collective-permute-start(bf16[264,1152]{1,0:T(8,128)(2,1)S(1)} %image2.1.refs_2_), channel_id=1, source_target_pairs={{0,2},{1,3},{2,0},{3,1},{4,6},{5,7},{6,4},{7,5},{8,10},{9,11},{10,... | collective-permute-start | bytes 1824776 | tf_op jit(solution)/shard_map/ppermute | solution.py:46
  50.3 1.1 %collective-permute-start.17 = (bf16[264,1152]{1,0:T(8,128)(2,1)S(1)}, bf16[264,1152]{1,0:T(8,128)(2,1)S(1)}, u32[]{:S(2)}, u32[]{:S(2)}) collective-permute-start(bf16[264,1152]{1,0:T(8,128)(2,1)S(1)} %image3.1.refs_6_), channel_id=1, source_target_pairs={{0,1},{1,2},{2,3},{3,0},{4,5},{5,6},{6,7},{7,4},{8,9},{9,10},{10,1... | collective-permute-start | bytes 1824776 | tf_op jit(solution)/shard_map/ppermute | solution.py:46
  51.4 1.6 %collective-permute-start.15 = (bf16[264,1152]{1,0:T(8,128)(2,1)S(1)}, bf16[264,1152]{1,0:T(8,128)(2,1)S(1)}, u32[]{:S(2)}, u32[]{:S(2)}) collective-permute-start(bf16[264,1152]{1,0:T(8,128)(2,1)S(1)} %image1.1.refs_4_), channel_id=1, source_target_pairs={{0,3},{1,0},{2,1},{3,2},{4,7},{5,4},{6,5},{7,6},{8,11},{9,8},{10,9... | collective-permute-start | bytes 1824776 | tf_op jit(solution)/shard_map/ppermute | solution.py:46
  53.5 7.8 %collective-permute-done.18.refs_2_ = bf16[192,1152]{1,0:T(8,128)(2,1)S(1)} collective-permute-done((bf16[192,1152]{1,0:T(8,128)(2,1)S(1)}, bf16[192,1152]{1,0:T(8,128)(2,1)S(1)}, u32[]{:S(2)}, u32[]{:S(2)}) %collective-permute-start.18) | collective-permute-done | bytes 442400 | tf_op jit(solution)/shard_map/ppermute | solution.py:52
  61.5 1.5 %collective-permute-start.22 = (bf16[128,1152]{1,0:T(8,128)(2,1)S(1)}, bf16[128,1152]{1,0:T(8,128)(2,1)S(1)}, u32[]{:S(2)}, u32[]{:S(2)}) collective-permute-start(bf16[128,1152]{1,0:T(8,128)(2,1)S(1)} %get-tuple-element.76.refs_5_), channel_id=1, source_target_pairs={{0,28},{1,29},{2,30},{3,31},{4,0},{5,1},{6,2},{7,3},{8,4},{9,5},{1... | collective-permute-start | bytes 884744 | tf_op jit(solution)/shard_map/ppermute | solution.py:52
  63.0 2.8 %collective-permute-done.17.refs_4_ = bf16[264,1152]{1,0:T(8,128)(2,1)S(1)} collective-permute-done((bf16[264,1152]{1,0:T(8,128)(2,1)S(1)}, bf16[264,1152]{1,0:T(8,128)(2,1)S(1)}, u32[]{:S(2)}, u32[]{:S(2)}) %collective-permute-start.17) | collective-permute-done | bytes 608288 | tf_op jit(solution)/shard_map/ppermute | solution.py:46
  66.1 1.9 %collective-permute-start.19 = (bf16[72,1152]{1,0:T(8,128)(2,1)S(1)}, bf16[72,1152]{1,0:T(8,128)(2,1)S(1)}, u32[]{:S(2)}, u32[]{:S(2)}) collective-permute-start(bf16[72,1152]{1,0:T(8,128)(2,1)S(1)} %get-tuple-element.79), channel_id=1, source_target_pairs={{0,192},{1,193},{2,194},{3,195},{4,196},{5,197},{6,198},{7,199},{8... | collective-permute-start | bytes 497672 | tf_op jit(solution)/shard_map/ppermute | solution.py:40
  68.7 3.7 %collective-permute-done.23.refs_2_.refs_9_ = bf16[128,1152]{1,0:T(8,128)(2,1)S(1)} collective-permute-done((bf16[128,1152]{1,0:T(8,128)(2,1)S(1)}, bf16[128,1152]{1,0:T(8,128)(2,1)S(1)}, u32[]{:S(2)}, u32[]{:S(2)}) %collective-permute-start.23) | collective-permute-done | bytes 294944 | tf_op jit(solution)/shard_map/ppermute | solution.py:52
  72.4 2.5 %collective-permute-done.22.refs_1_.refs_8_ = bf16[128,1152]{1,0:T(8,128)(2,1)S(1)} collective-permute-done((bf16[128,1152]{1,0:T(8,128)(2,1)S(1)}, bf16[128,1152]{1,0:T(8,128)(2,1)S(1)}, u32[]{:S(2)}, u32[]{:S(2)}) %collective-permute-start.22) | collective-permute-done | bytes 294944 | tf_op jit(solution)/shard_map/ppermute | solution.py:52
  75.0 1.0 %collective-permute-start.24 = (bf16[64,1152]{1,0:T(8,128)(2,1)S(1)}, bf16[64,1152]{1,0:T(8,128)(2,1)S(1)}, u32[]{:S(2)}, u32[]{:S(2)}) collective-permute-start(bf16[64,1152]{1,0:T(8,128)(2,1)S(1)} %step3.1), channel_id=1, source_target_pairs={{0,32},{1,33},{2,34},{3,35},{4,36},{5,37},{6,38},{7,39},{8,40},{9,... | collective-permute-start | bytes 442376 | tf_op jit(solution)/shard_map/ppermute | solution.py:56
  76.0 1.0 %collective-permute-done.24.refs_10_ = bf16[64,1152]{1,0:T(8,128)(2,1)S(1)} collective-permute-done((bf16[64,1152]{1,0:T(8,128)(2,1)S(1)}, bf16[64,1152]{1,0:T(8,128)(2,1)S(1)}, u32[]{:S(2)}, u32[]{:S(2)}) %collective-permute-start.24) | collective-permute-done | bytes 147488 | tf_op jit(solution)/shard_map/ppermute | solution.py:56
  77.0 1.1 %finish.1 = (f32[64,1152]{1,0:T(8,128)}, f32[64,1152]{1,0:T(8,128)}, f32[1,64]{1,0:T(1,128)}) custom-call(f32[64,1152]{1,0:T(8,128)S(1)} %get-tuple-element.77.refs_0_, f32[8,256]{1,0:T(8,128)S(1)} %get-tuple-element.78.refs_1_, bf16[72,1152]{1,0:T(8,128)(2,1)S(1)} %collective-permute-done.19.refs_2_, bf16[72,1152]{1,0:T(8,128)(2,1)S(1)} %collective-permute-done.20.refs_3_, ...), custom_call_target="tpu_custom_call" | custom-call | flops 1 | bytes 1 | tf_op jit(solution)/shard_map/finish/pallas_call | solution.py:66
  (45 shorter events, 6.2 us)
Async XLA Ops:
  1.8 5.4 %collective-permute-start.5 = (bf16[64,1152]{1,0:T(8,128)(2,1)S(1)}, bf16[64,1152]{1,0:T(8,128)(2,1)S(1)}, u32[]{:S(2)}, u32[]{:S(2)}) collective-permute-start(bf16[64,1152]{1,0:T(8,128)(2,1)S(1)} %get-tuple-element.47.refs_0_), channel_id=1, source_target_pairs={{0,32},{1,33},{2,34},{3,35},{4,36},{5,37},{6,38},{7,39},{8,40},{9,... | collective-permute-start | bytes 442376 | tf_op jit(solution)/shard_map/ppermute | solution.py:56
  5.1 8.9 %collective-permute-start.2 = (bf16[64,1152]{1,0:T(8,128)(2,1)S(1)}, bf16[64,1152]{1,0:T(8,128)(2,1)S(1)}, u32[]{:S(2)}, u32[]{:S(2)}) collective-permute-start(bf16[64,1152]{1,0:T(8,128)(2,1)S(1)} %get-tuple-element.46.refs_0_), channel_id=1, source_target_pairs={{0,192},{1,193},{2,194},{3,195},{4,196},{5,197},{6,198},{7,199},{8... | collective-permute-start | bytes 442376 | tf_op jit(solution)/shard_map/ppermute | solution.py:40
  6.1 7.9 %collective-permute-start.1 = (bf16[64,1152]{1,0:T(8,128)(2,1)S(1)}, bf16[64,1152]{1,0:T(8,128)(2,1)S(1)}, u32[]{:S(2)}, u32[]{:S(2)}) collective-permute-start(bf16[64,1152]{1,0:T(8,128)(2,1)S(1)} %get-tuple-element.46.refs_0_), channel_id=1, source_target_pairs={{0,128},{1,129},{2,130},{3,131},{4,132},{5,133},{6,134},{7,135},{8... | collective-permute-start | bytes 442376 | tf_op jit(solution)/shard_map/ppermute | solution.py:40
  6.5 7.6 %collective-permute-start = (bf16[64,1152]{1,0:T(8,128)(2,1)S(1)}, bf16[64,1152]{1,0:T(8,128)(2,1)S(1)}, u32[]{:S(2)}, u32[]{:S(2)}) collective-permute-start(bf16[64,1152]{1,0:T(8,128)(2,1)S(1)} %get-tuple-element.46.refs_0_), channel_id=1, source_target_pairs={{0,64},{1,65},{2,66},{3,67},{4,68},{5,69},{6,70},{7,71},{8,72},{9,... | collective-permute-start | bytes 442376 | tf_op jit(solution)/shard_map/ppermute | solution.py:40
  7.2 12.9 %collective-permute-start.7 = (bf16[128,1152]{1,0:T(8,128)(2,1)S(1)}, bf16[128,1152]{1,0:T(8,128)(2,1)S(1)}, u32[]{:S(2)}, u32[]{:S(2)}) collective-permute-start(bf16[128,1152]{1,0:T(8,128)(2,1)S(1)} %pair.1.refs_1_), channel_id=1, source_target_pairs={{0,8},{1,9},{2,10},{3,11},{4,12},{5,13},{6,14},{7,15},{8,16},{9,17... | collective-permute-start | bytes 884744 | tf_op jit(solution)/shard_map/ppermute | solution.py:52
  13.3 10.0 %collective-permute-start.6 = (bf16[128,1152]{1,0:T(8,128)(2,1)S(1)}, bf16[128,1152]{1,0:T(8,128)(2,1)S(1)}, u32[]{:S(2)}, u32[]{:S(2)}) collective-permute-start(bf16[128,1152]{1,0:T(8,128)(2,1)S(1)} %pair.1.refs_1_), channel_id=1, source_target_pairs={{0,4},{1,5},{2,6},{3,7},{4,8},{5,9},{6,10},{7,11},{8,12},{9,13},{1... | collective-permute-start | bytes 884744 | tf_op jit(solution)/shard_map/ppermute | solution.py:52
  14.1 15.6 %collective-permute-start.3 = (bf16[264,1152]{1,0:T(8,128)(2,1)S(1)}, bf16[264,1152]{1,0:T(8,128)(2,1)S(1)}, u32[]{:S(2)}, u32[]{:S(2)}) collective-permute-start(bf16[264,1152]{1,0:T(8,128)(2,1)S(1)} %group.1.refs_2_), channel_id=1, source_target_pairs={{0,1},{1,2},{2,3},{3,0},{4,5},{5,6},{6,7},{7,4},{8,9},{9,10},{10,1... | collective-permute-start | bytes 1824776 | tf_op jit(solution)/shard_map/ppermute | solution.py:46
  15.4 16.9 %collective-permute-start.4 = (bf16[264,1152]{1,0:T(8,128)(2,1)S(1)}, bf16[264,1152]{1,0:T(8,128)(2,1)S(1)}, u32[]{:S(2)}, u32[]{:S(2)}) collective-permute-start(bf16[264,1152]{1,0:T(8,128)(2,1)S(1)} %group.1.refs_2_), channel_id=1, source_target_pairs={{0,3},{1,0},{2,1},{3,2},{4,7},{5,4},{6,5},{7,6},{8,11},{9,8},{10,9... | collective-permute-start | bytes 1824776 | tf_op jit(solution)/shard_map/ppermute | solution.py:46
  23.4 9.4 %collective-permute-start.8 = (bf16[256,1152]{1,0:T(8,128)(2,1)S(1)}, bf16[256,1152]{1,0:T(8,128)(2,1)S(1)}, u32[]{:S(2)}, u32[]{:S(2)}) collective-permute-start(bf16[256,1152]{1,0:T(8,128)(2,1)S(1)} %get-tuple-element.48.refs_3_.refs_11_.refs_2_.refs_6_), channel_id=1, source_target_pairs={{0,32},{1,33},{2,34},{3,35},{4,36},{5,37},{6,38},{7,39},{8,40},{9,... | collective-permute-start | bytes 1769480 | tf_op jit(solution)/shard_map/ppermute | solution.py:56
  25.1 11.0 %collective-permute-start.10 = (bf16[128,1152]{1,0:T(8,128)(2,1)S(1)}, bf16[128,1152]{1,0:T(8,128)(2,1)S(1)}, u32[]{:S(2)}, u32[]{:S(2)}) collective-permute-start(bf16[128,1152]{1,0:T(8,128)(2,1)S(1)} %collective-permute-done.7.refs_1_), channel_id=1, source_target_pairs={{0,4},{1,5},{2,6},{3,7},{4,8},{5,9},{6,10},{7,11},{8,12},{9,13},{1... | collective-permute-start | bytes 884744 | tf_op jit(solution)/shard_map/ppermute | solution.py:52
  26.9 14.4 %collective-permute-start.12 = (bf16[264,1152]{1,0:T(8,128)(2,1)S(1)}, bf16[264,1152]{1,0:T(8,128)(2,1)S(1)}, u32[]{:S(2)}, u32[]{:S(2)}) collective-permute-start(bf16[264,1152]{1,0:T(8,128)(2,1)S(1)} %group.1.refs_2_), channel_id=1, source_target_pairs={{0,2},{1,3},{2,0},{3,1},{4,6},{5,7},{6,4},{7,5},{8,10},{9,11},{10,... | collective-permute-start | bytes 1824776 | tf_op jit(solution)/shard_map/ppermute | solution.py:46
  29.7 6.4 %collective-permute-start.9 = (bf16[64,1152]{1,0:T(8,128)(2,1)S(1)}, bf16[64,1152]{1,0:T(8,128)(2,1)S(1)}, u32[]{:S(2)}, u32[]{:S(2)}) collective-permute-start(bf16[64,1152]{1,0:T(8,128)(2,1)S(1)} %get-tuple-element.56), channel_id=1, source_target_pairs={{0,8},{1,9},{2,10},{3,11},{4,12},{5,13},{6,14},{7,15},{8,16},{9,17... | collective-permute-start | bytes 442376 | tf_op jit(solution)/shard_map/ppermute | solution.py:52
  36.1 3.6 %collective-permute-start.11 = (bf16[192,1152]{1,0:T(8,128)(2,1)S(1)}, bf16[192,1152]{1,0:T(8,128)(2,1)S(1)}, u32[]{:S(2)}, u32[]{:S(2)}) collective-permute-start(bf16[192,1152]{1,0:T(8,128)(2,1)S(1)} %far_mine.1.refs_4_.refs_0_), channel_id=1, source_target_pairs={{0,32},{1,33},{2,34},{3,35},{4,36},{5,37},{6,38},{7,39},{8,40},{9,... | collective-permute-start | bytes 1327112 | tf_op jit(solution)/shard_map/ppermute | solution.py:56
  44.1 2.7 %collective-permute-start.14 = (bf16[256,1152]{1,0:T(8,128)(2,1)S(1)}, bf16[256,1152]{1,0:T(8,128)(2,1)S(1)}, u32[]{:S(2)}, u32[]{:S(2)}) collective-permute-start(bf16[256,1152]{1,0:T(8,128)(2,1)S(1)} %get-tuple-element.74), channel_id=1, source_target_pairs={{0,32},{1,33},{2,34},{3,35},{4,36},{5,37},{6,38},{7,39},{8,40},{9,... | collective-permute-start | bytes 1769480 | tf_op jit(solution)/shard_map/ppermute | solution.py:56
  44.5 2.3 %collective-permute-start.13 = (bf16[192,1152]{1,0:T(8,128)(2,1)S(1)}, bf16[192,1152]{1,0:T(8,128)(2,1)S(1)}, u32[]{:S(2)}, u32[]{:S(2)}) collective-permute-start(bf16[192,1152]{1,0:T(8,128)(2,1)S(1)} %get-tuple-element.68.refs_4_), channel_id=1, source_target_pairs={{0,32},{1,33},{2,34},{3,35},{4,36},{5,37},{6,38},{7,39},{8,40},{9,... | collective-permute-start | bytes 1327112 | tf_op jit(solution)/shard_map/ppermute | solution.py:56
  46.9 14.4 %collective-permute-start.18 = (bf16[192,1152]{1,0:T(8,128)(2,1)S(1)}, bf16[192,1152]{1,0:T(8,128)(2,1)S(1)}, u32[]{:S(2)}, u32[]{:S(2)}) collective-permute-start(bf16[192,1152]{1,0:T(8,128)(2,1)S(1)} %step1.1.refs_3_), channel_id=1, source_target_pairs={{0,24},{1,25},{2,26},{3,27},{4,28},{5,29},{6,30},{7,31},{8,0},{9,1... | collective-permute-start | bytes 1327112 | tf_op jit(solution)/shard_map/ppermute | solution.py:52
  48.7 14.3 %collective-permute-start.16 = (bf16[264,1152]{1,0:T(8,128)(2,1)S(1)}, bf16[264,1152]{1,0:T(8,128)(2,1)S(1)}, u32[]{:S(2)}, u32[]{:S(2)}) collective-permute-start(bf16[264,1152]{1,0:T(8,128)(2,1)S(1)} %image2.1.refs_2_), channel_id=1, source_target_pairs={{0,2},{1,3},{2,0},{3,1},{4,6},{5,7},{6,4},{7,5},{8,10},{9,11},{10,... | collective-permute-start | bytes 1824776 | tf_op jit(solution)/shard_map/ppermute | solution.py:46
  50.3 15.5 %collective-permute-start.17 = (bf16[264,1152]{1,0:T(8,128)(2,1)S(1)}, bf16[264,1152]{1,0:T(8,128)(2,1)S(1)}, u32[]{:S(2)}, u32[]{:S(2)}) collective-permute-start(bf16[264,1152]{1,0:T(8,128)(2,1)S(1)} %image3.1.refs_6_), channel_id=1, source_target_pairs={{0,1},{1,2},{2,3},{3,0},{4,5},{5,6},{6,7},{7,4},{8,9},{9,10},{10,1... | collective-permute-start | bytes 1824776 | tf_op jit(solution)/shard_map/ppermute | solution.py:46
  51.4 14.4 %collective-permute-start.15 = (bf16[264,1152]{1,0:T(8,128)(2,1)S(1)}, bf16[264,1152]{1,0:T(8,128)(2,1)S(1)}, u32[]{:S(2)}, u32[]{:S(2)}) collective-permute-start(bf16[264,1152]{1,0:T(8,128)(2,1)S(1)} %image1.1.refs_4_), channel_id=1, source_target_pairs={{0,3},{1,0},{2,1},{3,2},{4,7},{5,4},{6,5},{7,6},{8,11},{9,8},{10,9... | collective-permute-start | bytes 1824776 | tf_op jit(solution)/shard_map/ppermute | solution.py:46
  61.4 11.0 %collective-permute-start.23 = (bf16[128,1152]{1,0:T(8,128)(2,1)S(1)}, bf16[128,1152]{1,0:T(8,128)(2,1)S(1)}, u32[]{:S(2)}, u32[]{:S(2)}) collective-permute-start(bf16[128,1152]{1,0:T(8,128)(2,1)S(1)} %get-tuple-element.84), channel_id=1, source_target_pairs={{0,24},{1,25},{2,26},{3,27},{4,28},{5,29},{6,30},{7,31},{8,0},{9,1... | collective-permute-start | bytes 884744 | tf_op jit(solution)/shard_map/ppermute | solution.py:52
  61.5 13.4 %collective-permute-start.22 = (bf16[128,1152]{1,0:T(8,128)(2,1)S(1)}, bf16[128,1152]{1,0:T(8,128)(2,1)S(1)}, u32[]{:S(2)}, u32[]{:S(2)}) collective-permute-start(bf16[128,1152]{1,0:T(8,128)(2,1)S(1)} %get-tuple-element.76.refs_5_), channel_id=1, source_target_pairs={{0,28},{1,29},{2,30},{3,31},{4,0},{5,1},{6,2},{7,3},{8,4},{9,5},{1... | collective-permute-start | bytes 884744 | tf_op jit(solution)/shard_map/ppermute | solution.py:52
  66.1 10.9 %copy-start = (bf16[64,1152]{1,0:T(8,128)(2,1)S(1)}, bf16[64,1152]{1,0:T(8,128)(2,1)}, u32[]{:S(2)}) copy-start(bf16[64,1152]{1,0:T(8,128)(2,1)} %refs_5_.1) | copy-start | bytes 442372
  66.1 10.9 %copy-start.1 = (bf16[64,1152]{1,0:T(8,128)(2,1)S(1)}, bf16[64,1152]{1,0:T(8,128)(2,1)}, u32[]{:S(2)}) copy-start(bf16[64,1152]{1,0:T(8,128)(2,1)} %refs_11_.1) | copy-start | bytes 442372
  66.1 9.9 %collective-permute-start.19 = (bf16[72,1152]{1,0:T(8,128)(2,1)S(1)}, bf16[72,1152]{1,0:T(8,128)(2,1)S(1)}, u32[]{:S(2)}, u32[]{:S(2)}) collective-permute-start(bf16[72,1152]{1,0:T(8,128)(2,1)S(1)} %get-tuple-element.79), channel_id=1, source_target_pairs={{0,192},{1,193},{2,194},{3,195},{4,196},{5,197},{6,198},{7,199},{8... | collective-permute-start | bytes 497672 | tf_op jit(solution)/shard_map/ppermute | solution.py:40
  68.0 8.0 %collective-permute-start.20 = (bf16[72,1152]{1,0:T(8,128)(2,1)S(1)}, bf16[72,1152]{1,0:T(8,128)(2,1)S(1)}, u32[]{:S(2)}, u32[]{:S(2)}) collective-permute-start(bf16[72,1152]{1,0:T(8,128)(2,1)S(1)} %get-tuple-element.80), channel_id=1, source_target_pairs={{0,128},{1,129},{2,130},{3,131},{4,132},{5,133},{6,134},{7,135},{8... | collective-permute-start | bytes 497672 | tf_op jit(solution)/shard_map/ppermute | solution.py:40
  68.3 7.7 %collective-permute-start.21 = (bf16[72,1152]{1,0:T(8,128)(2,1)S(1)}, bf16[72,1152]{1,0:T(8,128)(2,1)S(1)}, u32[]{:S(2)}, u32[]{:S(2)}) collective-permute-start(bf16[72,1152]{1,0:T(8,128)(2,1)S(1)} %get-tuple-element.81.refs_3_), channel_id=1, source_target_pairs={{0,64},{1,65},{2,66},{3,67},{4,68},{5,69},{6,70},{7,71},{8,72},{9,... | collective-permute-start | bytes 497672 | tf_op jit(solution)/shard_map/ppermute | solution.py:40
  75.0 2.0 %collective-permute-start.24 = (bf16[64,1152]{1,0:T(8,128)(2,1)S(1)}, bf16[64,1152]{1,0:T(8,128)(2,1)S(1)}, u32[]{:S(2)}, u32[]{:S(2)}) collective-permute-start(bf16[64,1152]{1,0:T(8,128)(2,1)S(1)} %step3.1), channel_id=1, source_target_pairs={{0,32},{1,33},{2,34},{3,35},{4,36},{5,37},{6,38},{7,39},{8,40},{9,... | collective-permute-start | bytes 442376 | tf_op jit(solution)/shard_map/ppermute | solution.py:56
